TPU v7x, 32 devices: a whole 2x2x4 slice. The times are simulated.
32 devices in a mesh: dom: 8 (over z, core), four: 4 (over y, x).
Axes of the slice: x: 2, y: 2, z: 4, core: 2. Of those that a mesh axis runs over, the one named last changes fastest.
Arguments:
- velocity: float32 [3, 128, 18432], P(None, 'four', 'dom'), may hold values from -16 to 16
- partner: int32 [8, 4], P('dom'), may hold values from -1 to 7, as said below
- partner_side: int32 [8, 4], P('dom'), may hold values from -1 to 3, as said below
- flipped: int32 [8, 4], P('dom'), may hold values from 0 to 1, as said below
Outputs:
- new_velocity: float32 [3, 128, 18432], P(None, 'four', 'dom')
- residual: float32 [3, 128, 18432], P(None, 'four', 'dom')
Inputs may be any that keep to these rules, and one draw needn't show every extreme that they name: `partner`: sides are numbered 0 bottom, 1 right, 2 top, 3 left. Gluing is symmetric: if side s of partition p is glued to side s2 of partition q, then side s2 of q is glued to side s of p with the same flipped value. No side is glued to itself, and exactly 4 sides are walls (-1). `partner_side`: -1 exactly where partner is -1. `flipped`: 0 on wall sides.
All inputs are finite; a program needn't handle non-finite values.
Results may differ from a plain program's by a relative error of at most 0.0003.
Values sent between devices are 32-bit elements; how exact they have to be, the bound alone decides.
No kernel may reach another device: no remote copies, remote signals or barrier semaphores. Data moves between devices by JAX's collectives and lax.ppermute only.
A program may use at most 128 MiB of HBM per device.

v0:
```python
import math

import jax
import jax.numpy as jnp
import numpy as np
from jax import lax
from jax.sharding import PartitionSpec as P

ITERS = 4


REACTION = 2.0
WAVE_STEP = 0.0625
HIGHEST = lax.Precision.HIGHEST


def gll_tables():
    inner_near = math.sqrt(1.0 / 3.0 - 2.0 * math.sqrt(7.0) / 21.0)
    inner_far = math.sqrt(1.0 / 3.0 + 2.0 * math.sqrt(7.0) / 21.0)
    points = np.array([-1.0, -inner_far, -inner_near, inner_near, inner_far, 1.0])
    values = (63.0 * points**5 - 70.0 * points**3 + 15.0 * points) / 8.0
    weights = 2.0 / (30.0 * values * values)
    spacing = points[:, None] - points[None, :]
    same_point = spacing == 0.0
    derivative = np.where(
        same_point, 0.0, values[:, None] / (values[None, :] * np.where(same_point, 1.0, spacing))
    )
    end_fix = np.array([-7.5, 0.0, 0.0, 0.0, 0.0, 7.5])
    derivative = derivative + np.eye(6) * end_fix[None, :]
    stiffness = derivative.T @ (weights[:, None] * derivative)
    return (weights, derivative, stiffness)


def block_tables(blocks):
    weights, derivative, stiffness = gll_tables()
    identity = np.eye(blocks)
    weights_line = jnp.asarray(np.tile(weights, blocks), dtype=jnp.float32)
    deriv_block = jnp.asarray(np.kron(identity, derivative), dtype=jnp.float32)
    stiff_block = jnp.asarray(np.kron(identity, stiffness), dtype=jnp.float32)
    return (weights_line, deriv_block, stiff_block)


def fourier_tables(planes):
    plane_ids = jnp.arange(planes, dtype=jnp.int32)
    mode_ids = jnp.arange(planes, dtype=jnp.int32)
    waves = jnp.where(mode_ids < 2, 0, mode_ids // 2)
    phase_index = plane_ids[:, None] * waves[None, :] % planes
    angle = phase_index.astype(jnp.float32) * (2.0 * math.pi / planes)
    is_sine = (mode_ids % 2 == 1) & (mode_ids >= 2)
    basis = jnp.where(is_sine[None, :], jnp.sin(angle), jnp.cos(angle))
    alternating = jnp.where(plane_ids % 2 == 0, 1.0, -1.0).astype(jnp.float32)
    basis = jnp.where(mode_ids[None, :] == 1, alternating[:, None], basis)
    row_scale = jnp.where(mode_ids < 2, 1.0, 2.0).astype(jnp.float32) / planes
    forward = basis.T * row_scale[:, None]
    return (basis, forward)


def helmholtz_rates(mode_ids, planes):
    waves = jnp.where(mode_ids == 0, 0, jnp.where(mode_ids == 1, planes // 2, mode_ids // 2))
    scaled = waves.astype(jnp.float32) * WAVE_STEP
    return REACTION + scaled * scaled


def z_derivative(fields, mode_ids):
    waves = (mode_ids[0::2] // 2).astype(jnp.float32) * WAVE_STEP
    paired = fields.reshape(fields.shape[:1] + (-1, 2) + fields.shape[2:])
    cosine = paired[:, :, 0]
    sine = paired[:, :, 1]
    pair_waves = waves[None, :, None, None]
    result = jnp.stack([pair_waves * sine, -pair_waves * cosine], axis=2)
    return result.reshape(fields.shape)


def nonlinear_term(grids, mode_ids, deriv_block):
    along_x = jnp.matmul(grids[0:3], deriv_block.T, precision=HIGHEST)
    along_y = jnp.matmul(deriv_block, jnp.stack([grids[1], grids[3], grids[4]]), precision=HIGHEST)
    along_z = z_derivative(jnp.stack([grids[2], grids[4], grids[5]]), mode_ids)
    return -(along_x + along_y + along_z)


def pair_products(physical):
    return jnp.stack(
        [
            physical[0] * physical[0],
            physical[0] * physical[1],
            physical[0] * physical[2],
            physical[1] * physical[1],
            physical[1] * physical[2],
            physical[2] * physical[2],
        ]
    )


def junction_flags(side_nodes):
    positions = jnp.arange(side_nodes)
    at_end = (positions % 6 == 5) & (positions < side_nodes - 1)
    at_start = (positions % 6 == 0) & (positions > 0)
    return (at_end, at_start)


def dss_local(field):
    side_nodes = field.shape[-1]
    at_end, at_start = junction_flags(side_nodes)
    zero_col = jnp.zeros(field.shape[:-1] + (1,), field.dtype)
    from_right = jnp.concatenate([field[..., 1:], zero_col], axis=-1)
    from_left = jnp.concatenate([zero_col, field[..., :-1]], axis=-1)
    field = field + jnp.where(at_end, from_right, 0.0) + jnp.where(at_start, from_left, 0.0)
    zero_row = jnp.zeros(field.shape[:-2] + (1, side_nodes), field.dtype)
    from_below = jnp.concatenate([field[..., 1:, :], zero_row], axis=-2)
    from_above = jnp.concatenate([zero_row, field[..., :-1, :]], axis=-2)
    field = (
        field
        + jnp.where(at_end[:, None], from_below, 0.0)
        + jnp.where(at_start[:, None], from_above, 0.0)
    )
    return field


def side_values(grid):
    return jnp.stack(
        [grid[..., 0, :], grid[..., :, -1], grid[..., -1, :], grid[..., :, 0]], axis=-2
    )


def add_sides(grid, incoming):
    grid = grid.at[..., 0, :].add(incoming[..., 0, :])
    grid = grid.at[..., :, -1].add(incoming[..., 1, :])
    grid = grid.at[..., -1, :].add(incoming[..., 2, :])
    grid = grid.at[..., :, 0].add(incoming[..., 3, :])
    return grid


def edge_tables(partner_rows, side_nodes):
    positions = jnp.arange(side_nodes)
    rows_at = jnp.broadcast_to(positions[:, None], (side_nodes, side_nodes))
    cols_at = jnp.broadcast_to(positions[None, :], (side_nodes, side_nodes))
    on_side = jnp.stack(
        [rows_at == 0, cols_at == side_nodes - 1, rows_at == side_nodes - 1, cols_at == 0]
    )
    is_glued = (partner_rows >= 0)[..., :, None, None]
    wall_node = jnp.any(on_side & jnp.logical_not(is_glued), axis=-3)
    glued_node = jnp.any(on_side & is_glued, axis=-3)
    corner = ((rows_at == 0) | (rows_at == side_nodes - 1)) & (
        (cols_at == 0) | (cols_at == side_nodes - 1)
    )
    kept_node = jnp.logical_not(wall_node | corner)
    dirichlet_mask = kept_node.astype(jnp.float32)
    at_end, at_start = junction_flags(side_nodes)
    copies = jnp.where(at_end | at_start, 2.0, 1.0).astype(jnp.float32)
    weight = dirichlet_mask / (copies[:, None] * copies[None, :] * jnp.where(glued_node, 2.0, 1.0))
    return (dirichlet_mask, weight)


def apply_element(field, rates, weights_line, stiff_block):
    rows_part = jnp.matmul(stiff_block, field, precision=HIGHEST) * weights_line[None, :]
    cols_part = jnp.matmul(field, stiff_block, precision=HIGHEST) * weights_line[:, None]
    return rows_part + cols_part + rates * (weights_line[:, None] * weights_line[None, :]) * field


def inner_terms(weight, first_field, second_field):
    return jnp.sum(weight * first_field * second_field, axis=(-2, -1))


def shards(velocity, partner, partner_side, flipped):
    modes_here = velocity.shape[1]
    side_nodes = math.isqrt(velocity.shape[2])
    blocks = side_nodes // 6
    planes_all = modes_here * lax.axis_size("four")
    weights_line, deriv_block, stiff_block = block_tables(blocks)
    basis, forward = fourier_tables(planes_all)
    mode_ids = lax.axis_index("four") * modes_here + jnp.arange(modes_here, dtype=jnp.int32)
    mass_grid = weights_line[:, None] * weights_line[None, :]
    spread = lax.all_to_all(velocity, "four", split_axis=2, concat_axis=1, tiled=True)
    physical = jnp.einsum("jm,cmn->cjn", basis, spread, precision=HIGHEST)
    modal = jnp.einsum("mj,cjn->cmn", forward, pair_products(physical), precision=HIGHEST)
    returned = lax.all_to_all(modal, "four", split_axis=1, concat_axis=2, tiled=True)
    grids = returned.reshape(6, modes_here, side_nodes, side_nodes)
    nonlinear = nonlinear_term(grids, mode_ids, deriv_block)
    current = velocity.reshape(3, modes_here, side_nodes, side_nodes)
    local_rhs = mass_grid * (REACTION * current + nonlinear)
    partner_row = partner[0]
    side_row = partner_side[0]
    flip_row = flipped[0]
    dirichlet_mask, weight = edge_tables(partner, side_nodes)
    rates = helmholtz_rates(mode_ids, planes_all)[:, None, None]

    def assemble(field):
        joined = dss_local(field)
        edges = side_values(joined)
        leading = edges.shape[:2]
        packed = edges.reshape((1,) + leading + (4 * side_nodes,))
        piece = lax.all_gather(packed, "dom", axis=0, tiled=True)
        row_count = piece.shape[0]
        collected = []
        for side_index in range(4):
            offset_row = partner_row[side_index]
            inside = (offset_row >= 0) & (offset_row < row_count)
            chosen = lax.dynamic_index_in_dim(
                piece, jnp.clip(offset_row, 0, row_count - 1), 0, keepdims=False
            )
            segment = lax.dynamic_slice_in_dim(
                chosen, jnp.maximum(side_row[side_index], 0) * side_nodes, side_nodes, axis=2
            )
            segment = jnp.where(flip_row[side_index] == 1, segment[..., ::-1], segment)
            collected.append(jnp.where(inside, segment, 0.0))
        incoming = jnp.zeros(edges.shape, jnp.float32) + jnp.stack(collected, axis=2)
        return add_sides(joined, incoming)

    def operate(field):
        return dirichlet_mask * assemble(apply_element(field, rates, weights_line, stiff_block))

    def squares(residual):
        return lax.psum(inner_terms(weight, residual, residual), "dom")[..., None, None]

    def solve(rhs):
        solution = jnp.zeros_like(rhs)
        residual = rhs
        direction = rhs
        norm_now = squares(residual)
        for iteration in range(ITERS):
            image = operate(direction)
            alpha = (
                norm_now / lax.psum(inner_terms(weight, direction, image), "dom")[..., None, None]
            )
            solution = solution + alpha * direction
            residual = residual - alpha * image
            norm_next = squares(residual)
            direction = residual + norm_next / norm_now * direction
            norm_now = norm_next
        return (solution, residual)

    rhs_all = dirichlet_mask * assemble(local_rhs)
    results_each = [solve(rhs_all[component : component + 1]) for component in range(3)]
    solution = jnp.concatenate([outcome[0] for outcome in results_each], axis=0)
    residual = jnp.concatenate([outcome[1] for outcome in results_each], axis=0)
    new_velocity = solution.reshape(3, modes_here, side_nodes * side_nodes)
    return (new_velocity, residual.reshape(3, modes_here, side_nodes * side_nodes))


def solution(mesh):
    return jax.shard_map(
        shards,
        mesh=mesh,
        in_specs=(P(None, "four", "dom"), P("dom", None), P("dom", None), P("dom", None)),
        out_specs=(P(None, "four", "dom"), P(None, "four", "dom")),
        check_vma=False,
    )
```

profile of v0, /device:TPU:0, one launch (start us, length us, event | category | flops | bytes accessed | tf_op | source)
XLA Modules:
  0.0 1019.3 jit_solution(3872231014934521346)
XLA Ops:
  0.6 4.7 copy.6838
  5.3 5.6 reshape.2898
  10.9 5.2 all-to-all-start
  35.5 5.1 reshape.2899
  40.7 3.6 copy.6839
  50.6 4.4 all-to-all-start.1
  57.1 3.5 mul.537
  63.8 21.1 %all-to-all-done.1 = f32[6,128,576]{2,0,1:T(8,128)S(1)} async-done(((f32[6,128,576]{2,0,1:T(8,128)}), f32[6,128,576]{2,0,1:T(8,128)S(1)}, u32[]{:S(2)}, u32[]{:S(2)}) %all-to-all-start.1) | async-done | bytes 1769504 | tf_op jit(solution)/shard_map/all_to_all | solution.py:176
  108.9 3.5 copy.6853
  112.4 8.1 fusion.218
  120.6 3.8 fusion.9
  135.5 15.8 %all_gather.39 = f32[8,3,32,192]{3,2,1,0:T(8,128)S(1)} all-gather(f32[1,3,32,192]{3,2,1,0:T(8,128)S(1)} %reshape.2780), channel_id=1, replica_groups=mesh['dom'=8,'four'=4] {'dom'}, dimensions={0}, use_global_device_ids=true | all-gather | bytes 663552 | tf_op jit(solution)/shard_map/all_gather | solution.py:192
  154.0 12.7 %scatter-add.174 = f32[3,32,48,48]{2,3,1,0:T(8,128)S(1)} dynamic-update-slice(f32[3,32,48,48]{2,3,1,0:T(8,128)S(1)} %select_add_fusion, f32[3,32,1,48]{2,3,1,0:T(8,128)} %copy.6860, s32[]{:T(128)} %constant.2451.clone.1, s32[]{:T(128)} %constant.2451.clone.1, s32[]{:T(128)} %constant.2451.clone.1, s32[]{:T(128)} %constant.2451.clone.1) | dynamic-update-slice | bytes 36868 | tf_op jit(solution)/shard_map/scatter-add | solution.py:126
  176.3 19.5 %scatter-add.176 = f32[3,32,48,48]{2,3,1,0:T(8,128)S(1)} dynamic-update-slice(f32[3,32,48,48]{2,3,1,0:T(8,128)S(1)} %scatter-add.175, f32[3,32,1,48]{2,3,1,0:T(8,128)} %copy.6864, s32[]{:T(128)} %constant.2451.clone.1, s32[]{:T(128)} %constant.2451.clone.1, s32[]{:T(128)} %constant.2452.clone.1, s32[]{:T(128)} %constant.2451.clone.1) | dynamic-update-slice | bytes 36868 | tf_op jit(solution)/shard_map/scatter-add | solution.py:128
  211.7 3.4 pad_maximum_fusion.3
  216.8 14.7 %all_gather.40 = f32[8,1,32,192]{3,2,1,0:T(8,128)S(1)} all-gather(f32[1,1,32,192]{3,2,1,0:T(8,128)S(1)} %reshape.2786), channel_id=1, replica_groups=mesh['dom'=8,'four'=4] {'dom'}, dimensions={0}, use_global_device_ids=true | all-gather | bytes 221184 | tf_op jit(solution)/shard_map/all_gather | solution.py:192
  241.8 5.3 scatter-add.184
  247.6 17.0 %all-reduce.57 = (f32[1,32]{1,0:T(1,128)S(1)}, f32[1,32]{1,0:T(1,128)S(1)}) all-reduce(f32[1,32]{1,0:T(1,128)S(1)} %bitcast.716, f32[1,32]{1,0:T(1,128)S(1)} %bitcast.715), channel_id=1, replica_groups=mesh['dom'=8,'four'=4] {'dom'}, use_global_device_ids=true, to_apply=%region_3.4 | all-reduce | flops 64 | bytes 512 | tf_op jit(solution)/shard_map/psum | solution.py:213
  265.2 13.6 %psum.170 = f32[1,32]{1,0:T(1,128)S(1)} all-reduce(f32[1,32]{1,0:T(1,128)S(1)} %bitcast.723), channel_id=1, replica_groups=mesh['dom'=8,'four'=4] {'dom'}, use_global_device_ids=true, to_apply=%region_7.8 | all-reduce | flops 32 | bytes 256 | tf_op jit(solution)/shard_map/psum | solution.py:213
  298.2 3.6 pad_maximum_fusion.4
  303.5 14.2 %all_gather.41 = f32[8,1,32,192]{3,2,1,0:T(8,128)S(1)} all-gather(f32[1,1,32,192]{3,2,1,0:T(8,128)S(1)} %reshape.2792), channel_id=1, replica_groups=mesh['dom'=8,'four'=4] {'dom'}, dimensions={0}, use_global_device_ids=true | all-gather | bytes 221184 | tf_op jit(solution)/shard_map/all_gather | solution.py:192
  330.7 5.8 scatter-add.190
  336.5 3.4 pad_maximum_fusion.7
  341.6 14.2 %all_gather.44 = f32[8,1,32,192]{3,2,1,0:T(8,128)S(1)} all-gather(f32[1,1,32,192]{3,2,1,0:T(8,128)S(1)} %reshape.2810), channel_id=1, replica_groups=mesh['dom'=8,'four'=4] {'dom'}, dimensions={0}, use_global_device_ids=true | all-gather | bytes 221184 | tf_op jit(solution)/shard_map/all_gather | solution.py:192
  366.2 5.3 scatter-add.210
  374.9 13.9 %psum.171 = f32[1,32]{1,0:T(1,128)S(1)} all-reduce(f32[1,32]{1,0:T(1,128)S(1)} %bitcast.719), channel_id=1, replica_groups=mesh['dom'=8,'four'=4] {'dom'}, use_global_device_ids=true, to_apply=%region_9.10 | all-reduce | flops 32 | bytes 256 | tf_op jit(solution)/shard_map/psum | solution.py:223
  391.4 13.8 %psum.172 = f32[1,32]{1,0:T(1,128)S(1)} all-reduce(f32[1,32]{1,0:T(1,128)S(1)} %bitcast.717), channel_id=1, replica_groups=mesh['dom'=8,'four'=4] {'dom'}, use_global_device_ids=true, to_apply=%region_11.12 | all-reduce | flops 32 | bytes 256 | tf_op jit(solution)/shard_map/psum | solution.py:213
  421.1 3.4 pad_maximum_fusion.10
  426.2 14.2 %all_gather.48 = f32[8,1,32,192]{3,2,1,0:T(8,128)S(1)} all-gather(f32[1,1,32,192]{3,2,1,0:T(8,128)S(1)} %reshape.2834), channel_id=1, replica_groups=mesh['dom'=8,'four'=4] {'dom'}, dimensions={0}, use_global_device_ids=true | all-gather | bytes 221184 | tf_op jit(solution)/shard_map/all_gather | solution.py:192
  444.9 3.6 scatter-add.234
  453.9 5.8 scatter-add.236
  459.8 3.5 pad_maximum_fusion.5
  464.9 14.2 %all_gather.42 = f32[8,1,32,192]{3,2,1,0:T(8,128)S(1)} all-gather(f32[1,1,32,192]{3,2,1,0:T(8,128)S(1)} %reshape.2798), channel_id=1, replica_groups=mesh['dom'=8,'four'=4] {'dom'}, dimensions={0}, use_global_device_ids=true | all-gather | bytes 221184 | tf_op jit(solution)/shard_map/all_gather | solution.py:192
  489.5 5.3 scatter-add.196
  498.4 13.9 %all-reduce.56 = (f32[1,32]{1,0:T(1,128)S(1)}, f32[1,32]{1,0:T(1,128)S(1)}, f32[1,32]{1,0:T(1,128)S(1)}) all-reduce(f32[1,32]{1,0:T(1,128)S(1)} %bitcast.712, f32[1,32]{1,0:T(1,128)S(1)} %bitcast.711, f32[1,32]{1,0:T(1,128)S(1)} %bitcast.713), channel_id=1, replica_groups=mesh['dom'=8,'four'=4] {'dom'}, use_global_device_ids=true, to_apply=%region_35.36 | all-reduce | flops 96 | bytes 768 | tf_op jit(solution)/shard_map/psum | solution.py:213
  512.3 3.4 fusion.20
  515.7 13.8 %all-reduce.55 = (f32[1,32]{1,0:T(1,128)S(1)}, f32[1,32]{1,0:T(1,128)S(1)}, f32[1,32]{1,0:T(1,128)S(1)}, f32[1,32]{1,0:T(1,128)S(1)}) all-reduce(f32[1,32]{1,0:T(1,128)S(1)} %bitcast.704, f32[1,32]{1,0:T(1,128)S(1)} %bitcast.703, f32[1,32]{1,0:T(1,128)S(1)} %bitcast.702, ...), channel_id=1, replica_groups=mesh['dom'=8,'four'=4] {'dom'}, use_global_device_ids=true, to_apply=%region_39.40 | all-reduce | flops 128 | bytes 1024 | tf_op jit(solution)/shard_map/psum | solution.py:213
  549.7 3.4 pad_maximum_fusion.11
  554.7 14.4 %all_gather.49 = f32[8,1,32,192]{3,2,1,0:T(8,128)S(1)} all-gather(f32[1,1,32,192]{3,2,1,0:T(8,128)S(1)} %reshape.2840), channel_id=1, replica_groups=mesh['dom'=8,'four'=4] {'dom'}, dimensions={0}, use_global_device_ids=true | all-gather | bytes 221184 | tf_op jit(solution)/shard_map/all_gather | solution.py:192
  582.3 5.8 scatter-add.244
  588.1 3.5 pad_maximum_fusion.6
  593.3 14.2 %all_gather.43 = f32[8,1,32,192]{3,2,1,0:T(8,128)S(1)} all-gather(f32[1,1,32,192]{3,2,1,0:T(8,128)S(1)} %reshape.2804), channel_id=1, replica_groups=mesh['dom'=8,'four'=4] {'dom'}, dimensions={0}, use_global_device_ids=true | all-gather | bytes 221184 | tf_op jit(solution)/shard_map/all_gather | solution.py:192
  618.1 5.3 scatter-add.204
  627.2 14.3 %psum.178 = f32[1,32]{1,0:T(1,128)S(1)} all-reduce(f32[1,32]{1,0:T(1,128)S(1)} %bitcast.720), channel_id=1, replica_groups=mesh['dom'=8,'four'=4] {'dom'}, use_global_device_ids=true, to_apply=%region_23.24 | all-reduce | flops 32 | bytes 256 | tf_op jit(solution)/shard_map/psum | solution.py:213
  651.9 3.4 pad_maximum_fusion.8
  657.0 14.2 %all_gather.45 = f32[8,1,32,192]{3,2,1,0:T(8,128)S(1)} all-gather(f32[1,1,32,192]{3,2,1,0:T(8,128)S(1)} %reshape.2816), channel_id=1, replica_groups=mesh['dom'=8,'four'=4] {'dom'}, dimensions={0}, use_global_device_ids=true | all-gather | bytes 221184 | tf_op jit(solution)/shard_map/all_gather | solution.py:192
  684.3 5.8 scatter-add.216
  693.2 13.9 %psum.179 = f32[1,32]{1,0:T(1,128)S(1)} all-reduce(f32[1,32]{1,0:T(1,128)S(1)} %bitcast.724), channel_id=1, replica_groups=mesh['dom'=8,'four'=4] {'dom'}, use_global_device_ids=true, to_apply=%region_25.26 | all-reduce | flops 32 | bytes 256 | tf_op jit(solution)/shard_map/psum | solution.py:223
  709.8 13.8 %psum.180 = f32[1,32]{1,0:T(1,128)S(1)} all-reduce(f32[1,32]{1,0:T(1,128)S(1)} %bitcast.718), channel_id=1, replica_groups=mesh['dom'=8,'four'=4] {'dom'}, use_global_device_ids=true, to_apply=%region_27.28 | all-reduce | flops 32 | bytes 256 | tf_op jit(solution)/shard_map/psum | solution.py:213
  741.1 14.2 %all_gather.46 = f32[8,1,32,192]{3,2,1,0:T(8,128)S(1)} all-gather(f32[1,1,32,192]{3,2,1,0:T(8,128)S(1)} %reshape.2822), channel_id=1, replica_groups=mesh['dom'=8,'four'=4] {'dom'}, dimensions={0}, use_global_device_ids=true | all-gather | bytes 221184 | tf_op jit(solution)/shard_map/all_gather | solution.py:192
  767.4 5.8 scatter-add.224
  776.2 13.9 %all-reduce.54 = (f32[1,32]{1,0:T(1,128)S(1)}, f32[1,32]{1,0:T(1,128)S(1)}) all-reduce(f32[1,32]{1,0:T(1,128)S(1)} %bitcast.706, f32[1,32]{1,0:T(1,128)S(1)} %bitcast.721), channel_id=1, replica_groups=mesh['dom'=8,'four'=4] {'dom'}, use_global_device_ids=true, to_apply=%region_41.42 | all-reduce | flops 64 | bytes 512 | tf_op jit(solution)/shard_map/psum | solution.py:223
  793.5 13.9 %all-reduce.53 = (f32[1,32]{1,0:T(1,128)S(1)}, f32[1,32]{1,0:T(1,128)S(1)}) all-reduce(f32[1,32]{1,0:T(1,128)S(1)} %bitcast.709, f32[1,32]{1,0:T(1,128)S(1)} %bitcast.708), channel_id=1, replica_groups=mesh['dom'=8,'four'=4] {'dom'}, use_global_device_ids=true, to_apply=%region_43.44 | all-reduce | flops 64 | bytes 512 | tf_op jit(solution)/shard_map/psum | solution.py:213
  827.4 3.4 pad_maximum_fusion.12
  832.5 14.2 %all_gather.50 = f32[8,1,32,192]{3,2,1,0:T(8,128)S(1)} all-gather(f32[1,1,32,192]{3,2,1,0:T(8,128)S(1)} %reshape.2846), channel_id=1, replica_groups=mesh['dom'=8,'four'=4] {'dom'}, dimensions={0}, use_global_device_ids=true | all-gather | bytes 221184 | tf_op jit(solution)/shard_map/all_gather | solution.py:192
  859.8 5.8 scatter-add.250
  871.9 14.2 %all_gather.47 = f32[8,1,32,192]{3,2,1,0:T(8,128)S(1)} all-gather(f32[1,1,32,192]{3,2,1,0:T(8,128)S(1)} %reshape.2828), channel_id=1, replica_groups=mesh['dom'=8,'four'=4] {'dom'}, dimensions={0}, use_global_device_ids=true | all-gather | bytes 221184 | tf_op jit(solution)/shard_map/all_gather | solution.py:192
  898.6 4.8 scatter-add.230
  909.9 13.9 %psum.189 = f32[1,32]{1,0:T(1,128)S(1)} all-reduce(f32[1,32]{1,0:T(1,128)S(1)} %bitcast.722), channel_id=1, replica_groups=mesh['dom'=8,'four'=4] {'dom'}, use_global_device_ids=true, to_apply=%region_45.46 | all-reduce | flops 32 | bytes 256 | tf_op jit(solution)/shard_map/psum | solution.py:223
  928.2 13.8 %psum.190 = f32[1,32]{1,0:T(1,128)S(1)} all-reduce(f32[1,32]{1,0:T(1,128)S(1)} %bitcast.714), channel_id=1, replica_groups=mesh['dom'=8,'four'=4] {'dom'}, use_global_device_ids=true, to_apply=%region_47.48 | all-reduce | flops 32 | bytes 256 | tf_op jit(solution)/shard_map/psum | solution.py:213
  955.6 14.2 %all_gather.51 = f32[8,1,32,192]{3,2,1,0:T(8,128)S(1)} all-gather(f32[1,1,32,192]{3,2,1,0:T(8,128)S(1)} %reshape.2852), channel_id=1, replica_groups=mesh['dom'=8,'four'=4] {'dom'}, dimensions={0}, use_global_device_ids=true | all-gather | bytes 221184 | tf_op jit(solution)/shard_map/all_gather | solution.py:192
  978.1 5.3 scatter-add.256
  985.3 14.1 %all-reduce.52 = (f32[1,32]{1,0:T(1,128)S(1)}, f32[1,32]{1,0:T(1,128)S(1)}, f32[1,32]{1,0:T(1,128)S(1)}) all-reduce(f32[1,32]{1,0:T(1,128)S(1)} %bitcast.710, f32[1,32]{1,0:T(1,128)S(1)} %bitcast.707, f32[1,32]{1,0:T(1,128)S(1)} %bitcast.705), channel_id=1, replica_groups=mesh['dom'=8,'four'=4] {'dom'}, use_global_device_ids=true, to_apply=%region_49.50 | all-reduce | flops 96 | bytes 768 | tf_op jit(solution)/shard_map/psum | solution.py:223
  1003.4 3.4 multiply_subtract_fusion.1
  (571 shorter events, 410.2 us)
Async XLA Ops:
  5.3 10.8 %copy-start.43 = (s32[1,4]{1,0:T(1,128)S(1)}, s32[1,4]{1,0:T(1,128)}, u32[]{:S(2)}) copy-start(s32[1,4]{1,0:T(1,128)} %param.112) | copy-start | bytes 52
  5.3 10.8 %copy-start.42 = (s32[1,4]{1,0:T(1,128)S(1)}, s32[1,4]{1,0:T(1,128)}, u32[]{:S(2)}) copy-start(s32[1,4]{1,0:T(1,128)} %param.113) | copy-start | bytes 52
  5.3 23.0 %copy-start.44 = (s32[1,4]{1,0:T(1,128)S(1)}, s32[1,4]{1,0:T(1,128)}, u32[]{:S(2)}) copy-start(s32[1,4]{1,0:T(1,128)} %param.114) | copy-start | bytes 52
  10.9 20.9 %all-to-all-start = ((f32[4,1,55296]{2,1,0:T(1,128)}), f32[4,1,55296]{2,1,0:T(1,128)S(1)}, u32[]{:S(2)}, u32[]{:S(2)}) async-start(f32[4,1,55296]{2,1,0:T(1,128)} %reshape.2898), calls=%async_computation | async-start | bytes 1769472 | tf_op jit(solution)/shard_map/all_to_all | solution.py:173
  50.6 34.3 %all-to-all-start.1 = ((f32[6,128,576]{2,0,1:T(8,128)}), f32[6,128,576]{2,0,1:T(8,128)S(1)}, u32[]{:S(2)}, u32[]{:S(2)}) async-start(f32[6,128,576]{2,0,1:T(8,128)} %copy.6841), calls=%async_computation.1 | async-start | bytes 5242880 | tf_op jit(solution)/shard_map/all_to_all | solution.py:176
  60.6 3.2 copy-start.40
  104.5 2.5 copy-start.38
  108.9 3.5 copy-start.41
  112.4 8.1 copy-start.23
  112.4 8.1 copy-start.24
  198.5 0.7 copy-start.33
  199.2 4.2 copy-start.21
  203.4 0.7 copy-start.32
  203.6 79.7 %copy-start.17 = (f32[1,32,48,48]{2,3,1,0:T(8,128)}, f32[1,32,48,48]{2,3,1,0:T(8,128)S(1)}, u32[]{:S(2)}) copy-start(f32[1,32,48,48]{2,3,1,0:T(8,128)S(1)} %get-tuple-element.673) | copy-start | bytes 884740
  279.1 4.2 copy-start.6
  280.9 2.4 copy-start.35
  280.9 2.4 copy-start.36
  289.0 3.0 copy-start.3
  405.2 3.5 copy-start.22
  406.9 2.9 copy-start.8
  412.0 3.0 copy-start
  531.1 5.9 copy-start.20
  531.1 2.6 copy-start.31
  535.3 3.1 copy-start.9
  540.5 2.9 copy-start.1
  641.9 2.6 copy-start.5
  646.4 0.9 copy-start.4
  725.1 2.6 copy-start.16
  764.8 25.4 %copy-start.2 = (f32[1,32,48,48]{2,1,3,0:T(8,128)S(1)}, f32[1,32,48,48]{2,1,3,0:T(8,128)}, u32[]{:S(2)}) copy-start(f32[1,32,48,48]{2,1,3,0:T(8,128)} %constant_dynamic-update-slice_fusion.6) | copy-start | bytes 884740
  793.5 16.6 %copy-start.26 = (f32[1,32,48,48]{2,1,3,0:T(8,128)S(1)}, f32[1,32,48,48]{2,1,3,0:T(8,128)}, u32[]{:S(2)}) copy-start(f32[1,32,48,48]{2,1,3,0:T(8,128)} %get-tuple-element.663) | copy-start | bytes 884740
  810.1 2.5 copy-start.10
  810.1 2.5 copy-start.28
  811.0 5.5 copy-start.18
  820.4 2.0 copy-start.13
  821.0 2.9 copy-start.11
  923.8 2.9 copy-start.29
  923.8 2.9 copy-start.30
  943.2 2.7 copy-start.14
  975.7 23.7 %copy-start.7 = (f32[1,32,48,48]{2,1,3,0:T(8,128)S(1)}, f32[1,32,48,48]{2,1,3,0:T(8,128)}, u32[]{:S(2)}) copy-start(f32[1,32,48,48]{2,1,3,0:T(8,128)} %copy-done.6) | copy-start | bytes 884740
  999.4 3.9 copy-start.12
  999.4 3.9 copy-start.15
  999.5 3.9 copy-start.19
  999.5 3.9 copy-start.25
  999.5 3.9 copy-start.27
  999.5 3.9 copy-start.34
  999.5 3.9 copy-start.37
  1009.0 3.2 copy-start.39
where the time goes:
time: 1030 us; the launch traced here: 1020 us
  blocking collectives  385 us (37%)
  local copies, waits for them, and re-layouts  364 us (35%)
  other arithmetic  185 us (18%)
  matrix products  39.1 us (4%)
  waiting for transfers between devices  21.1 us (2%)
  between operations  15.8 us (2%)
    all_gather x13, blocking collectives, assemble(): piece = lax.all_gather(packed, 'dom', axis=0, tiled=True)  187 us
    psum x9, blocking collectives, squares(): lax.psum(inner_terms(weight, residual, residual), 'dom')[..., None, None]  128 us
    scatter-add x14, local copies, waits for them, and re-layouts, add_sides(): grid = grid.at[..., -1, :].add(incoming[..., 2, :])  88.5 us
    psum x5, blocking collectives, solve(): lax.psum(inner_terms(weight, direction, image), 'dom')[..., None, None]  69.8 us
    another operation x44, local copies, waits for them, and re-layouts  61.5 us
    another operation x46, local copies, waits for them, and re-layouts, side_values(): jnp.stack([grid[..., 0, :], grid[..., :, -1], grid[..., -1, :], grid[...,...  51.3 us
    scatter-add x13, local copies, waits for them, and re-layouts, add_sides(): grid = grid.at[..., 0, :].add(incoming[..., 0, :])  46.1 us
    another operation x13, other arithmetic, side_values(): jnp.stack([grid[..., 0, :], grid[..., :, -1], grid[..., -1, :], grid[...,...  37.4 us
  transfers between devices with their start and end apart: 2, of which 1 were waited for; matrix products, arithmetic and copies ran while one was open for 1% of the time, Pallas kernels for 0%

commit v1 on v0

v1 whole, which is shorter than its diff:
```python
import functools
import math

import jax
import jax.numpy as jnp
import numpy as np
from jax import lax
from jax.experimental import pallas as pl
from jax.experimental.pallas import tpu as pltpu
from jax.sharding import PartitionSpec as P

ITERS = 4
REACTION = 2.0
WAVE_STEP = 0.0625
LANES = 128
POINTS = 36
BLOCKS = 8
SIDE = 48
NODES = 2304
CENTRE = 9.0
SPREAD = 9.0
TWICE = 2.0 / SPREAD
SUM_ROWS = 16
VMEM_LIMIT = 56 * 1024 * 1024
F32 = jnp.float32
BF16 = jnp.bfloat16


def gll_tables():
    inner_near = math.sqrt(1.0 / 3.0 - 2.0 * math.sqrt(7.0) / 21.0)
    inner_far = math.sqrt(1.0 / 3.0 + 2.0 * math.sqrt(7.0) / 21.0)
    points = np.array([-1.0, -inner_far, -inner_near, inner_near, inner_far, 1.0])
    values = (63.0 * points**5 - 70.0 * points**3 + 15.0 * points) / 8.0
    weights = 2.0 / (30.0 * values * values)
    spacing = points[:, None] - points[None, :]
    same_point = spacing == 0.0
    derivative = np.where(
        same_point, 0.0, values[:, None] / (values[None, :] * np.where(same_point, 1.0, spacing))
    )
    end_fix = np.array([-7.5, 0.0, 0.0, 0.0, 0.0, 7.5])
    derivative = derivative + np.eye(6) * end_fix[None, :]
    stiffness = derivative.T @ (weights[:, None] * derivative)
    return (weights, derivative, stiffness)


WEIGHTS, DERIV, STIFF = gll_tables()
STIFF_HAT = STIFF / WEIGHTS[:, None]


def fourier_tables(planes):
    plane_ids = np.arange(planes)
    mode_ids = np.arange(planes)
    waves = np.where(mode_ids < 2, 0, mode_ids // 2)
    angle = (plane_ids[:, None] * waves[None, :] % planes) * (2.0 * math.pi / planes)
    is_sine = (mode_ids % 2 == 1) & (mode_ids >= 2)
    basis = np.where(is_sine[None, :], np.sin(angle), np.cos(angle))
    alternating = np.where(plane_ids % 2 == 0, 1.0, -1.0)
    basis = np.where(mode_ids[None, :] == 1, alternating[:, None], basis)
    row_scale = np.where(mode_ids < 2, 1.0, 2.0) / planes
    forward = basis.T * row_scale[:, None]
    rates = (np.arange(planes // 2) * WAVE_STEP)[:, None]
    forward_z = np.zeros_like(forward)
    forward_z[0::2] = rates * forward[1::2]
    forward_z[1::2] = -rates * forward[0::2]
    forward_z[0:2] = 0.0
    return (basis, forward, forward_z)


def split_table(table):
    high = np.asarray(table, np.float32).astype(jnp.bfloat16)
    low = (np.asarray(table, np.float64) - high.astype(np.float64)).astype(np.float32)
    return high, low.astype(jnp.bfloat16)


def transform_tables(count):
    planes = LANES
    modes = planes // count
    basis, forward, forward_z = fourier_tables(planes)
    inverse = np.zeros((count * LANES, 3 * planes))
    back = np.zeros((3 * 2 * planes, count * LANES))
    for block in range(count):
        ids = slice(block * modes, (block + 1) * modes)
        for comp in range(3):
            at = block * LANES + comp * modes
            inverse[at : at + modes, comp * planes : (comp + 1) * planes] = basis[:, ids].T
            row = comp * 2 * planes
            back[row : row + planes, at : at + modes] = -forward[ids].T
            back[row + planes : row + 2 * planes, at : at + modes] = -forward_z[ids].T
    return split_table(inverse), split_table(back)


def order_tables(count):
    group = BLOCKS * BLOCKS // count
    width = 0
    starts = []
    for index in range(count):
        first = group * index // BLOCKS * 6 * SIDE
        last = ((group * index + group - 1) // BLOCKS + 1) * 6 * SIDE
        start = first // LANES * LANES
        starts.append(start)
        width = max(width, -(-(last - start) // LANES) * LANES)
    starts = [min(start, NODES - width) for start in starts]
    tables = []
    which = []
    for index in range(count):
        table = np.zeros((POINTS * group, width), np.float32)
        for point in range(POINTS):
            for member in range(group):
                element = index * group + member
                row = 6 * (element // BLOCKS) + point // 6
                col = 6 * (element % BLOCKS) + point % 6
                table[point * group + member, row * SIDE + col - starts[index]] = 1.0
        for place, known in enumerate(tables):
            if np.array_equal(known, table):
                which.append(place)
                break
        else:
            which.append(len(tables))
            tables.append(table)
    return np.stack(tables).astype(jnp.bfloat16), which, starts


def halves(value):
    high = value.astype(BF16)
    low = (value - high.astype(F32)).astype(BF16)
    return high, low


def dot(left, right, dims):
    return lax.dot_general(left, right, (dims, ((), ())), preferred_element_type=F32)


def dot3(left, right_high, right_low):
    high, low = halves(left)
    dims = ((1,), (0,))
    return dot(high, right_high, dims) + (dot(low, right_high, dims) + dot(high, right_low, dims))


def start_of(point, ey):
    return pl.multiple_of(point * 64 + ey * 8, 8)


def get(ref, point, ey):
    return ref[pl.ds(start_of(point, ey), 8), :]


def put(ref, point, ey, value):
    ref[pl.ds(start_of(point, ey), 8), :] = value


def ex_ids():
    return lax.broadcasted_iota(jnp.int32, (8, LANES), 0)


def helmholtz_rates(four, modes):
    lane = lax.broadcasted_iota(jnp.int32, (8, LANES), 1)
    mode = four * modes + lax.rem(lane, jnp.int32(modes))
    wave = jnp.where(mode == 0, 0, jnp.where(mode == 1, LANES // 2, lax.div(mode, jnp.int32(2))))
    scaled = wave.astype(F32) * WAVE_STEP
    return REACTION + scaled * scaled


def glued_flags(partner_ref):
    return [jnp.where(partner_ref[0, side] >= 0, 1.0, 0.0).astype(F32) for side in range(4)]


def col_masks(flags):
    ex = ex_ids()
    return jnp.where(ex == 0, flags[3], 1.0), jnp.where(ex == 7, flags[1], 1.0)


def join_cols(first, last, masks):
    ex = ex_ids()
    from_right = jnp.where(ex < 7, pltpu.roll(first, 7, 0), 0.0)
    from_left = jnp.where(ex > 0, pltpu.roll(last, 1, 0), 0.0)
    return (first + from_left) * masks[0], (last + from_right) * masks[1]


def join_rows(ref, flags):
    ex = ex_ids()
    not_first = jnp.where(ex == 0, 0.0, 1.0)
    not_last = jnp.where(ex == 7, 0.0, 1.0)
    for ix in range(6):
        for ey in range(7):
            total = get(ref, 30 + ix, ey) + get(ref, ix, ey + 1)
            put(ref, 30 + ix, ey, total)
            put(ref, ix, ey + 1, total)
        low = get(ref, ix, 0) * flags[0]
        high = get(ref, 30 + ix, 7) * flags[2]
        if ix == 0:
            low, high = low * not_first, high * not_first
        if ix == 5:
            low, high = low * not_last, high * not_last
        put(ref, ix, 0, low)
        put(ref, 30 + ix, 7, high)


def line_product(line, table):
    sums = [line[j] + line[5 - j] for j in range(3)]
    gaps = [line[j] - line[5 - j] for j in range(3)]
    out = [None] * 6
    for i in range(3):
        even = None
        odd = None
        for j in range(3):
            even_term = sums[j] * float(0.5 * (table[i, j] + table[i, 5 - j]))
            odd_term = gaps[j] * float(0.5 * (table[i, j] - table[i, 5 - j]))
            even = even_term if even is None else even + even_term
            odd = odd_term if odd is None else odd + odd_term
        out[i] = even + odd
        out[5 - i] = even - odd
    return out


def apply_local(src, dst, rates, flags, energy=False):
    masks = col_masks(flags)

    def body(ey, total):
        for ix in range(6):
            line = [get(src, 6 * iy + ix, ey) for iy in range(6)]
            out = line_product(line, STIFF_HAT)
            for iy in range(6):
                put(dst, 6 * iy + ix, ey, out[iy] + rates * line[iy])
        for iy in range(6):
            line = [get(src, 6 * iy + ix, ey) for ix in range(6)]
            out = line_product(line, STIFF_HAT)
            full = [
                (get(dst, 6 * iy + ix, ey) + out[ix]) * float(WEIGHTS[iy] * WEIGHTS[ix])
                for ix in range(6)
            ]
            if energy:
                for ix in range(6):
                    total = total + full[ix] * line[ix]
            full[0], full[5] = join_cols(full[0], full[5], masks)
            for ix in range(6):
                put(dst, 6 * iy + ix, ey, full[ix])
        return total

    total = lax.fori_loop(0, BLOCKS, body, jnp.zeros((8, LANES), F32))
    join_rows(dst, flags)
    return total


def side_slice(side, i):
    if side == 0:
        return pl.ds(i * 64, 8)
    if side == 2:
        return pl.ds((30 + i) * 64 + 56, 8)
    if side == 1:
        return pl.ds((6 * i + 5) * 64 + 7, 8, stride=8)
    return pl.ds(6 * i * 64, 8, stride=8)


def read_line(ref, side):
    return [ref[side_slice(side, i), :] for i in range(6)]


def write_lines(ref, lines_ref, base):
    for side in range(4):
        line = read_line(ref, side)
        for i in range(6):
            lines_ref[pl.ds(base + side * SIDE + i * 8, 8), :] = line[i]


def add_lines(ref, lines):
    for side in range(4):
        for i in range(6):
            where = side_slice(side, i)
            ref[where, :] = ref[where, :] + lines[side][i]


def reverse_rows(value):
    ex = ex_ids()
    value = pltpu.roll(value, 4, 0)
    value = jnp.where((ex & 2) == 0, pltpu.roll(value, 6, 0), pltpu.roll(value, 2, 0))
    return jnp.where((ex & 1) == 0, pltpu.roll(value, 7, 0), pltpu.roll(value, 1, 0))


def incoming_lines(gath_ref, base, partner_ref, side_ref, flip_ref):
    lines = []
    for side in range(4):
        part = partner_ref[0, side]
        glued = part >= 0
        part = jnp.maximum(part, 0)
        start = base + jnp.maximum(side_ref[0, side], 0) * SIDE
        turned = flip_ref[0, side] == 1
        line = []
        for i in range(6):
            at = pl.multiple_of(start + jnp.where(turned, 5 - i, i) * 8, 8)
            value = gath_ref[part, pl.ds(at, 8), :]
            value = jnp.where(turned, reverse_rows(value), value)
            line.append(jnp.where(glued, value, 0.0))
        lines.append(line)
    return lines


def own_reaction(lines_ref, rates, flags, scale):
    ex = ex_ids()
    edge = float(WEIGHTS[0])
    corner = float(STIFF[0, 0])
    lines = []
    for side in range(4):
        line = [lines_ref[pl.ds(side * SIDE + i * 8, 8), :] for i in range(6)]
        along = line_product(line, STIFF_HAT)
        out = [
            (along[i] * edge + line[i] * (corner + rates * edge)) * float(WEIGHTS[i])
            for i in range(6)
        ]
        first = out[0] + pltpu.roll(out[5], 1, 0)
        last = out[5] + pltpu.roll(out[0], 7, 0)
        out[0] = jnp.where(ex > 0, first, 0.0)
        out[5] = jnp.where(ex < 7, last, 0.0)
        lines.append([value * (flags[side] * scale) for value in out])
    return lines


def combine(dst, terms):
    def body(ey, carry):
        for point in range(POINTS):
            total = None
            for factor, ref in terms:
                value = get(ref, point, ey)
                value = value if factor == 1.0 else value * factor
                total = value if total is None else total + value
            put(dst, point, ey, total)
        return carry

    lax.fori_loop(0, BLOCKS, body, 0)


def pack_kernel(which, starts, velocity_ref, order_ref, send_ref):
    modes = velocity_ref.shape[1]
    width = order_ref.shape[2]
    for index in range(len(starts)):
        window = pl.ds(starts[index], width)
        rows = [velocity_ref[comp, :, window] for comp in range(3)]
        pad = jnp.zeros((LANES - 3 * modes, width), F32)
        high, low = halves(jnp.concatenate(rows + [pad], axis=0))
        both = jnp.concatenate([high, low], axis=0)
        out = dot(order_ref[which[index]], both, ((1,), (1,)))
        send_ref[index] = out[:, :LANES] + out[:, LANES:]


def product_kernel(recv_ref, inv_high, inv_low, back_high, back_low, send_ref, phys, prod, out):
    count = recv_ref.shape[0]
    rows = recv_ref.shape[1]
    group = rows // POINTS
    total = None
    for index in range(count):
        where = pl.ds(index * LANES, LANES)
        part = dot3(recv_ref[index], inv_high[where, :], inv_low[where, :])
        total = part if total is None else total + part
    phys[...] = total
    step = min(group, 8)
    width = 2 * LANES

    def fields(point, base):
        return [
            phys[pl.ds(point * group + base, step), comp * LANES : (comp + 1) * LANES]
            for comp in range(3)
        ]

    for base in range(0, group, step):
        for comp in range(3):
            for iy in range(6):
                line = []
                for ix in range(6):
                    point = 6 * iy + ix
                    at = pl.ds(point * group + base, step)
                    value = fields(point, base)
                    line.append(value[comp] * value[0])
                    prod[at, comp * width + LANES : (comp + 1) * width] = value[comp] * value[2]
                for ix in range(6):
                    total = None
                    for j in range(6):
                        if DERIV[ix, j] != 0.0:
                            term = line[j] * float(DERIV[ix, j])
                            total = term if total is None else total + term
                    at = pl.ds((6 * iy + ix) * group + base, step)
                    prod[at, comp * width : comp * width + LANES] = total
            for ix in range(6):
                line = []
                for iy in range(6):
                    value = fields(6 * iy + ix, base)
                    line.append(value[comp] * value[1])
                for iy in range(6):
                    at = pl.ds((6 * iy + ix) * group + base, step)
                    total = prod[at, comp * width : comp * width + LANES]
                    for j in range(6):
                        if DERIV[iy, j] != 0.0:
                            total = total + line[j] * float(DERIV[iy, j])
                    prod[at, comp * width : comp * width + LANES] = total
    out[...] = dot3(prod[...], back_high[...], back_low[...])
    for index in range(count):
        for point in range(POINTS):
            at = pl.ds(point * group, group)
            mass = float(WEIGHTS[point // 6] * WEIGHTS[point % 6])
            nonlinear = out[at, index * LANES : (index + 1) * LANES]
            send_ref[index, at, :] = mass * (REACTION * recv_ref[index, at, :] + nonlinear)


def first_kernel(modes, four_ref, partner_ref, recv_ref, base_ref, lines_ref, work):
    count = recv_ref.shape[0]
    group = recv_ref.shape[1] // POINTS
    rates = helmholtz_rates(four_ref[0], modes)
    flags = glued_flags(partner_ref)
    for index in range(count):
        for point in range(POINTS):
            base_ref[pl.ds(point * 64 + index * group, group), :] = recv_ref[
                index, pl.ds(point * group, group), :
            ]
    masks = col_masks(flags)
    for ey in range(BLOCKS):
        for iy in range(6):
            first, last = join_cols(get(base_ref, 6 * iy, ey), get(base_ref, 6 * iy + 5, ey), masks)
            put(base_ref, 6 * iy, ey, first)
            put(base_ref, 6 * iy + 5, ey, last)
    join_rows(base_ref, flags)
    apply_local(base_ref, work, rates, flags)
    write_lines(base_ref, lines_ref, 0)
    write_lines(work, lines_ref, 4 * SIDE)


def second_kernel(
    modes, four_ref, partner_ref, side_ref, flip_ref, gath_ref, lines_ref, base_ref,
    k0_ref, k1_ref, k2_ref, next_ref, work,
):
    rates = helmholtz_rates(four_ref[0], modes)
    flags = glued_flags(partner_ref)
    tables = (partner_ref, side_ref, flip_ref)
    back = own_reaction(lines_ref, rates, flags, 1.0)
    k0_ref[...] = base_ref[...]
    add_lines(k0_ref, incoming_lines(gath_ref, 0, *tables))
    apply_local(k0_ref, work, rates, flags)
    add_lines(work, incoming_lines(gath_ref, 4 * SIDE, *tables))
    add_lines(work, back)
    combine(k1_ref, [(1.0 / SPREAD, work), (-CENTRE / SPREAD, k0_ref)])
    apply_local(k1_ref, work, rates, flags)
    write_lines(work, next_ref, 0)
    combine(k2_ref, [(TWICE, work), (-CENTRE * TWICE, k1_ref), (-1.0, k0_ref)])
    apply_local(k2_ref, work, rates, flags)
    write_lines(work, next_ref, 4 * SIDE)


def third_kernel(
    modes, four_ref, partner_ref, side_ref, flip_ref, gath_ref, lines_ref, k0_ref, k1_ref, base_ref,
    k2_ref, k3_ref, a3_ref, next_ref, work,
):
    rates = helmholtz_rates(four_ref[0], modes)
    flags = glued_flags(partner_ref)
    tables = (partner_ref, side_ref, flip_ref)
    back = own_reaction(lines_ref, rates, flags, TWICE)
    k2_ref[...] = base_ref[...]
    incoming = incoming_lines(gath_ref, 0, *tables)
    add_lines(k2_ref, [[value * TWICE for value in line] for line in incoming])
    apply_local(k2_ref, work, rates, flags)
    add_lines(work, incoming_lines(gath_ref, 4 * SIDE, *tables))
    add_lines(work, back)
    combine(k3_ref, [(TWICE, work), (-CENTRE * TWICE, k2_ref), (-1.0, k1_ref)])
    energy = apply_local(k3_ref, a3_ref, rates, flags, energy=True)
    write_lines(a3_ref, next_ref, 0)
    refs = (k0_ref, k1_ref, k2_ref, k3_ref)

    def body(ey, sums):
        sums = list(sums)
        for point in range(POINTS):
            ends = (point // 6 in (0, 5)) + (point % 6 in (0, 5))
            values = [get(ref, point, ey) for ref in refs]
            place = 0
            for i in range(4):
                scaled = values[i] * (0.5**ends) if ends else values[i]
                for j in range(i, 4):
                    sums[place] = sums[place] + scaled * values[j]
                    place += 1
        return tuple(sums)

    zero = jnp.zeros((8, LANES), F32)
    sums = lax.fori_loop(0, BLOCKS, body, (zero,) * 10)
    rows = [jnp.sum(value, axis=0, keepdims=True) for value in sums]
    rows.append(jnp.sum(energy, axis=0, keepdims=True))
    rows.append(jnp.zeros((SUM_ROWS - len(rows), LANES), F32))
    next_ref[pl.ds(4 * SIDE, SUM_ROWS), :] = jnp.concatenate(rows, axis=0)


def conjugate_coefficients(gram, energy):
    zero = jnp.zeros_like(energy)

    def image(vec):
        out = [zero] * 5
        for j in range(4):
            if vec[j] is None:
                continue
            out[j] = out[j] + CENTRE * vec[j]
            out[j + 1] = out[j + 1] + (SPREAD if j == 0 else 0.5 * SPREAD) * vec[j]
            if j > 0:
                out[j - 1] = out[j - 1] + 0.5 * SPREAD * vec[j]
        return out

    def inner(left, right):
        total = zero
        for i in range(4):
            for j in range(4):
                if left[i] is not None and right[j] is not None:
                    total = total + left[i] * right[j] * gram[i][j]
        return total

    moments = [[None] * 4 for _ in range(4)]
    for j in range(3):
        column = image([jnp.ones_like(energy) if i == j else None for i in range(4)])
        for i in range(4):
            total = zero
            for m in range(max(j - 1, 0), j + 2):
                total = total + column[m] * gram[i][m]
            moments[i][j] = total
    for i in range(3):
        moments[i][3] = moments[3][i]
    moments[3][3] = energy

    def pad(vec, size):
        return [vec[i] if i < size else None for i in range(4)]

    residual = [jnp.ones_like(energy), zero, zero, zero, zero]
    direction = list(residual)
    solution = [zero] * 4
    norm_now = gram[0][0]
    for step in range(ITERS):
        trimmed = pad(direction, step + 1)
        bend = zero
        for i in range(step + 1):
            for j in range(step + 1):
                bend = bend + direction[i] * direction[j] * moments[i][j]
        alpha = norm_now / bend
        moved = image(trimmed)
        for i in range(step + 1):
            solution[i] = solution[i] + alpha * direction[i]
        for i in range(step + 2):
            residual[i] = residual[i] - alpha * moved[i]
        if step < ITERS - 1:
            kept = pad(residual, step + 2)
            norm_next = inner(kept, kept)
            ratio = norm_next / norm_now
            direction = [residual[i] + ratio * direction[i] for i in range(5)]
            norm_now = norm_next
    return solution, residual


def last_kernel(
    which, starts, partner_ref, side_ref, flip_ref, gath_ref, k0_ref, k1_ref, k2_ref, k3_ref, base_ref,
    order_ref, sol_ref, res_ref, work, sol_rows, res_rows, flat,
):
    parts = gath_ref.shape[0]
    count, rows, _ = sol_rows.shape
    group = rows // POINTS
    modes = sol_ref.shape[1]
    width = order_ref.shape[2]
    sums = gath_ref[0, pl.ds(4 * SIDE, SUM_ROWS), :]
    for part in range(1, parts):
        sums = sums + gath_ref[part, pl.ds(4 * SIDE, SUM_ROWS), :]

    def row(place):
        return jnp.broadcast_to(sums[place : place + 1, :], (8, LANES))

    gram = [[None] * 4 for _ in range(4)]
    place = 0
    for i in range(4):
        for j in range(i, 4):
            gram[i][j] = row(place)
            gram[j][i] = gram[i][j]
            place += 1
    solution, residual = conjugate_coefficients(gram, row(place))
    work[...] = base_ref[...]
    add_lines(work, incoming_lines(gath_ref, 0, partner_ref, side_ref, flip_ref))
    on_a3 = residual[4] * TWICE
    on_k3 = residual[3] - on_a3 * CENTRE
    on_k2 = residual[2] - residual[4]

    def body(ey, carry):
        for point in range(POINTS):
            k0, k1, k2, k3, a3 = [
                get(ref, point, ey) for ref in (k0_ref, k1_ref, k2_ref, k3_ref, work)
            ]
            sol = (solution[0] * k0 + solution[1] * k1) + (solution[2] * k2 + solution[3] * k3)
            res = (residual[0] * k0 + residual[1] * k1) + (on_k2 * k2 + on_k3 * k3) + on_a3 * a3
            for ref, value in ((sol_rows, sol), (res_rows, res)):
                if group >= 8:
                    index = lax.div(ey * 8, jnp.int32(group))
                    at = pl.multiple_of(point * group + lax.rem(ey * 8, jnp.int32(group)), 8)
                    ref[index, pl.ds(at, 8), :] = value
                else:
                    for piece in range(8 // group):
                        ref[ey * (8 // group) + piece, pl.ds(point * group, group), :] = value[
                            piece * group : (piece + 1) * group, :
                        ]
        return carry

    lax.fori_loop(0, BLOCKS, body, 0)
    for ref, out_ref in ((sol_rows, sol_ref), (res_rows, res_ref)):
        flat[...] = jnp.zeros(flat.shape, F32)
        for index in range(count):
            high, low = halves(jnp.transpose(ref[index]))
            both = jnp.concatenate([high, low], axis=0)
            out = dot(both, order_ref[which[index]], ((1,), (0,)))
            window = pl.ds(starts[index], width)
            flat[:, window] = flat[:, window] + (out[:LANES] + out[LANES:])
        for comp in range(3):
            out_ref[comp] = flat[comp * modes : (comp + 1) * modes, :]


def call(kernel, name, out_shapes, args, scratch, scalars=0):
    smem = pl.BlockSpec(memory_space=pltpu.SMEM)
    vmem = pl.BlockSpec(memory_space=pltpu.VMEM)
    return pl.pallas_call(
        kernel,
        name=name,
        out_shape=[jax.ShapeDtypeStruct(shape, F32) for shape in out_shapes],
        in_specs=[smem] * scalars + [vmem] * (len(args) - scalars),
        out_specs=[vmem] * len(out_shapes),
        scratch_shapes=[pltpu.VMEM(shape, F32) for shape in scratch],
        compiler_params=pltpu.CompilerParams(vmem_limit_bytes=VMEM_LIMIT),
    )(*args)


def shards(velocity, partner, partner_side, flipped):
    modes = velocity.shape[1]
    count = lax.axis_size("four")
    rows = NODES // count
    (inv_high, inv_low), (back_high, back_low) = transform_tables(count)
    order, which, starts = order_tables(count)
    four = lax.axis_index("four").astype(jnp.int32).reshape(1)
    field = (NODES, LANES)
    swapped = (count, rows, LANES)

    (sent,) = call(
        functools.partial(pack_kernel, which, starts), "pack", [swapped], (velocity, order), []
    )
    spread = lax.all_to_all(sent, "four", split_axis=0, concat_axis=0, tiled=True)
    (sent,) = call(
        product_kernel,
        "products",
        [swapped],
        (spread, inv_high, inv_low, back_high, back_low),
        [(rows, 3 * LANES), (rows, 6 * LANES), (rows, count * LANES)],
    )
    local = lax.all_to_all(sent, "four", split_axis=0, concat_axis=0, tiled=True)

    base, lines = call(
        functools.partial(first_kernel, modes),
        "first",
        [field, (8 * SIDE, LANES)],
        (four, partner, local),
        [field],
        scalars=2,
    )
    tables = (partner, partner_side, flipped)
    gathered = lax.all_gather(lines, "dom", axis=0, tiled=False)
    k0, k1, base, lines = call(
        functools.partial(second_kernel, modes),
        "second",
        [field, field, field, (8 * SIDE, LANES)],
        (four, *tables, gathered, lines, base),
        [field],
        scalars=4,
    )
    gathered = lax.all_gather(lines, "dom", axis=0, tiled=False)
    k2, k3, a3, lines = call(
        functools.partial(third_kernel, modes),
        "third",
        [field, field, field, (4 * SIDE + SUM_ROWS, LANES)],
        (four, *tables, gathered, lines, k0, k1, base),
        [field],
        scalars=4,
    )
    gathered = lax.all_gather(lines, "dom", axis=0, tiled=False)
    outs = call(
        functools.partial(last_kernel, which, starts),
        "last",
        [velocity.shape, velocity.shape],
        (*tables, gathered, k0, k1, k2, k3, a3, order),
        [field, swapped, swapped, (LANES, NODES)],
        scalars=3,
    )
    return tuple(outs)


def solution(mesh):
    return jax.shard_map(
        shards,
        mesh=mesh,
        in_specs=(P(None, "four", "dom"), P("dom", None), P("dom", None), P("dom", None)),
        out_specs=(P(None, "four", "dom"), P(None, "four", "dom")),
        check_vma=False,
    )
```

time: 1030 us -> 159 us (0.15)
  local copies, waits for them, and re-layouts: 364 us -> 1.02 us
  blocking collectives: 385 us -> 38.3 us
  other arithmetic: 185 us -> 0 us
  waiting for transfers between devices: 21.1 us -> 64.2 us
  matrix products: 39.1 us -> 0 us
  Pallas kernels: 0 us -> 37.3 us
    psum x14 -> x0, blocking collectives: 198 us -> none  [the longest x9 128 us: squares(): lax.psum(inner_terms(weight, residual, residual), 'dom')[..., None, None]]
    all_gather x13 -> x1, blocking collectives: 187 us -> 16.9 us  [shards(): gathered = lax.all_gather(lines, 'dom', axis=0, tiled=False)]
    scatter-add x32 -> x0, local copies, waits for them, and re-layouts: 145 us -> none  [the longest x14 88.5 us: add_sides(): grid = grid.at[..., -1, :].add(incoming[..., 2, :])]
    another operation x99 -> x0, local copies, waits for them, and re-layouts: 123 us -> none
    add x74 -> x0, other arithmetic: 88.4 us -> none  [the longest x13 27.1 us: add_sides(): grid = grid.at[..., -1, :].add(incoming[..., 2, :])]
    all_gather x0 -> x2, waiting for transfers between devices: none -> 49.8 us  [shards(): gathered = lax.all_gather(lines, 'dom', axis=0, tiled=False)]
    another operation x37 -> x0, other arithmetic: 39.2 us -> none  [the longest x13 37.4 us: side_values(): jnp.stack([grid[..., 0, :], grid[..., :, -1], grid[..., -1, :], grid[...,...]
    pallas_call x0 -> x6, Pallas kernels: none -> 37.3 us  [call(): pl.pallas_call(kernel, name=name, out_shape=[jax.ShapeDtypeStruct(shape,...]
  transfers between devices with their start and end apart: 2 -> 3, of which waited for: 1 -> 3; matrix products, arithmetic and copies ran while one was open for 1% -> 0% of each run, Pallas kernels for 0% -> 0%
where the time goes in v1:
time: 159 us
  waiting for transfers between devices  64.2 us (40%)
  blocking collectives  38.3 us (24%)
  Pallas kernels  37.3 us (23%)
  between operations  14.1 us (9%)
  starting transfers between devices  3.61 us (2%)
    all_gather x2, waiting for transfers between devices, shards(): gathered = lax.all_gather(lines, 'dom', axis=0, tiled=False)  49.8 us
    pallas_call x6, Pallas kernels, call(): pl.pallas_call(kernel, name=name, out_shape=[jax.ShapeDtypeStruct(shape,...  37.3 us
    all_to_all x1, blocking collectives, shards(): lax.all_to_all(sent, 'four', split_axis=0, concat_axis=0, tiled=True)  21.4 us
    all_gather x1, blocking collectives, shards(): gathered = lax.all_gather(lines, 'dom', axis=0, tiled=False)  16.9 us
    all_to_all x1, waiting for transfers between devices, shards(): lax.all_to_all(sent, 'four', split_axis=0, concat_axis=0, tiled=True)  14.3 us
    all_to_all x1, starting transfers between devices, shards(): lax.all_to_all(sent, 'four', split_axis=0, concat_axis=0, tiled=True)  3.53 us
  transfers between devices with their start and end apart: 3, of which 3 were waited for; matrix products, arithmetic and copies ran while one was open for 0% of the time, Pallas kernels for 0%

profile of v1, /device:TPU:0, one launch (start us, length us, event | category | flops | bytes accessed | tf_op | source)
XLA Modules:
  0.0 158.5 jit_solution(18089927973831461976)
XLA Ops:
  7.2 3.8 %pack.1 = f32[4,576,128]{2,1,0:T(8,128)} custom-call(f32[3,32,2304]{2,1,0:T(8,128)} %velocity_ref.1, bf16[2,576,640]{2,1,0:T(8,128)(2,1)} %constant.14.clone.order_ref), custom_call_target="tpu_custom_call" | custom-call | tf_op jit(solution)/shard_map/pack/pallas_call | solution.py:612
  11.0 21.4 %all_to_all.10.recv_ref = f32[4,576,128]{2,1,0:T(8,128)} all-to-all(f32[4,576,128]{2,1,0:T(8,128)} %pack.1), channel_id=1, replica_groups=mesh['dom'=8,'four'=4] {'four'}, dimensions={0} | all-to-all | bytes 2359296 | tf_op jit(solution)/shard_map/all_to_all | solution.py:636
  32.4 7.1 %products.1 = f32[4,576,128]{2,1,0:T(8,128)} custom-call(f32[4,576,128]{2,1,0:T(8,128)} %all_to_all.10.recv_ref, bf16[512,384]{1,0:T(8,128)(2,1)} %constant.15.clone.inv_high, bf16[512,384]{1,0:T(8,128)(2,1)} %constant.16.clone.inv_low, bf16[768,512]{1,0:T(8,128)(2,1)} %constant.17.clone.back_high, bf16[768,512]{1,0:T(8,128)(2,1)} %constant.18.clone.back_low), custom_call_target="tpu_custom_call" | custom-call | tf_op jit(solution)/shard_map/products/pallas_call | solution.py:612
  39.5 3.5 %all-to-all-start.1 = ((f32[4,576,128]{2,1,0:T(8,128)}), f32[4,576,128]{2,1,0:T(8,128)S(1)}, u32[]{:S(2)}, u32[]{:S(2)}) async-start(f32[4,576,128]{2,1,0:T(8,128)} %products.1), calls=%async_computation.1 | async-start | bytes 2359296 | tf_op jit(solution)/shard_map/all_to_all | solution.py:644
  43.0 0.0 all-gather.6.cloned.1.call-start
  43.1 14.3 %all-to-all-done.1.recv_ref = f32[4,576,128]{2,1,0:T(8,128)S(1)} async-done(((f32[4,576,128]{2,1,0:T(8,128)}), f32[4,576,128]{2,1,0:T(8,128)S(1)}, u32[]{:S(2)}, u32[]{:S(2)}) %all-to-all-start.1) | async-done | bytes 1179680 | tf_op jit(solution)/shard_map/all_to_all | solution.py:644
  57.4 0.0 copy-start
  57.4 1.0 copy-done
  58.4 3.2 %first.1 = (f32[2304,128]{1,0:T(8,128)}, f32[384,128]{1,0:T(8,128)}) custom-call(s32[1]{0:T(128)} %bitcast.four_ref, s32[1,4]{1,0:T(1,128)} %partner_ref.7, f32[4,576,128]{2,1,0:T(8,128)} %copy-done), custom_call_target="tpu_custom_call" | custom-call | tf_op jit(solution)/shard_map/first/pallas_call | solution.py:612
  61.7 0.0 all-gather.6.cloned.1.call-update
  61.7 0.0 all-gather.8.cloned.1.call-start
  61.8 25.1 %all-gather.6.cloned.1.call-done = f32[3072,128]{1,0:T(8,128)} async-done(((f32[384,128]{1,0:T(8,128)}), f32[3072,128]{1,0:T(8,128)}) %all-gather.6.cloned.1.call-update) | async-done | bytes 1572880 | tf_op jit(solution)/shard_map/all_gather | solution.py:655
  86.8 7.5 %second.1 = (f32[2304,128]{1,0:T(8,128)}, f32[2304,128]{1,0:T(8,128)}, f32[2304,128]{1,0:T(8,128)}, f32[384,128]{1,0:T(8,128)}) custom-call(s32[1]{0:T(128)} %bitcast.four_ref, s32[1,4]{1,0:T(1,128)} %partner_ref.7, s32[1,4]{1,0:T(1,128)} %side_ref.5, s32[1,4]{1,0:T(1,128)} %flip_ref.5, f32[8,384,128]{2,1,0:T(8,128)} %bitcast.5, ...), custom_call_target="tpu_custom_call" | custom-call | tf_op jit(solution)/shard_map/second/pallas_call | solution.py:612
  94.3 0.0 all-gather.8.cloned.1.call-update
  94.3 24.7 %all-gather.8.cloned.1.call-done = f32[3072,128]{1,0:T(8,128)} async-done(((f32[384,128]{1,0:T(8,128)}), f32[3072,128]{1,0:T(8,128)}) %all-gather.8.cloned.1.call-update) | async-done | bytes 1572880 | tf_op jit(solution)/shard_map/all_gather | solution.py:664
  119.1 7.9 %third.1 = (f32[2304,128]{1,0:T(8,128)}, f32[2304,128]{1,0:T(8,128)}, f32[2304,128]{1,0:T(8,128)}, f32[208,128]{1,0:T(8,128)}) custom-call(s32[1]{0:T(128)} %bitcast.four_ref, s32[1,4]{1,0:T(1,128)} %partner_ref.7, s32[1,4]{1,0:T(1,128)} %side_ref.5, s32[1,4]{1,0:T(1,128)} %flip_ref.5, f32[8,384,128]{2,1,0:T(8,128)} %bitcast.6, ...), custom_call_target="tpu_custom_call" | custom-call | tf_op jit(solution)/shard_map/third/pallas_call | solution.py:612
  126.9 16.9 %all-gather.2 = f32[1664,128]{1,0:T(8,128)} all-gather(f32[208,128]{1,0:T(8,128)} %get-tuple-element.18), channel_id=4, replica_groups=mesh['dom'=8,'four'=4] {'dom'}, dimensions={0}, use_global_device_ids=true | all-gather | bytes 958464 | tf_op jit(solution)/shard_map/all_gather | solution.py:673
  143.8 7.9 %last.1 = (f32[3,32,2304]{2,1,0:T(8,128)}, f32[3,32,2304]{2,1,0:T(8,128)}) custom-call(s32[1,4]{1,0:T(1,128)} %partner_ref.7, s32[1,4]{1,0:T(1,128)} %side_ref.5, s32[1,4]{1,0:T(1,128)} %flip_ref.5, f32[8,208,128]{2,1,0:T(8,128)} %bitcast.4, f32[2304,128]{1,0:T(8,128)} %get-tuple-element.15.k0_ref, f32[2304,128]{1,0:T(8,128)} %get-tuple-element.16.k1_ref, ...), custom_call_target="tpu_custom_call" | custom-call | tf_op jit(solution)/shard_map/last/pallas_call | solution.py:612
Async XLA Ops:
  39.5 17.9 %all-to-all-start.1 = ((f32[4,576,128]{2,1,0:T(8,128)}), f32[4,576,128]{2,1,0:T(8,128)S(1)}, u32[]{:S(2)}, u32[]{:S(2)}) async-start(f32[4,576,128]{2,1,0:T(8,128)} %products.1), calls=%async_computation.1 | async-start | bytes 2359296 | tf_op jit(solution)/shard_map/all_to_all | solution.py:644
  43.0 43.8 %all-gather.6.cloned.1.call-start = ((), (), s32[]{:S(2)}) async-start(), calls=%async_computation.2 | async-start | bytes 1769472 | tf_op jit(solution)/shard_map/all_gather | solution.py:655
  57.4 1.0 copy-start
  61.7 57.3 %all-gather.8.cloned.1.call-start = ((), (), s32[]{:S(2)}) async-start(), calls=%async_computation.3 | async-start | bytes 1769472 | tf_op jit(solution)/shard_map/all_gather | solution.py:664
Sparse Core Ops, SparseCore 0:
  61.8 24.9 all-gather.5
  94.4 24.5 all-gather.7

commit v2 on v1

--- a/solution.py
+++ b/solution.py
@@ -76,40 +76,39 @@
     planes = LANES
     modes = planes // count
     basis, forward, forward_z = fourier_tables(planes)
-    inverse = np.zeros((count * LANES, 3 * planes))
-    back = np.zeros((3 * 2 * planes, count * LANES))
+    inverse = np.zeros((count, LANES, 3 * planes))
     for block in range(count):
         ids = slice(block * modes, (block + 1) * modes)
         for comp in range(3):
-            at = block * LANES + comp * modes
-            inverse[at : at + modes, comp * planes : (comp + 1) * planes] = basis[:, ids].T
-            row = comp * 2 * planes
-            back[row : row + planes, at : at + modes] = -forward[ids].T
-            back[row + planes : row + 2 * planes, at : at + modes] = -forward_z[ids].T
+            at = comp * modes
+            inverse[block, at : at + modes, comp * planes : (comp + 1) * planes] = basis[:, ids].T
+    back = -np.concatenate([forward.T, forward_z.T], axis=0)
     return split_table(inverse), split_table(back)
 
 
+def chunk_sizes(count):
+    group = BLOCKS * BLOCKS // count
+    step = min(group, BLOCKS)
+    return step, group // step
+
+
 def order_tables(count):
-    group = BLOCKS * BLOCKS // count
-    width = 0
+    step, _ = chunk_sizes(count)
+    units = BLOCKS * BLOCKS // step
+    width = 3 * LANES
     starts = []
-    for index in range(count):
-        first = group * index // BLOCKS * 6 * SIDE
-        last = ((group * index + group - 1) // BLOCKS + 1) * 6 * SIDE
-        start = first // LANES * LANES
-        starts.append(start)
-        width = max(width, -(-(last - start) // LANES) * LANES)
-    starts = [min(start, NODES - width) for start in starts]
     tables = []
     which = []
-    for index in range(count):
-        table = np.zeros((POINTS * group, width), np.float32)
+    for index in range(units):
+        start = step * index // BLOCKS * 6 * SIDE // LANES * LANES
+        starts.append(start)
+        table = np.zeros((POINTS * step, width), np.float32)
         for point in range(POINTS):
-            for member in range(group):
-                element = index * group + member
+            for member in range(step):
+                element = index * step + member
                 row = 6 * (element // BLOCKS) + point // 6
                 col = 6 * (element % BLOCKS) + point % 6
-                table[point * group + member, row * SIDE + col - starts[index]] = 1.0
+                table[point * step + member, row * SIDE + col - start] = 1.0
         for place, known in enumerate(tables):
             if np.array_equal(known, table):
                 which.append(place)
@@ -195,7 +194,7 @@
         put(ref, 30 + ix, 7, high)
 
 
-def line_product(line, table):
+def line_product(line, table, mirrored=1.0):
     sums = [line[j] + line[5 - j] for j in range(3)]
     gaps = [line[j] - line[5 - j] for j in range(3)]
     out = [None] * 6
@@ -208,7 +207,7 @@
             even = even_term if even is None else even + even_term
             odd = odd_term if odd is None else odd + odd_term
         out[i] = even + odd
-        out[5 - i] = even - odd
+        out[5 - i] = even - odd if mirrored > 0 else odd - even
     return out
 
 
@@ -255,11 +254,61 @@
     return [ref[side_slice(side, i), :] for i in range(6)]
 
 
-def write_lines(ref, lines_ref, base):
+def lane_ids():
+    return lax.broadcasted_iota(jnp.int32, (8, LANES), 1)
+
+
+def is_packed(modes):
+    return 3 * modes + modes == LANES
+
+
+def pack_lanes(values, modes):
+    if not is_packed(modes):
+        return values
+    third = len(values) // 4
+    inside = lane_ids() < 3 * modes
+    return [
+        jnp.where(
+            inside,
+            values[comp * third + at],
+            pltpu.roll(values[3 * third + at], (3 - comp) * modes, 1),
+        )
+        for comp in range(3)
+        for at in range(third)
+    ]
+
+
+def unpack_last(pieces, modes):
+    block = lax.div(lane_ids(), jnp.int32(modes))
+    turned = [pltpu.roll(pieces[comp], (comp + 1) * modes, 1) for comp in range(3)]
+    return jnp.where(block == 0, turned[0], jnp.where(block == 1, turned[1], turned[2]))
+
+
+def unpack_lanes(values, modes):
+    if not is_packed(modes):
+        return values
+    third = len(values) // 3
+    return values + [
+        unpack_last([values[comp * third + at] for comp in range(3)], modes) for at in range(third)
+    ]
+
+
+def line_rows(modes):
+    return 3 * SIDE if is_packed(modes) else 4 * SIDE
+
+
+def write_lines(ref, lines_ref, base, modes):
+    values = []
     for side in range(4):
-        line = read_line(ref, side)
-        for i in range(6):
-            lines_ref[pl.ds(base + side * SIDE + i * 8, 8), :] = line[i]
+        values += read_line(ref, side)
+    for at, value in enumerate(pack_lanes(values, modes)):
+        lines_ref[pl.ds(base + at * 8, 8), :] = value
+
+
+def load_lines(lines_ref, modes):
+    count = line_rows(modes) // 8
+    values = unpack_lanes([lines_ref[pl.ds(at * 8, 8), :] for at in range(count)], modes)
+    return [values[side * 6 : side * 6 + 6] for side in range(4)]
 
 
 def add_lines(ref, lines):
@@ -276,31 +325,71 @@
     return jnp.where((ex & 1) == 0, pltpu.roll(value, 7, 0), pltpu.roll(value, 1, 0))
 
 
-def incoming_lines(gath_ref, base, partner_ref, side_ref, flip_ref):
+def collect_sides(gath_refs, own, partner_ref, side_ref, sides, modes):
+    sets = sides.shape[1] // SIDE
+    step = line_rows(modes)
+
+    def copy_side(side, load):
+        there = jnp.maximum(side_ref[0, side], 0)
+
+        def plain():
+            for place in range(sets):
+                for i in range(6):
+                    at = pl.multiple_of(place * step + there * SIDE + i * 8, 8)
+                    sides[side, pl.ds(place * SIDE + i * 8, 8), :] = load(at)
+
+        if not is_packed(modes):
+            plain()
+            return
+        pl.when(there < 3)(plain)
+
+        @pl.when(there == 3)
+        def _():
+            for place in range(sets):
+                for i in range(6):
+                    pieces = [load(place * step + comp * SIDE + i * 8) for comp in range(3)]
+                    sides[side, pl.ds(place * SIDE + i * 8, 8), :] = unpack_last(pieces, modes)
+
+    def body(side, carry):
+        part = partner_ref[0, side]
+        if len(gath_refs) == 1:
+            source = jnp.maximum(part, 0)
+            copy_side(side, lambda at: gath_refs[0][source, pl.ds(at, 8), :])
+            return carry
+        for slot, ref in enumerate(gath_refs):
+            here = jnp.logical_and(part >= 0, jnp.bitwise_xor(part, own) == slot)
+
+            @pl.when(here)
+            def _(ref=ref):
+                copy_side(side, lambda at: ref[pl.ds(at, 8), :])
+
+        return carry
+
+    lax.fori_loop(0, 4, body, 0)
+
+
+def incoming_lines(sides, place, partner_ref, flip_ref):
     lines = []
     for side in range(4):
-        part = partner_ref[0, side]
-        glued = part >= 0
-        part = jnp.maximum(part, 0)
-        start = base + jnp.maximum(side_ref[0, side], 0) * SIDE
+        glued = partner_ref[0, side] >= 0
         turned = flip_ref[0, side] == 1
         line = []
         for i in range(6):
-            at = pl.multiple_of(start + jnp.where(turned, 5 - i, i) * 8, 8)
-            value = gath_ref[part, pl.ds(at, 8), :]
+            at = pl.multiple_of(place * SIDE + jnp.where(turned, 5 - i, i) * 8, 8)
+            value = sides[side, pl.ds(at, 8), :]
             value = jnp.where(turned, reverse_rows(value), value)
             line.append(jnp.where(glued, value, 0.0))
         lines.append(line)
     return lines
 
 
-def own_reaction(lines_ref, rates, flags, scale):
+def own_reaction(own_lines, rates, flags, scale):
     ex = ex_ids()
     edge = float(WEIGHTS[0])
     corner = float(STIFF[0, 0])
     lines = []
     for side in range(4):
-        line = [lines_ref[pl.ds(side * SIDE + i * 8, 8), :] for i in range(6)]
+        line = own_lines[side]
         along = line_product(line, STIFF_HAT)
         out = [
             (along[i] * edge + line[i] * (corner + rates * edge)) * float(WEIGHTS[i])
@@ -328,87 +417,118 @@
     lax.fori_loop(0, BLOCKS, body, 0)
 
 
-def pack_kernel(which, starts, velocity_ref, order_ref, send_ref):
+def block_of(place, four):
+    return place if isinstance(four, int) else jnp.bitwise_xor(four, place)
+
+
+def pack_kernel(step, count, dynamic, ids_ref, which_ref, starts_ref, velocity_ref, order_ref, *send_refs):
     modes = velocity_ref.shape[1]
     width = order_ref.shape[2]
-    for index in range(len(starts)):
-        window = pl.ds(starts[index], width)
+    four = ids_ref[1] if dynamic else 0
+    for place in range(count):
+        index = block_of(place, four)
+        window = pl.ds(pl.multiple_of(starts_ref[index], LANES), width)
         rows = [velocity_ref[comp, :, window] for comp in range(3)]
         pad = jnp.zeros((LANES - 3 * modes, width), F32)
         high, low = halves(jnp.concatenate(rows + [pad], axis=0))
         both = jnp.concatenate([high, low], axis=0)
-        out = dot(order_ref[which[index]], both, ((1,), (1,)))
-        send_ref[index] = out[:, :LANES] + out[:, LANES:]
-
-
-def product_kernel(recv_ref, inv_high, inv_low, back_high, back_low, send_ref, phys, prod, out):
-    count = recv_ref.shape[0]
-    rows = recv_ref.shape[1]
-    group = rows // POINTS
+        out = dot(order_ref[which_ref[index]], both, ((1,), (1,)))
+        out = out[:, :LANES] + out[:, LANES:]
+        if not is_packed(modes):
+            send_refs[place][...] = out
+            continue
+        values = [out[point * step : (point + 1) * step] for point in range(POINTS)]
+        for at, value in enumerate(pack_lanes(values, modes)):
+            send_refs[place][pl.ds(at * step, step), :] = value
+
+
+def product_kernel(modes, step, count, dynamic, ids_ref, *refs):
+    recv_refs = refs[:count]
+    inv_high, inv_low, back_high, back_low = refs[count : count + 4]
+    send_refs = refs[count + 4 : 2 * count + 4]
+    full, phys, prod, spec = refs[2 * count + 4 :]
+    four = ids_ref[1] if dynamic else 0
+    packed = is_packed(modes)
     total = None
-    for index in range(count):
-        where = pl.ds(index * LANES, LANES)
-        part = dot3(recv_ref[index], inv_high[where, :], inv_low[where, :])
+    for place in range(count):
+        index = block_of(place, four)
+        if packed:
+            ready = 3 * POINTS // 4
+            values = [recv_refs[place][pl.ds(at * step, step), :] for at in range(ready)]
+            for at, value in enumerate(unpack_lanes(values, modes)):
+                full[place, pl.ds(at * step, step), :] = value
+        else:
+            full[place] = recv_refs[place][...]
+        part = dot3(full[place], inv_high[index], inv_low[index])
         total = part if total is None else total + part
     phys[...] = total
-    step = min(group, 8)
     width = 2 * LANES
 
-    def fields(point, base):
-        return [
-            phys[pl.ds(point * group + base, step), comp * LANES : (comp + 1) * LANES]
-            for comp in range(3)
-        ]
-
-    for base in range(0, group, step):
-        for comp in range(3):
+    def field(point, comp):
+        return phys[pl.ds(point * step, step), comp * LANES : (comp + 1) * LANES]
+
+    for comp in range(3):
+        wide = pl.ds(comp * width, LANES)
+        for iy in range(6):
+            line = []
+            for ix in range(6):
+                point = 6 * iy + ix
+                value = field(point, comp)
+                line.append(value * field(point, 0))
+                prod[pl.ds(point * step, step), pl.ds(comp * width + LANES, LANES)] = (
+                    value * field(point, 2)
+                )
+            out = line_product(line, DERIV, -1.0)
+            for ix in range(6):
+                prod[pl.ds((6 * iy + ix) * step, step), wide] = out[ix]
+        for ix in range(6):
+            line = [field(6 * iy + ix, comp) * field(6 * iy + ix, 1) for iy in range(6)]
+            out = line_product(line, DERIV, -1.0)
             for iy in range(6):
-                line = []
-                for ix in range(6):
-                    point = 6 * iy + ix
-                    at = pl.ds(point * group + base, step)
-                    value = fields(point, base)
-                    line.append(value[comp] * value[0])
-                    prod[at, comp * width + LANES : (comp + 1) * width] = value[comp] * value[2]
-                for ix in range(6):
-                    total = None
-                    for j in range(6):
-                        if DERIV[ix, j] != 0.0:
-                            term = line[j] * float(DERIV[ix, j])
-                            total = term if total is None else total + term
-                    at = pl.ds((6 * iy + ix) * group + base, step)
-                    prod[at, comp * width : comp * width + LANES] = total
-            for ix in range(6):
-                line = []
-                for iy in range(6):
-                    value = fields(6 * iy + ix, base)
-                    line.append(value[comp] * value[1])
-                for iy in range(6):
-                    at = pl.ds((6 * iy + ix) * group + base, step)
-                    total = prod[at, comp * width : comp * width + LANES]
-                    for j in range(6):
-                        if DERIV[iy, j] != 0.0:
-                            total = total + line[j] * float(DERIV[iy, j])
-                    prod[at, comp * width : comp * width + LANES] = total
-    out[...] = dot3(prod[...], back_high[...], back_low[...])
-    for index in range(count):
-        for point in range(POINTS):
-            at = pl.ds(point * group, group)
-            mass = float(WEIGHTS[point // 6] * WEIGHTS[point % 6])
-            nonlinear = out[at, index * LANES : (index + 1) * LANES]
-            send_ref[index, at, :] = mass * (REACTION * recv_ref[index, at, :] + nonlinear)
-
-
-def first_kernel(modes, four_ref, partner_ref, recv_ref, base_ref, lines_ref, work):
-    count = recv_ref.shape[0]
-    group = recv_ref.shape[1] // POINTS
-    rates = helmholtz_rates(four_ref[0], modes)
+                at = pl.ds((6 * iy + ix) * step, step)
+                prod[at, wide] = prod[at, wide] + out[iy]
+        spec[comp] = dot3(prod[:, comp * width : (comp + 1) * width], back_high[...], back_low[...])
+
+    lane_block = lax.div(lax.broadcasted_iota(jnp.int32, (step, LANES), 1), jnp.int32(modes))
+    masks = []
+    shifts = []
+    for place in range(count):
+        index = block_of(place, four)
+        masks.append([lane_block == lax.rem(index + comp, count) for comp in range(2)])
+        shifts.append(lax.rem(LANES - index * modes, LANES))
+    kept = []
+    for point in range(POINTS):
+        at = pl.ds(point * step, step)
+        mass = float(WEIGHTS[point // 6] * WEIGHTS[point % 6])
+        turned = [spec[0, at, :]]
+        turned += [pltpu.roll(spec[comp, at, :], comp * modes, 1) for comp in (1, 2)]
+        for place in range(count):
+            mask = masks[place]
+            mixed = jnp.where(mask[0], turned[0], jnp.where(mask[1], turned[1], turned[2]))
+            nonlinear = pltpu.roll(mixed, shifts[place], 1)
+            full[place, at, :] = mass * (REACTION * full[place, at, :] + nonlinear)
+    for place in range(count):
+        values = [full[place, pl.ds(point * step, step), :] for point in range(POINTS)]
+        for at, value in enumerate(pack_lanes(values, modes)):
+            send_refs[place][pl.ds(at * step, step), :] = value
+
+
+def first_kernel(modes, step, count, chunks, dynamic, ids_ref, partner_ref, *refs):
+    recv_refs = refs[: count * chunks]
+    base_ref, lines_ref, work = refs[count * chunks :]
+    four = ids_ref[1] if dynamic else 0
+    rates = helmholtz_rates(ids_ref[1], modes)
     flags = glued_flags(partner_ref)
-    for index in range(count):
-        for point in range(POINTS):
-            base_ref[pl.ds(point * 64 + index * group, group), :] = recv_ref[
-                index, pl.ds(point * group, group), :
-            ]
+    for chunk in range(chunks):
+        for place in range(count):
+            ref = recv_refs[chunk * count + place]
+            ready = ref.shape[0] // step
+            first = (block_of(place, four) * chunks + chunk) * step
+            values = unpack_lanes([ref[pl.ds(at * step, step), :] for at in range(ready)], modes)
+            for point in range(POINTS):
+                at = point * 64 + first
+                at = at if isinstance(at, int) else pl.multiple_of(at, step)
+                base_ref[pl.ds(at, step), :] = values[point]
     masks = col_masks(flags)
     for ey in range(BLOCKS):
         for iy in range(6):
@@ -417,48 +537,47 @@
             put(base_ref, 6 * iy + 5, ey, last)
     join_rows(base_ref, flags)
     apply_local(base_ref, work, rates, flags)
-    write_lines(base_ref, lines_ref, 0)
-    write_lines(work, lines_ref, 4 * SIDE)
-
-
-def second_kernel(
-    modes, four_ref, partner_ref, side_ref, flip_ref, gath_ref, lines_ref, base_ref,
-    k0_ref, k1_ref, k2_ref, next_ref, work,
-):
-    rates = helmholtz_rates(four_ref[0], modes)
+    write_lines(base_ref, lines_ref, 0, modes)
+    write_lines(work, lines_ref, line_rows(modes), modes)
+
+
+def second_kernel(modes, slots, ids_ref, partner_ref, side_ref, flip_ref, *refs):
+    gath_refs = refs[:slots]
+    lines_ref, base_ref, k0_ref, k1_ref, k2_ref, next_ref, work, sides = refs[slots:]
+    rates = helmholtz_rates(ids_ref[1], modes)
     flags = glued_flags(partner_ref)
-    tables = (partner_ref, side_ref, flip_ref)
-    back = own_reaction(lines_ref, rates, flags, 1.0)
+    collect_sides(gath_refs, ids_ref[0], partner_ref, side_ref, sides, modes)
+    back = own_reaction(load_lines(lines_ref, modes), rates, flags, 1.0)
     k0_ref[...] = base_ref[...]
-    add_lines(k0_ref, incoming_lines(gath_ref, 0, *tables))
+    add_lines(k0_ref, incoming_lines(sides, 0, partner_ref, flip_ref))
     apply_local(k0_ref, work, rates, flags)
-    add_lines(work, incoming_lines(gath_ref, 4 * SIDE, *tables))
+    add_lines(work, incoming_lines(sides, 1, partner_ref, flip_ref))
     add_lines(work, back)
     combine(k1_ref, [(1.0 / SPREAD, work), (-CENTRE / SPREAD, k0_ref)])
     apply_local(k1_ref, work, rates, flags)
-    write_lines(work, next_ref, 0)
+    write_lines(work, next_ref, 0, modes)
     combine(k2_ref, [(TWICE, work), (-CENTRE * TWICE, k1_ref), (-1.0, k0_ref)])
     apply_local(k2_ref, work, rates, flags)
-    write_lines(work, next_ref, 4 * SIDE)
-
-
-def third_kernel(
-    modes, four_ref, partner_ref, side_ref, flip_ref, gath_ref, lines_ref, k0_ref, k1_ref, base_ref,
-    k2_ref, k3_ref, a3_ref, next_ref, work,
-):
-    rates = helmholtz_rates(four_ref[0], modes)
+    write_lines(work, next_ref, line_rows(modes), modes)
+
+
+def third_kernel(modes, slots, ids_ref, partner_ref, side_ref, flip_ref, *refs):
+    gath_refs = refs[:slots]
+    lines_ref, k0_ref, k1_ref, base_ref = refs[slots : slots + 4]
+    k2_ref, k3_ref, a3_ref, next_ref, work, sides = refs[slots + 4 :]
+    rates = helmholtz_rates(ids_ref[1], modes)
     flags = glued_flags(partner_ref)
-    tables = (partner_ref, side_ref, flip_ref)
-    back = own_reaction(lines_ref, rates, flags, TWICE)
+    collect_sides(gath_refs, ids_ref[0], partner_ref, side_ref, sides, modes)
+    back = own_reaction(load_lines(lines_ref, modes), rates, flags, TWICE)
     k2_ref[...] = base_ref[...]
-    incoming = incoming_lines(gath_ref, 0, *tables)
+    incoming = incoming_lines(sides, 0, partner_ref, flip_ref)
     add_lines(k2_ref, [[value * TWICE for value in line] for line in incoming])
     apply_local(k2_ref, work, rates, flags)
-    add_lines(work, incoming_lines(gath_ref, 4 * SIDE, *tables))
+    add_lines(work, incoming_lines(sides, 1, partner_ref, flip_ref))
     add_lines(work, back)
     combine(k3_ref, [(TWICE, work), (-CENTRE * TWICE, k2_ref), (-1.0, k1_ref)])
     energy = apply_local(k3_ref, a3_ref, rates, flags, energy=True)
-    write_lines(a3_ref, next_ref, 0)
+    write_lines(a3_ref, next_ref, 0, modes)
     refs = (k0_ref, k1_ref, k2_ref, k3_ref)
 
     def body(ey, sums):
@@ -479,7 +598,7 @@
     rows = [jnp.sum(value, axis=0, keepdims=True) for value in sums]
     rows.append(jnp.sum(energy, axis=0, keepdims=True))
     rows.append(jnp.zeros((SUM_ROWS - len(rows), LANES), F32))
-    next_ref[pl.ds(4 * SIDE, SUM_ROWS), :] = jnp.concatenate(rows, axis=0)
+    next_ref[pl.ds(line_rows(modes), SUM_ROWS), :] = jnp.concatenate(rows, axis=0)
 
 
 def conjugate_coefficients(gram, energy):
@@ -544,18 +663,21 @@
     return solution, residual
 
 
-def last_kernel(
-    which, starts, partner_ref, side_ref, flip_ref, gath_ref, k0_ref, k1_ref, k2_ref, k3_ref, base_ref,
-    order_ref, sol_ref, res_ref, work, sol_rows, res_rows, flat,
-):
-    parts = gath_ref.shape[0]
+def last_kernel(which, starts, slots, ids_ref, partner_ref, side_ref, flip_ref, *refs):
+    gath_refs = refs[:slots]
+    k0_ref, k1_ref, k2_ref, k3_ref, base_ref, order_ref, sol_ref, res_ref = refs[slots : slots + 8]
+    work, sol_rows, res_rows, flat, sides = refs[slots + 8 :]
     count, rows, _ = sol_rows.shape
     group = rows // POINTS
     modes = sol_ref.shape[1]
     width = order_ref.shape[2]
-    sums = gath_ref[0, pl.ds(4 * SIDE, SUM_ROWS), :]
-    for part in range(1, parts):
-        sums = sums + gath_ref[part, pl.ds(4 * SIDE, SUM_ROWS), :]
+    where = pl.ds(line_rows(modes), SUM_ROWS)
+    if slots == 1:
+        parts = [gath_refs[0][part, where, :] for part in range(gath_refs[0].shape[0])]
+    else:
+        parts = [ref[where, :] for ref in gath_refs]
+    sums = functools.reduce(lambda left, right: left + right, parts)
+    collect_sides(gath_refs, ids_ref[0], partner_ref, side_ref, sides, modes)
 
     def row(place):
         return jnp.broadcast_to(sums[place : place + 1, :], (8, LANES))
@@ -569,7 +691,7 @@
             place += 1
     solution, residual = conjugate_coefficients(gram, row(place))
     work[...] = base_ref[...]
-    add_lines(work, incoming_lines(gath_ref, 0, partner_ref, side_ref, flip_ref))
+    add_lines(work, incoming_lines(sides, 0, partner_ref, flip_ref))
     on_a3 = residual[4] * TWICE
     on_k3 = residual[3] - on_a3 * CENTRE
     on_k2 = residual[2] - residual[4]
@@ -620,64 +742,111 @@
     )(*args)
 
 
+def swap_blocks(blocks, dynamic):
+    if not dynamic:
+        stacked = lax.all_to_all(jnp.stack(blocks), "four", split_axis=0, concat_axis=0, tiled=True)
+        return [stacked[place] for place in range(len(blocks))]
+    size = len(blocks)
+    return [blocks[0]] + [
+        lax.ppermute(blocks[place], "four", [(i, i ^ place) for i in range(size)])
+        for place in range(1, size)
+    ]
+
+
+def share_lines(lines):
+    parts = lax.axis_size("dom")
+    if parts != 8:
+        return [lax.all_gather(lines, "dom", axis=0, tiled=False)]
+    slots = [lines] + [None] * (parts - 1)
+    for slot in range(2, parts, 2):
+        slots[slot] = lax.ppermute(lines, "dom", [(i, i ^ slot) for i in range(parts)])
+    for slot in range(0, parts, 2):
+        slots[slot + 1] = lax.ppermute(slots[slot], "dom", [(i, i ^ 1) for i in range(parts)])
+    return slots
+
+
 def shards(velocity, partner, partner_side, flipped):
     modes = velocity.shape[1]
     count = lax.axis_size("four")
-    rows = NODES // count
+    step, chunks = chunk_sizes(count)
+    rows = POINTS * step
+    sent_rows = 3 * rows // 4 if is_packed(modes) else rows
+    dynamic = step == BLOCKS
     (inv_high, inv_low), (back_high, back_low) = transform_tables(count)
     order, which, starts = order_tables(count)
-    four = lax.axis_index("four").astype(jnp.int32).reshape(1)
+    ids = jnp.stack([lax.axis_index("dom"), lax.axis_index("four")]).astype(jnp.int32)
     field = (NODES, LANES)
-    swapped = (count, rows, LANES)
-
-    (sent,) = call(
-        functools.partial(pack_kernel, which, starts), "pack", [swapped], (velocity, order), []
-    )
-    spread = lax.all_to_all(sent, "four", split_axis=0, concat_axis=0, tiled=True)
-    (sent,) = call(
-        product_kernel,
-        "products",
-        [swapped],
-        (spread, inv_high, inv_low, back_high, back_low),
-        [(rows, 3 * LANES), (rows, 6 * LANES), (rows, count * LANES)],
-    )
-    local = lax.all_to_all(sent, "four", split_axis=0, concat_axis=0, tiled=True)
+    blocks = [(sent_rows, LANES)] * count
+    lined = line_rows(modes)
+
+    spread = []
+    for chunk in range(chunks):
+        mine = which[chunk::chunks]
+        used = sorted(set(mine))
+        sent = call(
+            functools.partial(pack_kernel, step, count, dynamic),
+            "pack",
+            blocks,
+            (
+                ids,
+                np.array([used.index(one) for one in mine], np.int32),
+                np.array(starts[chunk::chunks], np.int32),
+                velocity,
+                order[np.array(used)],
+            ),
+            [],
+            scalars=3,
+        )
+        spread.append(swap_blocks(sent, dynamic))
+    local = []
+    for chunk in range(chunks):
+        sent = call(
+            functools.partial(product_kernel, modes, step, count, dynamic),
+            "products",
+            blocks,
+            (ids, *spread[chunk], inv_high, inv_low, back_high, back_low),
+            [(count, rows, LANES), (rows, 3 * LANES), (rows, 6 * LANES), (3, rows, LANES)],
+            scalars=1,
+        )
+        local += swap_blocks(sent, dynamic)
 
     base, lines = call(
-        functools.partial(first_kernel, modes),
+        functools.partial(first_kernel, modes, step, count, chunks, dynamic),
         "first",
-        [field, (8 * SIDE, LANES)],
-        (four, partner, local),
+        [field, (2 * lined, LANES)],
+        (ids, partner, *local),
         [field],
         scalars=2,
     )
-    tables = (partner, partner_side, flipped)
-    gathered = lax.all_gather(lines, "dom", axis=0, tiled=False)
+    tables = (ids, partner, partner_side, flipped)
+    gathered = share_lines(lines)
+    slots = len(gathered)
     k0, k1, base, lines = call(
-        functools.partial(second_kernel, modes),
+        functools.partial(second_kernel, modes, slots),
         "second",
-        [field, field, field, (8 * SIDE, LANES)],
-        (four, *tables, gathered, lines, base),
-        [field],
+        [field, field, field, (2 * lined, LANES)],
+        (*tables, *gathered, lines, base),
+        [field, (4, 2 * SIDE, LANES)],
         scalars=4,
     )
-    gathered = lax.all_gather(lines, "dom", axis=0, tiled=False)
+    gathered = share_lines(lines)
     k2, k3, a3, lines = call(
-        functools.partial(third_kernel, modes),
+        functools.partial(third_kernel, modes, slots),
         "third",
-        [field, field, field, (4 * SIDE + SUM_ROWS, LANES)],
-        (four, *tables, gathered, lines, k0, k1, base),
-        [field],
+        [field, field, field, (lined + SUM_ROWS, LANES)],
+        (*tables, *gathered, lines, k0, k1, base),
+        [field, (4, 2 * SIDE, LANES)],
         scalars=4,
     )
-    gathered = lax.all_gather(lines, "dom", axis=0, tiled=False)
+    gathered = share_lines(lines)
+    units = count * chunks
     outs = call(
-        functools.partial(last_kernel, which, starts),
+        functools.partial(last_kernel, which, starts, slots),
         "last",
         [velocity.shape, velocity.shape],
-        (*tables, gathered, k0, k1, k2, k3, a3, order),
-        [field, swapped, swapped, (LANES, NODES)],
-        scalars=3,
+        (*tables, *gathered, k0, k1, k2, k3, a3, order),
+        [field, (units, rows, LANES), (units, rows, LANES), (LANES, NODES), (4, SIDE, LANES)],
+        scalars=4,
     )
     return tuple(outs)
 

time: 159 us -> 108 us (0.68)
  blocking collectives: 38.3 us -> 0 us
  waiting for transfers between devices: 64.2 us -> 33 us
  starting transfers between devices: 3.61 us -> 29.7 us
  between operations: 14.1 us -> 0.86 us
  local copies, waits for them, and re-layouts: 1.02 us -> 3.87 us
  Pallas kernels: 37.3 us -> 40.1 us
    all_gather x2 -> x0, waiting for transfers between devices: 49.8 us -> none  [shards(): gathered = lax.all_gather(lines, 'dom', axis=0, tiled=False)]
    ppermute x0 -> x33, waiting for transfers between devices: none -> 33 us  [the longest x9 24.2 us: share_lines(): lax.ppermute(lines, 'dom', [(i, i ^ slot) for i in range(parts)])]
    ppermute x0 -> x33, starting transfers between devices: none -> 29.7 us  [the longest x12 15 us: swap_blocks(): lax.ppermute(blocks[place], 'four', [(i, i ^ place) for i in range(size)])]
    all_to_all x1 -> x0, blocking collectives: 21.4 us -> none  [shards(): lax.all_to_all(sent, 'four', split_axis=0, concat_axis=0, tiled=True)]
    all_gather x1 -> x0, blocking collectives: 16.9 us -> none  [shards(): gathered = lax.all_gather(lines, 'dom', axis=0, tiled=False)]
    all_to_all x1 -> x0, waiting for transfers between devices: 14.3 us -> none  [shards(): lax.all_to_all(sent, 'four', split_axis=0, concat_axis=0, tiled=True)]
    all_to_all x1 -> x0, starting transfers between devices: 3.53 us -> none  [shards(): lax.all_to_all(sent, 'four', split_axis=0, concat_axis=0, tiled=True)]
    unnamed x2 -> x66, local copies, waits for them, and re-layouts: 1.02 us -> 3.87 us
  transfers between devices with their start and end apart: 3 -> 33, of which waited for: 3 -> 15; matrix products, arithmetic and copies ran while one was open for 0% -> 0% of each run, Pallas kernels for 0% -> 10%
where the time goes in v2:
time: 108 us
  Pallas kernels  40.1 us (37%)
  waiting for transfers between devices  33 us (31%)
  starting transfers between devices  29.7 us (28%)
  local copies, waits for them, and re-layouts  3.87 us (4%)
    pallas_call x8, Pallas kernels, call(): pl.pallas_call(kernel, name=name, out_shape=[jax.ShapeDtypeStruct(shape,...  40.1 us
    ppermute x9, waiting for transfers between devices, share_lines(): lax.ppermute(lines, 'dom', [(i, i ^ slot) for i in range(parts)])  24.2 us
    ppermute x12, starting transfers between devices, swap_blocks(): lax.ppermute(blocks[place], 'four', [(i, i ^ place) for i in range(size)])  15 us
    ppermute x9, starting transfers between devices, share_lines(): lax.ppermute(lines, 'dom', [(i, i ^ slot) for i in range(parts)])  13.2 us
    ppermute x12, waiting for transfers between devices, swap_blocks(): lax.ppermute(blocks[place], 'four', [(i, i ^ place) for i in range(size)])  5.82 us
    unnamed x66, local copies, waits for them, and re-layouts  3.87 us
    ppermute x12, waiting for transfers between devices, share_lines(): lax.ppermute(slots[slot], 'dom', [(i, i ^ 1) for i in range(parts)])  3 us
  transfers between devices with their start and end apart: 33, of which 15 were waited for; matrix products, arithmetic and copies ran while one was open for 0% of the time, Pallas kernels for 10%

profile of v2, /device:TPU:0, one launch (start us, length us, event | category | flops | bytes accessed | tf_op | source)
XLA Modules:
  0.0 108.1 jit_solution(13137027044019693032)
XLA Ops:
  0.6 0.6 pad_add_fusion.ids_ref
  1.2 2.6 %pack.2 = (f32[216,128]{1,0:T(8,128)}, f32[216,128]{1,0:T(8,128)}, f32[216,128]{1,0:T(8,128)}, f32[216,128]{1,0:T(8,128)}) custom-call(s32[2]{0:T(128)} %pad_add_fusion.ids_ref, s32[4]{0:T(128)} %constant.29.clone.which_ref, s32[4]{0:T(128)} %constant.30.clone.starts_ref, f32[3,32,2304]{2,1,0:T(8,128)} %velocity_ref.3, ...), custom_call_target="tpu_custom_call" | custom-call | tf_op jit(solution)/shard_map/pack/pallas_call | solution.py:734
  3.8 2.9 %collective-permute-start = (f32[216,128]{1,0:T(8,128)}, f32[216,128]{1,0:T(8,128)S(1)}, u32[]{:S(2)}, u32[]{:S(2)}) collective-permute-start(f32[216,128]{1,0:T(8,128)} %get-tuple-element.29), channel_id=1, source_target_pairs={{0,1},{1,0},{2,3},{3,2},{4,5},{5,4},{6,7},{7,6},{8,9},{9,8},{10,11... | collective-permute-start | bytes 331784 | tf_op jit(solution)/shard_map/ppermute | solution.py:751
  6.7 1.5 %collective-permute-start.1 = (f32[216,128]{1,0:T(8,128)}, f32[216,128]{1,0:T(8,128)S(1)}, u32[]{:S(2)}, u32[]{:S(2)}) collective-permute-start(f32[216,128]{1,0:T(8,128)} %get-tuple-element.30), channel_id=1, source_target_pairs={{0,2},{1,3},{2,0},{3,1},{4,6},{5,7},{6,4},{7,5},{8,10},{9,11},{10,... | collective-permute-start | bytes 331784 | tf_op jit(solution)/shard_map/ppermute | solution.py:751
  8.3 0.0 collective-permute-start.2
  8.3 2.6 %pack.3 = (f32[216,128]{1,0:T(8,128)}, f32[216,128]{1,0:T(8,128)}, f32[216,128]{1,0:T(8,128)}, f32[216,128]{1,0:T(8,128)}) custom-call(s32[2]{0:T(128)} %pad_add_fusion.ids_ref, s32[4]{0:T(128)} %constant.29.clone.which_ref, s32[4]{0:T(128)} %constant.32.clone.starts_ref, f32[3,32,2304]{2,1,0:T(8,128)} %velocity_ref.3, ...), custom_call_target="tpu_custom_call" | custom-call | tf_op jit(solution)/shard_map/pack/pallas_call | solution.py:734
  10.9 2.0 %collective-permute-start.6 = (f32[216,128]{1,0:T(8,128)}, f32[216,128]{1,0:T(8,128)S(1)}, u32[]{:S(2)}, u32[]{:S(2)}) collective-permute-start(f32[216,128]{1,0:T(8,128)} %get-tuple-element.37), channel_id=1, source_target_pairs={{0,1},{1,0},{2,3},{3,2},{4,5},{5,4},{6,7},{7,6},{8,9},{9,8},{10,11... | collective-permute-start | bytes 331784 | tf_op jit(solution)/shard_map/ppermute | solution.py:751
  12.8 1.5 %collective-permute-start.7 = (f32[216,128]{1,0:T(8,128)}, f32[216,128]{1,0:T(8,128)S(1)}, u32[]{:S(2)}, u32[]{:S(2)}) collective-permute-start(f32[216,128]{1,0:T(8,128)} %get-tuple-element.38), channel_id=1, source_target_pairs={{0,2},{1,3},{2,0},{3,1},{4,6},{5,7},{6,4},{7,5},{8,10},{9,11},{10,... | collective-permute-start | bytes 331784 | tf_op jit(solution)/shard_map/ppermute | solution.py:751
  14.4 0.0 collective-permute-done.refs_1_
  14.4 0.0 collective-permute-start.8
  14.4 0.6 copy-done.17
  15.0 0.0 copy-done.18
  15.0 0.0 copy-done.19
  15.1 4.1 %products.2 = (f32[216,128]{1,0:T(8,128)}, f32[216,128]{1,0:T(8,128)}, f32[216,128]{1,0:T(8,128)}, f32[216,128]{1,0:T(8,128)}) custom-call(s32[2]{0:T(128)} %pad_add_fusion.ids_ref, f32[216,128]{1,0:T(8,128)} %get-tuple-element.28.refs_0_, f32[216,128]{1,0:T(8,128)} %copy-done.17, f32[216,128]{1,0:T(8,128)} %copy-done.18, f32[216,128]{1,0:T(8,128)} %copy-done.19, ...), custom_call_target="tpu_custom_call" | custom-call | tf_op jit(solution)/shard_map/products/pallas_call | solution.py:734
  19.2 2.0 %collective-permute-start.3 = (f32[216,128]{1,0:T(8,128)}, f32[216,128]{1,0:T(8,128)S(1)}, u32[]{:S(2)}, u32[]{:S(2)}) collective-permute-start(f32[216,128]{1,0:T(8,128)} %get-tuple-element.33), channel_id=1, source_target_pairs={{0,1},{1,0},{2,3},{3,2},{4,5},{5,4},{6,7},{7,6},{8,9},{9,8},{10,11... | collective-permute-start | bytes 331784 | tf_op jit(solution)/shard_map/ppermute | solution.py:751
  21.1 1.5 %collective-permute-start.4 = (f32[216,128]{1,0:T(8,128)}, f32[216,128]{1,0:T(8,128)S(1)}, u32[]{:S(2)}, u32[]{:S(2)}) collective-permute-start(f32[216,128]{1,0:T(8,128)} %get-tuple-element.34), channel_id=1, source_target_pairs={{0,2},{1,3},{2,0},{3,1},{4,6},{5,7},{6,4},{7,5},{8,10},{9,11},{10,... | collective-permute-start | bytes 331784 | tf_op jit(solution)/shard_map/ppermute | solution.py:751
  22.7 0.0 collective-permute-start.5
  22.7 0.0 collective-permute-done.8.refs_3_
  22.7 0.6 copy-done.14
  23.3 0.0 copy-done.15
  23.3 0.0 copy-done.16
  23.4 4.1 %products.3 = (f32[216,128]{1,0:T(8,128)}, f32[216,128]{1,0:T(8,128)}, f32[216,128]{1,0:T(8,128)}, f32[216,128]{1,0:T(8,128)}) custom-call(s32[2]{0:T(128)} %pad_add_fusion.ids_ref, f32[216,128]{1,0:T(8,128)} %get-tuple-element.36.refs_0_, f32[216,128]{1,0:T(8,128)} %copy-done.14, f32[216,128]{1,0:T(8,128)} %copy-done.15, f32[216,128]{1,0:T(8,128)} %copy-done.16, ...), custom_call_target="tpu_custom_call" | custom-call | tf_op jit(solution)/shard_map/products/pallas_call | solution.py:734
  27.4 1.9 %collective-permute-start.9 = (f32[216,128]{1,0:T(8,128)}, f32[216,128]{1,0:T(8,128)S(1)}, u32[]{:S(2)}, u32[]{:S(2)}) collective-permute-start(f32[216,128]{1,0:T(8,128)} %get-tuple-element.41), channel_id=1, source_target_pairs={{0,1},{1,0},{2,3},{3,2},{4,5},{5,4},{6,7},{7,6},{8,9},{9,8},{10,11... | collective-permute-start | bytes 331784 | tf_op jit(solution)/shard_map/ppermute | solution.py:751
  29.4 1.5 %collective-permute-start.10 = (f32[216,128]{1,0:T(8,128)}, f32[216,128]{1,0:T(8,128)S(1)}, u32[]{:S(2)}, u32[]{:S(2)}) collective-permute-start(f32[216,128]{1,0:T(8,128)} %get-tuple-element.42), channel_id=1, source_target_pairs={{0,2},{1,3},{2,0},{3,1},{4,6},{5,7},{6,4},{7,5},{8,10},{9,11},{10,... | collective-permute-start | bytes 331784 | tf_op jit(solution)/shard_map/ppermute | solution.py:751
  30.9 0.0 collective-permute-done.3.refs_1_
  30.9 0.0 collective-permute-start.11
  30.9 0.0 collective-permute-done.4.refs_2_
  31.0 1.8 %collective-permute-done.9.refs_5_ = f32[216,128]{1,0:T(8,128)S(1)} collective-permute-done((f32[216,128]{1,0:T(8,128)}, f32[216,128]{1,0:T(8,128)S(1)}, u32[]{:S(2)}, u32[]{:S(2)}) %collective-permute-start.9) | collective-permute-done | bytes 110624 | tf_op jit(solution)/shard_map/ppermute | solution.py:751
  32.8 1.6 %collective-permute-done.10.refs_6_ = f32[216,128]{1,0:T(8,128)S(1)} collective-permute-done((f32[216,128]{1,0:T(8,128)}, f32[216,128]{1,0:T(8,128)S(1)}, u32[]{:S(2)}, u32[]{:S(2)}) %collective-permute-start.10) | collective-permute-done | bytes 110624 | tf_op jit(solution)/shard_map/ppermute | solution.py:751
  34.3 2.4 %collective-permute-done.11.refs_7_ = f32[216,128]{1,0:T(8,128)S(1)} collective-permute-done((f32[216,128]{1,0:T(8,128)}, f32[216,128]{1,0:T(8,128)S(1)}, u32[]{:S(2)}, u32[]{:S(2)}) %collective-permute-start.11) | collective-permute-done | bytes 110624 | tf_op jit(solution)/shard_map/ppermute | solution.py:751
  36.8 0.6 copy-done.25
  37.4 3.8 %first.1 = (f32[2304,128]{1,0:T(8,128)}, f32[288,128]{1,0:T(8,128)}) custom-call(s32[2]{0:T(128)} %pad_add_fusion.ids_ref, s32[1,4]{1,0:T(1,128)} %partner_ref.7, f32[216,128]{1,0:T(8,128)} %get-tuple-element.32.refs_0_, f32[216,128]{1,0:T(8,128)} %copy-done.20, f32[216,128]{1,0:T(8,128)} %copy-done.21, f32[216,128]{1,0:T(8,128)} %copy-done.22, ...), custom_call_target="tpu_custom_call" | custom-call | tf_op jit(solution)/shard_map/first/pallas_call | solution.py:734
  41.2 3.6 %collective-permute-start.17 = (f32[288,128]{1,0:T(8,128)}, f32[288,128]{1,0:T(8,128)S(1)}, u32[]{:S(2)}, u32[]{:S(2)}) collective-permute-start(f32[288,128]{1,0:T(8,128)} %get-tuple-element.44.refs_0_.refs_8_), channel_id=1, source_target_pairs={{0,24},{4,28},{8,16},{12,20},{16,8},{20,12},{24,0},{28,4},{1,25},{... | collective-permute-start | bytes 442376 | tf_op jit(solution)/shard_map/ppermute | solution.py:762
  44.8 0.8 collective-permute-start.13
  45.6 2.9 %collective-permute-done.17.refs_6_ = f32[288,128]{1,0:T(8,128)S(1)} collective-permute-done((f32[288,128]{1,0:T(8,128)}, f32[288,128]{1,0:T(8,128)S(1)}, u32[]{:S(2)}, u32[]{:S(2)}) %collective-permute-start.17) | collective-permute-done | bytes 147488 | tf_op jit(solution)/shard_map/ppermute | solution.py:762
  48.4 4.8 %collective-permute-done.15.refs_4_ = f32[288,128]{1,0:T(8,128)S(1)} collective-permute-done((f32[288,128]{1,0:T(8,128)}, f32[288,128]{1,0:T(8,128)S(1)}, u32[]{:S(2)}, u32[]{:S(2)}) %collective-permute-start.15) | collective-permute-done | bytes 147488 | tf_op jit(solution)/shard_map/ppermute | solution.py:762
  53.3 0.5 collective-permute-start.14
  53.8 0.8 collective-permute-done.16.refs_5_
  54.6 0.2 collective-permute-done.14.refs_3_
  54.9 0.4 copy-done.10
  55.3 0.2 copy-done.12
  55.5 7.5 %second.1 = (f32[2304,128]{1,0:T(8,128)}, f32[2304,128]{1,0:T(8,128)}, f32[2304,128]{1,0:T(8,128)}, f32[288,128]{1,0:T(8,128)}) custom-call(s32[2]{0:T(128)} %pad_add_fusion.ids_ref, s32[1,4]{1,0:T(1,128)} %partner_ref.7, s32[1,4]{1,0:T(1,128)} %side_ref.5, s32[1,4]{1,0:T(1,128)} %flip_ref.5, f32[288,128]{1,0:T(8,128)} %get-tuple-element.44.refs_0_.refs_8_, ...), custom_call_target="tpu_custom_call" | custom-call | tf_op jit(solution)/shard_map/second/pallas_call | solution.py:734
  63.0 2.6 %collective-permute-start.24 = (f32[288,128]{1,0:T(8,128)}, f32[288,128]{1,0:T(8,128)S(1)}, u32[]{:S(2)}, u32[]{:S(2)}) collective-permute-start(f32[288,128]{1,0:T(8,128)} %get-tuple-element.46.refs_0_.refs_8_), channel_id=1, source_target_pairs={{0,24},{4,28},{8,16},{12,20},{16,8},{20,12},{24,0},{28,4},{1,25},{... | collective-permute-start | bytes 442376 | tf_op jit(solution)/shard_map/ppermute | solution.py:762
  65.5 1.8 %collective-permute-start.20 = (f32[288,128]{1,0:T(8,128)}, f32[288,128]{1,0:T(8,128)S(1)}, u32[]{:S(2)}, u32[]{:S(2)}) collective-permute-start(f32[288,128]{1,0:T(8,128)} %get-tuple-element.46.refs_0_.refs_8_), channel_id=1, source_target_pairs={{0,8},{4,12},{8,0},{12,4},{16,24},{20,28},{24,16},{28,20},{1,9},{5... | collective-permute-start | bytes 442376 | tf_op jit(solution)/shard_map/ppermute | solution.py:762
  67.4 4.4 %collective-permute-done.24.refs_6_ = f32[288,128]{1,0:T(8,128)S(1)} collective-permute-done((f32[288,128]{1,0:T(8,128)}, f32[288,128]{1,0:T(8,128)S(1)}, u32[]{:S(2)}, u32[]{:S(2)}) %collective-permute-start.24) | collective-permute-done | bytes 147488 | tf_op jit(solution)/shard_map/ppermute | solution.py:762
  71.8 6.1 %collective-permute-done.22.refs_4_ = f32[288,128]{1,0:T(8,128)S(1)} collective-permute-done((f32[288,128]{1,0:T(8,128)}, f32[288,128]{1,0:T(8,128)S(1)}, u32[]{:S(2)}, u32[]{:S(2)}) %collective-permute-start.22) | collective-permute-done | bytes 147488 | tf_op jit(solution)/shard_map/ppermute | solution.py:762
  77.9 0.0 copy-start.5
  77.9 0.5 collective-permute-start.21
  78.4 0.8 collective-permute-done.23.refs_5_
  79.3 0.2 collective-permute-done.21.refs_3_
  79.5 0.4 copy-done.11
  79.9 0.2 copy-done.13
  80.2 8.0 %third.1 = (f32[2304,128]{1,0:T(8,128)}, f32[2304,128]{1,0:T(8,128)}, f32[2304,128]{1,0:T(8,128)}, f32[160,128]{1,0:T(8,128)}) custom-call(s32[2]{0:T(128)} %pad_add_fusion.ids_ref, s32[1,4]{1,0:T(1,128)} %partner_ref.7, s32[1,4]{1,0:T(1,128)} %side_ref.5, s32[1,4]{1,0:T(1,128)} %flip_ref.5, f32[288,128]{1,0:T(8,128)} %get-tuple-element.46.refs_0_.refs_8_, ...), custom_call_target="tpu_custom_call" | custom-call | tf_op jit(solution)/shard_map/third/pallas_call | solution.py:734
  88.2 2.1 %collective-permute-start.31 = (f32[160,128]{1,0:T(8,128)}, f32[160,128]{1,0:T(8,128)S(1)}, u32[]{:S(2)}, u32[]{:S(2)}) collective-permute-start(f32[160,128]{1,0:T(8,128)} %get-tuple-element.50.refs_0_), channel_id=1, source_target_pairs={{0,24},{4,28},{8,16},{12,20},{16,8},{20,12},{24,0},{28,4},{1,25},{... | collective-permute-start | bytes 245768 | tf_op jit(solution)/shard_map/ppermute | solution.py:762
  90.3 2.2 %collective-permute-start.27 = (f32[160,128]{1,0:T(8,128)}, f32[160,128]{1,0:T(8,128)S(1)}, u32[]{:S(2)}, u32[]{:S(2)}) collective-permute-start(f32[160,128]{1,0:T(8,128)} %get-tuple-element.50.refs_0_), channel_id=1, source_target_pairs={{0,8},{4,12},{8,0},{12,4},{16,24},{20,28},{24,16},{28,20},{1,9},{5... | collective-permute-start | bytes 245768 | tf_op jit(solution)/shard_map/ppermute | solution.py:762
  92.6 3.0 %collective-permute-done.31.refs_6_ = f32[160,128]{1,0:T(8,128)S(1)} collective-permute-done((f32[160,128]{1,0:T(8,128)}, f32[160,128]{1,0:T(8,128)S(1)}, u32[]{:S(2)}, u32[]{:S(2)}) %collective-permute-start.31) | collective-permute-done | bytes 81952 | tf_op jit(solution)/shard_map/ppermute | solution.py:762
  95.5 3.0 %collective-permute-done.29.refs_4_ = f32[160,128]{1,0:T(8,128)S(1)} collective-permute-done((f32[160,128]{1,0:T(8,128)}, f32[160,128]{1,0:T(8,128)S(1)}, u32[]{:S(2)}, u32[]{:S(2)}) %collective-permute-start.29) | collective-permute-done | bytes 81952 | tf_op jit(solution)/shard_map/ppermute | solution.py:762
  98.6 0.0 collective-permute-start.30
  98.6 0.5 collective-permute-start.28
  99.1 0.7 collective-permute-done.30.refs_5_
  99.8 0.2 collective-permute-done.28.refs_3_
  100.0 0.4 copy-done.31
  100.5 0.2 copy-done.32
  100.6 7.5 %last.1 = (f32[3,32,2304]{2,1,0:T(8,128)}, f32[3,32,2304]{2,1,0:T(8,128)}) custom-call(s32[2]{0:T(128)} %pad_add_fusion.ids_ref, s32[1,4]{1,0:T(1,128)} %partner_ref.7, s32[1,4]{1,0:T(1,128)} %side_ref.5, s32[1,4]{1,0:T(1,128)} %flip_ref.5, f32[160,128]{1,0:T(8,128)} %get-tuple-element.50.refs_0_, f32[160,128]{1,0:T(8,128)} %copy-done.29, ...), custom_call_target="tpu_custom_call" | custom-call | tf_op jit(solution)/shard_map/last/pallas_call | solution.py:734
  (77 shorter events, 0.2 us)
Async XLA Ops:
  3.8 10.6 %collective-permute-start = (f32[216,128]{1,0:T(8,128)}, f32[216,128]{1,0:T(8,128)S(1)}, u32[]{:S(2)}, u32[]{:S(2)}) collective-permute-start(f32[216,128]{1,0:T(8,128)} %get-tuple-element.29), channel_id=1, source_target_pairs={{0,1},{1,0},{2,3},{3,2},{4,5},{5,4},{6,7},{7,6},{8,9},{9,8},{10,11... | collective-permute-start | bytes 331784 | tf_op jit(solution)/shard_map/ppermute | solution.py:751
  6.7 7.7 %collective-permute-start.1 = (f32[216,128]{1,0:T(8,128)}, f32[216,128]{1,0:T(8,128)S(1)}, u32[]{:S(2)}, u32[]{:S(2)}) collective-permute-start(f32[216,128]{1,0:T(8,128)} %get-tuple-element.30), channel_id=1, source_target_pairs={{0,2},{1,3},{2,0},{3,1},{4,6},{5,7},{6,4},{7,5},{8,10},{9,11},{10,... | collective-permute-start | bytes 331784 | tf_op jit(solution)/shard_map/ppermute | solution.py:751
  8.3 6.1 %collective-permute-start.2 = (f32[216,128]{1,0:T(8,128)}, f32[216,128]{1,0:T(8,128)S(1)}, u32[]{:S(2)}, u32[]{:S(2)}) collective-permute-start(f32[216,128]{1,0:T(8,128)} %get-tuple-element.31), channel_id=1, source_target_pairs={{0,3},{1,2},{2,1},{3,0},{4,7},{5,6},{6,5},{7,4},{8,11},{9,10},{10,... | collective-permute-start | bytes 331784 | tf_op jit(solution)/shard_map/ppermute | solution.py:751
  10.9 11.8 %collective-permute-start.6 = (f32[216,128]{1,0:T(8,128)}, f32[216,128]{1,0:T(8,128)S(1)}, u32[]{:S(2)}, u32[]{:S(2)}) collective-permute-start(f32[216,128]{1,0:T(8,128)} %get-tuple-element.37), channel_id=1, source_target_pairs={{0,1},{1,0},{2,3},{3,2},{4,5},{5,4},{6,7},{7,6},{8,9},{9,8},{10,11... | collective-permute-start | bytes 331784 | tf_op jit(solution)/shard_map/ppermute | solution.py:751
  12.8 9.9 %collective-permute-start.7 = (f32[216,128]{1,0:T(8,128)}, f32[216,128]{1,0:T(8,128)S(1)}, u32[]{:S(2)}, u32[]{:S(2)}) collective-permute-start(f32[216,128]{1,0:T(8,128)} %get-tuple-element.38), channel_id=1, source_target_pairs={{0,2},{1,3},{2,0},{3,1},{4,6},{5,7},{6,4},{7,5},{8,10},{9,11},{10,... | collective-permute-start | bytes 331784 | tf_op jit(solution)/shard_map/ppermute | solution.py:751
  14.4 0.6 copy-start.17
  14.4 8.3 %collective-permute-start.8 = (f32[216,128]{1,0:T(8,128)}, f32[216,128]{1,0:T(8,128)S(1)}, u32[]{:S(2)}, u32[]{:S(2)}) collective-permute-start(f32[216,128]{1,0:T(8,128)} %get-tuple-element.39), channel_id=1, source_target_pairs={{0,3},{1,2},{2,1},{3,0},{4,7},{5,6},{6,5},{7,4},{8,11},{9,10},{10,... | collective-permute-start | bytes 331784 | tf_op jit(solution)/shard_map/ppermute | solution.py:751
  14.4 0.6 copy-start.18
  14.4 0.7 copy-start.19
  19.2 11.7 %collective-permute-start.3 = (f32[216,128]{1,0:T(8,128)}, f32[216,128]{1,0:T(8,128)S(1)}, u32[]{:S(2)}, u32[]{:S(2)}) collective-permute-start(f32[216,128]{1,0:T(8,128)} %get-tuple-element.33), channel_id=1, source_target_pairs={{0,1},{1,0},{2,3},{3,2},{4,5},{5,4},{6,7},{7,6},{8,9},{9,8},{10,11... | collective-permute-start | bytes 331784 | tf_op jit(solution)/shard_map/ppermute | solution.py:751
  21.1 9.8 %collective-permute-start.4 = (f32[216,128]{1,0:T(8,128)}, f32[216,128]{1,0:T(8,128)S(1)}, u32[]{:S(2)}, u32[]{:S(2)}) collective-permute-start(f32[216,128]{1,0:T(8,128)} %get-tuple-element.34), channel_id=1, source_target_pairs={{0,2},{1,3},{2,0},{3,1},{4,6},{5,7},{6,4},{7,5},{8,10},{9,11},{10,... | collective-permute-start | bytes 331784 | tf_op jit(solution)/shard_map/ppermute | solution.py:751
  22.7 0.6 copy-start.14
  22.7 8.3 %collective-permute-start.5 = (f32[216,128]{1,0:T(8,128)}, f32[216,128]{1,0:T(8,128)S(1)}, u32[]{:S(2)}, u32[]{:S(2)}) collective-permute-start(f32[216,128]{1,0:T(8,128)} %get-tuple-element.35), channel_id=1, source_target_pairs={{0,3},{1,2},{2,1},{3,0},{4,7},{5,6},{6,5},{7,4},{8,11},{9,10},{10,... | collective-permute-start | bytes 331784 | tf_op jit(solution)/shard_map/ppermute | solution.py:751
  22.7 0.6 copy-start.15
  22.7 0.7 copy-start.16
  27.4 5.3 %collective-permute-start.9 = (f32[216,128]{1,0:T(8,128)}, f32[216,128]{1,0:T(8,128)S(1)}, u32[]{:S(2)}, u32[]{:S(2)}) collective-permute-start(f32[216,128]{1,0:T(8,128)} %get-tuple-element.41), channel_id=1, source_target_pairs={{0,1},{1,0},{2,3},{3,2},{4,5},{5,4},{6,7},{7,6},{8,9},{9,8},{10,11... | collective-permute-start | bytes 331784 | tf_op jit(solution)/shard_map/ppermute | solution.py:751
  29.4 5.0 %collective-permute-start.10 = (f32[216,128]{1,0:T(8,128)}, f32[216,128]{1,0:T(8,128)S(1)}, u32[]{:S(2)}, u32[]{:S(2)}) collective-permute-start(f32[216,128]{1,0:T(8,128)} %get-tuple-element.42), channel_id=1, source_target_pairs={{0,2},{1,3},{2,0},{3,1},{4,6},{5,7},{6,4},{7,5},{8,10},{9,11},{10,... | collective-permute-start | bytes 331784 | tf_op jit(solution)/shard_map/ppermute | solution.py:751
  30.9 5.9 %copy-start.20 = (f32[216,128]{1,0:T(8,128)}, f32[216,128]{1,0:T(8,128)S(1)}, u32[]{:S(2)}) copy-start(f32[216,128]{1,0:T(8,128)S(1)} %collective-permute-done.3.refs_1_) | copy-start | bytes 331780
  30.9 5.9 %collective-permute-start.11 = (f32[216,128]{1,0:T(8,128)}, f32[216,128]{1,0:T(8,128)S(1)}, u32[]{:S(2)}, u32[]{:S(2)}) collective-permute-start(f32[216,128]{1,0:T(8,128)} %get-tuple-element.43), channel_id=1, source_target_pairs={{0,3},{1,2},{2,1},{3,0},{4,7},{5,6},{6,5},{7,4},{8,11},{9,10},{10,... | collective-permute-start | bytes 331784 | tf_op jit(solution)/shard_map/ppermute | solution.py:751
  30.9 5.8 %copy-start.21 = (f32[216,128]{1,0:T(8,128)}, f32[216,128]{1,0:T(8,128)S(1)}, u32[]{:S(2)}) copy-start(f32[216,128]{1,0:T(8,128)S(1)} %collective-permute-done.4.refs_2_) | copy-start | bytes 331780
  31.0 5.8 %copy-start.22 = (f32[216,128]{1,0:T(8,128)}, f32[216,128]{1,0:T(8,128)S(1)}, u32[]{:S(2)}) copy-start(f32[216,128]{1,0:T(8,128)S(1)} %collective-permute-done.5.refs_3_) | copy-start | bytes 331780
  32.8 4.0 %copy-start.23 = (f32[216,128]{1,0:T(8,128)}, f32[216,128]{1,0:T(8,128)S(1)}, u32[]{:S(2)}) copy-start(f32[216,128]{1,0:T(8,128)S(1)} %collective-permute-done.9.refs_5_) | copy-start | bytes 331780
  34.3 2.5 %copy-start.24 = (f32[216,128]{1,0:T(8,128)}, f32[216,128]{1,0:T(8,128)S(1)}, u32[]{:S(2)}) copy-start(f32[216,128]{1,0:T(8,128)S(1)} %collective-permute-done.10.refs_6_) | copy-start | bytes 331780
  36.8 0.6 copy-start.25
  41.2 7.3 %collective-permute-start.17 = (f32[288,128]{1,0:T(8,128)}, f32[288,128]{1,0:T(8,128)S(1)}, u32[]{:S(2)}, u32[]{:S(2)}) collective-permute-start(f32[288,128]{1,0:T(8,128)} %get-tuple-element.44.refs_0_.refs_8_), channel_id=1, source_target_pairs={{0,24},{4,28},{8,16},{12,20},{16,8},{20,12},{24,0},{28,4},{1,25},{... | collective-permute-start | bytes 442376 | tf_op jit(solution)/shard_map/ppermute | solution.py:762
  44.8 8.5 %collective-permute-start.15 = (f32[288,128]{1,0:T(8,128)}, f32[288,128]{1,0:T(8,128)S(1)}, u32[]{:S(2)}, u32[]{:S(2)}) collective-permute-start(f32[288,128]{1,0:T(8,128)} %get-tuple-element.44.refs_0_.refs_8_), channel_id=1, source_target_pairs={{0,16},{4,20},{8,24},{12,28},{16,0},{20,4},{24,8},{28,12},{1,17},{... | collective-permute-start | bytes 442376 | tf_op jit(solution)/shard_map/ppermute | solution.py:762
  44.8 8.5 %collective-permute-start.13 = (f32[288,128]{1,0:T(8,128)}, f32[288,128]{1,0:T(8,128)S(1)}, u32[]{:S(2)}, u32[]{:S(2)}) collective-permute-start(f32[288,128]{1,0:T(8,128)} %get-tuple-element.44.refs_0_.refs_8_), channel_id=1, source_target_pairs={{0,8},{4,12},{8,0},{12,4},{16,24},{20,28},{24,16},{28,20},{1,9},{5... | collective-permute-start | bytes 442376 | tf_op jit(solution)/shard_map/ppermute | solution.py:762
  45.6 8.2 %collective-permute-start.12 = (f32[288,128]{1,0:T(8,128)}, f32[288,128]{1,0:T(8,128)S(1)}, u32[]{:S(2)}, u32[]{:S(2)}) collective-permute-start(f32[288,128]{1,0:T(8,128)} %get-tuple-element.44.refs_0_.refs_8_), channel_id=1, source_target_pairs={{0,4},{4,0},{8,12},{12,8},{16,20},{20,16},{24,28},{28,24},{1,5},{5... | collective-permute-start | bytes 442376 | tf_op jit(solution)/shard_map/ppermute | solution.py:764
  48.4 6.4 %copy-start = (f32[288,128]{1,0:T(8,128)}, f32[288,128]{1,0:T(8,128)S(1)}, u32[]{:S(2)}) copy-start(f32[288,128]{1,0:T(8,128)S(1)} %collective-permute-done.17.refs_6_) | copy-start | bytes 442372
  48.4 5.3 %collective-permute-start.18 = (f32[288,128]{1,0:T(8,128)S(1)}, f32[288,128]{1,0:T(8,128)S(1)}, u32[]{:S(2)}, u32[]{:S(2)}) collective-permute-start(f32[288,128]{1,0:T(8,128)S(1)} %collective-permute-done.17.refs_6_), channel_id=1, source_target_pairs={{0,4},{4,0},{8,12},{12,8},{16,20},{20,16},{24,28},{28,24},{1,5},{5... | collective-permute-start | bytes 442376 | tf_op jit(solution)/shard_map/ppermute | solution.py:764
  53.2 1.6 %copy-start.2 = (f32[288,128]{1,0:T(8,128)}, f32[288,128]{1,0:T(8,128)S(1)}, u32[]{:S(2)}) copy-start(f32[288,128]{1,0:T(8,128)S(1)} %collective-permute-done.15.refs_4_) | copy-start | bytes 442372
  53.3 1.4 %collective-permute-start.16 = (f32[288,128]{1,0:T(8,128)S(1)}, f32[288,128]{1,0:T(8,128)S(1)}, u32[]{:S(2)}, u32[]{:S(2)}) collective-permute-start(f32[288,128]{1,0:T(8,128)S(1)} %collective-permute-done.15.refs_4_), channel_id=1, source_target_pairs={{0,4},{4,0},{8,12},{12,8},{16,20},{20,16},{24,28},{28,24},{1,5},{5... | collective-permute-start | bytes 442376 | tf_op jit(solution)/shard_map/ppermute | solution.py:764
  53.3 1.6 %copy-start.4 = (f32[288,128]{1,0:T(8,128)}, f32[288,128]{1,0:T(8,128)S(1)}, u32[]{:S(2)}) copy-start(f32[288,128]{1,0:T(8,128)S(1)} %collective-permute-done.13.refs_2_) | copy-start | bytes 442372
  53.3 1.6 %collective-permute-start.14 = (f32[288,128]{1,0:T(8,128)S(1)}, f32[288,128]{1,0:T(8,128)S(1)}, u32[]{:S(2)}, u32[]{:S(2)}) collective-permute-start(f32[288,128]{1,0:T(8,128)S(1)} %collective-permute-done.13.refs_2_), channel_id=1, source_target_pairs={{0,4},{4,0},{8,12},{12,8},{16,20},{20,16},{24,28},{28,24},{1,5},{5... | collective-permute-start | bytes 442376 | tf_op jit(solution)/shard_map/ppermute | solution.py:764
  53.8 1.1 copy-start.6
  53.8 1.1 copy-start.8
  54.6 0.7 copy-start.10
  54.8 0.7 copy-start.12
  63.0 8.8 %collective-permute-start.24 = (f32[288,128]{1,0:T(8,128)}, f32[288,128]{1,0:T(8,128)S(1)}, u32[]{:S(2)}, u32[]{:S(2)}) collective-permute-start(f32[288,128]{1,0:T(8,128)} %get-tuple-element.46.refs_0_.refs_8_), channel_id=1, source_target_pairs={{0,24},{4,28},{8,16},{12,20},{16,8},{20,12},{24,0},{28,4},{1,25},{... | collective-permute-start | bytes 442376 | tf_op jit(solution)/shard_map/ppermute | solution.py:762
  65.5 12.4 %collective-permute-start.22 = (f32[288,128]{1,0:T(8,128)}, f32[288,128]{1,0:T(8,128)S(1)}, u32[]{:S(2)}, u32[]{:S(2)}) collective-permute-start(f32[288,128]{1,0:T(8,128)} %get-tuple-element.46.refs_0_.refs_8_), channel_id=1, source_target_pairs={{0,16},{4,20},{8,24},{12,28},{16,0},{20,4},{24,8},{28,12},{1,17},{... | collective-permute-start | bytes 442376 | tf_op jit(solution)/shard_map/ppermute | solution.py:762
  65.5 12.4 %collective-permute-start.20 = (f32[288,128]{1,0:T(8,128)}, f32[288,128]{1,0:T(8,128)S(1)}, u32[]{:S(2)}, u32[]{:S(2)}) collective-permute-start(f32[288,128]{1,0:T(8,128)} %get-tuple-element.46.refs_0_.refs_8_), channel_id=1, source_target_pairs={{0,8},{4,12},{8,0},{12,4},{16,24},{20,28},{24,16},{28,20},{1,9},{5... | collective-permute-start | bytes 442376 | tf_op jit(solution)/shard_map/ppermute | solution.py:762
  67.4 11.1 %collective-permute-start.19 = (f32[288,128]{1,0:T(8,128)}, f32[288,128]{1,0:T(8,128)S(1)}, u32[]{:S(2)}, u32[]{:S(2)}) collective-permute-start(f32[288,128]{1,0:T(8,128)} %get-tuple-element.46.refs_0_.refs_8_), channel_id=1, source_target_pairs={{0,4},{4,0},{8,12},{12,8},{16,20},{20,16},{24,28},{28,24},{1,5},{5... | collective-permute-start | bytes 442376 | tf_op jit(solution)/shard_map/ppermute | solution.py:764
  71.8 7.7 %copy-start.1 = (f32[288,128]{1,0:T(8,128)}, f32[288,128]{1,0:T(8,128)S(1)}, u32[]{:S(2)}) copy-start(f32[288,128]{1,0:T(8,128)S(1)} %collective-permute-done.24.refs_6_) | copy-start | bytes 442372
  71.8 6.7 %collective-permute-start.25 = (f32[288,128]{1,0:T(8,128)S(1)}, f32[288,128]{1,0:T(8,128)S(1)}, u32[]{:S(2)}, u32[]{:S(2)}) collective-permute-start(f32[288,128]{1,0:T(8,128)S(1)} %collective-permute-done.24.refs_6_), channel_id=1, source_target_pairs={{0,4},{4,0},{8,12},{12,8},{16,20},{20,16},{24,28},{28,24},{1,5},{5... | collective-permute-start | bytes 442376 | tf_op jit(solution)/shard_map/ppermute | solution.py:764
  77.9 1.6 %copy-start.3 = (f32[288,128]{1,0:T(8,128)}, f32[288,128]{1,0:T(8,128)S(1)}, u32[]{:S(2)}) copy-start(f32[288,128]{1,0:T(8,128)S(1)} %collective-permute-done.22.refs_4_) | copy-start | bytes 442372
  77.9 1.4 %collective-permute-start.23 = (f32[288,128]{1,0:T(8,128)S(1)}, f32[288,128]{1,0:T(8,128)S(1)}, u32[]{:S(2)}, u32[]{:S(2)}) collective-permute-start(f32[288,128]{1,0:T(8,128)S(1)} %collective-permute-done.22.refs_4_), channel_id=1, source_target_pairs={{0,4},{4,0},{8,12},{12,8},{16,20},{20,16},{24,28},{28,24},{1,5},{5... | collective-permute-start | bytes 442376 | tf_op jit(solution)/shard_map/ppermute | solution.py:764
  77.9 1.6 %copy-start.5 = (f32[288,128]{1,0:T(8,128)}, f32[288,128]{1,0:T(8,128)S(1)}, u32[]{:S(2)}) copy-start(f32[288,128]{1,0:T(8,128)S(1)} %collective-permute-done.20.refs_2_) | copy-start | bytes 442372
  77.9 1.6 %collective-permute-start.21 = (f32[288,128]{1,0:T(8,128)S(1)}, f32[288,128]{1,0:T(8,128)S(1)}, u32[]{:S(2)}, u32[]{:S(2)}) collective-permute-start(f32[288,128]{1,0:T(8,128)S(1)} %collective-permute-done.20.refs_2_), channel_id=1, source_target_pairs={{0,4},{4,0},{8,12},{12,8},{16,20},{20,16},{24,28},{28,24},{1,5},{5... | collective-permute-start | bytes 442376 | tf_op jit(solution)/shard_map/ppermute | solution.py:764
  78.4 1.1 copy-start.7
  78.4 1.1 copy-start.9
  79.3 0.7 copy-start.11
  79.5 0.7 copy-start.13
  88.2 7.3 %collective-permute-start.31 = (f32[160,128]{1,0:T(8,128)}, f32[160,128]{1,0:T(8,128)S(1)}, u32[]{:S(2)}, u32[]{:S(2)}) collective-permute-start(f32[160,128]{1,0:T(8,128)} %get-tuple-element.50.refs_0_), channel_id=1, source_target_pairs={{0,24},{4,28},{8,16},{12,20},{16,8},{20,12},{24,0},{28,4},{1,25},{... | collective-permute-start | bytes 245768 | tf_op jit(solution)/shard_map/ppermute | solution.py:762
  90.3 8.2 %collective-permute-start.29 = (f32[160,128]{1,0:T(8,128)}, f32[160,128]{1,0:T(8,128)S(1)}, u32[]{:S(2)}, u32[]{:S(2)}) collective-permute-start(f32[160,128]{1,0:T(8,128)} %get-tuple-element.50.refs_0_), channel_id=1, source_target_pairs={{0,16},{4,20},{8,24},{12,28},{16,0},{20,4},{24,8},{28,12},{1,17},{... | collective-permute-start | bytes 245768 | tf_op jit(solution)/shard_map/ppermute | solution.py:762
  90.3 8.2 %collective-permute-start.27 = (f32[160,128]{1,0:T(8,128)}, f32[160,128]{1,0:T(8,128)S(1)}, u32[]{:S(2)}, u32[]{:S(2)}) collective-permute-start(f32[160,128]{1,0:T(8,128)} %get-tuple-element.50.refs_0_), channel_id=1, source_target_pairs={{0,8},{4,12},{8,0},{12,4},{16,24},{20,28},{24,16},{28,20},{1,9},{5... | collective-permute-start | bytes 245768 | tf_op jit(solution)/shard_map/ppermute | solution.py:762
  92.6 6.5 %collective-permute-start.26 = (f32[160,128]{1,0:T(8,128)}, f32[160,128]{1,0:T(8,128)S(1)}, u32[]{:S(2)}, u32[]{:S(2)}) collective-permute-start(f32[160,128]{1,0:T(8,128)} %get-tuple-element.50.refs_0_), channel_id=1, source_target_pairs={{0,4},{4,0},{8,12},{12,8},{16,20},{20,16},{24,28},{28,24},{1,5},{5... | collective-permute-start | bytes 245768 | tf_op jit(solution)/shard_map/ppermute | solution.py:764
  95.5 4.5 %copy-start.26 = (f32[160,128]{1,0:T(8,128)}, f32[160,128]{1,0:T(8,128)S(1)}, u32[]{:S(2)}) copy-start(f32[160,128]{1,0:T(8,128)S(1)} %collective-permute-done.31.refs_6_) | copy-start | bytes 245764
  95.5 3.5 %collective-permute-start.32 = (f32[160,128]{1,0:T(8,128)S(1)}, f32[160,128]{1,0:T(8,128)S(1)}, u32[]{:S(2)}, u32[]{:S(2)}) collective-permute-start(f32[160,128]{1,0:T(8,128)S(1)} %collective-permute-done.31.refs_6_), channel_id=1, source_target_pairs={{0,4},{4,0},{8,12},{12,8},{16,20},{20,16},{24,28},{28,24},{1,5},{5... | collective-permute-start | bytes 245768 | tf_op jit(solution)/shard_map/ppermute | solution.py:764
  98.5 1.4 %copy-start.27 = (f32[160,128]{1,0:T(8,128)}, f32[160,128]{1,0:T(8,128)S(1)}, u32[]{:S(2)}) copy-start(f32[160,128]{1,0:T(8,128)S(1)} %collective-permute-done.29.refs_4_) | copy-start | bytes 245764
  98.6 1.3 %collective-permute-start.30 = (f32[160,128]{1,0:T(8,128)S(1)}, f32[160,128]{1,0:T(8,128)S(1)}, u32[]{:S(2)}, u32[]{:S(2)}) collective-permute-start(f32[160,128]{1,0:T(8,128)S(1)} %collective-permute-done.29.refs_4_), channel_id=1, source_target_pairs={{0,4},{4,0},{8,12},{12,8},{16,20},{20,16},{24,28},{28,24},{1,5},{5... | collective-permute-start | bytes 245768 | tf_op jit(solution)/shard_map/ppermute | solution.py:764
  98.6 1.4 %copy-start.28 = (f32[160,128]{1,0:T(8,128)}, f32[160,128]{1,0:T(8,128)S(1)}, u32[]{:S(2)}) copy-start(f32[160,128]{1,0:T(8,128)S(1)} %collective-permute-done.27.refs_2_) | copy-start | bytes 245764
  98.6 1.4 %collective-permute-start.28 = (f32[160,128]{1,0:T(8,128)S(1)}, f32[160,128]{1,0:T(8,128)S(1)}, u32[]{:S(2)}, u32[]{:S(2)}) collective-permute-start(f32[160,128]{1,0:T(8,128)S(1)} %collective-permute-done.27.refs_2_), channel_id=1, source_target_pairs={{0,4},{4,0},{8,12},{12,8},{16,20},{20,16},{24,28},{28,24},{1,5},{5... | collective-permute-start | bytes 245768 | tf_op jit(solution)/shard_map/ppermute | solution.py:764
  99.1 0.9 copy-start.29
  99.1 0.9 copy-start.30
  (2 other events, 1.3 us)

commit v3 on v2

--- a/solution.py
+++ b/solution.py
@@ -21,7 +21,7 @@
 SPREAD = 9.0
 TWICE = 2.0 / SPREAD
 SUM_ROWS = 16
-VMEM_LIMIT = 56 * 1024 * 1024
+VMEM_LIMIT = 32 * 1024 * 1024
 F32 = jnp.float32
 BF16 = jnp.bfloat16
 
@@ -728,18 +728,22 @@
             out_ref[comp] = flat[comp * modes : (comp + 1) * modes, :]
 
 
-def call(kernel, name, out_shapes, args, scratch, scalars=0):
+def call(kernel, name, out_shapes, args, scratch, scalars=0, keep=True):
     smem = pl.BlockSpec(memory_space=pltpu.SMEM)
     vmem = pl.BlockSpec(memory_space=pltpu.VMEM)
     return pl.pallas_call(
         kernel,
         name=name,
-        out_shape=[jax.ShapeDtypeStruct(shape, F32) for shape in out_shapes],
+        out_shape=[pltpu.VMEM(shape, F32) if keep else jax.ShapeDtypeStruct(shape, F32) for shape in out_shapes],
         in_specs=[smem] * scalars + [vmem] * (len(args) - scalars),
         out_specs=[vmem] * len(out_shapes),
         scratch_shapes=[pltpu.VMEM(shape, F32) for shape in scratch],
         compiler_params=pltpu.CompilerParams(vmem_limit_bytes=VMEM_LIMIT),
-    )(*args)
+    )(*args[:scalars], *[held(arg) for arg in args[scalars:]])
+
+
+def held(arg):
+    return arg if isinstance(arg, np.ndarray) else pltpu.with_memory_space_constraint(arg, pltpu.VMEM)
 
 
 def swap_blocks(blocks, dynamic):
@@ -847,6 +851,7 @@
         (*tables, *gathered, k0, k1, k2, k3, a3, order),
         [field, (units, rows, LANES), (units, rows, LANES), (LANES, NODES), (4, SIDE, LANES)],
         scalars=4,
+        keep=False,
     )
     return tuple(outs)
 

time: 108 us -> 92.1 us (0.85)
  Pallas kernels: 40.1 us -> 23.5 us
    pallas_call x8, Pallas kernels: 40.1 us -> 23.5 us  [call(): pl.pallas_call(kernel, name=name, out_shape=[pltpu.VMEM(shape, F32) if ke...]
    unnamed x66 -> x30, local copies, waits for them, and re-layouts: 3.87 us -> 4.55 us
  transfers between devices with their start and end apart: 33 -> 33, of which waited for: 15 -> 16; matrix products, arithmetic and copies ran while one was open for 0% -> 0% of each run, Pallas kernels for 10% -> 7%
where the time goes in v3:
time: 92.1 us; the launch traced here: 91.8 us
  waiting for transfers between devices  32.7 us (36%)
  starting transfers between devices  30.1 us (33%)
  Pallas kernels  23.5 us (26%)
  local copies, waits for them, and re-layouts  4.55 us (5%)
    ppermute x9, waiting for transfers between devices, share_lines(): lax.ppermute(lines, 'dom', [(i, i ^ slot) for i in range(parts)])  24 us
    pallas_call x8, Pallas kernels, call(): pl.pallas_call(kernel, name=name, out_shape=[pltpu.VMEM(shape, F32) if ke...  23.5 us
    ppermute x12, starting transfers between devices, swap_blocks(): lax.ppermute(blocks[place], 'four', [(i, i ^ place) for i in range(size)])  15.2 us
    ppermute x9, starting transfers between devices, share_lines(): lax.ppermute(lines, 'dom', [(i, i ^ slot) for i in range(parts)])  13.4 us
    ppermute x12, waiting for transfers between devices, swap_blocks(): lax.ppermute(blocks[place], 'four', [(i, i ^ place) for i in range(size)])  5.66 us
    unnamed x30, local copies, waits for them, and re-layouts  4.55 us
    ppermute x12, waiting for transfers between devices, share_lines(): lax.ppermute(slots[slot], 'dom', [(i, i ^ 1) for i in range(parts)])  3.05 us
  transfers between devices with their start and end apart: 33, of which 16 were waited for; matrix products, arithmetic and copies ran while one was open for 0% of the time, Pallas kernels for 7%

profile of v3, /device:TPU:0, one launch (start us, length us, event | category | flops | bytes accessed | tf_op | source)
XLA Modules:
  0.0 91.8 jit_solution(9315064546861643327)
XLA Ops:
  0.6 0.0 copy-start.13
  0.6 0.1 pad_add_fusion.ids_ref
  0.7 1.2 %copy-done = f32[3,32,2304]{2,1,0:T(8,128)S(1)} copy-done((f32[3,32,2304]{2,1,0:T(8,128)S(1)}, f32[3,32,2304]{2,1,0:T(8,128)}, u32[]{:S(2)}) %copy-start) | copy-done | bytes 884760
  1.9 1.0 %copy-done.6 = bf16[2,288,384]{2,1,0:T(8,128)(2,1)S(1)} copy-done((bf16[2,288,384]{2,1,0:T(8,128)(2,1)S(1)}, bf16[2,288,384]{2,1,0:T(8,128)(2,1)}, u32[]{:S(2)}) %copy-start.6) | copy-done | bytes 442392
  2.9 0.7 copy-done.12
  3.6 0.7 copy-done.14
  4.2 1.2 %pack.2 = (f32[216,128]{1,0:T(8,128)S(1)}, f32[216,128]{1,0:T(8,128)S(1)}, f32[216,128]{1,0:T(8,128)S(1)}, f32[216,128]{1,0:T(8,128)S(1)}) custom-call(s32[2]{0:T(128)S(1)} %pad_add_fusion.ids_ref, s32[4]{0:T(128)S(1)} %copy-done.12, s32[4]{0:T(128)S(1)} %copy-done.14, f32[3,32,2304]{2,1,0:T(8,128)S(1)} %copy-done, bf16[2,288,384]{2,1,0:T(8,128)(2,1)S(1)} %copy-done.6), custom_call_target="tpu_custom_call" | custom-call | tf_op jit(solution)/shard_map/pack/pallas_call | solution.py:734
  5.4 3.0 %collective-permute-start = (f32[216,128]{1,0:T(8,128)S(1)}, f32[216,128]{1,0:T(8,128)S(1)}, u32[]{:S(2)}, u32[]{:S(2)}) collective-permute-start(f32[216,128]{1,0:T(8,128)S(1)} %get-tuple-element.29), channel_id=1, source_target_pairs={{0,1},{1,0},{2,3},{3,2},{4,5},{5,4},{6,7},{7,6},{8,9},{9,8},{10,11... | collective-permute-start | bytes 331784 | tf_op jit(solution)/shard_map/ppermute | solution.py:755
  8.4 1.5 %collective-permute-start.1 = (f32[216,128]{1,0:T(8,128)S(1)}, f32[216,128]{1,0:T(8,128)S(1)}, u32[]{:S(2)}, u32[]{:S(2)}) collective-permute-start(f32[216,128]{1,0:T(8,128)S(1)} %get-tuple-element.30), channel_id=1, source_target_pairs={{0,2},{1,3},{2,0},{3,1},{4,6},{5,7},{6,4},{7,5},{8,10},{9,11},{10,... | collective-permute-start | bytes 331784 | tf_op jit(solution)/shard_map/ppermute | solution.py:755
  9.9 0.0 collective-permute-start.2
  9.9 1.0 %copy-done.5 = bf16[2,288,384]{2,1,0:T(8,128)(2,1)S(1)} copy-done((bf16[2,288,384]{2,1,0:T(8,128)(2,1)S(1)}, bf16[2,288,384]{2,1,0:T(8,128)(2,1)}, u32[]{:S(2)}) %copy-start.5) | copy-done | bytes 442392
  11.0 1.2 %pack.3 = (f32[216,128]{1,0:T(8,128)S(1)}, f32[216,128]{1,0:T(8,128)S(1)}, f32[216,128]{1,0:T(8,128)S(1)}, f32[216,128]{1,0:T(8,128)S(1)}) custom-call(s32[2]{0:T(128)S(1)} %pad_add_fusion.ids_ref, s32[4]{0:T(128)S(1)} %copy-done.12, s32[4]{0:T(128)S(1)} %copy-done.13, f32[3,32,2304]{2,1,0:T(8,128)S(1)} %copy-done.1, bf16[2,288,384]{2,1,0:T(8,128)(2,1)S(1)} %copy-done.5), custom_call_target="tpu_custom_call" | custom-call | tf_op jit(solution)/shard_map/pack/pallas_call | solution.py:734
  12.1 2.0 %collective-permute-start.6 = (f32[216,128]{1,0:T(8,128)S(1)}, f32[216,128]{1,0:T(8,128)S(1)}, u32[]{:S(2)}, u32[]{:S(2)}) collective-permute-start(f32[216,128]{1,0:T(8,128)S(1)} %get-tuple-element.37), channel_id=1, source_target_pairs={{0,1},{1,0},{2,3},{3,2},{4,5},{5,4},{6,7},{7,6},{8,9},{9,8},{10,11... | collective-permute-start | bytes 331784 | tf_op jit(solution)/shard_map/ppermute | solution.py:755
  14.2 1.5 %collective-permute-start.7 = (f32[216,128]{1,0:T(8,128)S(1)}, f32[216,128]{1,0:T(8,128)S(1)}, u32[]{:S(2)}, u32[]{:S(2)}) collective-permute-start(f32[216,128]{1,0:T(8,128)S(1)} %get-tuple-element.38), channel_id=1, source_target_pairs={{0,2},{1,3},{2,0},{3,1},{4,6},{5,7},{6,4},{7,5},{8,10},{9,11},{10,... | collective-permute-start | bytes 331784 | tf_op jit(solution)/shard_map/ppermute | solution.py:755
  15.7 0.0 collective-permute-start.8
  15.7 0.2 collective-permute-done.2.refs_3_
  16.0 0.0 copy-start.9
  16.0 2.6 %products.2 = (f32[216,128]{1,0:T(8,128)S(1)}, f32[216,128]{1,0:T(8,128)S(1)}, f32[216,128]{1,0:T(8,128)S(1)}, f32[216,128]{1,0:T(8,128)S(1)}) custom-call(s32[2]{0:T(128)S(1)} %pad_add_fusion.ids_ref, f32[216,128]{1,0:T(8,128)S(1)} %get-tuple-element.28.refs_0_, f32[216,128]{1,0:T(8,128)S(1)} %collective-permute-done.refs_1_, ...), custom_call_target="tpu_custom_call" | custom-call | tf_op jit(solution)/shard_map/products/pallas_call | solution.py:734
  18.6 0.0 copy-start.10
  18.6 0.0 copy-start.11
  18.6 1.8 %collective-permute-start.3 = (f32[216,128]{1,0:T(8,128)S(1)}, f32[216,128]{1,0:T(8,128)S(1)}, u32[]{:S(2)}, u32[]{:S(2)}) collective-permute-start(f32[216,128]{1,0:T(8,128)S(1)} %get-tuple-element.33), channel_id=1, source_target_pairs={{0,1},{1,0},{2,3},{3,2},{4,5},{5,4},{6,7},{7,6},{8,9},{9,8},{10,11... | collective-permute-start | bytes 331784 | tf_op jit(solution)/shard_map/ppermute | solution.py:755
  20.4 1.5 %collective-permute-start.4 = (f32[216,128]{1,0:T(8,128)S(1)}, f32[216,128]{1,0:T(8,128)S(1)}, u32[]{:S(2)}, u32[]{:S(2)}) collective-permute-start(f32[216,128]{1,0:T(8,128)S(1)} %get-tuple-element.34), channel_id=1, source_target_pairs={{0,2},{1,3},{2,0},{3,1},{4,6},{5,7},{6,4},{7,5},{8,10},{9,11},{10,... | collective-permute-start | bytes 331784 | tf_op jit(solution)/shard_map/ppermute | solution.py:755
  21.9 0.0 collective-permute-done.6.refs_1_
  21.9 0.2 collective-permute-start.5
  22.2 0.0 collective-permute-done.8.refs_3_
  22.2 2.6 %products.3 = (f32[216,128]{1,0:T(8,128)S(1)}, f32[216,128]{1,0:T(8,128)S(1)}, f32[216,128]{1,0:T(8,128)S(1)}, f32[216,128]{1,0:T(8,128)S(1)}) custom-call(s32[2]{0:T(128)S(1)} %pad_add_fusion.ids_ref, f32[216,128]{1,0:T(8,128)S(1)} %get-tuple-element.36.refs_0_, f32[216,128]{1,0:T(8,128)S(1)} %collective-permute-done.6.refs_1_, ...), custom_call_target="tpu_custom_call" | custom-call | tf_op jit(solution)/shard_map/products/pallas_call | solution.py:734
  24.7 1.8 %collective-permute-start.9 = (f32[216,128]{1,0:T(8,128)S(1)}, f32[216,128]{1,0:T(8,128)S(1)}, u32[]{:S(2)}, u32[]{:S(2)}) collective-permute-start(f32[216,128]{1,0:T(8,128)S(1)} %get-tuple-element.41), channel_id=1, source_target_pairs={{0,1},{1,0},{2,3},{3,2},{4,5},{5,4},{6,7},{7,6},{8,9},{9,8},{10,11... | collective-permute-start | bytes 331784 | tf_op jit(solution)/shard_map/ppermute | solution.py:755
  26.5 1.5 %collective-permute-start.10 = (f32[216,128]{1,0:T(8,128)S(1)}, f32[216,128]{1,0:T(8,128)S(1)}, u32[]{:S(2)}, u32[]{:S(2)}) collective-permute-start(f32[216,128]{1,0:T(8,128)S(1)} %get-tuple-element.42), channel_id=1, source_target_pairs={{0,2},{1,3},{2,0},{3,1},{4,6},{5,7},{6,4},{7,5},{8,10},{9,11},{10,... | collective-permute-start | bytes 331784 | tf_op jit(solution)/shard_map/ppermute | solution.py:755
  28.0 0.0 collective-permute-done.3.refs_1_
  28.0 0.2 collective-permute-start.11
  28.3 0.0 collective-permute-done.4.refs_2_
  28.3 0.0 collective-permute-done.5.refs_3_
  28.3 1.4 %collective-permute-done.9.refs_5_ = f32[216,128]{1,0:T(8,128)S(1)} collective-permute-done((f32[216,128]{1,0:T(8,128)S(1)}, f32[216,128]{1,0:T(8,128)S(1)}, u32[]{:S(2)}, u32[]{:S(2)}) %collective-permute-start.9) | collective-permute-done | bytes 110624 | tf_op jit(solution)/shard_map/ppermute | solution.py:755
  29.7 1.6 %collective-permute-done.10.refs_6_ = f32[216,128]{1,0:T(8,128)S(1)} collective-permute-done((f32[216,128]{1,0:T(8,128)S(1)}, f32[216,128]{1,0:T(8,128)S(1)}, u32[]{:S(2)}, u32[]{:S(2)}) %collective-permute-start.10) | collective-permute-done | bytes 110624 | tf_op jit(solution)/shard_map/ppermute | solution.py:755
  31.3 2.4 %collective-permute-done.11.refs_7_ = f32[216,128]{1,0:T(8,128)S(1)} collective-permute-done((f32[216,128]{1,0:T(8,128)S(1)}, f32[216,128]{1,0:T(8,128)S(1)}, u32[]{:S(2)}, u32[]{:S(2)}) %collective-permute-start.11) | collective-permute-done | bytes 110624 | tf_op jit(solution)/shard_map/ppermute | solution.py:755
  33.7 2.1 %first.1 = (f32[2304,128]{1,0:T(8,128)S(1)}, f32[288,128]{1,0:T(8,128)S(1)}) custom-call(s32[2]{0:T(128)S(1)} %pad_add_fusion.ids_ref, s32[1,4]{1,0:T(1,128)S(1)} %copy-done.9, f32[216,128]{1,0:T(8,128)S(1)} %get-tuple-element.32.refs_0_, f32[216,128]{1,0:T(8,128)S(1)} %collective-permute-done.3.refs_1_, f32[216,128]{1,0:T(8,128)S(1)} %collective-permute-done.4.refs_2_, ...), custom_call_target="tpu_custom_call" | custom-call | tf_op jit(solution)/shard_map/first/pallas_call | solution.py:734
  35.8 3.7 %collective-permute-start.17 = (f32[288,128]{1,0:T(8,128)S(1)}, f32[288,128]{1,0:T(8,128)S(1)}, u32[]{:S(2)}, u32[]{:S(2)}) collective-permute-start(f32[288,128]{1,0:T(8,128)S(1)} %get-tuple-element.44.refs_0_.refs_8_), channel_id=1, source_target_pairs={{0,24},{4,28},{8,16},{12,20},{16,8},{20,12},{24,0},{28,4},{1,25},{... | collective-permute-start | bytes 442376 | tf_op jit(solution)/shard_map/ppermute | solution.py:766
  39.5 0.8 collective-permute-start.13
  40.3 0.0 collective-permute-start.12
  40.3 3.0 %collective-permute-done.17.refs_6_ = f32[288,128]{1,0:T(8,128)S(1)} collective-permute-done((f32[288,128]{1,0:T(8,128)S(1)}, f32[288,128]{1,0:T(8,128)S(1)}, u32[]{:S(2)}, u32[]{:S(2)}) %collective-permute-start.17) | collective-permute-done | bytes 147488 | tf_op jit(solution)/shard_map/ppermute | solution.py:766
  43.3 5.0 %collective-permute-done.15.refs_4_ = f32[288,128]{1,0:T(8,128)S(1)} collective-permute-done((f32[288,128]{1,0:T(8,128)S(1)}, f32[288,128]{1,0:T(8,128)S(1)}, u32[]{:S(2)}, u32[]{:S(2)}) %collective-permute-start.15) | collective-permute-done | bytes 147488 | tf_op jit(solution)/shard_map/ppermute | solution.py:766
  48.2 0.0 collective-permute-start.16
  48.2 0.0 collective-permute-done.13.refs_2_
  48.2 0.5 collective-permute-start.14
  48.8 0.9 collective-permute-done.16.refs_5_
  49.6 0.2 collective-permute-done.14.refs_3_
  49.8 4.7 %second.1 = (f32[2304,128]{1,0:T(8,128)S(1)}, f32[2304,128]{1,0:T(8,128)S(1)}, f32[2304,128]{1,0:T(8,128)S(1)}, f32[288,128]{1,0:T(8,128)S(1)}) custom-call(s32[2]{0:T(128)S(1)} %pad_add_fusion.ids_ref, s32[1,4]{1,0:T(1,128)S(1)} %copy-done.9, s32[1,4]{1,0:T(1,128)S(1)} %copy-done.10, s32[1,4]{1,0:T(1,128)S(1)} %copy-done.11, ...), custom_call_target="tpu_custom_call" | custom-call | tf_op jit(solution)/shard_map/second/pallas_call | solution.py:734
  54.6 2.6 %collective-permute-start.24 = (f32[288,128]{1,0:T(8,128)S(1)}, f32[288,128]{1,0:T(8,128)S(1)}, u32[]{:S(2)}, u32[]{:S(2)}) collective-permute-start(f32[288,128]{1,0:T(8,128)S(1)} %get-tuple-element.46.refs_0_.refs_8_), channel_id=1, source_target_pairs={{0,24},{4,28},{8,16},{12,20},{16,8},{20,12},{24,0},{28,4},{1,25},{... | collective-permute-start | bytes 442376 | tf_op jit(solution)/shard_map/ppermute | solution.py:766
  57.1 1.9 %collective-permute-start.20 = (f32[288,128]{1,0:T(8,128)S(1)}, f32[288,128]{1,0:T(8,128)S(1)}, u32[]{:S(2)}, u32[]{:S(2)}) collective-permute-start(f32[288,128]{1,0:T(8,128)S(1)} %get-tuple-element.46.refs_0_.refs_8_), channel_id=1, source_target_pairs={{0,8},{4,12},{8,0},{12,4},{16,24},{20,28},{24,16},{28,20},{1,9},{5... | collective-permute-start | bytes 442376 | tf_op jit(solution)/shard_map/ppermute | solution.py:766
  59.0 4.2 %collective-permute-done.24.refs_6_ = f32[288,128]{1,0:T(8,128)S(1)} collective-permute-done((f32[288,128]{1,0:T(8,128)S(1)}, f32[288,128]{1,0:T(8,128)S(1)}, u32[]{:S(2)}, u32[]{:S(2)}) %collective-permute-start.24) | collective-permute-done | bytes 147488 | tf_op jit(solution)/shard_map/ppermute | solution.py:766
  63.2 6.2 %collective-permute-done.22.refs_4_ = f32[288,128]{1,0:T(8,128)S(1)} collective-permute-done((f32[288,128]{1,0:T(8,128)S(1)}, f32[288,128]{1,0:T(8,128)S(1)}, u32[]{:S(2)}, u32[]{:S(2)}) %collective-permute-start.22) | collective-permute-done | bytes 147488 | tf_op jit(solution)/shard_map/ppermute | solution.py:766
  69.4 0.5 collective-permute-start.21
  69.9 0.9 collective-permute-done.23.refs_5_
  70.7 0.2 collective-permute-done.21.refs_3_
  71.0 4.3 %third.1 = (f32[2304,128]{1,0:T(8,128)S(1)}, f32[2304,128]{1,0:T(8,128)S(1)}, f32[2304,128]{1,0:T(8,128)S(1)}, f32[160,128]{1,0:T(8,128)S(1)}) custom-call(s32[2]{0:T(128)S(1)} %pad_add_fusion.ids_ref, s32[1,4]{1,0:T(1,128)S(1)} %copy-done.9, s32[1,4]{1,0:T(1,128)S(1)} %copy-done.10, s32[1,4]{1,0:T(1,128)S(1)} %copy-done.11, ...), custom_call_target="tpu_custom_call" | custom-call | tf_op jit(solution)/shard_map/third/pallas_call | solution.py:734
  75.3 2.2 %collective-permute-start.31 = (f32[160,128]{1,0:T(8,128)S(1)}, f32[160,128]{1,0:T(8,128)S(1)}, u32[]{:S(2)}, u32[]{:S(2)}) collective-permute-start(f32[160,128]{1,0:T(8,128)S(1)} %get-tuple-element.50.refs_0_), channel_id=1, source_target_pairs={{0,24},{4,28},{8,16},{12,20},{16,8},{20,12},{24,0},{28,4},{1,25},{... | collective-permute-start | bytes 245768 | tf_op jit(solution)/shard_map/ppermute | solution.py:766
  77.5 2.2 %collective-permute-start.27 = (f32[160,128]{1,0:T(8,128)S(1)}, f32[160,128]{1,0:T(8,128)S(1)}, u32[]{:S(2)}, u32[]{:S(2)}) collective-permute-start(f32[160,128]{1,0:T(8,128)S(1)} %get-tuple-element.50.refs_0_), channel_id=1, source_target_pairs={{0,8},{4,12},{8,0},{12,4},{16,24},{20,28},{24,16},{28,20},{1,9},{5... | collective-permute-start | bytes 245768 | tf_op jit(solution)/shard_map/ppermute | solution.py:766
  79.8 2.8 %collective-permute-done.31.refs_6_ = f32[160,128]{1,0:T(8,128)S(1)} collective-permute-done((f32[160,128]{1,0:T(8,128)S(1)}, f32[160,128]{1,0:T(8,128)S(1)}, u32[]{:S(2)}, u32[]{:S(2)}) %collective-permute-start.31) | collective-permute-done | bytes 81952 | tf_op jit(solution)/shard_map/ppermute | solution.py:766
  82.5 2.9 %collective-permute-done.29.refs_4_ = f32[160,128]{1,0:T(8,128)S(1)} collective-permute-done((f32[160,128]{1,0:T(8,128)S(1)}, f32[160,128]{1,0:T(8,128)S(1)}, u32[]{:S(2)}, u32[]{:S(2)}) %collective-permute-start.29) | collective-permute-done | bytes 81952 | tf_op jit(solution)/shard_map/ppermute | solution.py:766
  85.5 0.0 collective-permute-start.30
  85.5 0.5 collective-permute-start.28
  86.0 0.8 collective-permute-done.30.refs_5_
  86.7 0.2 collective-permute-done.28.refs_3_
  86.9 4.9 %last.1 = (f32[3,32,2304]{2,1,0:T(8,128)}, f32[3,32,2304]{2,1,0:T(8,128)}) custom-call(s32[2]{0:T(128)S(1)} %pad_add_fusion.ids_ref, s32[1,4]{1,0:T(1,128)S(1)} %copy-done.9, s32[1,4]{1,0:T(1,128)S(1)} %copy-done.10, s32[1,4]{1,0:T(1,128)S(1)} %copy-done.11, f32[160,128]{1,0:T(8,128)S(1)} %get-tuple-element.50.refs_0_, ...), custom_call_target="tpu_custom_call" | custom-call | tf_op jit(solution)/shard_map/last/pallas_call | solution.py:734
  (41 shorter events, 0.1 us)
Async XLA Ops:
  0.6 9.3 %copy-start.13 = (s32[4]{0:T(128)S(1)}, s32[4]{0:T(128)}, u32[]{:S(2)}) copy-start(s32[4]{0:T(128)} %constant.32.clone.starts_ref) | copy-start | bytes 52
  0.7 1.2 %copy-start = (f32[3,32,2304]{2,1,0:T(8,128)S(1)}, f32[3,32,2304]{2,1,0:T(8,128)}, u32[]{:S(2)}) copy-start(f32[3,32,2304]{2,1,0:T(8,128)} %velocity_ref.3) | copy-start | bytes 2654212
  1.9 1.0 %copy-start.6 = (bf16[2,288,384]{2,1,0:T(8,128)(2,1)S(1)}, bf16[2,288,384]{2,1,0:T(8,128)(2,1)}, u32[]{:S(2)}) copy-start(bf16[2,288,384]{2,1,0:T(8,128)(2,1)} %constant.31.clone.order_ref) | copy-start | bytes 1327108
  2.9 0.7 copy-start.12
  3.6 0.7 copy-start.14
  4.2 5.7 %copy-start.1 = (f32[3,32,2304]{2,1,0:T(8,128)S(1)}, f32[3,32,2304]{2,1,0:T(8,128)}, u32[]{:S(2)}) copy-start(f32[3,32,2304]{2,1,0:T(8,128)} %velocity_ref.3) | copy-start | bytes 2654212
  4.2 11.7 %copy-start.2 = (bf16[4,128,384]{2,1,0:T(8,128)(2,1)S(1)}, bf16[4,128,384]{2,1,0:T(8,128)(2,1)}, u32[]{:S(2)}) copy-start(bf16[4,128,384]{2,1,0:T(8,128)(2,1)} %constant.35.clone.refs_5_) | copy-start | bytes 1179652
  4.2 11.7 %copy-start.3 = (bf16[4,128,384]{2,1,0:T(8,128)(2,1)S(1)}, bf16[4,128,384]{2,1,0:T(8,128)(2,1)}, u32[]{:S(2)}) copy-start(bf16[4,128,384]{2,1,0:T(8,128)(2,1)} %constant.34.clone.refs_4_) | copy-start | bytes 1179652
  5.4 10.3 %collective-permute-start = (f32[216,128]{1,0:T(8,128)S(1)}, f32[216,128]{1,0:T(8,128)S(1)}, u32[]{:S(2)}, u32[]{:S(2)}) collective-permute-start(f32[216,128]{1,0:T(8,128)S(1)} %get-tuple-element.29), channel_id=1, source_target_pairs={{0,1},{1,0},{2,3},{3,2},{4,5},{5,4},{6,7},{7,6},{8,9},{9,8},{10,11... | collective-permute-start | bytes 331784 | tf_op jit(solution)/shard_map/ppermute | solution.py:755
  8.4 7.3 %collective-permute-start.1 = (f32[216,128]{1,0:T(8,128)S(1)}, f32[216,128]{1,0:T(8,128)S(1)}, u32[]{:S(2)}, u32[]{:S(2)}) collective-permute-start(f32[216,128]{1,0:T(8,128)S(1)} %get-tuple-element.30), channel_id=1, source_target_pairs={{0,2},{1,3},{2,0},{3,1},{4,6},{5,7},{6,4},{7,5},{8,10},{9,11},{10,... | collective-permute-start | bytes 331784 | tf_op jit(solution)/shard_map/ppermute | solution.py:755
  9.9 6.0 %collective-permute-start.2 = (f32[216,128]{1,0:T(8,128)S(1)}, f32[216,128]{1,0:T(8,128)S(1)}, u32[]{:S(2)}, u32[]{:S(2)}) collective-permute-start(f32[216,128]{1,0:T(8,128)S(1)} %get-tuple-element.31), channel_id=1, source_target_pairs={{0,3},{1,2},{2,1},{3,0},{4,7},{5,6},{6,5},{7,4},{8,11},{9,10},{10,... | collective-permute-start | bytes 331784 | tf_op jit(solution)/shard_map/ppermute | solution.py:755
  9.9 1.0 %copy-start.5 = (bf16[2,288,384]{2,1,0:T(8,128)(2,1)S(1)}, bf16[2,288,384]{2,1,0:T(8,128)(2,1)}, u32[]{:S(2)}) copy-start(bf16[2,288,384]{2,1,0:T(8,128)(2,1)} %constant.33.clone.order_ref) | copy-start | bytes 1327108
  11.0 5.0 %copy-start.7 = (bf16[256,128]{1,0:T(8,128)(2,1)S(1)}, bf16[256,128]{1,0:T(8,128)(2,1)}, u32[]{:S(2)}) copy-start(bf16[256,128]{1,0:T(8,128)(2,1)} %constant.37.clone.refs_7_) | copy-start | bytes 196612
  11.0 5.0 %copy-start.8 = (bf16[256,128]{1,0:T(8,128)(2,1)S(1)}, bf16[256,128]{1,0:T(8,128)(2,1)}, u32[]{:S(2)}) copy-start(bf16[256,128]{1,0:T(8,128)(2,1)} %constant.36.clone.refs_6_) | copy-start | bytes 196612
  12.1 9.8 %collective-permute-start.6 = (f32[216,128]{1,0:T(8,128)S(1)}, f32[216,128]{1,0:T(8,128)S(1)}, u32[]{:S(2)}, u32[]{:S(2)}) collective-permute-start(f32[216,128]{1,0:T(8,128)S(1)} %get-tuple-element.37), channel_id=1, source_target_pairs={{0,1},{1,0},{2,3},{3,2},{4,5},{5,4},{6,7},{7,6},{8,9},{9,8},{10,11... | collective-permute-start | bytes 331784 | tf_op jit(solution)/shard_map/ppermute | solution.py:755
  14.2 8.0 %collective-permute-start.7 = (f32[216,128]{1,0:T(8,128)S(1)}, f32[216,128]{1,0:T(8,128)S(1)}, u32[]{:S(2)}, u32[]{:S(2)}) collective-permute-start(f32[216,128]{1,0:T(8,128)S(1)} %get-tuple-element.38), channel_id=1, source_target_pairs={{0,2},{1,3},{2,0},{3,1},{4,6},{5,7},{6,4},{7,5},{8,10},{9,11},{10,... | collective-permute-start | bytes 331784 | tf_op jit(solution)/shard_map/ppermute | solution.py:755
  15.7 6.5 %collective-permute-start.8 = (f32[216,128]{1,0:T(8,128)S(1)}, f32[216,128]{1,0:T(8,128)S(1)}, u32[]{:S(2)}, u32[]{:S(2)}) collective-permute-start(f32[216,128]{1,0:T(8,128)S(1)} %get-tuple-element.39), channel_id=1, source_target_pairs={{0,3},{1,2},{2,1},{3,0},{4,7},{5,6},{6,5},{7,4},{8,11},{9,10},{10,... | collective-permute-start | bytes 331784 | tf_op jit(solution)/shard_map/ppermute | solution.py:755
  16.0 17.7 %copy-start.9 = (s32[1,4]{1,0:T(1,128)S(1)}, s32[1,4]{1,0:T(1,128)}, u32[]{:S(2)}) copy-start(s32[1,4]{1,0:T(1,128)} %partner_ref.7) | copy-start | bytes 52
  18.6 31.3 %copy-start.10 = (s32[1,4]{1,0:T(1,128)S(1)}, s32[1,4]{1,0:T(1,128)}, u32[]{:S(2)}) copy-start(s32[1,4]{1,0:T(1,128)} %side_ref.5) | copy-start | bytes 52
  18.6 31.3 %copy-start.11 = (s32[1,4]{1,0:T(1,128)S(1)}, s32[1,4]{1,0:T(1,128)}, u32[]{:S(2)}) copy-start(s32[1,4]{1,0:T(1,128)} %flip_ref.5) | copy-start | bytes 52
  18.6 9.5 %collective-permute-start.3 = (f32[216,128]{1,0:T(8,128)S(1)}, f32[216,128]{1,0:T(8,128)S(1)}, u32[]{:S(2)}, u32[]{:S(2)}) collective-permute-start(f32[216,128]{1,0:T(8,128)S(1)} %get-tuple-element.33), channel_id=1, source_target_pairs={{0,1},{1,0},{2,3},{3,2},{4,5},{5,4},{6,7},{7,6},{8,9},{9,8},{10,11... | collective-permute-start | bytes 331784 | tf_op jit(solution)/shard_map/ppermute | solution.py:755
  20.4 7.9 %collective-permute-start.4 = (f32[216,128]{1,0:T(8,128)S(1)}, f32[216,128]{1,0:T(8,128)S(1)}, u32[]{:S(2)}, u32[]{:S(2)}) collective-permute-start(f32[216,128]{1,0:T(8,128)S(1)} %get-tuple-element.34), channel_id=1, source_target_pairs={{0,2},{1,3},{2,0},{3,1},{4,6},{5,7},{6,4},{7,5},{8,10},{9,11},{10,... | collective-permute-start | bytes 331784 | tf_op jit(solution)/shard_map/ppermute | solution.py:755
  21.9 6.4 %collective-permute-start.5 = (f32[216,128]{1,0:T(8,128)S(1)}, f32[216,128]{1,0:T(8,128)S(1)}, u32[]{:S(2)}, u32[]{:S(2)}) collective-permute-start(f32[216,128]{1,0:T(8,128)S(1)} %get-tuple-element.35), channel_id=1, source_target_pairs={{0,3},{1,2},{2,1},{3,0},{4,7},{5,6},{6,5},{7,4},{8,11},{9,10},{10,... | collective-permute-start | bytes 331784 | tf_op jit(solution)/shard_map/ppermute | solution.py:755
  24.7 5.0 %collective-permute-start.9 = (f32[216,128]{1,0:T(8,128)S(1)}, f32[216,128]{1,0:T(8,128)S(1)}, u32[]{:S(2)}, u32[]{:S(2)}) collective-permute-start(f32[216,128]{1,0:T(8,128)S(1)} %get-tuple-element.41), channel_id=1, source_target_pairs={{0,1},{1,0},{2,3},{3,2},{4,5},{5,4},{6,7},{7,6},{8,9},{9,8},{10,11... | collective-permute-start | bytes 331784 | tf_op jit(solution)/shard_map/ppermute | solution.py:755
  26.5 4.7 %collective-permute-start.10 = (f32[216,128]{1,0:T(8,128)S(1)}, f32[216,128]{1,0:T(8,128)S(1)}, u32[]{:S(2)}, u32[]{:S(2)}) collective-permute-start(f32[216,128]{1,0:T(8,128)S(1)} %get-tuple-element.42), channel_id=1, source_target_pairs={{0,2},{1,3},{2,0},{3,1},{4,6},{5,7},{6,4},{7,5},{8,10},{9,11},{10,... | collective-permute-start | bytes 331784 | tf_op jit(solution)/shard_map/ppermute | solution.py:755
  28.0 5.6 %collective-permute-start.11 = (f32[216,128]{1,0:T(8,128)S(1)}, f32[216,128]{1,0:T(8,128)S(1)}, u32[]{:S(2)}, u32[]{:S(2)}) collective-permute-start(f32[216,128]{1,0:T(8,128)S(1)} %get-tuple-element.43), channel_id=1, source_target_pairs={{0,3},{1,2},{2,1},{3,0},{4,7},{5,6},{6,5},{7,4},{8,11},{9,10},{10,... | collective-permute-start | bytes 331784 | tf_op jit(solution)/shard_map/ppermute | solution.py:755
  35.8 7.5 %collective-permute-start.17 = (f32[288,128]{1,0:T(8,128)S(1)}, f32[288,128]{1,0:T(8,128)S(1)}, u32[]{:S(2)}, u32[]{:S(2)}) collective-permute-start(f32[288,128]{1,0:T(8,128)S(1)} %get-tuple-element.44.refs_0_.refs_8_), channel_id=1, source_target_pairs={{0,24},{4,28},{8,16},{12,20},{16,8},{20,12},{24,0},{28,4},{1,25},{... | collective-permute-start | bytes 442376 | tf_op jit(solution)/shard_map/ppermute | solution.py:766
  39.5 8.8 %collective-permute-start.15 = (f32[288,128]{1,0:T(8,128)S(1)}, f32[288,128]{1,0:T(8,128)S(1)}, u32[]{:S(2)}, u32[]{:S(2)}) collective-permute-start(f32[288,128]{1,0:T(8,128)S(1)} %get-tuple-element.44.refs_0_.refs_8_), channel_id=1, source_target_pairs={{0,16},{4,20},{8,24},{12,28},{16,0},{20,4},{24,8},{28,12},{1,17},{... | collective-permute-start | bytes 442376 | tf_op jit(solution)/shard_map/ppermute | solution.py:766
  39.5 8.8 %collective-permute-start.13 = (f32[288,128]{1,0:T(8,128)S(1)}, f32[288,128]{1,0:T(8,128)S(1)}, u32[]{:S(2)}, u32[]{:S(2)}) collective-permute-start(f32[288,128]{1,0:T(8,128)S(1)} %get-tuple-element.44.refs_0_.refs_8_), channel_id=1, source_target_pairs={{0,8},{4,12},{8,0},{12,4},{16,24},{20,28},{24,16},{28,20},{1,9},{5... | collective-permute-start | bytes 442376 | tf_op jit(solution)/shard_map/ppermute | solution.py:766
  40.3 8.5 %collective-permute-start.12 = (f32[288,128]{1,0:T(8,128)S(1)}, f32[288,128]{1,0:T(8,128)S(1)}, u32[]{:S(2)}, u32[]{:S(2)}) collective-permute-start(f32[288,128]{1,0:T(8,128)S(1)} %get-tuple-element.44.refs_0_.refs_8_), channel_id=1, source_target_pairs={{0,4},{4,0},{8,12},{12,8},{16,20},{20,16},{24,28},{28,24},{1,5},{5... | collective-permute-start | bytes 442376 | tf_op jit(solution)/shard_map/ppermute | solution.py:768
  43.3 5.5 %collective-permute-start.18 = (f32[288,128]{1,0:T(8,128)S(1)}, f32[288,128]{1,0:T(8,128)S(1)}, u32[]{:S(2)}, u32[]{:S(2)}) collective-permute-start(f32[288,128]{1,0:T(8,128)S(1)} %collective-permute-done.17.refs_6_), channel_id=1, source_target_pairs={{0,4},{4,0},{8,12},{12,8},{16,20},{20,16},{24,28},{28,24},{1,5},{5... | collective-permute-start | bytes 442376 | tf_op jit(solution)/shard_map/ppermute | solution.py:768
  48.2 1.4 %collective-permute-start.16 = (f32[288,128]{1,0:T(8,128)S(1)}, f32[288,128]{1,0:T(8,128)S(1)}, u32[]{:S(2)}, u32[]{:S(2)}) collective-permute-start(f32[288,128]{1,0:T(8,128)S(1)} %collective-permute-done.15.refs_4_), channel_id=1, source_target_pairs={{0,4},{4,0},{8,12},{12,8},{16,20},{20,16},{24,28},{28,24},{1,5},{5... | collective-permute-start | bytes 442376 | tf_op jit(solution)/shard_map/ppermute | solution.py:768
  48.2 1.6 %collective-permute-start.14 = (f32[288,128]{1,0:T(8,128)S(1)}, f32[288,128]{1,0:T(8,128)S(1)}, u32[]{:S(2)}, u32[]{:S(2)}) collective-permute-start(f32[288,128]{1,0:T(8,128)S(1)} %collective-permute-done.13.refs_2_), channel_id=1, source_target_pairs={{0,4},{4,0},{8,12},{12,8},{16,20},{20,16},{24,28},{28,24},{1,5},{5... | collective-permute-start | bytes 442376 | tf_op jit(solution)/shard_map/ppermute | solution.py:768
  54.6 8.7 %collective-permute-start.24 = (f32[288,128]{1,0:T(8,128)S(1)}, f32[288,128]{1,0:T(8,128)S(1)}, u32[]{:S(2)}, u32[]{:S(2)}) collective-permute-start(f32[288,128]{1,0:T(8,128)S(1)} %get-tuple-element.46.refs_0_.refs_8_), channel_id=1, source_target_pairs={{0,24},{4,28},{8,16},{12,20},{16,8},{20,12},{24,0},{28,4},{1,25},{... | collective-permute-start | bytes 442376 | tf_op jit(solution)/shard_map/ppermute | solution.py:766
  57.1 12.3 %collective-permute-start.22 = (f32[288,128]{1,0:T(8,128)S(1)}, f32[288,128]{1,0:T(8,128)S(1)}, u32[]{:S(2)}, u32[]{:S(2)}) collective-permute-start(f32[288,128]{1,0:T(8,128)S(1)} %get-tuple-element.46.refs_0_.refs_8_), channel_id=1, source_target_pairs={{0,16},{4,20},{8,24},{12,28},{16,0},{20,4},{24,8},{28,12},{1,17},{... | collective-permute-start | bytes 442376 | tf_op jit(solution)/shard_map/ppermute | solution.py:766
  57.1 12.3 %collective-permute-start.20 = (f32[288,128]{1,0:T(8,128)S(1)}, f32[288,128]{1,0:T(8,128)S(1)}, u32[]{:S(2)}, u32[]{:S(2)}) collective-permute-start(f32[288,128]{1,0:T(8,128)S(1)} %get-tuple-element.46.refs_0_.refs_8_), channel_id=1, source_target_pairs={{0,8},{4,12},{8,0},{12,4},{16,24},{20,28},{24,16},{28,20},{1,9},{5... | collective-permute-start | bytes 442376 | tf_op jit(solution)/shard_map/ppermute | solution.py:766
  59.0 10.9 %collective-permute-start.19 = (f32[288,128]{1,0:T(8,128)S(1)}, f32[288,128]{1,0:T(8,128)S(1)}, u32[]{:S(2)}, u32[]{:S(2)}) collective-permute-start(f32[288,128]{1,0:T(8,128)S(1)} %get-tuple-element.46.refs_0_.refs_8_), channel_id=1, source_target_pairs={{0,4},{4,0},{8,12},{12,8},{16,20},{20,16},{24,28},{28,24},{1,5},{5... | collective-permute-start | bytes 442376 | tf_op jit(solution)/shard_map/ppermute | solution.py:768
  63.2 6.7 %collective-permute-start.25 = (f32[288,128]{1,0:T(8,128)S(1)}, f32[288,128]{1,0:T(8,128)S(1)}, u32[]{:S(2)}, u32[]{:S(2)}) collective-permute-start(f32[288,128]{1,0:T(8,128)S(1)} %collective-permute-done.24.refs_6_), channel_id=1, source_target_pairs={{0,4},{4,0},{8,12},{12,8},{16,20},{20,16},{24,28},{28,24},{1,5},{5... | collective-permute-start | bytes 442376 | tf_op jit(solution)/shard_map/ppermute | solution.py:768
  69.4 1.4 %collective-permute-start.23 = (f32[288,128]{1,0:T(8,128)S(1)}, f32[288,128]{1,0:T(8,128)S(1)}, u32[]{:S(2)}, u32[]{:S(2)}) collective-permute-start(f32[288,128]{1,0:T(8,128)S(1)} %collective-permute-done.22.refs_4_), channel_id=1, source_target_pairs={{0,4},{4,0},{8,12},{12,8},{16,20},{20,16},{24,28},{28,24},{1,5},{5... | collective-permute-start | bytes 442376 | tf_op jit(solution)/shard_map/ppermute | solution.py:768
  69.4 1.6 %collective-permute-start.21 = (f32[288,128]{1,0:T(8,128)S(1)}, f32[288,128]{1,0:T(8,128)S(1)}, u32[]{:S(2)}, u32[]{:S(2)}) collective-permute-start(f32[288,128]{1,0:T(8,128)S(1)} %collective-permute-done.20.refs_2_), channel_id=1, source_target_pairs={{0,4},{4,0},{8,12},{12,8},{16,20},{20,16},{24,28},{28,24},{1,5},{5... | collective-permute-start | bytes 442376 | tf_op jit(solution)/shard_map/ppermute | solution.py:768
  71.0 15.9 %copy-start.4 = (bf16[4,288,384]{2,1,0:T(8,128)(2,1)S(1)}, bf16[4,288,384]{2,1,0:T(8,128)(2,1)}, u32[]{:S(2)}) copy-start(bf16[4,288,384]{2,1,0:T(8,128)(2,1)} %constant.38.clone.refs_13_) | copy-start | bytes 2654212
  75.3 7.2 %collective-permute-start.31 = (f32[160,128]{1,0:T(8,128)S(1)}, f32[160,128]{1,0:T(8,128)S(1)}, u32[]{:S(2)}, u32[]{:S(2)}) collective-permute-start(f32[160,128]{1,0:T(8,128)S(1)} %get-tuple-element.50.refs_0_), channel_id=1, source_target_pairs={{0,24},{4,28},{8,16},{12,20},{16,8},{20,12},{24,0},{28,4},{1,25},{... | collective-permute-start | bytes 245768 | tf_op jit(solution)/shard_map/ppermute | solution.py:766
  77.5 7.9 %collective-permute-start.29 = (f32[160,128]{1,0:T(8,128)S(1)}, f32[160,128]{1,0:T(8,128)S(1)}, u32[]{:S(2)}, u32[]{:S(2)}) collective-permute-start(f32[160,128]{1,0:T(8,128)S(1)} %get-tuple-element.50.refs_0_), channel_id=1, source_target_pairs={{0,16},{4,20},{8,24},{12,28},{16,0},{20,4},{24,8},{28,12},{1,17},{... | collective-permute-start | bytes 245768 | tf_op jit(solution)/shard_map/ppermute | solution.py:766
  77.5 8.0 %collective-permute-start.27 = (f32[160,128]{1,0:T(8,128)S(1)}, f32[160,128]{1,0:T(8,128)S(1)}, u32[]{:S(2)}, u32[]{:S(2)}) collective-permute-start(f32[160,128]{1,0:T(8,128)S(1)} %get-tuple-element.50.refs_0_), channel_id=1, source_target_pairs={{0,8},{4,12},{8,0},{12,4},{16,24},{20,28},{24,16},{28,20},{1,9},{5... | collective-permute-start | bytes 245768 | tf_op jit(solution)/shard_map/ppermute | solution.py:766
  79.8 6.2 %collective-permute-start.26 = (f32[160,128]{1,0:T(8,128)S(1)}, f32[160,128]{1,0:T(8,128)S(1)}, u32[]{:S(2)}, u32[]{:S(2)}) collective-permute-start(f32[160,128]{1,0:T(8,128)S(1)} %get-tuple-element.50.refs_0_), channel_id=1, source_target_pairs={{0,4},{4,0},{8,12},{12,8},{16,20},{20,16},{24,28},{28,24},{1,5},{5... | collective-permute-start | bytes 245768 | tf_op jit(solution)/shard_map/ppermute | solution.py:768
  82.5 3.5 %collective-permute-start.32 = (f32[160,128]{1,0:T(8,128)S(1)}, f32[160,128]{1,0:T(8,128)S(1)}, u32[]{:S(2)}, u32[]{:S(2)}) collective-permute-start(f32[160,128]{1,0:T(8,128)S(1)} %collective-permute-done.31.refs_6_), channel_id=1, source_target_pairs={{0,4},{4,0},{8,12},{12,8},{16,20},{20,16},{24,28},{28,24},{1,5},{5... | collective-permute-start | bytes 245768 | tf_op jit(solution)/shard_map/ppermute | solution.py:768
  85.5 1.3 %collective-permute-start.30 = (f32[160,128]{1,0:T(8,128)S(1)}, f32[160,128]{1,0:T(8,128)S(1)}, u32[]{:S(2)}, u32[]{:S(2)}) collective-permute-start(f32[160,128]{1,0:T(8,128)S(1)} %collective-permute-done.29.refs_4_), channel_id=1, source_target_pairs={{0,4},{4,0},{8,12},{12,8},{16,20},{20,16},{24,28},{28,24},{1,5},{5... | collective-permute-start | bytes 245768 | tf_op jit(solution)/shard_map/ppermute | solution.py:768
  85.5 1.4 %collective-permute-start.28 = (f32[160,128]{1,0:T(8,128)S(1)}, f32[160,128]{1,0:T(8,128)S(1)}, u32[]{:S(2)}, u32[]{:S(2)}) collective-permute-start(f32[160,128]{1,0:T(8,128)S(1)} %collective-permute-done.27.refs_2_), channel_id=1, source_target_pairs={{0,4},{4,0},{8,12},{12,8},{16,20},{20,16},{24,28},{28,24},{1,5},{5... | collective-permute-start | bytes 245768 | tf_op jit(solution)/shard_map/ppermute | solution.py:768

commit v4 on v3

--- a/solution.py
+++ b/solution.py
@@ -20,7 +20,7 @@
 CENTRE = 9.0
 SPREAD = 9.0
 TWICE = 2.0 / SPREAD
-SUM_ROWS = 16
+SUM_ROWS = 8
 VMEM_LIMIT = 32 * 1024 * 1024
 F32 = jnp.float32
 BF16 = jnp.bfloat16
@@ -211,12 +211,30 @@
     return out
 
 
-def apply_local(src, dst, rates, flags, energy=False):
+def apply_local(src, dst, rates, flags, terms=(), products=(), energy=False):
     masks = col_masks(flags)
 
-    def body(ey, total):
+    def body(ey, sums):
+        sums = list(sums)
         for ix in range(6):
-            line = [get(src, 6 * iy + ix, ey) for iy in range(6)]
+            line = []
+            for iy in range(6):
+                point = 6 * iy + ix
+                if not terms:
+                    line.append(get(src, point, ey))
+                    continue
+                values = [get(ref, point, ey) for _, ref in terms]
+                value = None
+                for (factor, _), part in zip(terms, values):
+                    part = -part if factor == -1.0 else part * factor
+                    value = part if value is None else value + part
+                put(src, point, ey, value)
+                line.append(value)
+                values.append(value)
+                ends = (iy in (0, 5)) + (ix in (0, 5))
+                for place, (left, right) in enumerate(products):
+                    both = values[left] * values[right]
+                    sums[place] = sums[place] + (both * (0.5**ends) if ends else both)
             out = line_product(line, STIFF_HAT)
             for iy in range(6):
                 put(dst, 6 * iy + ix, ey, out[iy] + rates * line[iy])
@@ -229,15 +247,16 @@
             ]
             if energy:
                 for ix in range(6):
-                    total = total + full[ix] * line[ix]
+                    sums[-1] = sums[-1] + full[ix] * line[ix]
             full[0], full[5] = join_cols(full[0], full[5], masks)
             for ix in range(6):
                 put(dst, 6 * iy + ix, ey, full[ix])
-        return total
-
-    total = lax.fori_loop(0, BLOCKS, body, jnp.zeros((8, LANES), F32))
+        return tuple(sums)
+
+    zero = jnp.zeros((8, LANES), F32)
+    sums = lax.fori_loop(0, BLOCKS, body, (zero,) * (len(products) + int(energy)))
     join_rows(dst, flags)
-    return total
+    return sums
 
 
 def side_slice(side, i):
@@ -403,36 +422,33 @@
     return lines
 
 
-def combine(dst, terms):
-    def body(ey, carry):
-        for point in range(POINTS):
-            total = None
-            for factor, ref in terms:
-                value = get(ref, point, ey)
-                value = value if factor == 1.0 else value * factor
-                total = value if total is None else total + value
-            put(dst, point, ey, total)
-        return carry
-
-    lax.fori_loop(0, BLOCKS, body, 0)
+def pick(index, values):
+    if isinstance(index, int):
+        return values[index]
+    chosen = jnp.int32(values[0])
+    for place in range(1, len(values)):
+        chosen = jnp.where(index == place, jnp.int32(values[place]), chosen)
+    return chosen
 
 
 def block_of(place, four):
     return place if isinstance(four, int) else jnp.bitwise_xor(four, place)
 
 
-def pack_kernel(step, count, dynamic, ids_ref, which_ref, starts_ref, velocity_ref, order_ref, *send_refs):
+def pack_kernel(step, count, dynamic, which, starts, ids_ref, velocity_ref, order_ref, *send_refs):
     modes = velocity_ref.shape[1]
     width = order_ref.shape[2]
     four = ids_ref[1] if dynamic else 0
     for place in range(count):
         index = block_of(place, four)
-        window = pl.ds(pl.multiple_of(starts_ref[index], LANES), width)
+        start = pick(index, starts)
+        start = start if isinstance(start, int) else pl.multiple_of(start, LANES)
+        window = pl.ds(start, width)
         rows = [velocity_ref[comp, :, window] for comp in range(3)]
         pad = jnp.zeros((LANES - 3 * modes, width), F32)
         high, low = halves(jnp.concatenate(rows + [pad], axis=0))
         both = jnp.concatenate([high, low], axis=0)
-        out = dot(order_ref[which_ref[index]], both, ((1,), (1,)))
+        out = dot(order_ref[pick(index, which)], both, ((1,), (1,)))
         out = out[:, :LANES] + out[:, LANES:]
         if not is_packed(modes):
             send_refs[place][...] = out
@@ -541,64 +557,88 @@
     write_lines(work, lines_ref, line_rows(modes), modes)
 
 
+def sum_rows(sums):
+    return [jnp.sum(value, axis=0, keepdims=True) for value in sums]
+
+
 def second_kernel(modes, slots, ids_ref, partner_ref, side_ref, flip_ref, *refs):
     gath_refs = refs[:slots]
-    lines_ref, base_ref, k0_ref, k1_ref, k2_ref, next_ref, work, sides = refs[slots:]
+    lines_ref, _, k0_ref, k1_ref, k2_ref, next_ref, sums_ref, work, sides = refs[slots:]
     rates = helmholtz_rates(ids_ref[1], modes)
     flags = glued_flags(partner_ref)
     collect_sides(gath_refs, ids_ref[0], partner_ref, side_ref, sides, modes)
     back = own_reaction(load_lines(lines_ref, modes), rates, flags, 1.0)
-    k0_ref[...] = base_ref[...]
     add_lines(k0_ref, incoming_lines(sides, 0, partner_ref, flip_ref))
     apply_local(k0_ref, work, rates, flags)
     add_lines(work, incoming_lines(sides, 1, partner_ref, flip_ref))
     add_lines(work, back)
-    combine(k1_ref, [(1.0 / SPREAD, work), (-CENTRE / SPREAD, k0_ref)])
-    apply_local(k1_ref, work, rates, flags)
+    sums = apply_local(
+        k1_ref, work, rates, flags,
+        terms=[(1.0 / SPREAD, work), (-CENTRE / SPREAD, k0_ref)],
+        products=[(1, 1), (1, -1), (-1, -1)],
+    )
     write_lines(work, next_ref, 0, modes)
-    combine(k2_ref, [(TWICE, work), (-CENTRE * TWICE, k1_ref), (-1.0, k0_ref)])
-    apply_local(k2_ref, work, rates, flags)
+    apply_local(
+        k2_ref, work, rates, flags,
+        terms=[(TWICE, work), (-CENTRE * TWICE, k1_ref), (-1.0, k0_ref)],
+    )
     write_lines(work, next_ref, line_rows(modes), modes)
+    sums_ref[...] = jnp.concatenate(sum_rows(sums) + [jnp.zeros((5, LANES), F32)], axis=0)
 
 
 def third_kernel(modes, slots, ids_ref, partner_ref, side_ref, flip_ref, *refs):
     gath_refs = refs[:slots]
-    lines_ref, k0_ref, k1_ref, base_ref = refs[slots : slots + 4]
+    lines_ref, k1_ref, sums_ref, _ = refs[slots : slots + 4]
     k2_ref, k3_ref, a3_ref, next_ref, work, sides = refs[slots + 4 :]
     rates = helmholtz_rates(ids_ref[1], modes)
     flags = glued_flags(partner_ref)
     collect_sides(gath_refs, ids_ref[0], partner_ref, side_ref, sides, modes)
     back = own_reaction(load_lines(lines_ref, modes), rates, flags, TWICE)
-    k2_ref[...] = base_ref[...]
     incoming = incoming_lines(sides, 0, partner_ref, flip_ref)
     add_lines(k2_ref, [[value * TWICE for value in line] for line in incoming])
     apply_local(k2_ref, work, rates, flags)
     add_lines(work, incoming_lines(sides, 1, partner_ref, flip_ref))
     add_lines(work, back)
-    combine(k3_ref, [(TWICE, work), (-CENTRE * TWICE, k2_ref), (-1.0, k1_ref)])
-    energy = apply_local(k3_ref, a3_ref, rates, flags, energy=True)
+    sums = apply_local(
+        k3_ref, a3_ref, rates, flags,
+        terms=[(TWICE, work), (-CENTRE * TWICE, k2_ref), (-1.0, k1_ref)],
+        products=[(2, 1), (1, 1), (1, -1), (-1, -1)],
+        energy=True,
+    )
     write_lines(a3_ref, next_ref, 0, modes)
-    refs = (k0_ref, k1_ref, k2_ref, k3_ref)
-
-    def body(ey, sums):
-        sums = list(sums)
-        for point in range(POINTS):
-            ends = (point // 6 in (0, 5)) + (point % 6 in (0, 5))
-            values = [get(ref, point, ey) for ref in refs]
-            place = 0
-            for i in range(4):
-                scaled = values[i] * (0.5**ends) if ends else values[i]
-                for j in range(i, 4):
-                    sums[place] = sums[place] + scaled * values[j]
-                    place += 1
-        return tuple(sums)
-
-    zero = jnp.zeros((8, LANES), F32)
-    sums = lax.fori_loop(0, BLOCKS, body, (zero,) * 10)
-    rows = [jnp.sum(value, axis=0, keepdims=True) for value in sums]
-    rows.append(jnp.sum(energy, axis=0, keepdims=True))
-    rows.append(jnp.zeros((SUM_ROWS - len(rows), LANES), F32))
-    next_ref[pl.ds(line_rows(modes), SUM_ROWS), :] = jnp.concatenate(rows, axis=0)
+    next_ref[pl.ds(line_rows(modes), SUM_ROWS), :] = jnp.concatenate(
+        [sums_ref[:3, :]] + sum_rows(sums), axis=0
+    )
+
+
+def turn_kernel(which, starts, fields, has_scatter, *refs):
+    field_refs = refs[:fields]
+    order_ref = refs[fields]
+    out_refs = refs[fields + 1 : 2 * fields + 1]
+    rows = refs[-1]
+    step = rows.shape[0] // POINTS
+    used = out_refs[0].shape[0]
+    width = order_ref.shape[2]
+    for field_ref, out_ref in zip(field_refs, out_refs):
+        out_ref[...] = jnp.zeros(out_ref.shape, F32)
+        for unit in range(len(starts)):
+            for point in range(POINTS):
+                rows[pl.ds(point * step, step), :] = field_ref[pl.ds(point * 64 + unit * step, step), :]
+            high, low = halves(jnp.transpose(rows[...])[:used])
+            both = jnp.concatenate([high, low], axis=0)
+            out = dot(both, order_ref[which[unit]], ((1,), (0,)))
+            window = pl.ds(starts[unit], width)
+            out_ref[:, window] = out_ref[:, window] + (out[:used] + out[used:])
+    if has_scatter:
+        scatter_ref = refs[2 * fields + 1]
+        place = lax.broadcasted_iota(jnp.int32, (SIDE, NODES), 0)
+        at = 6 * jnp.bitwise_and(place, 7) + lax.shift_right_logical(place, 3)
+        node = lax.broadcasted_iota(jnp.int32, (SIDE, NODES), 1)
+        targets = (at, at * SIDE + SIDE - 1, at + (SIDE - 1) * SIDE, at * SIDE)
+        for side, target in enumerate(targets):
+            scatter_ref[side * SIDE : (side + 1) * SIDE, :] = jnp.where(
+                node == target, 1.0, 0.0
+            ).astype(BF16)
 
 
 def conjugate_coefficients(gram, energy):
@@ -663,14 +703,12 @@
     return solution, residual
 
 
-def last_kernel(which, starts, slots, ids_ref, partner_ref, side_ref, flip_ref, *refs):
+def last_kernel(slots, ids_ref, partner_ref, side_ref, flip_ref, *refs):
     gath_refs = refs[:slots]
-    k0_ref, k1_ref, k2_ref, k3_ref, base_ref, order_ref, sol_ref, res_ref = refs[slots : slots + 8]
-    work, sol_rows, res_rows, flat, sides = refs[slots + 8 :]
-    count, rows, _ = sol_rows.shape
-    group = rows // POINTS
+    turned = refs[slots : slots + 5]
+    scatter_ref, sol_ref, res_ref, lines, sides = refs[slots + 5 :]
     modes = sol_ref.shape[1]
-    width = order_ref.shape[2]
+    used = 3 * modes
     where = pl.ds(line_rows(modes), SUM_ROWS)
     if slots == 1:
         parts = [gath_refs[0][part, where, :] for part in range(gath_refs[0].shape[0])]
@@ -678,66 +716,59 @@
         parts = [ref[where, :] for ref in gath_refs]
     sums = functools.reduce(lambda left, right: left + right, parts)
     collect_sides(gath_refs, ids_ref[0], partner_ref, side_ref, sides, modes)
-
-    def row(place):
-        return jnp.broadcast_to(sums[place : place + 1, :], (8, LANES))
-
-    gram = [[None] * 4 for _ in range(4)]
-    place = 0
-    for i in range(4):
-        for j in range(i, 4):
-            gram[i][j] = row(place)
-            gram[j][i] = gram[i][j]
-            place += 1
-    solution, residual = conjugate_coefficients(gram, row(place))
-    work[...] = base_ref[...]
-    add_lines(work, incoming_lines(sides, 0, partner_ref, flip_ref))
+    g00, g01, g11, g12, g22, g23, g33, energy = [
+        jnp.broadcast_to(sums[place : place + 1, :], (8, LANES)) for place in range(8)
+    ]
+    g02 = 2.0 * g11 - g00
+    g03 = 2.0 * g12 - g01
+    g13 = (g22 - g00) + g11
+    gram = [
+        [g00, g01, g02, g03],
+        [g01, g11, g12, g13],
+        [g02, g12, g22, g23],
+        [g03, g13, g23, g33],
+    ]
+    solution, residual = conjugate_coefficients(gram, energy)
     on_a3 = residual[4] * TWICE
     on_k3 = residual[3] - on_a3 * CENTRE
     on_k2 = residual[2] - residual[4]
-
-    def body(ey, carry):
-        for point in range(POINTS):
-            k0, k1, k2, k3, a3 = [
-                get(ref, point, ey) for ref in (k0_ref, k1_ref, k2_ref, k3_ref, work)
-            ]
-            sol = (solution[0] * k0 + solution[1] * k1) + (solution[2] * k2 + solution[3] * k3)
-            res = (residual[0] * k0 + residual[1] * k1) + (on_k2 * k2 + on_k3 * k3) + on_a3 * a3
-            for ref, value in ((sol_rows, sol), (res_rows, res)):
-                if group >= 8:
-                    index = lax.div(ey * 8, jnp.int32(group))
-                    at = pl.multiple_of(point * group + lax.rem(ey * 8, jnp.int32(group)), 8)
-                    ref[index, pl.ds(at, 8), :] = value
-                else:
-                    for piece in range(8 // group):
-                        ref[ey * (8 // group) + piece, pl.ds(point * group, group), :] = value[
-                            piece * group : (piece + 1) * group, :
-                        ]
-        return carry
-
-    lax.fori_loop(0, BLOCKS, body, 0)
-    for ref, out_ref in ((sol_rows, sol_ref), (res_rows, res_ref)):
-        flat[...] = jnp.zeros(flat.shape, F32)
-        for index in range(count):
-            high, low = halves(jnp.transpose(ref[index]))
-            both = jnp.concatenate([high, low], axis=0)
-            out = dot(both, order_ref[which[index]], ((1,), (0,)))
-            window = pl.ds(starts[index], width)
-            flat[:, window] = flat[:, window] + (out[:LANES] + out[LANES:])
-        for comp in range(3):
-            out_ref[comp] = flat[comp * modes : (comp + 1) * modes, :]
-
-
-def call(kernel, name, out_shapes, args, scratch, scalars=0, keep=True):
+    factors = list(solution) + [residual[0], residual[1], on_k2, on_k3, on_a3]
+    columns = jnp.transpose(
+        jnp.concatenate([value[:1] for value in factors] + [jnp.zeros((LANES - 9, LANES), F32)], axis=0)
+    )
+    incoming = incoming_lines(sides, 0, partner_ref, flip_ref)
+    for side in range(4):
+        for i in range(6):
+            lines[pl.ds(side * SIDE + i * 8, 8), :] = incoming[side][i] * on_a3
+    high, low = halves(jnp.transpose(lines[...])[:used])
+    added = dot(jnp.concatenate([high, low], axis=0), scatter_ref[...], ((1,), (0,)))
+    for comp in range(3):
+        for first in range(0, modes, 8):
+            at = comp * modes + first
+            rows = [ref[at : at + 8, :] for ref in turned]
+            scale = [columns[at : at + 8, place : place + 1] for place in range(9)]
+            sol_ref[comp, first : first + 8, :] = (scale[0] * rows[0] + scale[1] * rows[1]) + (
+                scale[2] * rows[2] + scale[3] * rows[3]
+            )
+            res_ref[comp, first : first + 8, :] = (
+                (scale[4] * rows[0] + scale[5] * rows[1])
+                + (scale[6] * rows[2] + scale[7] * rows[3])
+                + (scale[8] * rows[4] + (added[at : at + 8] + added[used + at : used + at + 8]))
+            )
+
+
+def call(kernel, name, out_shapes, args, scratch, scalars=0, keep=True, aliases=None):
     smem = pl.BlockSpec(memory_space=pltpu.SMEM)
     vmem = pl.BlockSpec(memory_space=pltpu.VMEM)
+    shapes = [shape if isinstance(shape, jax.ShapeDtypeStruct) else jax.ShapeDtypeStruct(shape, F32) for shape in out_shapes]
     return pl.pallas_call(
         kernel,
         name=name,
-        out_shape=[pltpu.VMEM(shape, F32) if keep else jax.ShapeDtypeStruct(shape, F32) for shape in out_shapes],
+        out_shape=[pltpu.VMEM(one.shape, one.dtype) if keep else one for one in shapes],
         in_specs=[smem] * scalars + [vmem] * (len(args) - scalars),
         out_specs=[vmem] * len(out_shapes),
         scratch_shapes=[pltpu.VMEM(shape, F32) for shape in scratch],
+        input_output_aliases=aliases or {},
         compiler_params=pltpu.CompilerParams(vmem_limit_bytes=VMEM_LIMIT),
     )(*args[:scalars], *[held(arg) for arg in args[scalars:]])
 
@@ -757,16 +788,18 @@
     ]
 
 
-def share_lines(lines):
+def share_lines(lines, beside=()):
     parts = lax.axis_size("dom")
     if parts != 8:
-        return [lax.all_gather(lines, "dom", axis=0, tiled=False)]
+        return [lax.all_gather(lines, "dom", axis=0, tiled=False)], list(beside)
     slots = [lines] + [None] * (parts - 1)
     for slot in range(2, parts, 2):
         slots[slot] = lax.ppermute(lines, "dom", [(i, i ^ slot) for i in range(parts)])
+        if beside and slot == 2:
+            slots[slot], *beside = lax.optimization_barrier((slots[slot], *beside))
     for slot in range(0, parts, 2):
         slots[slot + 1] = lax.ppermute(slots[slot], "dom", [(i, i ^ 1) for i in range(parts)])
-    return slots
+    return slots, list(beside)
 
 
 def shards(velocity, partner, partner_side, flipped):
@@ -785,21 +818,15 @@
 
     spread = []
     for chunk in range(chunks):
-        mine = which[chunk::chunks]
-        used = sorted(set(mine))
         sent = call(
-            functools.partial(pack_kernel, step, count, dynamic),
+            functools.partial(
+                pack_kernel, step, count, dynamic, which[chunk::chunks], starts[chunk::chunks]
+            ),
             "pack",
             blocks,
-            (
-                ids,
-                np.array([used.index(one) for one in mine], np.int32),
-                np.array(starts[chunk::chunks], np.int32),
-                velocity,
-                order[np.array(used)],
-            ),
+            (ids, velocity, order),
             [],
-            scalars=3,
+            scalars=1,
         )
         spread.append(swap_blocks(sent, dynamic))
     local = []
@@ -823,33 +850,49 @@
         scalars=2,
     )
     tables = (ids, partner, partner_side, flipped)
-    gathered = share_lines(lines)
+    gathered, _ = share_lines(lines)
     slots = len(gathered)
-    k0, k1, base, lines = call(
+    k0, k1, base, lines, sums = call(
         functools.partial(second_kernel, modes, slots),
         "second",
-        [field, field, field, (2 * lined, LANES)],
+        [field, field, field, (2 * lined, LANES), (8, LANES)],
         (*tables, *gathered, lines, base),
         [field, (4, 2 * SIDE, LANES)],
         scalars=4,
-    )
-    gathered = share_lines(lines)
+        aliases={4 + slots + 1: 0},
+    )
+    flat = (3 * modes, NODES)
+    turned = call(
+        functools.partial(turn_kernel, which, starts, 2, True),
+        "turn",
+        [flat, flat, jax.ShapeDtypeStruct((4 * SIDE, NODES), BF16)],
+        (k0, k1, order),
+        [(rows, LANES)],
+    )
+    gathered, (t0, t1, scatter) = share_lines(lines, turned)
     k2, k3, a3, lines = call(
         functools.partial(third_kernel, modes, slots),
         "third",
         [field, field, field, (lined + SUM_ROWS, LANES)],
-        (*tables, *gathered, lines, k0, k1, base),
+        (*tables, *gathered, lines, k1, sums, base),
         [field, (4, 2 * SIDE, LANES)],
         scalars=4,
-    )
-    gathered = share_lines(lines)
-    units = count * chunks
+        aliases={4 + slots + 3: 0},
+    )
+    turned = call(
+        functools.partial(turn_kernel, which, starts, 3, False),
+        "turn",
+        [flat, flat, flat],
+        (k2, k3, a3, order),
+        [(rows, LANES)],
+    )
+    gathered, (t2, t3, ta) = share_lines(lines, turned)
     outs = call(
-        functools.partial(last_kernel, which, starts, slots),
+        functools.partial(last_kernel, slots),
         "last",
         [velocity.shape, velocity.shape],
-        (*tables, *gathered, k0, k1, k2, k3, a3, order),
-        [field, (units, rows, LANES), (units, rows, LANES), (LANES, NODES), (4, SIDE, LANES)],
+        (*tables, *gathered, t0, t1, t2, t3, ta, scatter),
+        [(4 * SIDE, LANES), (4, SIDE, LANES)],
         scalars=4,
         keep=False,
     )

time: 92.1 us -> 90.2 us (0.979)
  local copies, waits for them, and re-layouts: 4.55 us -> 2.38 us
  Pallas kernels: 23.5 us -> 25.4 us
  starting transfers between devices: 30.1 us -> 28.7 us
    unnamed x30 -> x20, local copies, waits for them, and re-layouts: 4.55 us -> 2.38 us
    pallas_call x8 -> x10, Pallas kernels: 23.5 us -> 25.4 us  [call(): pl.pallas_call(kernel, name=name, out_shape=[pltpu.VMEM(one.shape, one.dt...]
    ppermute x9, starting transfers between devices: 13.4 us -> 11.5 us  [share_lines(): lax.ppermute(lines, 'dom', [(i, i ^ slot) for i in range(parts)])]
  transfers between devices with their start and end apart: 33 -> 33, of which waited for: 16 -> 17; matrix products, arithmetic and copies ran while one was open for 0% -> 0% of each run, Pallas kernels for 7% -> 12%
where the time goes in v4:
time: 90.2 us; the launch traced here: 90.1 us
  waiting for transfers between devices  32.7 us (36%)
  starting transfers between devices  28.7 us (32%)
  Pallas kernels  25.4 us (28%)
  local copies, waits for them, and re-layouts  2.38 us (3%)
    pallas_call x10, Pallas kernels, call(): pl.pallas_call(kernel, name=name, out_shape=[pltpu.VMEM(one.shape, one.dt...  25.4 us
    ppermute x9, waiting for transfers between devices, share_lines(): lax.ppermute(lines, 'dom', [(i, i ^ slot) for i in range(parts)])  24.4 us
    ppermute x12, starting transfers between devices, swap_blocks(): lax.ppermute(blocks[place], 'four', [(i, i ^ place) for i in range(size)])  15.6 us
    ppermute x9, starting transfers between devices, share_lines(): lax.ppermute(lines, 'dom', [(i, i ^ slot) for i in range(parts)])  11.5 us
    ppermute x12, waiting for transfers between devices, swap_blocks(): lax.ppermute(blocks[place], 'four', [(i, i ^ place) for i in range(size)])  5.24 us
    ppermute x12, waiting for transfers between devices, share_lines(): lax.ppermute(slots[slot], 'dom', [(i, i ^ 1) for i in range(parts)])  3.05 us
    unnamed x20, local copies, waits for them, and re-layouts  2.38 us
  transfers between devices with their start and end apart: 33, of which 17 were waited for; matrix products, arithmetic and copies ran while one was open for 0% of the time, Pallas kernels for 12%

profile of v4, /device:TPU:0, one launch (start us, length us, event | category | flops | bytes accessed | tf_op | source)
XLA Modules:
  0.0 90.1 jit_solution(11995699392723535194)
XLA Ops:
  0.6 0.1 pad_add_fusion.ids_ref
  0.7 1.2 %copy-done = bf16[4,288,384]{2,1,0:T(8,128)(2,1)S(1)} copy-done((bf16[4,288,384]{2,1,0:T(8,128)(2,1)S(1)}, bf16[4,288,384]{2,1,0:T(8,128)(2,1)}, u32[]{:S(2)}) %copy-start) | copy-done | bytes 884760
  1.9 1.2 %copy-done.2 = f32[3,32,2304]{2,1,0:T(8,128)S(1)} copy-done((f32[3,32,2304]{2,1,0:T(8,128)S(1)}, f32[3,32,2304]{2,1,0:T(8,128)}, u32[]{:S(2)}) %copy-start.2) | copy-done | bytes 884760
  3.0 1.2 %pack.3 = (f32[216,128]{1,0:T(8,128)S(1)}, f32[216,128]{1,0:T(8,128)S(1)}, f32[216,128]{1,0:T(8,128)S(1)}, f32[216,128]{1,0:T(8,128)S(1)}) custom-call(s32[2]{0:T(128)S(1)} %pad_add_fusion.ids_ref, f32[3,32,2304]{2,1,0:T(8,128)S(1)} %copy-done.2, bf16[4,288,384]{2,1,0:T(8,128)(2,1)S(1)} %copy-done), custom_call_target="tpu_custom_call" | custom-call | tf_op jit(solution)/shard_map/pack/pallas_call | solution.py:764
  4.2 0.0 copy-start.3
  4.2 0.0 copy-start.4
  4.2 0.0 copy-start.5
  4.2 0.0 copy-start.6
  4.3 3.0 %collective-permute-start.6 = (f32[216,128]{1,0:T(8,128)S(1)}, f32[216,128]{1,0:T(8,128)S(1)}, u32[]{:S(2)}, u32[]{:S(2)}) collective-permute-start(f32[216,128]{1,0:T(8,128)S(1)} %get-tuple-element.52), channel_id=1, source_target_pairs={{0,1},{1,0},{2,3},{3,2},{4,5},{5,4},{6,7},{7,6},{8,9},{9,8},{10,11... | collective-permute-start | bytes 331784 | tf_op jit(solution)/shard_map/ppermute | solution.py:786
  7.3 1.5 %collective-permute-start.7 = (f32[216,128]{1,0:T(8,128)S(1)}, f32[216,128]{1,0:T(8,128)S(1)}, u32[]{:S(2)}, u32[]{:S(2)}) collective-permute-start(f32[216,128]{1,0:T(8,128)S(1)} %get-tuple-element.53), channel_id=1, source_target_pairs={{0,2},{1,3},{2,0},{3,1},{4,6},{5,7},{6,4},{7,5},{8,10},{9,11},{10,... | collective-permute-start | bytes 331784 | tf_op jit(solution)/shard_map/ppermute | solution.py:786
  8.8 0.0 collective-permute-start.8
  8.8 1.2 %pack.2 = (f32[216,128]{1,0:T(8,128)S(1)}, f32[216,128]{1,0:T(8,128)S(1)}, f32[216,128]{1,0:T(8,128)S(1)}, f32[216,128]{1,0:T(8,128)S(1)}) custom-call(s32[2]{0:T(128)S(1)} %pad_add_fusion.ids_ref, f32[3,32,2304]{2,1,0:T(8,128)S(1)} %copy-done.2, bf16[4,288,384]{2,1,0:T(8,128)(2,1)S(1)} %copy-done), custom_call_target="tpu_custom_call" | custom-call | tf_op jit(solution)/shard_map/pack/pallas_call | solution.py:764
  10.0 2.0 %collective-permute-start = (f32[216,128]{1,0:T(8,128)S(1)}, f32[216,128]{1,0:T(8,128)S(1)}, u32[]{:S(2)}, u32[]{:S(2)}) collective-permute-start(f32[216,128]{1,0:T(8,128)S(1)} %get-tuple-element.44), channel_id=1, source_target_pairs={{0,1},{1,0},{2,3},{3,2},{4,5},{5,4},{6,7},{7,6},{8,9},{9,8},{10,11... | collective-permute-start | bytes 331784 | tf_op jit(solution)/shard_map/ppermute | solution.py:786
  12.0 1.5 %collective-permute-start.1 = (f32[216,128]{1,0:T(8,128)S(1)}, f32[216,128]{1,0:T(8,128)S(1)}, u32[]{:S(2)}, u32[]{:S(2)}) collective-permute-start(f32[216,128]{1,0:T(8,128)S(1)} %get-tuple-element.45), channel_id=1, source_target_pairs={{0,2},{1,3},{2,0},{3,1},{4,6},{5,7},{6,4},{7,5},{8,10},{9,11},{10,... | collective-permute-start | bytes 331784 | tf_op jit(solution)/shard_map/ppermute | solution.py:786
  13.5 0.0 collective-permute-done.6.refs_1_
  13.5 0.4 collective-permute-start.2
  13.9 0.0 collective-permute-done.7.refs_2_
  13.9 1.5 %collective-permute-done.8.refs_3_ = f32[216,128]{1,0:T(8,128)S(1)} collective-permute-done((f32[216,128]{1,0:T(8,128)S(1)}, f32[216,128]{1,0:T(8,128)S(1)}, u32[]{:S(2)}, u32[]{:S(2)}) %collective-permute-start.8) | collective-permute-done | bytes 110624 | tf_op jit(solution)/shard_map/ppermute | solution.py:786
  15.5 0.0 copy-start.7
  15.5 2.6 %products.3 = (f32[216,128]{1,0:T(8,128)S(1)}, f32[216,128]{1,0:T(8,128)S(1)}, f32[216,128]{1,0:T(8,128)S(1)}, f32[216,128]{1,0:T(8,128)S(1)}) custom-call(s32[2]{0:T(128)S(1)} %pad_add_fusion.ids_ref, f32[216,128]{1,0:T(8,128)S(1)} %get-tuple-element.51.refs_0_, f32[216,128]{1,0:T(8,128)S(1)} %collective-permute-done.6.refs_1_, ...), custom_call_target="tpu_custom_call" | custom-call | tf_op jit(solution)/shard_map/products/pallas_call | solution.py:764
  18.0 0.0 copy-start.8
  18.1 0.0 copy-start.9
  18.1 0.8 collective-permute-start.9
  18.9 0.8 collective-permute-start.10
  19.7 1.9 %collective-permute-start.11 = (f32[216,128]{1,0:T(8,128)S(1)}, f32[216,128]{1,0:T(8,128)S(1)}, u32[]{:S(2)}, u32[]{:S(2)}) collective-permute-start(f32[216,128]{1,0:T(8,128)S(1)} %get-tuple-element.58), channel_id=1, source_target_pairs={{0,3},{1,2},{2,1},{3,0},{4,7},{5,6},{6,5},{7,4},{8,11},{9,10},{10,... | collective-permute-start | bytes 331784 | tf_op jit(solution)/shard_map/ppermute | solution.py:786
  21.6 0.0 collective-permute-done.1.refs_2_
  21.6 2.6 %products.2 = (f32[216,128]{1,0:T(8,128)S(1)}, f32[216,128]{1,0:T(8,128)S(1)}, f32[216,128]{1,0:T(8,128)S(1)}, f32[216,128]{1,0:T(8,128)S(1)}) custom-call(s32[2]{0:T(128)S(1)} %pad_add_fusion.ids_ref, f32[216,128]{1,0:T(8,128)S(1)} %get-tuple-element.43.refs_0_, f32[216,128]{1,0:T(8,128)S(1)} %collective-permute-done.refs_1_, ...), custom_call_target="tpu_custom_call" | custom-call | tf_op jit(solution)/shard_map/products/pallas_call | solution.py:764
  24.2 0.8 collective-permute-start.3
  25.0 0.8 collective-permute-start.4
  25.9 1.9 %collective-permute-start.5 = (f32[216,128]{1,0:T(8,128)S(1)}, f32[216,128]{1,0:T(8,128)S(1)}, u32[]{:S(2)}, u32[]{:S(2)}) collective-permute-start(f32[216,128]{1,0:T(8,128)S(1)} %get-tuple-element.50), channel_id=1, source_target_pairs={{0,3},{1,2},{2,1},{3,0},{4,7},{5,6},{6,5},{7,4},{8,11},{9,10},{10,... | collective-permute-start | bytes 331784 | tf_op jit(solution)/shard_map/ppermute | solution.py:786
  27.8 0.0 collective-permute-done.10.refs_6_
  27.8 1.2 %collective-permute-done.3.refs_1_ = f32[216,128]{1,0:T(8,128)S(1)} collective-permute-done((f32[216,128]{1,0:T(8,128)S(1)}, f32[216,128]{1,0:T(8,128)S(1)}, u32[]{:S(2)}, u32[]{:S(2)}) %collective-permute-start.3) | collective-permute-done | bytes 110624 | tf_op jit(solution)/shard_map/ppermute | solution.py:786
  29.0 0.8 collective-permute-done.4.refs_2_
  29.8 1.7 %collective-permute-done.5.refs_3_ = f32[216,128]{1,0:T(8,128)S(1)} collective-permute-done((f32[216,128]{1,0:T(8,128)S(1)}, f32[216,128]{1,0:T(8,128)S(1)}, u32[]{:S(2)}, u32[]{:S(2)}) %collective-permute-start.5) | collective-permute-done | bytes 110624 | tf_op jit(solution)/shard_map/ppermute | solution.py:786
  31.5 2.1 %first.1 = (f32[2304,128]{1,0:T(8,128)S(1)}, f32[288,128]{1,0:T(8,128)S(1)}) custom-call(s32[2]{0:T(128)S(1)} %pad_add_fusion.ids_ref, s32[1,4]{1,0:T(1,128)S(1)} %copy-done.7, f32[216,128]{1,0:T(8,128)S(1)} %get-tuple-element.47.refs_0_, f32[216,128]{1,0:T(8,128)S(1)} %collective-permute-done.3.refs_1_, f32[216,128]{1,0:T(8,128)S(1)} %collective-permute-done.4.refs_2_, ...), custom_call_target="tpu_custom_call" | custom-call | tf_op jit(solution)/shard_map/first/pallas_call | solution.py:764
  33.6 3.7 %collective-permute-start.17 = (f32[288,128]{1,0:T(8,128)S(1)}, f32[288,128]{1,0:T(8,128)S(1)}, u32[]{:S(2)}, u32[]{:S(2)}) collective-permute-start(f32[288,128]{1,0:T(8,128)S(1)} %get-tuple-element.59.refs_0_.refs_8_), channel_id=1, source_target_pairs={{0,24},{4,28},{8,16},{12,20},{16,8},{20,12},{24,0},{28,4},{1,25},{... | collective-permute-start | bytes 442376 | tf_op jit(solution)/shard_map/ppermute | solution.py:797
  37.3 0.8 collective-permute-start.13
  38.1 3.5 %collective-permute-done.17.refs_6_ = f32[288,128]{1,0:T(8,128)S(1)} collective-permute-done((f32[288,128]{1,0:T(8,128)S(1)}, f32[288,128]{1,0:T(8,128)S(1)}, u32[]{:S(2)}, u32[]{:S(2)}) %collective-permute-start.17) | collective-permute-done | bytes 147488 | tf_op jit(solution)/shard_map/ppermute | solution.py:797
  41.6 5.0 %collective-permute-done.15.refs_4_ = f32[288,128]{1,0:T(8,128)S(1)} collective-permute-done((f32[288,128]{1,0:T(8,128)S(1)}, f32[288,128]{1,0:T(8,128)S(1)}, u32[]{:S(2)}, u32[]{:S(2)}) %collective-permute-start.15) | collective-permute-done | bytes 147488 | tf_op jit(solution)/shard_map/ppermute | solution.py:797
  46.6 0.5 collective-permute-start.14
  47.1 0.9 collective-permute-done.16.refs_5_
  48.0 0.2 collective-permute-done.14.refs_3_
  48.2 4.6 %second.1 = (f32[2304,128]{1,0:T(8,128)S(1)}, f32[2304,128]{1,0:T(8,128)S(1)}, f32[2304,128]{1,0:T(8,128)S(1)}, f32[288,128]{1,0:T(8,128)S(1)}, f32[8,128]{1,0:T(8,128)S(1)}) custom-call(s32[2]{0:T(128)S(1)} %pad_add_fusion.ids_ref, s32[1,4]{1,0:T(1,128)S(1)} %copy-done.7, s32[1,4]{1,0:T(1,128)S(1)} %copy-done.8, ...), custom_call_target="tpu_custom_call", output_to_operand_aliasing={{0}: (13, {})} | custom-call | tf_op jit(solution)/shard_map/second/pallas_call | solution.py:764
  52.8 0.1 collective-permute-start.20
  52.9 2.4 %collective-permute-start.24 = (f32[288,128]{1,0:T(8,128)S(1)}, f32[288,128]{1,0:T(8,128)S(1)}, u32[]{:S(2)}, u32[]{:S(2)}) collective-permute-start(f32[288,128]{1,0:T(8,128)S(1)} %get-tuple-element.61.refs_0_.refs_8_), channel_id=1, source_target_pairs={{0,24},{4,28},{8,16},{12,20},{16,8},{20,12},{24,0},{28,4},{1,25},{... | collective-permute-start | bytes 442376 | tf_op jit(solution)/shard_map/ppermute | solution.py:797
  55.4 1.0 %collective-permute-start.22 = (f32[288,128]{1,0:T(8,128)S(1)}, f32[288,128]{1,0:T(8,128)S(1)}, u32[]{:S(2)}, u32[]{:S(2)}) collective-permute-start(f32[288,128]{1,0:T(8,128)S(1)} %get-tuple-element.61.refs_0_.refs_8_), channel_id=1, source_target_pairs={{0,16},{4,20},{8,24},{12,28},{16,0},{20,4},{24,8},{28,12},{1,17},{... | collective-permute-start | bytes 442376 | tf_op jit(solution)/shard_map/ppermute | solution.py:797
  56.4 2.0 %turn.2 = (f32[96,2304]{1,0:T(8,128)S(1)}, f32[96,2304]{1,0:T(8,128)S(1)}, bf16[192,2304]{1,0:T(8,128)(2,1)S(1)}) custom-call(f32[2304,128]{1,0:T(8,128)S(1)} %get-tuple-element.62.refs_0_, f32[2304,128]{1,0:T(8,128)S(1)} %get-tuple-element.63.refs_1_.refs_9_, bf16[4,288,384]{2,1,0:T(8,128)(2,1)S(1)} %copy-done.1), custom_call_target="tpu_custom_call" | custom-call | tf_op jit(solution)/shard_map/turn/pallas_call | solution.py:764
  58.5 0.5 collective-permute-done.20.refs_2_
  59.0 4.2 %collective-permute-done.24.refs_6_ = f32[288,128]{1,0:T(8,128)S(1)} collective-permute-done((f32[288,128]{1,0:T(8,128)S(1)}, f32[288,128]{1,0:T(8,128)S(1)}, u32[]{:S(2)}, u32[]{:S(2)}) %collective-permute-start.24) | collective-permute-done | bytes 147488 | tf_op jit(solution)/shard_map/ppermute | solution.py:797
  63.2 6.4 %collective-permute-done.22.refs_4_ = f32[288,128]{1,0:T(8,128)S(1)} collective-permute-done((f32[288,128]{1,0:T(8,128)S(1)}, f32[288,128]{1,0:T(8,128)S(1)}, u32[]{:S(2)}, u32[]{:S(2)}) %collective-permute-start.22) | collective-permute-done | bytes 147488 | tf_op jit(solution)/shard_map/ppermute | solution.py:797
  69.6 0.5 collective-permute-start.21
  70.1 0.9 collective-permute-done.23.refs_5_
  71.0 0.2 collective-permute-done.21.refs_3_
  71.2 3.7 %third.1 = (f32[2304,128]{1,0:T(8,128)S(1)}, f32[2304,128]{1,0:T(8,128)S(1)}, f32[2304,128]{1,0:T(8,128)S(1)}, f32[152,128]{1,0:T(8,128)S(1)}) custom-call(s32[2]{0:T(128)S(1)} %pad_add_fusion.ids_ref, s32[1,4]{1,0:T(1,128)S(1)} %copy-done.7, s32[1,4]{1,0:T(1,128)S(1)} %copy-done.8, s32[1,4]{1,0:T(1,128)S(1)} %copy-done.9, ...), custom_call_target="tpu_custom_call", output_to_operand_aliasing={{0}: (15, {})} | custom-call | tf_op jit(solution)/shard_map/third/pallas_call | solution.py:764
  74.9 0.1 collective-permute-start.27
  75.0 2.3 %collective-permute-start.31 = (f32[152,128]{1,0:T(8,128)S(1)}, f32[152,128]{1,0:T(8,128)S(1)}, u32[]{:S(2)}, u32[]{:S(2)}) collective-permute-start(f32[152,128]{1,0:T(8,128)S(1)} %get-tuple-element.70.refs_0_), channel_id=1, source_target_pairs={{0,24},{4,28},{8,16},{12,20},{16,8},{20,12},{24,0},{28,4},{1,25},{... | collective-permute-start | bytes 233480 | tf_op jit(solution)/shard_map/ppermute | solution.py:797
  77.2 1.2 %collective-permute-start.29 = (f32[152,128]{1,0:T(8,128)S(1)}, f32[152,128]{1,0:T(8,128)S(1)}, u32[]{:S(2)}, u32[]{:S(2)}) collective-permute-start(f32[152,128]{1,0:T(8,128)S(1)} %get-tuple-element.70.refs_0_), channel_id=1, source_target_pairs={{0,16},{4,20},{8,24},{12,28},{16,0},{20,4},{24,8},{28,12},{1,17},{... | collective-permute-start | bytes 233480 | tf_op jit(solution)/shard_map/ppermute | solution.py:797
  78.4 2.5 %turn.3 = (f32[96,2304]{1,0:T(8,128)S(1)}, f32[96,2304]{1,0:T(8,128)S(1)}, f32[96,2304]{1,0:T(8,128)S(1)}) custom-call(f32[2304,128]{1,0:T(8,128)S(1)} %get-tuple-element.71.refs_0_, f32[2304,128]{1,0:T(8,128)S(1)} %get-tuple-element.72.refs_1_, f32[2304,128]{1,0:T(8,128)S(1)} %get-tuple-element.73.refs_2_, bf16[4,288,384]{2,1,0:T(8,128)(2,1)S(1)} %copy-done.1), custom_call_target="tpu_custom_call" | custom-call | tf_op jit(solution)/shard_map/turn/pallas_call | solution.py:764
  80.9 1.2 %collective-permute-done.31.refs_6_ = f32[152,128]{1,0:T(8,128)S(1)} collective-permute-done((f32[152,128]{1,0:T(8,128)S(1)}, f32[152,128]{1,0:T(8,128)S(1)}, u32[]{:S(2)}, u32[]{:S(2)}) %collective-permute-start.31) | collective-permute-done | bytes 77856 | tf_op jit(solution)/shard_map/ppermute | solution.py:797
  82.1 3.6 %collective-permute-done.29.refs_4_ = f32[152,128]{1,0:T(8,128)S(1)} collective-permute-done((f32[152,128]{1,0:T(8,128)S(1)}, f32[152,128]{1,0:T(8,128)S(1)}, u32[]{:S(2)}, u32[]{:S(2)}) %collective-permute-start.29) | collective-permute-done | bytes 77856 | tf_op jit(solution)/shard_map/ppermute | solution.py:797
  85.7 0.5 collective-permute-start.28
  86.2 0.8 collective-permute-done.30.refs_5_
  86.9 0.2 collective-permute-done.28.refs_3_
  87.1 3.0 %last.1 = (f32[3,32,2304]{2,1,0:T(8,128)}, f32[3,32,2304]{2,1,0:T(8,128)}) custom-call(s32[2]{0:T(128)S(1)} %pad_add_fusion.ids_ref, s32[1,4]{1,0:T(1,128)S(1)} %copy-done.7, s32[1,4]{1,0:T(1,128)S(1)} %copy-done.8, s32[1,4]{1,0:T(1,128)S(1)} %copy-done.9, f32[152,128]{1,0:T(8,128)S(1)} %get-tuple-element.70.refs_0_, ...), custom_call_target="tpu_custom_call" | custom-call | tf_op jit(solution)/shard_map/last/pallas_call | solution.py:764
  (33 shorter events, 0.1 us)
Async XLA Ops:
  0.7 1.2 %copy-start = (bf16[4,288,384]{2,1,0:T(8,128)(2,1)S(1)}, bf16[4,288,384]{2,1,0:T(8,128)(2,1)}, u32[]{:S(2)}) copy-start(bf16[4,288,384]{2,1,0:T(8,128)(2,1)} %constant.19.clone.order_ref.refs_2_.refs_3_) | copy-start | bytes 2654212
  1.9 1.2 %copy-start.2 = (f32[3,32,2304]{2,1,0:T(8,128)S(1)}, f32[3,32,2304]{2,1,0:T(8,128)}, u32[]{:S(2)}) copy-start(f32[3,32,2304]{2,1,0:T(8,128)} %velocity_ref.3) | copy-start | bytes 2654212
  4.2 11.2 %copy-start.3 = (bf16[4,128,384]{2,1,0:T(8,128)(2,1)S(1)}, bf16[4,128,384]{2,1,0:T(8,128)(2,1)}, u32[]{:S(2)}) copy-start(bf16[4,128,384]{2,1,0:T(8,128)(2,1)} %constant.21.clone.refs_5_) | copy-start | bytes 1179652
  4.2 11.2 %copy-start.4 = (bf16[4,128,384]{2,1,0:T(8,128)(2,1)S(1)}, bf16[4,128,384]{2,1,0:T(8,128)(2,1)}, u32[]{:S(2)}) copy-start(bf16[4,128,384]{2,1,0:T(8,128)(2,1)} %constant.20.clone.refs_4_) | copy-start | bytes 1179652
  4.2 11.2 %copy-start.5 = (bf16[256,128]{1,0:T(8,128)(2,1)S(1)}, bf16[256,128]{1,0:T(8,128)(2,1)}, u32[]{:S(2)}) copy-start(bf16[256,128]{1,0:T(8,128)(2,1)} %constant.23.clone.refs_7_) | copy-start | bytes 196612
  4.2 11.2 %copy-start.6 = (bf16[256,128]{1,0:T(8,128)(2,1)S(1)}, bf16[256,128]{1,0:T(8,128)(2,1)}, u32[]{:S(2)}) copy-start(bf16[256,128]{1,0:T(8,128)(2,1)} %constant.22.clone.refs_6_) | copy-start | bytes 196612
  4.3 9.2 %collective-permute-start.6 = (f32[216,128]{1,0:T(8,128)S(1)}, f32[216,128]{1,0:T(8,128)S(1)}, u32[]{:S(2)}, u32[]{:S(2)}) collective-permute-start(f32[216,128]{1,0:T(8,128)S(1)} %get-tuple-element.52), channel_id=1, source_target_pairs={{0,1},{1,0},{2,3},{3,2},{4,5},{5,4},{6,7},{7,6},{8,9},{9,8},{10,11... | collective-permute-start | bytes 331784 | tf_op jit(solution)/shard_map/ppermute | solution.py:786
  7.3 6.7 %collective-permute-start.7 = (f32[216,128]{1,0:T(8,128)S(1)}, f32[216,128]{1,0:T(8,128)S(1)}, u32[]{:S(2)}, u32[]{:S(2)}) collective-permute-start(f32[216,128]{1,0:T(8,128)S(1)} %get-tuple-element.53), channel_id=1, source_target_pairs={{0,2},{1,3},{2,0},{3,1},{4,6},{5,7},{6,4},{7,5},{8,10},{9,11},{10,... | collective-permute-start | bytes 331784 | tf_op jit(solution)/shard_map/ppermute | solution.py:786
  8.8 6.6 %collective-permute-start.8 = (f32[216,128]{1,0:T(8,128)S(1)}, f32[216,128]{1,0:T(8,128)S(1)}, u32[]{:S(2)}, u32[]{:S(2)}) collective-permute-start(f32[216,128]{1,0:T(8,128)S(1)} %get-tuple-element.54), channel_id=1, source_target_pairs={{0,3},{1,2},{2,1},{3,0},{4,7},{5,6},{6,5},{7,4},{8,11},{9,10},{10,... | collective-permute-start | bytes 331784 | tf_op jit(solution)/shard_map/ppermute | solution.py:786
  10.0 9.8 %collective-permute-start = (f32[216,128]{1,0:T(8,128)S(1)}, f32[216,128]{1,0:T(8,128)S(1)}, u32[]{:S(2)}, u32[]{:S(2)}) collective-permute-start(f32[216,128]{1,0:T(8,128)S(1)} %get-tuple-element.44), channel_id=1, source_target_pairs={{0,1},{1,0},{2,3},{3,2},{4,5},{5,4},{6,7},{7,6},{8,9},{9,8},{10,11... | collective-permute-start | bytes 331784 | tf_op jit(solution)/shard_map/ppermute | solution.py:786
  12.0 9.6 %collective-permute-start.1 = (f32[216,128]{1,0:T(8,128)S(1)}, f32[216,128]{1,0:T(8,128)S(1)}, u32[]{:S(2)}, u32[]{:S(2)}) collective-permute-start(f32[216,128]{1,0:T(8,128)S(1)} %get-tuple-element.45), channel_id=1, source_target_pairs={{0,2},{1,3},{2,0},{3,1},{4,6},{5,7},{6,4},{7,5},{8,10},{9,11},{10,... | collective-permute-start | bytes 331784 | tf_op jit(solution)/shard_map/ppermute | solution.py:786
  13.5 8.1 %collective-permute-start.2 = (f32[216,128]{1,0:T(8,128)S(1)}, f32[216,128]{1,0:T(8,128)S(1)}, u32[]{:S(2)}, u32[]{:S(2)}) collective-permute-start(f32[216,128]{1,0:T(8,128)S(1)} %get-tuple-element.46), channel_id=1, source_target_pairs={{0,3},{1,2},{2,1},{3,0},{4,7},{5,6},{6,5},{7,4},{8,11},{9,10},{10,... | collective-permute-start | bytes 331784 | tf_op jit(solution)/shard_map/ppermute | solution.py:786
  15.5 16.1 %copy-start.7 = (s32[1,4]{1,0:T(1,128)S(1)}, s32[1,4]{1,0:T(1,128)}, u32[]{:S(2)}) copy-start(s32[1,4]{1,0:T(1,128)} %partner_ref.7) | copy-start | bytes 52
  18.0 30.1 %copy-start.8 = (s32[1,4]{1,0:T(1,128)S(1)}, s32[1,4]{1,0:T(1,128)}, u32[]{:S(2)}) copy-start(s32[1,4]{1,0:T(1,128)} %side_ref.5) | copy-start | bytes 52
  18.1 30.1 %copy-start.9 = (s32[1,4]{1,0:T(1,128)S(1)}, s32[1,4]{1,0:T(1,128)}, u32[]{:S(2)}) copy-start(s32[1,4]{1,0:T(1,128)} %flip_ref.5) | copy-start | bytes 52
  18.1 7.8 %collective-permute-start.9 = (f32[216,128]{1,0:T(8,128)S(1)}, f32[216,128]{1,0:T(8,128)S(1)}, u32[]{:S(2)}, u32[]{:S(2)}) collective-permute-start(f32[216,128]{1,0:T(8,128)S(1)} %get-tuple-element.56), channel_id=1, source_target_pairs={{0,1},{1,0},{2,3},{3,2},{4,5},{5,4},{6,7},{7,6},{8,9},{9,8},{10,11... | collective-permute-start | bytes 331784 | tf_op jit(solution)/shard_map/ppermute | solution.py:786
  18.9 8.9 %collective-permute-start.10 = (f32[216,128]{1,0:T(8,128)S(1)}, f32[216,128]{1,0:T(8,128)S(1)}, u32[]{:S(2)}, u32[]{:S(2)}) collective-permute-start(f32[216,128]{1,0:T(8,128)S(1)} %get-tuple-element.57), channel_id=1, source_target_pairs={{0,2},{1,3},{2,0},{3,1},{4,6},{5,7},{6,4},{7,5},{8,10},{9,11},{10,... | collective-permute-start | bytes 331784 | tf_op jit(solution)/shard_map/ppermute | solution.py:786
  19.7 8.1 %collective-permute-start.11 = (f32[216,128]{1,0:T(8,128)S(1)}, f32[216,128]{1,0:T(8,128)S(1)}, u32[]{:S(2)}, u32[]{:S(2)}) collective-permute-start(f32[216,128]{1,0:T(8,128)S(1)} %get-tuple-element.58), channel_id=1, source_target_pairs={{0,3},{1,2},{2,1},{3,0},{4,7},{5,6},{6,5},{7,4},{8,11},{9,10},{10,... | collective-permute-start | bytes 331784 | tf_op jit(solution)/shard_map/ppermute | solution.py:786
  24.2 4.8 %collective-permute-start.3 = (f32[216,128]{1,0:T(8,128)S(1)}, f32[216,128]{1,0:T(8,128)S(1)}, u32[]{:S(2)}, u32[]{:S(2)}) collective-permute-start(f32[216,128]{1,0:T(8,128)S(1)} %get-tuple-element.48), channel_id=1, source_target_pairs={{0,1},{1,0},{2,3},{3,2},{4,5},{5,4},{6,7},{7,6},{8,9},{9,8},{10,11... | collective-permute-start | bytes 331784 | tf_op jit(solution)/shard_map/ppermute | solution.py:786
  25.0 4.7 %collective-permute-start.4 = (f32[216,128]{1,0:T(8,128)S(1)}, f32[216,128]{1,0:T(8,128)S(1)}, u32[]{:S(2)}, u32[]{:S(2)}) collective-permute-start(f32[216,128]{1,0:T(8,128)S(1)} %get-tuple-element.49), channel_id=1, source_target_pairs={{0,2},{1,3},{2,0},{3,1},{4,6},{5,7},{6,4},{7,5},{8,10},{9,11},{10,... | collective-permute-start | bytes 331784 | tf_op jit(solution)/shard_map/ppermute | solution.py:786
  25.9 5.6 %collective-permute-start.5 = (f32[216,128]{1,0:T(8,128)S(1)}, f32[216,128]{1,0:T(8,128)S(1)}, u32[]{:S(2)}, u32[]{:S(2)}) collective-permute-start(f32[216,128]{1,0:T(8,128)S(1)} %get-tuple-element.50), channel_id=1, source_target_pairs={{0,3},{1,2},{2,1},{3,0},{4,7},{5,6},{6,5},{7,4},{8,11},{9,10},{10,... | collective-permute-start | bytes 331784 | tf_op jit(solution)/shard_map/ppermute | solution.py:786
  33.6 7.9 %collective-permute-start.17 = (f32[288,128]{1,0:T(8,128)S(1)}, f32[288,128]{1,0:T(8,128)S(1)}, u32[]{:S(2)}, u32[]{:S(2)}) collective-permute-start(f32[288,128]{1,0:T(8,128)S(1)} %get-tuple-element.59.refs_0_.refs_8_), channel_id=1, source_target_pairs={{0,24},{4,28},{8,16},{12,20},{16,8},{20,12},{24,0},{28,4},{1,25},{... | collective-permute-start | bytes 442376 | tf_op jit(solution)/shard_map/ppermute | solution.py:797
  37.3 9.3 %collective-permute-start.15 = (f32[288,128]{1,0:T(8,128)S(1)}, f32[288,128]{1,0:T(8,128)S(1)}, u32[]{:S(2)}, u32[]{:S(2)}) collective-permute-start(f32[288,128]{1,0:T(8,128)S(1)} %get-tuple-element.59.refs_0_.refs_8_), channel_id=1, source_target_pairs={{0,16},{4,20},{8,24},{12,28},{16,0},{20,4},{24,8},{28,12},{1,17},{... | collective-permute-start | bytes 442376 | tf_op jit(solution)/shard_map/ppermute | solution.py:797
  37.3 9.3 %collective-permute-start.13 = (f32[288,128]{1,0:T(8,128)S(1)}, f32[288,128]{1,0:T(8,128)S(1)}, u32[]{:S(2)}, u32[]{:S(2)}) collective-permute-start(f32[288,128]{1,0:T(8,128)S(1)} %get-tuple-element.59.refs_0_.refs_8_), channel_id=1, source_target_pairs={{0,8},{4,12},{8,0},{12,4},{16,24},{20,28},{24,16},{28,20},{1,9},{5... | collective-permute-start | bytes 442376 | tf_op jit(solution)/shard_map/ppermute | solution.py:797
  38.1 9.0 %collective-permute-start.12 = (f32[288,128]{1,0:T(8,128)S(1)}, f32[288,128]{1,0:T(8,128)S(1)}, u32[]{:S(2)}, u32[]{:S(2)}) collective-permute-start(f32[288,128]{1,0:T(8,128)S(1)} %get-tuple-element.59.refs_0_.refs_8_), channel_id=1, source_target_pairs={{0,4},{4,0},{8,12},{12,8},{16,20},{20,16},{24,28},{28,24},{1,5},{5... | collective-permute-start | bytes 442376 | tf_op jit(solution)/shard_map/ppermute | solution.py:801
  41.6 5.5 %collective-permute-start.18 = (f32[288,128]{1,0:T(8,128)S(1)}, f32[288,128]{1,0:T(8,128)S(1)}, u32[]{:S(2)}, u32[]{:S(2)}) collective-permute-start(f32[288,128]{1,0:T(8,128)S(1)} %collective-permute-done.17.refs_6_), channel_id=1, source_target_pairs={{0,4},{4,0},{8,12},{12,8},{16,20},{20,16},{24,28},{28,24},{1,5},{5... | collective-permute-start | bytes 442376 | tf_op jit(solution)/shard_map/ppermute | solution.py:801
  46.6 1.4 %collective-permute-start.16 = (f32[288,128]{1,0:T(8,128)S(1)}, f32[288,128]{1,0:T(8,128)S(1)}, u32[]{:S(2)}, u32[]{:S(2)}) collective-permute-start(f32[288,128]{1,0:T(8,128)S(1)} %collective-permute-done.15.refs_4_), channel_id=1, source_target_pairs={{0,4},{4,0},{8,12},{12,8},{16,20},{20,16},{24,28},{28,24},{1,5},{5... | collective-permute-start | bytes 442376 | tf_op jit(solution)/shard_map/ppermute | solution.py:801
  46.6 1.6 %collective-permute-start.14 = (f32[288,128]{1,0:T(8,128)S(1)}, f32[288,128]{1,0:T(8,128)S(1)}, u32[]{:S(2)}, u32[]{:S(2)}) collective-permute-start(f32[288,128]{1,0:T(8,128)S(1)} %collective-permute-done.13.refs_2_), channel_id=1, source_target_pairs={{0,4},{4,0},{8,12},{12,8},{16,20},{20,16},{24,28},{28,24},{1,5},{5... | collective-permute-start | bytes 442376 | tf_op jit(solution)/shard_map/ppermute | solution.py:801
  48.2 8.2 %copy-start.1 = (bf16[4,288,384]{2,1,0:T(8,128)(2,1)S(1)}, bf16[4,288,384]{2,1,0:T(8,128)(2,1)}, u32[]{:S(2)}) copy-start(bf16[4,288,384]{2,1,0:T(8,128)(2,1)} %constant.19.clone.order_ref.refs_2_.refs_3_) | copy-start | bytes 2654212
  52.8 6.1 %collective-permute-start.20 = (f32[288,128]{1,0:T(8,128)S(1)}, f32[288,128]{1,0:T(8,128)S(1)}, u32[]{:S(2)}, u32[]{:S(2)}) collective-permute-start(f32[288,128]{1,0:T(8,128)S(1)} %get-tuple-element.61.refs_0_.refs_8_), channel_id=1, source_target_pairs={{0,8},{4,12},{8,0},{12,4},{16,24},{20,28},{24,16},{28,20},{1,9},{5... | collective-permute-start | bytes 442376 | tf_op jit(solution)/shard_map/ppermute | solution.py:797
  52.9 10.2 %collective-permute-start.24 = (f32[288,128]{1,0:T(8,128)S(1)}, f32[288,128]{1,0:T(8,128)S(1)}, u32[]{:S(2)}, u32[]{:S(2)}) collective-permute-start(f32[288,128]{1,0:T(8,128)S(1)} %get-tuple-element.61.refs_0_.refs_8_), channel_id=1, source_target_pairs={{0,24},{4,28},{8,16},{12,20},{16,8},{20,12},{24,0},{28,4},{1,25},{... | collective-permute-start | bytes 442376 | tf_op jit(solution)/shard_map/ppermute | solution.py:797
  55.4 14.3 %collective-permute-start.22 = (f32[288,128]{1,0:T(8,128)S(1)}, f32[288,128]{1,0:T(8,128)S(1)}, u32[]{:S(2)}, u32[]{:S(2)}) collective-permute-start(f32[288,128]{1,0:T(8,128)S(1)} %get-tuple-element.61.refs_0_.refs_8_), channel_id=1, source_target_pairs={{0,16},{4,20},{8,24},{12,28},{16,0},{20,4},{24,8},{28,12},{1,17},{... | collective-permute-start | bytes 442376 | tf_op jit(solution)/shard_map/ppermute | solution.py:797
  56.4 13.7 %collective-permute-start.19 = (f32[288,128]{1,0:T(8,128)S(1)}, f32[288,128]{1,0:T(8,128)S(1)}, u32[]{:S(2)}, u32[]{:S(2)}) collective-permute-start(f32[288,128]{1,0:T(8,128)S(1)} %get-tuple-element.61.refs_0_.refs_8_), channel_id=1, source_target_pairs={{0,4},{4,0},{8,12},{12,8},{16,20},{20,16},{24,28},{28,24},{1,5},{5... | collective-permute-start | bytes 442376 | tf_op jit(solution)/shard_map/ppermute | solution.py:801
  63.2 7.0 %collective-permute-start.25 = (f32[288,128]{1,0:T(8,128)S(1)}, f32[288,128]{1,0:T(8,128)S(1)}, u32[]{:S(2)}, u32[]{:S(2)}) collective-permute-start(f32[288,128]{1,0:T(8,128)S(1)} %collective-permute-done.24.refs_6_), channel_id=1, source_target_pairs={{0,4},{4,0},{8,12},{12,8},{16,20},{20,16},{24,28},{28,24},{1,5},{5... | collective-permute-start | bytes 442376 | tf_op jit(solution)/shard_map/ppermute | solution.py:801
  69.6 1.4 %collective-permute-start.23 = (f32[288,128]{1,0:T(8,128)S(1)}, f32[288,128]{1,0:T(8,128)S(1)}, u32[]{:S(2)}, u32[]{:S(2)}) collective-permute-start(f32[288,128]{1,0:T(8,128)S(1)} %collective-permute-done.22.refs_4_), channel_id=1, source_target_pairs={{0,4},{4,0},{8,12},{12,8},{16,20},{20,16},{24,28},{28,24},{1,5},{5... | collective-permute-start | bytes 442376 | tf_op jit(solution)/shard_map/ppermute | solution.py:801
  69.6 1.6 %collective-permute-start.21 = (f32[288,128]{1,0:T(8,128)S(1)}, f32[288,128]{1,0:T(8,128)S(1)}, u32[]{:S(2)}, u32[]{:S(2)}) collective-permute-start(f32[288,128]{1,0:T(8,128)S(1)} %collective-permute-done.20.refs_2_), channel_id=1, source_target_pairs={{0,4},{4,0},{8,12},{12,8},{16,20},{20,16},{24,28},{28,24},{1,5},{5... | collective-permute-start | bytes 442376 | tf_op jit(solution)/shard_map/ppermute | solution.py:801
  74.9 6.1 %collective-permute-start.27 = (f32[152,128]{1,0:T(8,128)S(1)}, f32[152,128]{1,0:T(8,128)S(1)}, u32[]{:S(2)}, u32[]{:S(2)}) collective-permute-start(f32[152,128]{1,0:T(8,128)S(1)} %get-tuple-element.70.refs_0_), channel_id=1, source_target_pairs={{0,8},{4,12},{8,0},{12,4},{16,24},{20,28},{24,16},{28,20},{1,9},{5... | collective-permute-start | bytes 233480 | tf_op jit(solution)/shard_map/ppermute | solution.py:797
  75.0 7.1 %collective-permute-start.31 = (f32[152,128]{1,0:T(8,128)S(1)}, f32[152,128]{1,0:T(8,128)S(1)}, u32[]{:S(2)}, u32[]{:S(2)}) collective-permute-start(f32[152,128]{1,0:T(8,128)S(1)} %get-tuple-element.70.refs_0_), channel_id=1, source_target_pairs={{0,24},{4,28},{8,16},{12,20},{16,8},{20,12},{24,0},{28,4},{1,25},{... | collective-permute-start | bytes 233480 | tf_op jit(solution)/shard_map/ppermute | solution.py:797
  77.2 8.5 %collective-permute-start.29 = (f32[152,128]{1,0:T(8,128)S(1)}, f32[152,128]{1,0:T(8,128)S(1)}, u32[]{:S(2)}, u32[]{:S(2)}) collective-permute-start(f32[152,128]{1,0:T(8,128)S(1)} %get-tuple-element.70.refs_0_), channel_id=1, source_target_pairs={{0,16},{4,20},{8,24},{12,28},{16,0},{20,4},{24,8},{28,12},{1,17},{... | collective-permute-start | bytes 233480 | tf_op jit(solution)/shard_map/ppermute | solution.py:797
  78.4 7.8 %collective-permute-start.26 = (f32[152,128]{1,0:T(8,128)S(1)}, f32[152,128]{1,0:T(8,128)S(1)}, u32[]{:S(2)}, u32[]{:S(2)}) collective-permute-start(f32[152,128]{1,0:T(8,128)S(1)} %get-tuple-element.70.refs_0_), channel_id=1, source_target_pairs={{0,4},{4,0},{8,12},{12,8},{16,20},{20,16},{24,28},{28,24},{1,5},{5... | collective-permute-start | bytes 233480 | tf_op jit(solution)/shard_map/ppermute | solution.py:801
  82.1 4.1 %collective-permute-start.32 = (f32[152,128]{1,0:T(8,128)S(1)}, f32[152,128]{1,0:T(8,128)S(1)}, u32[]{:S(2)}, u32[]{:S(2)}) collective-permute-start(f32[152,128]{1,0:T(8,128)S(1)} %collective-permute-done.31.refs_6_), channel_id=1, source_target_pairs={{0,4},{4,0},{8,12},{12,8},{16,20},{20,16},{24,28},{28,24},{1,5},{5... | collective-permute-start | bytes 233480 | tf_op jit(solution)/shard_map/ppermute | solution.py:801
  85.7 1.3 %collective-permute-start.30 = (f32[152,128]{1,0:T(8,128)S(1)}, f32[152,128]{1,0:T(8,128)S(1)}, u32[]{:S(2)}, u32[]{:S(2)}) collective-permute-start(f32[152,128]{1,0:T(8,128)S(1)} %collective-permute-done.29.refs_4_), channel_id=1, source_target_pairs={{0,4},{4,0},{8,12},{12,8},{16,20},{20,16},{24,28},{28,24},{1,5},{5... | collective-permute-start | bytes 233480 | tf_op jit(solution)/shard_map/ppermute | solution.py:801
  85.7 1.4 %collective-permute-start.28 = (f32[152,128]{1,0:T(8,128)S(1)}, f32[152,128]{1,0:T(8,128)S(1)}, u32[]{:S(2)}, u32[]{:S(2)}) collective-permute-start(f32[152,128]{1,0:T(8,128)S(1)} %collective-permute-done.27.refs_2_), channel_id=1, source_target_pairs={{0,4},{4,0},{8,12},{12,8},{16,20},{20,16},{24,28},{28,24},{1,5},{5... | collective-permute-start | bytes 233480 | tf_op jit(solution)/shard_map/ppermute | solution.py:801

commit v5 on v4

--- a/solution.py
+++ b/solution.py
@@ -76,12 +76,12 @@
     planes = LANES
     modes = planes // count
     basis, forward, forward_z = fourier_tables(planes)
-    inverse = np.zeros((count, LANES, 3 * planes))
+    inverse = np.zeros((count * LANES, 3 * planes))
     for block in range(count):
         ids = slice(block * modes, (block + 1) * modes)
         for comp in range(3):
-            at = comp * modes
-            inverse[block, at : at + modes, comp * planes : (comp + 1) * planes] = basis[:, ids].T
+            at = block * LANES + comp * modes
+            inverse[at : at + modes, comp * planes : (comp + 1) * planes] = basis[:, ids].T
     back = -np.concatenate([forward.T, forward_z.T], axis=0)
     return split_table(inverse), split_table(back)
 
@@ -92,31 +92,26 @@
     return step, group // step
 
 
-def order_tables(count):
+def unit_windows(count):
     step, _ = chunk_sizes(count)
-    units = BLOCKS * BLOCKS // step
-    width = 3 * LANES
     starts = []
-    tables = []
-    which = []
-    for index in range(units):
-        start = step * index // BLOCKS * 6 * SIDE // LANES * LANES
-        starts.append(start)
-        table = np.zeros((POINTS * step, width), np.float32)
-        for point in range(POINTS):
-            for member in range(step):
-                element = index * step + member
-                row = 6 * (element // BLOCKS) + point // 6
-                col = 6 * (element % BLOCKS) + point % 6
-                table[point * step + member, row * SIDE + col - start] = 1.0
-        for place, known in enumerate(tables):
-            if np.array_equal(known, table):
-                which.append(place)
-                break
-        else:
-            which.append(len(tables))
-            tables.append(table)
-    return np.stack(tables).astype(jnp.bfloat16), which, starts
+    offsets = []
+    for index in range(BLOCKS * BLOCKS // step):
+        element = index * step
+        first = element // BLOCKS * 6 * SIDE
+        starts.append(first // LANES * LANES)
+        offsets.append(first % LANES + 6 * (element % BLOCKS))
+    return starts, offsets
+
+
+def order_table(step, offset, scratch):
+    width = scratch.shape[1]
+    lane = lax.broadcasted_iota(jnp.int32, (step, width), 1)
+    gap = lane - 6 * lax.broadcasted_iota(jnp.int32, (step, width), 0) - offset
+    for point in range(POINTS):
+        hit = gap == point // 6 * SIDE + point % 6
+        scratch[pl.ds(point * step, step), :] = jnp.where(hit, 1.0, 0.0)
+    return scratch[...].astype(BF16)
 
 
 def halves(value):
@@ -431,16 +426,35 @@
     return chosen
 
 
-def block_of(place, four):
-    return place if isinstance(four, int) else jnp.bitwise_xor(four, place)
-
-
-def pack_kernel(step, count, dynamic, which, starts, ids_ref, velocity_ref, order_ref, *send_refs):
+def offset_of(place, size):
+    return (0, 3, 1, 2)[place] if size == 4 else place
+
+
+def block_of(place, four, size):
+    return place if isinstance(four, int) else jnp.bitwise_xor(four, offset_of(place, size))
+
+
+def pack_kernel(step, count, dynamic, load, starts, offsets, ids_ref, velocity_ref, *refs):
+    send_refs = refs[:count]
+    scratch = refs[-2] if load else refs[-1]
+    width = scratch.shape[1]
     modes = velocity_ref.shape[1]
-    width = order_ref.shape[2]
     four = ids_ref[1] if dynamic else 0
+    copies = []
+    if load:
+        copies = [
+            pltpu.make_async_copy(velocity_ref.at[comp], refs[count].at[comp], refs[-1].at[comp])
+            for comp in range(3)
+        ]
+        velocity_ref = refs[count]
+    for copy in copies:
+        copy.start()
     for place in range(count):
-        index = block_of(place, four)
+        index = block_of(place, four, count)
+        table = order_table(step, pick(index, offsets), scratch)
+        if place == 0:
+            for copy in copies:
+                copy.wait()
         start = pick(index, starts)
         start = start if isinstance(start, int) else pl.multiple_of(start, LANES)
         window = pl.ds(start, width)
@@ -448,7 +462,7 @@
         pad = jnp.zeros((LANES - 3 * modes, width), F32)
         high, low = halves(jnp.concatenate(rows + [pad], axis=0))
         both = jnp.concatenate([high, low], axis=0)
-        out = dot(order_ref[pick(index, which)], both, ((1,), (1,)))
+        out = dot(table, both, ((1,), (1,)))
         out = out[:, :LANES] + out[:, LANES:]
         if not is_packed(modes):
             send_refs[place][...] = out
@@ -462,12 +476,11 @@
     recv_refs = refs[:count]
     inv_high, inv_low, back_high, back_low = refs[count : count + 4]
     send_refs = refs[count + 4 : 2 * count + 4]
-    full, phys, prod, spec = refs[2 * count + 4 :]
+    full, lined, phys, prod, spec = refs[2 * count + 4 :]
     four = ids_ref[1] if dynamic else 0
     packed = is_packed(modes)
-    total = None
     for place in range(count):
-        index = block_of(place, four)
+        index = block_of(place, four, count)
         if packed:
             ready = 3 * POINTS // 4
             values = [recv_refs[place][pl.ds(at * step, step), :] for at in range(ready)]
@@ -475,9 +488,10 @@
                 full[place, pl.ds(at * step, step), :] = value
         else:
             full[place] = recv_refs[place][...]
-        part = dot3(full[place], inv_high[index], inv_low[index])
-        total = part if total is None else total + part
-    phys[...] = total
+        first = index * LANES
+        first = first if isinstance(first, int) else pl.multiple_of(first, LANES)
+        lined[:, pl.ds(first, LANES)] = full[place]
+    phys[...] = dot3(lined[...], inv_high[...], inv_low[...])
     width = 2 * LANES
 
     def field(point, comp):
@@ -509,7 +523,7 @@
     masks = []
     shifts = []
     for place in range(count):
-        index = block_of(place, four)
+        index = block_of(place, four, count)
         masks.append([lane_block == lax.rem(index + comp, count) for comp in range(2)])
         shifts.append(lax.rem(LANES - index * modes, LANES))
     kept = []
@@ -539,7 +553,7 @@
         for place in range(count):
             ref = recv_refs[chunk * count + place]
             ready = ref.shape[0] // step
-            first = (block_of(place, four) * chunks + chunk) * step
+            first = (block_of(place, four, count) * chunks + chunk) * step
             values = unpack_lanes([ref[pl.ds(at * step, step), :] for at in range(ready)], modes)
             for point in range(POINTS):
                 at = point * 64 + first
@@ -611,26 +625,27 @@
     )
 
 
-def turn_kernel(which, starts, fields, has_scatter, *refs):
+def turn_kernel(starts, offsets, fields, has_scatter, *refs):
     field_refs = refs[:fields]
-    order_ref = refs[fields]
-    out_refs = refs[fields + 1 : 2 * fields + 1]
-    rows = refs[-1]
+    out_refs = refs[fields : 2 * fields]
+    scratch, rows = refs[-2:]
     step = rows.shape[0] // POINTS
     used = out_refs[0].shape[0]
-    width = order_ref.shape[2]
-    for field_ref, out_ref in zip(field_refs, out_refs):
+    width = scratch.shape[1]
+    for out_ref in out_refs:
         out_ref[...] = jnp.zeros(out_ref.shape, F32)
-        for unit in range(len(starts)):
+    for unit in range(len(starts)):
+        table = order_table(step, offsets[unit], scratch)
+        for field_ref, out_ref in zip(field_refs, out_refs):
             for point in range(POINTS):
                 rows[pl.ds(point * step, step), :] = field_ref[pl.ds(point * 64 + unit * step, step), :]
             high, low = halves(jnp.transpose(rows[...])[:used])
             both = jnp.concatenate([high, low], axis=0)
-            out = dot(both, order_ref[which[unit]], ((1,), (0,)))
+            out = dot(both, table, ((1,), (0,)))
             window = pl.ds(starts[unit], width)
             out_ref[:, window] = out_ref[:, window] + (out[:used] + out[used:])
     if has_scatter:
-        scatter_ref = refs[2 * fields + 1]
+        scatter_ref = refs[2 * fields]
         place = lax.broadcasted_iota(jnp.int32, (SIDE, NODES), 0)
         at = 6 * jnp.bitwise_and(place, 7) + lax.shift_right_logical(place, 3)
         node = lax.broadcasted_iota(jnp.int32, (SIDE, NODES), 1)
@@ -757,7 +772,7 @@
             )
 
 
-def call(kernel, name, out_shapes, args, scratch, scalars=0, keep=True, aliases=None):
+def call(kernel, name, out_shapes, args, scratch, scalars=0, keep=True, aliases=None, outside=False):
     smem = pl.BlockSpec(memory_space=pltpu.SMEM)
     vmem = pl.BlockSpec(memory_space=pltpu.VMEM)
     shapes = [shape if isinstance(shape, jax.ShapeDtypeStruct) else jax.ShapeDtypeStruct(shape, F32) for shape in out_shapes]
@@ -765,16 +780,16 @@
         kernel,
         name=name,
         out_shape=[pltpu.VMEM(one.shape, one.dtype) if keep else one for one in shapes],
-        in_specs=[smem] * scalars + [vmem] * (len(args) - scalars),
+        in_specs=[smem] * scalars + [pl.BlockSpec(memory_space=pltpu.HBM) if outside else vmem] * (len(args) - scalars),
         out_specs=[vmem] * len(out_shapes),
-        scratch_shapes=[pltpu.VMEM(shape, F32) for shape in scratch],
+        scratch_shapes=[pltpu.VMEM(one, F32) if isinstance(one, tuple) else one for one in scratch],
         input_output_aliases=aliases or {},
         compiler_params=pltpu.CompilerParams(vmem_limit_bytes=VMEM_LIMIT),
-    )(*args[:scalars], *[held(arg) for arg in args[scalars:]])
-
-
-def held(arg):
-    return arg if isinstance(arg, np.ndarray) else pltpu.with_memory_space_constraint(arg, pltpu.VMEM)
+    )(*args[:scalars], *[held(arg, pltpu.HBM if outside else pltpu.VMEM) for arg in args[scalars:]])
+
+
+def held(arg, space):
+    return arg if isinstance(arg, np.ndarray) else pltpu.with_memory_space_constraint(arg, space)
 
 
 def swap_blocks(blocks, dynamic):
@@ -782,10 +797,10 @@
         stacked = lax.all_to_all(jnp.stack(blocks), "four", split_axis=0, concat_axis=0, tiled=True)
         return [stacked[place] for place in range(len(blocks))]
     size = len(blocks)
-    return [blocks[0]] + [
-        lax.ppermute(blocks[place], "four", [(i, i ^ place) for i in range(size)])
-        for place in range(1, size)
-    ]
+    swapped = list(blocks)
+    for place in range(size - 1, 0, -1):
+        swapped[place] = lax.ppermute(blocks[place], "four", [(i, i ^ offset_of(place, size)) for i in range(size)])
+    return swapped
 
 
 def share_lines(lines, beside=()):
@@ -795,7 +810,7 @@
     slots = [lines] + [None] * (parts - 1)
     for slot in range(2, parts, 2):
         slots[slot] = lax.ppermute(lines, "dom", [(i, i ^ slot) for i in range(parts)])
-        if beside and slot == 2:
+        if beside and slot == parts - 2:
             slots[slot], *beside = lax.optimization_barrier((slots[slot], *beside))
     for slot in range(0, parts, 2):
         slots[slot + 1] = lax.ppermute(slots[slot], "dom", [(i, i ^ 1) for i in range(parts)])
@@ -810,24 +825,30 @@
     sent_rows = 3 * rows // 4 if is_packed(modes) else rows
     dynamic = step == BLOCKS
     (inv_high, inv_low), (back_high, back_low) = transform_tables(count)
-    order, which, starts = order_tables(count)
+    starts, offsets = unit_windows(count)
+    table = (rows, 3 * LANES)
     ids = jnp.stack([lax.axis_index("dom"), lax.axis_index("four")]).astype(jnp.int32)
     field = (NODES, LANES)
     blocks = [(sent_rows, LANES)] * count
     lined = line_rows(modes)
 
     spread = []
+    held_velocity = velocity
     for chunk in range(chunks):
+        load = chunk == 0
         sent = call(
             functools.partial(
-                pack_kernel, step, count, dynamic, which[chunk::chunks], starts[chunk::chunks]
+                pack_kernel, step, count, dynamic, load, starts[chunk::chunks], offsets[chunk::chunks]
             ),
             "pack",
-            blocks,
-            (ids, velocity, order),
-            [],
+            blocks + [velocity.shape] * load,
+            (ids, held_velocity),
+            [table] + [pltpu.SemaphoreType.DMA((3,))] * load,
             scalars=1,
+            outside=load,
         )
+        if load:
+            *sent, held_velocity = sent
         spread.append(swap_blocks(sent, dynamic))
     local = []
     for chunk in range(chunks):
@@ -836,7 +857,7 @@
             "products",
             blocks,
             (ids, *spread[chunk], inv_high, inv_low, back_high, back_low),
-            [(count, rows, LANES), (rows, 3 * LANES), (rows, 6 * LANES), (3, rows, LANES)],
+            [(count, rows, LANES), (rows, count * LANES), (rows, 3 * LANES), (rows, 6 * LANES), (3, rows, LANES)],
             scalars=1,
         )
         local += swap_blocks(sent, dynamic)
@@ -863,11 +884,11 @@
     )
     flat = (3 * modes, NODES)
     turned = call(
-        functools.partial(turn_kernel, which, starts, 2, True),
+        functools.partial(turn_kernel, starts, offsets, 2, True),
         "turn",
         [flat, flat, jax.ShapeDtypeStruct((4 * SIDE, NODES), BF16)],
-        (k0, k1, order),
-        [(rows, LANES)],
+        (k0, k1),
+        [table, (rows, LANES)],
     )
     gathered, (t0, t1, scatter) = share_lines(lines, turned)
     k2, k3, a3, lines = call(
@@ -880,11 +901,11 @@
         aliases={4 + slots + 3: 0},
     )
     turned = call(
-        functools.partial(turn_kernel, which, starts, 3, False),
+        functools.partial(turn_kernel, starts, offsets, 3, False),
         "turn",
         [flat, flat, flat],
-        (k2, k3, a3, order),
-        [(rows, LANES)],
+        (k2, k3, a3),
+        [table, (rows, LANES)],
     )
     gathered, (t2, t3, ta) = share_lines(lines, turned)
     outs = call(

time: 90.2 us -> 86.1 us (0.955)
  waiting for transfers between devices: 32.7 us -> 26.5 us
  starting transfers between devices: 28.7 us -> 32.5 us
  local copies, waits for them, and re-layouts: 2.38 us -> 0.05 us
    ppermute x9, waiting for transfers between devices: 24.4 us -> 18.5 us  [share_lines(): lax.ppermute(lines, 'dom', [(i, i ^ slot) for i in range(parts)])]
    unnamed x20 -> x14, local copies, waits for them, and re-layouts: 2.38 us -> 0.05 us
    ppermute x9, starting transfers between devices: 11.5 us -> 13.7 us  [share_lines(): lax.ppermute(lines, 'dom', [(i, i ^ slot) for i in range(parts)])]
    ppermute x12, starting transfers between devices: 15.6 us -> 16.8 us  [swap_blocks(): lax.ppermute(blocks[place], 'four', [(i, i ^ offset_of(place, size)) for...]
  transfers between devices with their start and end apart: 33 -> 33, of which waited for: 17 -> 16; matrix products, arithmetic and copies ran while one was open for 0% -> 0% of each run, Pallas kernels for 12% -> 12%
where the time goes in v5:
time: 86.1 us; the launch traced here: 85.9 us
  starting transfers between devices  32.5 us (38%)
  waiting for transfers between devices  26.5 us (31%)
  Pallas kernels  26 us (30%)
    pallas_call x10, Pallas kernels, call(): pl.pallas_call(kernel, name=name, out_shape=[pltpu.VMEM(one.shape, one.dt...  26 us
    ppermute x9, waiting for transfers between devices, share_lines(): lax.ppermute(lines, 'dom', [(i, i ^ slot) for i in range(parts)])  18.5 us
    ppermute x12, starting transfers between devices, swap_blocks(): lax.ppermute(blocks[place], 'four', [(i, i ^ offset_of(place, size)) for...  16.8 us
    ppermute x9, starting transfers between devices, share_lines(): lax.ppermute(lines, 'dom', [(i, i ^ slot) for i in range(parts)])  13.7 us
    ppermute x12, waiting for transfers between devices, swap_blocks(): lax.ppermute(blocks[place], 'four', [(i, i ^ offset_of(place, size)) for...  4.67 us
    ppermute x12, waiting for transfers between devices, share_lines(): lax.ppermute(slots[slot], 'dom', [(i, i ^ 1) for i in range(parts)])  3.35 us
    ppermute x12, starting transfers between devices, share_lines(): lax.ppermute(slots[slot], 'dom', [(i, i ^ 1) for i in range(parts)])  1.92 us
  transfers between devices with their start and end apart: 33, of which 16 were waited for; matrix products, arithmetic and copies ran while one was open for 0% of the time, Pallas kernels for 12%

profile of v5, /device:TPU:0, one launch (start us, length us, event | category | flops | bytes accessed | tf_op | source)
XLA Modules:
  0.0 85.9 jit_solution(3403830703745350423)
XLA Ops:
  0.6 0.0 copy-start.2
  0.6 0.0 copy-start.3
  0.7 0.0 copy-start
  0.7 0.0 copy-start.1
  0.7 0.1 pad_add_fusion.ids_ref
  0.8 2.3 %pack.2 = (f32[216,128]{1,0:T(8,128)S(1)}, f32[216,128]{1,0:T(8,128)S(1)}, f32[216,128]{1,0:T(8,128)S(1)}, f32[216,128]{1,0:T(8,128)S(1)}, f32[3,32,2304]{2,1,0:T(8,128)S(1)}) custom-call(s32[2]{0:T(128)S(1)} %pad_add_fusion.ids_ref, f32[3,32,2304]{2,1,0:T(8,128)} %velocity_ref.1), custom_call_target="tpu_custom_call" | custom-call | tf_op jit(solution)/shard_map/pack/pallas_call | solution.py:779
  3.1 4.0 %collective-permute-start = (f32[216,128]{1,0:T(8,128)S(1)}, f32[216,128]{1,0:T(8,128)S(1)}, u32[]{:S(2)}, u32[]{:S(2)}) collective-permute-start(f32[216,128]{1,0:T(8,128)S(1)} %get-tuple-element.45), channel_id=1, source_target_pairs={{0,3},{1,2},{2,1},{3,0},{4,7},{5,6},{6,5},{7,4},{8,11},{9,10},{10,... | collective-permute-start | bytes 331784 | tf_op jit(solution)/shard_map/ppermute | solution.py:802
  7.1 0.5 collective-permute-start.1
  7.6 0.1 collective-permute-start.2
  7.7 1.2 %pack.3 = (f32[216,128]{1,0:T(8,128)S(1)}, f32[216,128]{1,0:T(8,128)S(1)}, f32[216,128]{1,0:T(8,128)S(1)}, f32[216,128]{1,0:T(8,128)S(1)}) custom-call(s32[2]{0:T(128)S(1)} %pad_add_fusion.ids_ref, f32[3,32,2304]{2,1,0:T(8,128)S(1)} %get-tuple-element.52.velocity_ref), custom_call_target="tpu_custom_call" | custom-call | tf_op jit(solution)/shard_map/pack/pallas_call | solution.py:779
  8.9 2.9 %collective-permute-start.6 = (f32[216,128]{1,0:T(8,128)S(1)}, f32[216,128]{1,0:T(8,128)S(1)}, u32[]{:S(2)}, u32[]{:S(2)}) collective-permute-start(f32[216,128]{1,0:T(8,128)S(1)} %get-tuple-element.54), channel_id=1, source_target_pairs={{0,3},{1,2},{2,1},{3,0},{4,7},{5,6},{6,5},{7,4},{8,11},{9,10},{10,... | collective-permute-start | bytes 331784 | tf_op jit(solution)/shard_map/ppermute | solution.py:802
  11.8 0.5 collective-permute-start.7
  12.3 0.0 collective-permute-done.refs_1_
  12.3 0.7 collective-permute-start.8
  13.0 0.6 collective-permute-done.1.refs_2_
  13.5 0.0 collective-permute-done.2.refs_3_
  13.6 0.0 copy-start.4
  13.6 2.4 %products.2 = (f32[216,128]{1,0:T(8,128)S(1)}, f32[216,128]{1,0:T(8,128)S(1)}, f32[216,128]{1,0:T(8,128)S(1)}, f32[216,128]{1,0:T(8,128)S(1)}) custom-call(s32[2]{0:T(128)S(1)} %pad_add_fusion.ids_ref, f32[216,128]{1,0:T(8,128)S(1)} %get-tuple-element.44.refs_0_, f32[216,128]{1,0:T(8,128)S(1)} %collective-permute-done.refs_1_, ...), custom_call_target="tpu_custom_call" | custom-call | tf_op jit(solution)/shard_map/products/pallas_call | solution.py:779
  16.0 0.0 copy-start.5
  16.0 0.0 copy-start.6
  16.0 3.9 %collective-permute-start.3 = (f32[216,128]{1,0:T(8,128)S(1)}, f32[216,128]{1,0:T(8,128)S(1)}, u32[]{:S(2)}, u32[]{:S(2)}) collective-permute-start(f32[216,128]{1,0:T(8,128)S(1)} %get-tuple-element.49), channel_id=1, source_target_pairs={{0,3},{1,2},{2,1},{3,0},{4,7},{5,6},{6,5},{7,4},{8,11},{9,10},{10,... | collective-permute-start | bytes 331784 | tf_op jit(solution)/shard_map/ppermute | solution.py:802
  20.0 0.0 collective-permute-start.4
  20.0 0.6 collective-permute-start.5
  20.6 2.4 %products.3 = (f32[216,128]{1,0:T(8,128)S(1)}, f32[216,128]{1,0:T(8,128)S(1)}, f32[216,128]{1,0:T(8,128)S(1)}, f32[216,128]{1,0:T(8,128)S(1)}) custom-call(s32[2]{0:T(128)S(1)} %pad_add_fusion.ids_ref, f32[216,128]{1,0:T(8,128)S(1)} %get-tuple-element.53.refs_0_, f32[216,128]{1,0:T(8,128)S(1)} %collective-permute-done.6.refs_1_, ...), custom_call_target="tpu_custom_call" | custom-call | tf_op jit(solution)/shard_map/products/pallas_call | solution.py:779
  23.1 2.9 %collective-permute-start.9 = (f32[216,128]{1,0:T(8,128)S(1)}, f32[216,128]{1,0:T(8,128)S(1)}, u32[]{:S(2)}, u32[]{:S(2)}) collective-permute-start(f32[216,128]{1,0:T(8,128)S(1)} %get-tuple-element.58), channel_id=1, source_target_pairs={{0,3},{1,2},{2,1},{3,0},{4,7},{5,6},{6,5},{7,4},{8,11},{9,10},{10,... | collective-permute-start | bytes 331784 | tf_op jit(solution)/shard_map/ppermute | solution.py:802
  26.0 0.6 collective-permute-start.11
  26.6 2.1 %collective-permute-done.9.refs_5_ = f32[216,128]{1,0:T(8,128)S(1)} collective-permute-done((f32[216,128]{1,0:T(8,128)S(1)}, f32[216,128]{1,0:T(8,128)S(1)}, u32[]{:S(2)}, u32[]{:S(2)}) %collective-permute-start.9) | collective-permute-done | bytes 110624 | tf_op jit(solution)/shard_map/ppermute | solution.py:802
  28.8 2.0 %collective-permute-done.10.refs_6_ = f32[216,128]{1,0:T(8,128)S(1)} collective-permute-done((f32[216,128]{1,0:T(8,128)S(1)}, f32[216,128]{1,0:T(8,128)S(1)}, u32[]{:S(2)}, u32[]{:S(2)}) %collective-permute-start.10) | collective-permute-done | bytes 110624 | tf_op jit(solution)/shard_map/ppermute | solution.py:802
  30.7 0.0 collective-permute-done.11.refs_7_
  30.7 2.1 %first.1 = (f32[2304,128]{1,0:T(8,128)S(1)}, f32[288,128]{1,0:T(8,128)S(1)}) custom-call(s32[2]{0:T(128)S(1)} %pad_add_fusion.ids_ref, s32[1,4]{1,0:T(1,128)S(1)} %copy-done.4, f32[216,128]{1,0:T(8,128)S(1)} %get-tuple-element.48.refs_0_, f32[216,128]{1,0:T(8,128)S(1)} %collective-permute-done.3.refs_1_, f32[216,128]{1,0:T(8,128)S(1)} %collective-permute-done.4.refs_2_, ...), custom_call_target="tpu_custom_call" | custom-call | tf_op jit(solution)/shard_map/first/pallas_call | solution.py:779
  32.8 4.2 %collective-permute-start.17 = (f32[288,128]{1,0:T(8,128)S(1)}, f32[288,128]{1,0:T(8,128)S(1)}, u32[]{:S(2)}, u32[]{:S(2)}) collective-permute-start(f32[288,128]{1,0:T(8,128)S(1)} %get-tuple-element.61.refs_0_.refs_8_), channel_id=1, source_target_pairs={{0,24},{4,28},{8,16},{12,20},{16,8},{20,12},{24,0},{28,4},{1,25},{... | collective-permute-start | bytes 442376 | tf_op jit(solution)/shard_map/ppermute | solution.py:812
  37.0 0.0 collective-permute-start.15
  37.0 0.6 collective-permute-start.13
  37.7 2.9 %collective-permute-done.17.refs_6_ = f32[288,128]{1,0:T(8,128)S(1)} collective-permute-done((f32[288,128]{1,0:T(8,128)S(1)}, f32[288,128]{1,0:T(8,128)S(1)}, u32[]{:S(2)}, u32[]{:S(2)}) %collective-permute-start.17) | collective-permute-done | bytes 147488 | tf_op jit(solution)/shard_map/ppermute | solution.py:812
  40.6 5.0 %collective-permute-done.15.refs_4_ = f32[288,128]{1,0:T(8,128)S(1)} collective-permute-done((f32[288,128]{1,0:T(8,128)S(1)}, f32[288,128]{1,0:T(8,128)S(1)}, u32[]{:S(2)}, u32[]{:S(2)}) %collective-permute-start.15) | collective-permute-done | bytes 147488 | tf_op jit(solution)/shard_map/ppermute | solution.py:812
  45.6 0.5 collective-permute-start.14
  46.1 0.0 collective-permute-done.12.refs_1_
  46.1 0.0 collective-permute-done.18.refs_7_
  46.1 0.9 collective-permute-done.16.refs_5_
  47.0 0.2 collective-permute-done.14.refs_3_
  47.2 4.5 %second.1 = (f32[2304,128]{1,0:T(8,128)S(1)}, f32[2304,128]{1,0:T(8,128)S(1)}, f32[2304,128]{1,0:T(8,128)S(1)}, f32[288,128]{1,0:T(8,128)S(1)}, f32[8,128]{1,0:T(8,128)S(1)}) custom-call(s32[2]{0:T(128)S(1)} %pad_add_fusion.ids_ref, s32[1,4]{1,0:T(1,128)S(1)} %copy-done.4, s32[1,4]{1,0:T(1,128)S(1)} %copy-done.5, ...), custom_call_target="tpu_custom_call", output_to_operand_aliasing={{0}: (13, {})} | custom-call | tf_op jit(solution)/shard_map/second/pallas_call | solution.py:779
  51.7 2.5 %collective-permute-start.24 = (f32[288,128]{1,0:T(8,128)S(1)}, f32[288,128]{1,0:T(8,128)S(1)}, u32[]{:S(2)}, u32[]{:S(2)}) collective-permute-start(f32[288,128]{1,0:T(8,128)S(1)} %get-tuple-element.63.refs_0_.refs_8_), channel_id=1, source_target_pairs={{0,24},{4,28},{8,16},{12,20},{16,8},{20,12},{24,0},{28,4},{1,25},{... | collective-permute-start | bytes 442376 | tf_op jit(solution)/shard_map/ppermute | solution.py:812
  54.2 0.0 collective-permute-start.22
  54.2 2.0 %collective-permute-start.20 = (f32[288,128]{1,0:T(8,128)S(1)}, f32[288,128]{1,0:T(8,128)S(1)}, u32[]{:S(2)}, u32[]{:S(2)}) collective-permute-start(f32[288,128]{1,0:T(8,128)S(1)} %get-tuple-element.63.refs_0_.refs_8_), channel_id=1, source_target_pairs={{0,8},{4,12},{8,0},{12,4},{16,24},{20,28},{24,16},{28,20},{1,9},{5... | collective-permute-start | bytes 442376 | tf_op jit(solution)/shard_map/ppermute | solution.py:812
  56.2 2.0 %turn.2 = (f32[96,2304]{1,0:T(8,128)S(1)}, f32[96,2304]{1,0:T(8,128)S(1)}, bf16[192,2304]{1,0:T(8,128)(2,1)S(1)}) custom-call(f32[2304,128]{1,0:T(8,128)S(1)} %get-tuple-element.64.refs_0_, f32[2304,128]{1,0:T(8,128)S(1)} %get-tuple-element.65.refs_1_.refs_9_), custom_call_target="tpu_custom_call" | custom-call | tf_op jit(solution)/shard_map/turn/pallas_call | solution.py:779
  58.2 2.2 %collective-permute-done.24.refs_6_ = f32[288,128]{1,0:T(8,128)S(1)} collective-permute-done((f32[288,128]{1,0:T(8,128)S(1)}, f32[288,128]{1,0:T(8,128)S(1)}, u32[]{:S(2)}, u32[]{:S(2)}) %collective-permute-start.24) | collective-permute-done | bytes 147488 | tf_op jit(solution)/shard_map/ppermute | solution.py:812
  60.4 6.1 %collective-permute-done.22.refs_4_ = f32[288,128]{1,0:T(8,128)S(1)} collective-permute-done((f32[288,128]{1,0:T(8,128)S(1)}, f32[288,128]{1,0:T(8,128)S(1)}, u32[]{:S(2)}, u32[]{:S(2)}) %collective-permute-start.22) | collective-permute-done | bytes 147488 | tf_op jit(solution)/shard_map/ppermute | solution.py:812
  66.5 0.5 collective-permute-start.21
  67.0 0.0 collective-permute-start.25
  67.0 0.8 collective-permute-done.23.refs_5_
  67.9 0.2 collective-permute-done.21.refs_3_
  68.1 0.3 collective-permute-done.25.refs_7_
  68.4 3.6 %third.1 = (f32[2304,128]{1,0:T(8,128)S(1)}, f32[2304,128]{1,0:T(8,128)S(1)}, f32[2304,128]{1,0:T(8,128)S(1)}, f32[152,128]{1,0:T(8,128)S(1)}) custom-call(s32[2]{0:T(128)S(1)} %pad_add_fusion.ids_ref, s32[1,4]{1,0:T(1,128)S(1)} %copy-done.4, s32[1,4]{1,0:T(1,128)S(1)} %copy-done.5, s32[1,4]{1,0:T(1,128)S(1)} %copy-done.6, ...), custom_call_target="tpu_custom_call", output_to_operand_aliasing={{0}: (15, {})} | custom-call | tf_op jit(solution)/shard_map/third/pallas_call | solution.py:779
  72.0 2.0 %collective-permute-start.31 = (f32[152,128]{1,0:T(8,128)S(1)}, f32[152,128]{1,0:T(8,128)S(1)}, u32[]{:S(2)}, u32[]{:S(2)}) collective-permute-start(f32[152,128]{1,0:T(8,128)S(1)} %get-tuple-element.72.refs_0_), channel_id=1, source_target_pairs={{0,24},{4,28},{8,16},{12,20},{16,8},{20,12},{24,0},{28,4},{1,25},{... | collective-permute-start | bytes 233480 | tf_op jit(solution)/shard_map/ppermute | solution.py:812
  74.0 2.4 %collective-permute-start.27 = (f32[152,128]{1,0:T(8,128)S(1)}, f32[152,128]{1,0:T(8,128)S(1)}, u32[]{:S(2)}, u32[]{:S(2)}) collective-permute-start(f32[152,128]{1,0:T(8,128)S(1)} %get-tuple-element.72.refs_0_), channel_id=1, source_target_pairs={{0,8},{4,12},{8,0},{12,4},{16,24},{20,28},{24,16},{28,20},{1,9},{5... | collective-permute-start | bytes 233480 | tf_op jit(solution)/shard_map/ppermute | solution.py:812
  76.4 2.5 %turn.3 = (f32[96,2304]{1,0:T(8,128)S(1)}, f32[96,2304]{1,0:T(8,128)S(1)}, f32[96,2304]{1,0:T(8,128)S(1)}) custom-call(f32[2304,128]{1,0:T(8,128)S(1)} %get-tuple-element.73.refs_0_, f32[2304,128]{1,0:T(8,128)S(1)} %get-tuple-element.74.refs_1_, f32[2304,128]{1,0:T(8,128)S(1)} %get-tuple-element.75.refs_2_), custom_call_target="tpu_custom_call" | custom-call | tf_op jit(solution)/shard_map/turn/pallas_call | solution.py:779
  78.9 0.2 collective-permute-done.31.refs_6_
  79.1 0.4 collective-permute-start.32
  79.5 2.0 %collective-permute-done.29.refs_4_ = f32[152,128]{1,0:T(8,128)S(1)} collective-permute-done((f32[152,128]{1,0:T(8,128)S(1)}, f32[152,128]{1,0:T(8,128)S(1)}, u32[]{:S(2)}, u32[]{:S(2)}) %collective-permute-start.29) | collective-permute-done | bytes 77856 | tf_op jit(solution)/shard_map/ppermute | solution.py:812
  81.5 0.0 collective-permute-start.30
  81.6 0.5 collective-permute-start.28
  82.1 0.8 collective-permute-done.30.refs_5_
  82.8 0.2 collective-permute-done.28.refs_3_
  83.0 3.0 %last.1 = (f32[3,32,2304]{2,1,0:T(8,128)}, f32[3,32,2304]{2,1,0:T(8,128)}) custom-call(s32[2]{0:T(128)S(1)} %pad_add_fusion.ids_ref, s32[1,4]{1,0:T(1,128)S(1)} %copy-done.4, s32[1,4]{1,0:T(1,128)S(1)} %copy-done.5, s32[1,4]{1,0:T(1,128)S(1)} %copy-done.6, f32[152,128]{1,0:T(8,128)S(1)} %get-tuple-element.72.refs_0_, ...), custom_call_target="tpu_custom_call" | custom-call | tf_op jit(solution)/shard_map/last/pallas_call | solution.py:779
  (27 shorter events, 0.1 us)
Async XLA Ops:
  0.6 12.9 %copy-start.2 = (bf16[256,128]{1,0:T(8,128)(2,1)S(1)}, bf16[256,128]{1,0:T(8,128)(2,1)}, u32[]{:S(2)}) copy-start(bf16[256,128]{1,0:T(8,128)(2,1)} %constant.20.clone.refs_7_) | copy-start | bytes 196612
  0.6 12.9 %copy-start.3 = (bf16[256,128]{1,0:T(8,128)(2,1)S(1)}, bf16[256,128]{1,0:T(8,128)(2,1)}, u32[]{:S(2)}) copy-start(bf16[256,128]{1,0:T(8,128)(2,1)} %constant.19.clone.refs_6_) | copy-start | bytes 196612
  0.7 12.9 %copy-start = (bf16[512,384]{1,0:T(8,128)(2,1)S(1)}, bf16[512,384]{1,0:T(8,128)(2,1)}, u32[]{:S(2)}) copy-start(bf16[512,384]{1,0:T(8,128)(2,1)} %constant.18.clone.refs_5_) | copy-start | bytes 1179652
  0.7 12.9 %copy-start.1 = (bf16[512,384]{1,0:T(8,128)(2,1)S(1)}, bf16[512,384]{1,0:T(8,128)(2,1)}, u32[]{:S(2)}) copy-start(bf16[512,384]{1,0:T(8,128)(2,1)} %constant.17.clone.refs_4_) | copy-start | bytes 1179652
  3.1 9.2 %collective-permute-start = (f32[216,128]{1,0:T(8,128)S(1)}, f32[216,128]{1,0:T(8,128)S(1)}, u32[]{:S(2)}, u32[]{:S(2)}) collective-permute-start(f32[216,128]{1,0:T(8,128)S(1)} %get-tuple-element.45), channel_id=1, source_target_pairs={{0,3},{1,2},{2,1},{3,0},{4,7},{5,6},{6,5},{7,4},{8,11},{9,10},{10,... | collective-permute-start | bytes 331784 | tf_op jit(solution)/shard_map/ppermute | solution.py:802
  7.1 6.5 %collective-permute-start.1 = (f32[216,128]{1,0:T(8,128)S(1)}, f32[216,128]{1,0:T(8,128)S(1)}, u32[]{:S(2)}, u32[]{:S(2)}) collective-permute-start(f32[216,128]{1,0:T(8,128)S(1)} %get-tuple-element.46), channel_id=1, source_target_pairs={{0,1},{1,0},{2,3},{3,2},{4,5},{5,4},{6,7},{7,6},{8,9},{9,8},{10,11... | collective-permute-start | bytes 331784 | tf_op jit(solution)/shard_map/ppermute | solution.py:802
  7.6 5.9 %collective-permute-start.2 = (f32[216,128]{1,0:T(8,128)S(1)}, f32[216,128]{1,0:T(8,128)S(1)}, u32[]{:S(2)}, u32[]{:S(2)}) collective-permute-start(f32[216,128]{1,0:T(8,128)S(1)} %get-tuple-element.47), channel_id=1, source_target_pairs={{0,2},{1,3},{2,0},{3,1},{4,6},{5,7},{6,4},{7,5},{8,10},{9,11},{10,... | collective-permute-start | bytes 331784 | tf_op jit(solution)/shard_map/ppermute | solution.py:802
  8.9 11.1 %collective-permute-start.6 = (f32[216,128]{1,0:T(8,128)S(1)}, f32[216,128]{1,0:T(8,128)S(1)}, u32[]{:S(2)}, u32[]{:S(2)}) collective-permute-start(f32[216,128]{1,0:T(8,128)S(1)} %get-tuple-element.54), channel_id=1, source_target_pairs={{0,3},{1,2},{2,1},{3,0},{4,7},{5,6},{6,5},{7,4},{8,11},{9,10},{10,... | collective-permute-start | bytes 331784 | tf_op jit(solution)/shard_map/ppermute | solution.py:802
  11.8 8.8 %collective-permute-start.7 = (f32[216,128]{1,0:T(8,128)S(1)}, f32[216,128]{1,0:T(8,128)S(1)}, u32[]{:S(2)}, u32[]{:S(2)}) collective-permute-start(f32[216,128]{1,0:T(8,128)S(1)} %get-tuple-element.55), channel_id=1, source_target_pairs={{0,1},{1,0},{2,3},{3,2},{4,5},{5,4},{6,7},{7,6},{8,9},{9,8},{10,11... | collective-permute-start | bytes 331784 | tf_op jit(solution)/shard_map/ppermute | solution.py:802
  12.3 8.3 %collective-permute-start.8 = (f32[216,128]{1,0:T(8,128)S(1)}, f32[216,128]{1,0:T(8,128)S(1)}, u32[]{:S(2)}, u32[]{:S(2)}) collective-permute-start(f32[216,128]{1,0:T(8,128)S(1)} %get-tuple-element.56), channel_id=1, source_target_pairs={{0,2},{1,3},{2,0},{3,1},{4,6},{5,7},{6,4},{7,5},{8,10},{9,11},{10,... | collective-permute-start | bytes 331784 | tf_op jit(solution)/shard_map/ppermute | solution.py:802
  13.6 17.2 %copy-start.4 = (s32[1,4]{1,0:T(1,128)S(1)}, s32[1,4]{1,0:T(1,128)}, u32[]{:S(2)}) copy-start(s32[1,4]{1,0:T(1,128)} %partner_ref.7) | copy-start | bytes 52
  16.0 31.2 %copy-start.5 = (s32[1,4]{1,0:T(1,128)S(1)}, s32[1,4]{1,0:T(1,128)}, u32[]{:S(2)}) copy-start(s32[1,4]{1,0:T(1,128)} %side_ref.5) | copy-start | bytes 52
  16.0 31.2 %copy-start.6 = (s32[1,4]{1,0:T(1,128)S(1)}, s32[1,4]{1,0:T(1,128)}, u32[]{:S(2)}) copy-start(s32[1,4]{1,0:T(1,128)} %flip_ref.5) | copy-start | bytes 52
  16.0 10.0 %collective-permute-start.3 = (f32[216,128]{1,0:T(8,128)S(1)}, f32[216,128]{1,0:T(8,128)S(1)}, u32[]{:S(2)}, u32[]{:S(2)}) collective-permute-start(f32[216,128]{1,0:T(8,128)S(1)} %get-tuple-element.49), channel_id=1, source_target_pairs={{0,3},{1,2},{2,1},{3,0},{4,7},{5,6},{6,5},{7,4},{8,11},{9,10},{10,... | collective-permute-start | bytes 331784 | tf_op jit(solution)/shard_map/ppermute | solution.py:802
  20.0 6.6 %collective-permute-start.4 = (f32[216,128]{1,0:T(8,128)S(1)}, f32[216,128]{1,0:T(8,128)S(1)}, u32[]{:S(2)}, u32[]{:S(2)}) collective-permute-start(f32[216,128]{1,0:T(8,128)S(1)} %get-tuple-element.50), channel_id=1, source_target_pairs={{0,1},{1,0},{2,3},{3,2},{4,5},{5,4},{6,7},{7,6},{8,9},{9,8},{10,11... | collective-permute-start | bytes 331784 | tf_op jit(solution)/shard_map/ppermute | solution.py:802
  20.0 6.6 %collective-permute-start.5 = (f32[216,128]{1,0:T(8,128)S(1)}, f32[216,128]{1,0:T(8,128)S(1)}, u32[]{:S(2)}, u32[]{:S(2)}) collective-permute-start(f32[216,128]{1,0:T(8,128)S(1)} %get-tuple-element.51), channel_id=1, source_target_pairs={{0,2},{1,3},{2,0},{3,1},{4,6},{5,7},{6,4},{7,5},{8,10},{9,11},{10,... | collective-permute-start | bytes 331784 | tf_op jit(solution)/shard_map/ppermute | solution.py:802
  23.1 5.7 %collective-permute-start.9 = (f32[216,128]{1,0:T(8,128)S(1)}, f32[216,128]{1,0:T(8,128)S(1)}, u32[]{:S(2)}, u32[]{:S(2)}) collective-permute-start(f32[216,128]{1,0:T(8,128)S(1)} %get-tuple-element.58), channel_id=1, source_target_pairs={{0,3},{1,2},{2,1},{3,0},{4,7},{5,6},{6,5},{7,4},{8,11},{9,10},{10,... | collective-permute-start | bytes 331784 | tf_op jit(solution)/shard_map/ppermute | solution.py:802
  26.0 4.7 %collective-permute-start.10 = (f32[216,128]{1,0:T(8,128)S(1)}, f32[216,128]{1,0:T(8,128)S(1)}, u32[]{:S(2)}, u32[]{:S(2)}) collective-permute-start(f32[216,128]{1,0:T(8,128)S(1)} %get-tuple-element.59), channel_id=1, source_target_pairs={{0,1},{1,0},{2,3},{3,2},{4,5},{5,4},{6,7},{7,6},{8,9},{9,8},{10,11... | collective-permute-start | bytes 331784 | tf_op jit(solution)/shard_map/ppermute | solution.py:802
  26.0 4.7 %collective-permute-start.11 = (f32[216,128]{1,0:T(8,128)S(1)}, f32[216,128]{1,0:T(8,128)S(1)}, u32[]{:S(2)}, u32[]{:S(2)}) collective-permute-start(f32[216,128]{1,0:T(8,128)S(1)} %get-tuple-element.60), channel_id=1, source_target_pairs={{0,2},{1,3},{2,0},{3,1},{4,6},{5,7},{6,4},{7,5},{8,10},{9,11},{10,... | collective-permute-start | bytes 331784 | tf_op jit(solution)/shard_map/ppermute | solution.py:802
  32.8 7.8 %collective-permute-start.17 = (f32[288,128]{1,0:T(8,128)S(1)}, f32[288,128]{1,0:T(8,128)S(1)}, u32[]{:S(2)}, u32[]{:S(2)}) collective-permute-start(f32[288,128]{1,0:T(8,128)S(1)} %get-tuple-element.61.refs_0_.refs_8_), channel_id=1, source_target_pairs={{0,24},{4,28},{8,16},{12,20},{16,8},{20,12},{24,0},{28,4},{1,25},{... | collective-permute-start | bytes 442376 | tf_op jit(solution)/shard_map/ppermute | solution.py:812
  37.0 8.6 %collective-permute-start.15 = (f32[288,128]{1,0:T(8,128)S(1)}, f32[288,128]{1,0:T(8,128)S(1)}, u32[]{:S(2)}, u32[]{:S(2)}) collective-permute-start(f32[288,128]{1,0:T(8,128)S(1)} %get-tuple-element.61.refs_0_.refs_8_), channel_id=1, source_target_pairs={{0,16},{4,20},{8,24},{12,28},{16,0},{20,4},{24,8},{28,12},{1,17},{... | collective-permute-start | bytes 442376 | tf_op jit(solution)/shard_map/ppermute | solution.py:812
  37.0 8.6 %collective-permute-start.13 = (f32[288,128]{1,0:T(8,128)S(1)}, f32[288,128]{1,0:T(8,128)S(1)}, u32[]{:S(2)}, u32[]{:S(2)}) collective-permute-start(f32[288,128]{1,0:T(8,128)S(1)} %get-tuple-element.61.refs_0_.refs_8_), channel_id=1, source_target_pairs={{0,8},{4,12},{8,0},{12,4},{16,24},{20,28},{24,16},{28,20},{1,9},{5... | collective-permute-start | bytes 442376 | tf_op jit(solution)/shard_map/ppermute | solution.py:812
  37.7 8.4 %collective-permute-start.12 = (f32[288,128]{1,0:T(8,128)S(1)}, f32[288,128]{1,0:T(8,128)S(1)}, u32[]{:S(2)}, u32[]{:S(2)}) collective-permute-start(f32[288,128]{1,0:T(8,128)S(1)} %get-tuple-element.61.refs_0_.refs_8_), channel_id=1, source_target_pairs={{0,4},{4,0},{8,12},{12,8},{16,20},{20,16},{24,28},{28,24},{1,5},{5... | collective-permute-start | bytes 442376 | tf_op jit(solution)/shard_map/ppermute | solution.py:816
  40.6 5.5 %collective-permute-start.18 = (f32[288,128]{1,0:T(8,128)S(1)}, f32[288,128]{1,0:T(8,128)S(1)}, u32[]{:S(2)}, u32[]{:S(2)}) collective-permute-start(f32[288,128]{1,0:T(8,128)S(1)} %collective-permute-done.17.refs_6_), channel_id=1, source_target_pairs={{0,4},{4,0},{8,12},{12,8},{16,20},{20,16},{24,28},{28,24},{1,5},{5... | collective-permute-start | bytes 442376 | tf_op jit(solution)/shard_map/ppermute | solution.py:816
  45.6 1.4 %collective-permute-start.16 = (f32[288,128]{1,0:T(8,128)S(1)}, f32[288,128]{1,0:T(8,128)S(1)}, u32[]{:S(2)}, u32[]{:S(2)}) collective-permute-start(f32[288,128]{1,0:T(8,128)S(1)} %collective-permute-done.15.refs_4_), channel_id=1, source_target_pairs={{0,4},{4,0},{8,12},{12,8},{16,20},{20,16},{24,28},{28,24},{1,5},{5... | collective-permute-start | bytes 442376 | tf_op jit(solution)/shard_map/ppermute | solution.py:816
  45.6 1.6 %collective-permute-start.14 = (f32[288,128]{1,0:T(8,128)S(1)}, f32[288,128]{1,0:T(8,128)S(1)}, u32[]{:S(2)}, u32[]{:S(2)}) collective-permute-start(f32[288,128]{1,0:T(8,128)S(1)} %collective-permute-done.13.refs_2_), channel_id=1, source_target_pairs={{0,4},{4,0},{8,12},{12,8},{16,20},{20,16},{24,28},{28,24},{1,5},{5... | collective-permute-start | bytes 442376 | tf_op jit(solution)/shard_map/ppermute | solution.py:816
  51.7 8.7 %collective-permute-start.24 = (f32[288,128]{1,0:T(8,128)S(1)}, f32[288,128]{1,0:T(8,128)S(1)}, u32[]{:S(2)}, u32[]{:S(2)}) collective-permute-start(f32[288,128]{1,0:T(8,128)S(1)} %get-tuple-element.63.refs_0_.refs_8_), channel_id=1, source_target_pairs={{0,24},{4,28},{8,16},{12,20},{16,8},{20,12},{24,0},{28,4},{1,25},{... | collective-permute-start | bytes 442376 | tf_op jit(solution)/shard_map/ppermute | solution.py:812
  54.2 12.3 %collective-permute-start.22 = (f32[288,128]{1,0:T(8,128)S(1)}, f32[288,128]{1,0:T(8,128)S(1)}, u32[]{:S(2)}, u32[]{:S(2)}) collective-permute-start(f32[288,128]{1,0:T(8,128)S(1)} %get-tuple-element.63.refs_0_.refs_8_), channel_id=1, source_target_pairs={{0,16},{4,20},{8,24},{12,28},{16,0},{20,4},{24,8},{28,12},{1,17},{... | collective-permute-start | bytes 442376 | tf_op jit(solution)/shard_map/ppermute | solution.py:812
  54.2 12.3 %collective-permute-start.20 = (f32[288,128]{1,0:T(8,128)S(1)}, f32[288,128]{1,0:T(8,128)S(1)}, u32[]{:S(2)}, u32[]{:S(2)}) collective-permute-start(f32[288,128]{1,0:T(8,128)S(1)} %get-tuple-element.63.refs_0_.refs_8_), channel_id=1, source_target_pairs={{0,8},{4,12},{8,0},{12,4},{16,24},{20,28},{24,16},{28,20},{1,9},{5... | collective-permute-start | bytes 442376 | tf_op jit(solution)/shard_map/ppermute | solution.py:812
  56.2 10.9 %collective-permute-start.19 = (f32[288,128]{1,0:T(8,128)S(1)}, f32[288,128]{1,0:T(8,128)S(1)}, u32[]{:S(2)}, u32[]{:S(2)}) collective-permute-start(f32[288,128]{1,0:T(8,128)S(1)} %get-tuple-element.63.refs_0_.refs_8_), channel_id=1, source_target_pairs={{0,4},{4,0},{8,12},{12,8},{16,20},{20,16},{24,28},{28,24},{1,5},{5... | collective-permute-start | bytes 442376 | tf_op jit(solution)/shard_map/ppermute | solution.py:816
  66.5 1.4 %collective-permute-start.23 = (f32[288,128]{1,0:T(8,128)S(1)}, f32[288,128]{1,0:T(8,128)S(1)}, u32[]{:S(2)}, u32[]{:S(2)}) collective-permute-start(f32[288,128]{1,0:T(8,128)S(1)} %collective-permute-done.22.refs_4_), channel_id=1, source_target_pairs={{0,4},{4,0},{8,12},{12,8},{16,20},{20,16},{24,28},{28,24},{1,5},{5... | collective-permute-start | bytes 442376 | tf_op jit(solution)/shard_map/ppermute | solution.py:816
  66.5 1.6 %collective-permute-start.21 = (f32[288,128]{1,0:T(8,128)S(1)}, f32[288,128]{1,0:T(8,128)S(1)}, u32[]{:S(2)}, u32[]{:S(2)}) collective-permute-start(f32[288,128]{1,0:T(8,128)S(1)} %collective-permute-done.20.refs_2_), channel_id=1, source_target_pairs={{0,4},{4,0},{8,12},{12,8},{16,20},{20,16},{24,28},{28,24},{1,5},{5... | collective-permute-start | bytes 442376 | tf_op jit(solution)/shard_map/ppermute | solution.py:816
  67.0 1.4 %collective-permute-start.25 = (f32[288,128]{1,0:T(8,128)S(1)}, f32[288,128]{1,0:T(8,128)S(1)}, u32[]{:S(2)}, u32[]{:S(2)}) collective-permute-start(f32[288,128]{1,0:T(8,128)S(1)} %collective-permute-done.24.refs_6_), channel_id=1, source_target_pairs={{0,4},{4,0},{8,12},{12,8},{16,20},{20,16},{24,28},{28,24},{1,5},{5... | collective-permute-start | bytes 442376 | tf_op jit(solution)/shard_map/ppermute | solution.py:816
  72.0 7.2 %collective-permute-start.31 = (f32[152,128]{1,0:T(8,128)S(1)}, f32[152,128]{1,0:T(8,128)S(1)}, u32[]{:S(2)}, u32[]{:S(2)}) collective-permute-start(f32[152,128]{1,0:T(8,128)S(1)} %get-tuple-element.72.refs_0_), channel_id=1, source_target_pairs={{0,24},{4,28},{8,16},{12,20},{16,8},{20,12},{24,0},{28,4},{1,25},{... | collective-permute-start | bytes 233480 | tf_op jit(solution)/shard_map/ppermute | solution.py:812
  74.0 7.6 %collective-permute-start.29 = (f32[152,128]{1,0:T(8,128)S(1)}, f32[152,128]{1,0:T(8,128)S(1)}, u32[]{:S(2)}, u32[]{:S(2)}) collective-permute-start(f32[152,128]{1,0:T(8,128)S(1)} %get-tuple-element.72.refs_0_), channel_id=1, source_target_pairs={{0,16},{4,20},{8,24},{12,28},{16,0},{20,4},{24,8},{28,12},{1,17},{... | collective-permute-start | bytes 233480 | tf_op jit(solution)/shard_map/ppermute | solution.py:812
  74.0 7.6 %collective-permute-start.27 = (f32[152,128]{1,0:T(8,128)S(1)}, f32[152,128]{1,0:T(8,128)S(1)}, u32[]{:S(2)}, u32[]{:S(2)}) collective-permute-start(f32[152,128]{1,0:T(8,128)S(1)} %get-tuple-element.72.refs_0_), channel_id=1, source_target_pairs={{0,8},{4,12},{8,0},{12,4},{16,24},{20,28},{24,16},{28,20},{1,9},{5... | collective-permute-start | bytes 233480 | tf_op jit(solution)/shard_map/ppermute | solution.py:812
  76.4 5.6 %collective-permute-start.26 = (f32[152,128]{1,0:T(8,128)S(1)}, f32[152,128]{1,0:T(8,128)S(1)}, u32[]{:S(2)}, u32[]{:S(2)}) collective-permute-start(f32[152,128]{1,0:T(8,128)S(1)} %get-tuple-element.72.refs_0_), channel_id=1, source_target_pairs={{0,4},{4,0},{8,12},{12,8},{16,20},{20,16},{24,28},{28,24},{1,5},{5... | collective-permute-start | bytes 233480 | tf_op jit(solution)/shard_map/ppermute | solution.py:816
  79.1 2.9 %collective-permute-start.32 = (f32[152,128]{1,0:T(8,128)S(1)}, f32[152,128]{1,0:T(8,128)S(1)}, u32[]{:S(2)}, u32[]{:S(2)}) collective-permute-start(f32[152,128]{1,0:T(8,128)S(1)} %collective-permute-done.31.refs_6_), channel_id=1, source_target_pairs={{0,4},{4,0},{8,12},{12,8},{16,20},{20,16},{24,28},{28,24},{1,5},{5... | collective-permute-start | bytes 233480 | tf_op jit(solution)/shard_map/ppermute | solution.py:816
  81.5 1.3 %collective-permute-start.30 = (f32[152,128]{1,0:T(8,128)S(1)}, f32[152,128]{1,0:T(8,128)S(1)}, u32[]{:S(2)}, u32[]{:S(2)}) collective-permute-start(f32[152,128]{1,0:T(8,128)S(1)} %collective-permute-done.29.refs_4_), channel_id=1, source_target_pairs={{0,4},{4,0},{8,12},{12,8},{16,20},{20,16},{24,28},{28,24},{1,5},{5... | collective-permute-start | bytes 233480 | tf_op jit(solution)/shard_map/ppermute | solution.py:816
  81.6 1.4 %collective-permute-start.28 = (f32[152,128]{1,0:T(8,128)S(1)}, f32[152,128]{1,0:T(8,128)S(1)}, u32[]{:S(2)}, u32[]{:S(2)}) collective-permute-start(f32[152,128]{1,0:T(8,128)S(1)} %collective-permute-done.27.refs_2_), channel_id=1, source_target_pairs={{0,4},{4,0},{8,12},{12,8},{16,20},{20,16},{24,28},{28,24},{1,5},{5... | collective-permute-start | bytes 233480 | tf_op jit(solution)/shard_map/ppermute | solution.py:816

commit v6 on v5

--- a/solution.py
+++ b/solution.py
@@ -16,6 +16,7 @@
 POINTS = 36
 BLOCKS = 8
 SIDE = 48
+SENT = 40
 NODES = 2304
 CENTRE = 9.0
 SPREAD = 9.0
@@ -308,13 +309,17 @@
 
 
 def line_rows(modes):
-    return 3 * SIDE if is_packed(modes) else 4 * SIDE
+    return 3 * SENT if is_packed(modes) else 4 * SENT
+
+
+def first_points(last_points):
+    return jnp.where(ex_ids() > 0, pltpu.roll(last_points, 1, 0), 0.0)
 
 
 def write_lines(ref, lines_ref, base, modes):
     values = []
     for side in range(4):
-        values += read_line(ref, side)
+        values += read_line(ref, side)[1:]
     for at, value in enumerate(pack_lanes(values, modes)):
         lines_ref[pl.ds(base + at * 8, 8), :] = value
 
@@ -322,7 +327,8 @@
 def load_lines(lines_ref, modes):
     count = line_rows(modes) // 8
     values = unpack_lanes([lines_ref[pl.ds(at * 8, 8), :] for at in range(count)], modes)
-    return [values[side * 6 : side * 6 + 6] for side in range(4)]
+    sides = [values[side * 5 : side * 5 + 5] for side in range(4)]
+    return [[first_points(side[4])] + side for side in sides]
 
 
 def add_lines(ref, lines):
@@ -346,11 +352,14 @@
     def copy_side(side, load):
         there = jnp.maximum(side_ref[0, side], 0)
 
+        def fill(place, values):
+            for i, value in enumerate([first_points(values[4])] + values):
+                sides[side, pl.ds(place * SIDE + i * 8, 8), :] = value
+
         def plain():
             for place in range(sets):
-                for i in range(6):
-                    at = pl.multiple_of(place * step + there * SIDE + i * 8, 8)
-                    sides[side, pl.ds(place * SIDE + i * 8, 8), :] = load(at)
+                first = place * step + there * SENT
+                fill(place, [load(pl.multiple_of(first + i * 8, 8)) for i in range(5)])
 
         if not is_packed(modes):
             plain()
@@ -360,9 +369,12 @@
         @pl.when(there == 3)
         def _():
             for place in range(sets):
-                for i in range(6):
-                    pieces = [load(place * step + comp * SIDE + i * 8) for comp in range(3)]
-                    sides[side, pl.ds(place * SIDE + i * 8, 8), :] = unpack_last(pieces, modes)
+                first = place * step
+                values = []
+                for i in range(5):
+                    pieces = [load(first + comp * SENT + i * 8) for comp in range(3)]
+                    values.append(unpack_last(pieces, modes))
+                fill(place, values)
 
     def body(side, carry):
         part = partner_ref[0, side]
@@ -721,7 +733,7 @@
 def last_kernel(slots, ids_ref, partner_ref, side_ref, flip_ref, *refs):
     gath_refs = refs[:slots]
     turned = refs[slots : slots + 5]
-    scatter_ref, sol_ref, res_ref, lines, sides = refs[slots + 5 :]
+    scatter_ref, sol_out, res_out, lines, sides, sol_ref, res_ref, sems = refs[slots + 5 :]
     modes = sol_ref.shape[1]
     used = 3 * modes
     where = pl.ds(line_rows(modes), SUM_ROWS)
@@ -757,6 +769,7 @@
             lines[pl.ds(side * SIDE + i * 8, 8), :] = incoming[side][i] * on_a3
     high, low = halves(jnp.transpose(lines[...])[:used])
     added = dot(jnp.concatenate([high, low], axis=0), scatter_ref[...], ((1,), (0,)))
+    copies = []
     for comp in range(3):
         for first in range(0, modes, 8):
             at = comp * modes + first
@@ -770,6 +783,13 @@
                 + (scale[6] * rows[2] + scale[7] * rows[3])
                 + (scale[8] * rows[4] + (added[at : at + 8] + added[used + at : used + at + 8]))
             )
+        for place, (buffer, out) in enumerate(((sol_ref, sol_out), (res_ref, res_out))):
+            copies.append(
+                pltpu.make_async_copy(buffer.at[comp], out.at[comp], sems.at[2 * comp + place])
+            )
+            copies[-1].start()
+    for copy in copies:
+        copy.wait()
 
 
 def call(kernel, name, out_shapes, args, scratch, scalars=0, keep=True, aliases=None, outside=False):
@@ -781,7 +801,7 @@
         name=name,
         out_shape=[pltpu.VMEM(one.shape, one.dtype) if keep else one for one in shapes],
         in_specs=[smem] * scalars + [pl.BlockSpec(memory_space=pltpu.HBM) if outside else vmem] * (len(args) - scalars),
-        out_specs=[vmem] * len(out_shapes),
+        out_specs=[vmem if keep else pl.BlockSpec(memory_space=pltpu.HBM)] * len(out_shapes),
         scratch_shapes=[pltpu.VMEM(one, F32) if isinstance(one, tuple) else one for one in scratch],
         input_output_aliases=aliases or {},
         compiler_params=pltpu.CompilerParams(vmem_limit_bytes=VMEM_LIMIT),
@@ -913,7 +933,13 @@
         "last",
         [velocity.shape, velocity.shape],
         (*tables, *gathered, t0, t1, t2, t3, ta, scatter),
-        [(4 * SIDE, LANES), (4, SIDE, LANES)],
+        [
+            (4 * SIDE, LANES),
+            (4, SIDE, LANES),
+            velocity.shape,
+            velocity.shape,
+            pltpu.SemaphoreType.DMA((6,)),
+        ],
         scalars=4,
         keep=False,
     )

time: 86.1 us -> 82.1 us (0.954)
  waiting for transfers between devices: 26.5 us -> 22.4 us
    ppermute x9, waiting for transfers between devices: 18.5 us -> 14.5 us  [share_lines(): lax.ppermute(lines, 'dom', [(i, i ^ slot) for i in range(parts)])]
  transfers between devices with their start and end apart: 33 -> 33, of which waited for: 16 -> 15; matrix products, arithmetic and copies ran while one was open for 0% -> 0% of each run, Pallas kernels for 12% -> 13%
where the time goes in v6:
time: 82.1 us; the launch traced here: 81.9 us
  starting transfers between devices  32.7 us (40%)
  Pallas kernels  25.7 us (31%)
  waiting for transfers between devices  22.4 us (27%)
  between operations  0.96 us (1%)
    pallas_call x10, Pallas kernels, call(): pl.pallas_call(kernel, name=name, out_shape=[pltpu.VMEM(one.shape, one.dt...  25.7 us
    ppermute x12, starting transfers between devices, swap_blocks(): lax.ppermute(blocks[place], 'four', [(i, i ^ offset_of(place, size)) for...  16.8 us
    ppermute x9, waiting for transfers between devices, share_lines(): lax.ppermute(lines, 'dom', [(i, i ^ slot) for i in range(parts)])  14.5 us
    ppermute x9, starting transfers between devices, share_lines(): lax.ppermute(lines, 'dom', [(i, i ^ slot) for i in range(parts)])  13.7 us
    ppermute x12, waiting for transfers between devices, swap_blocks(): lax.ppermute(blocks[place], 'four', [(i, i ^ offset_of(place, size)) for...  4.67 us
    ppermute x12, waiting for transfers between devices, share_lines(): lax.ppermute(slots[slot], 'dom', [(i, i ^ 1) for i in range(parts)])  3.23 us
    ppermute x12, starting transfers between devices, share_lines(): lax.ppermute(slots[slot], 'dom', [(i, i ^ 1) for i in range(parts)])  2.12 us
  transfers between devices with their start and end apart: 33, of which 15 were waited for; matrix products, arithmetic and copies ran while one was open for 0% of the time, Pallas kernels for 13%

profile of v6, /device:TPU:0, one launch (start us, length us, event | category | flops | bytes accessed | tf_op | source)
XLA Modules:
  0.0 81.9 jit_solution(8828722950060321477)
XLA Ops:
  0.6 0.0 copy-start.2
  0.6 0.0 copy-start.3
  0.7 0.0 copy-start
  0.7 0.0 copy-start.1
  0.7 0.1 pad_add_fusion.ids_ref
  0.8 2.3 %pack.2 = (f32[216,128]{1,0:T(8,128)S(1)}, f32[216,128]{1,0:T(8,128)S(1)}, f32[216,128]{1,0:T(8,128)S(1)}, f32[216,128]{1,0:T(8,128)S(1)}, f32[3,32,2304]{2,1,0:T(8,128)S(1)}) custom-call(s32[2]{0:T(128)S(1)} %pad_add_fusion.ids_ref, f32[3,32,2304]{2,1,0:T(8,128)} %velocity_ref.1), custom_call_target="tpu_custom_call" | custom-call | tf_op jit(solution)/shard_map/pack/pallas_call | solution.py:799
  3.1 4.0 %collective-permute-start = (f32[216,128]{1,0:T(8,128)S(1)}, f32[216,128]{1,0:T(8,128)S(1)}, u32[]{:S(2)}, u32[]{:S(2)}) collective-permute-start(f32[216,128]{1,0:T(8,128)S(1)} %get-tuple-element.45), channel_id=1, source_target_pairs={{0,3},{1,2},{2,1},{3,0},{4,7},{5,6},{6,5},{7,4},{8,11},{9,10},{10,... | collective-permute-start | bytes 331784 | tf_op jit(solution)/shard_map/ppermute | solution.py:822
  7.1 0.5 collective-permute-start.1
  7.6 0.1 collective-permute-start.2
  7.7 1.2 %pack.3 = (f32[216,128]{1,0:T(8,128)S(1)}, f32[216,128]{1,0:T(8,128)S(1)}, f32[216,128]{1,0:T(8,128)S(1)}, f32[216,128]{1,0:T(8,128)S(1)}) custom-call(s32[2]{0:T(128)S(1)} %pad_add_fusion.ids_ref, f32[3,32,2304]{2,1,0:T(8,128)S(1)} %get-tuple-element.52.velocity_ref), custom_call_target="tpu_custom_call" | custom-call | tf_op jit(solution)/shard_map/pack/pallas_call | solution.py:799
  8.9 2.9 %collective-permute-start.6 = (f32[216,128]{1,0:T(8,128)S(1)}, f32[216,128]{1,0:T(8,128)S(1)}, u32[]{:S(2)}, u32[]{:S(2)}) collective-permute-start(f32[216,128]{1,0:T(8,128)S(1)} %get-tuple-element.54), channel_id=1, source_target_pairs={{0,3},{1,2},{2,1},{3,0},{4,7},{5,6},{6,5},{7,4},{8,11},{9,10},{10,... | collective-permute-start | bytes 331784 | tf_op jit(solution)/shard_map/ppermute | solution.py:822
  11.8 0.5 collective-permute-start.7
  12.3 0.7 collective-permute-start.8
  13.0 0.6 collective-permute-done.1.refs_2_
  13.5 0.0 collective-permute-done.2.refs_3_
  13.6 0.0 copy-start.4
  13.6 2.4 %products.2 = (f32[216,128]{1,0:T(8,128)S(1)}, f32[216,128]{1,0:T(8,128)S(1)}, f32[216,128]{1,0:T(8,128)S(1)}, f32[216,128]{1,0:T(8,128)S(1)}) custom-call(s32[2]{0:T(128)S(1)} %pad_add_fusion.ids_ref, f32[216,128]{1,0:T(8,128)S(1)} %get-tuple-element.44.refs_0_, f32[216,128]{1,0:T(8,128)S(1)} %collective-permute-done.refs_1_, ...), custom_call_target="tpu_custom_call" | custom-call | tf_op jit(solution)/shard_map/products/pallas_call | solution.py:799
  16.0 0.0 copy-start.5
  16.0 0.0 copy-start.6
  16.0 3.9 %collective-permute-start.3 = (f32[216,128]{1,0:T(8,128)S(1)}, f32[216,128]{1,0:T(8,128)S(1)}, u32[]{:S(2)}, u32[]{:S(2)}) collective-permute-start(f32[216,128]{1,0:T(8,128)S(1)} %get-tuple-element.49), channel_id=1, source_target_pairs={{0,3},{1,2},{2,1},{3,0},{4,7},{5,6},{6,5},{7,4},{8,11},{9,10},{10,... | collective-permute-start | bytes 331784 | tf_op jit(solution)/shard_map/ppermute | solution.py:822
  20.0 0.0 collective-permute-start.4
  20.0 0.0 collective-permute-done.6.refs_1_
  20.0 0.6 collective-permute-start.5
  20.6 0.0 collective-permute-done.7.refs_2_
  20.6 0.0 collective-permute-done.8.refs_3_
  20.6 2.4 %products.3 = (f32[216,128]{1,0:T(8,128)S(1)}, f32[216,128]{1,0:T(8,128)S(1)}, f32[216,128]{1,0:T(8,128)S(1)}, f32[216,128]{1,0:T(8,128)S(1)}) custom-call(s32[2]{0:T(128)S(1)} %pad_add_fusion.ids_ref, f32[216,128]{1,0:T(8,128)S(1)} %get-tuple-element.53.refs_0_, f32[216,128]{1,0:T(8,128)S(1)} %collective-permute-done.6.refs_1_, ...), custom_call_target="tpu_custom_call" | custom-call | tf_op jit(solution)/shard_map/products/pallas_call | solution.py:799
  23.1 2.9 %collective-permute-start.9 = (f32[216,128]{1,0:T(8,128)S(1)}, f32[216,128]{1,0:T(8,128)S(1)}, u32[]{:S(2)}, u32[]{:S(2)}) collective-permute-start(f32[216,128]{1,0:T(8,128)S(1)} %get-tuple-element.58), channel_id=1, source_target_pairs={{0,3},{1,2},{2,1},{3,0},{4,7},{5,6},{6,5},{7,4},{8,11},{9,10},{10,... | collective-permute-start | bytes 331784 | tf_op jit(solution)/shard_map/ppermute | solution.py:822
  26.0 0.0 collective-permute-start.10
  26.0 0.0 collective-permute-done.3.refs_1_
  26.0 0.6 collective-permute-start.11
  26.6 0.0 collective-permute-done.4.refs_2_
  26.6 2.1 %collective-permute-done.9.refs_5_ = f32[216,128]{1,0:T(8,128)S(1)} collective-permute-done((f32[216,128]{1,0:T(8,128)S(1)}, f32[216,128]{1,0:T(8,128)S(1)}, u32[]{:S(2)}, u32[]{:S(2)}) %collective-permute-start.9) | collective-permute-done | bytes 110624 | tf_op jit(solution)/shard_map/ppermute | solution.py:822
  28.8 2.0 %collective-permute-done.10.refs_6_ = f32[216,128]{1,0:T(8,128)S(1)} collective-permute-done((f32[216,128]{1,0:T(8,128)S(1)}, f32[216,128]{1,0:T(8,128)S(1)}, u32[]{:S(2)}, u32[]{:S(2)}) %collective-permute-start.10) | collective-permute-done | bytes 110624 | tf_op jit(solution)/shard_map/ppermute | solution.py:822
  30.7 0.0 collective-permute-done.11.refs_7_
  30.7 2.1 %first.1 = (f32[2304,128]{1,0:T(8,128)S(1)}, f32[240,128]{1,0:T(8,128)S(1)}) custom-call(s32[2]{0:T(128)S(1)} %pad_add_fusion.ids_ref, s32[1,4]{1,0:T(1,128)S(1)} %copy-done.4, f32[216,128]{1,0:T(8,128)S(1)} %get-tuple-element.48.refs_0_, f32[216,128]{1,0:T(8,128)S(1)} %collective-permute-done.3.refs_1_, f32[216,128]{1,0:T(8,128)S(1)} %collective-permute-done.4.refs_2_, ...), custom_call_target="tpu_custom_call" | custom-call | tf_op jit(solution)/shard_map/first/pallas_call | solution.py:799
  32.8 4.2 %collective-permute-start.17 = (f32[240,128]{1,0:T(8,128)S(1)}, f32[240,128]{1,0:T(8,128)S(1)}, u32[]{:S(2)}, u32[]{:S(2)}) collective-permute-start(f32[240,128]{1,0:T(8,128)S(1)} %get-tuple-element.61.refs_0_.refs_8_), channel_id=1, source_target_pairs={{0,24},{4,28},{8,16},{12,20},{16,8},{20,12},{24,0},{28,4},{1,25},{... | collective-permute-start | bytes 368648 | tf_op jit(solution)/shard_map/ppermute | solution.py:832
  37.0 0.6 collective-permute-start.13
  37.7 2.4 %collective-permute-done.17.refs_6_ = f32[240,128]{1,0:T(8,128)S(1)} collective-permute-done((f32[240,128]{1,0:T(8,128)S(1)}, f32[240,128]{1,0:T(8,128)S(1)}, u32[]{:S(2)}, u32[]{:S(2)}) %collective-permute-start.17) | collective-permute-done | bytes 122912 | tf_op jit(solution)/shard_map/ppermute | solution.py:832
  40.1 3.4 %collective-permute-done.15.refs_4_ = f32[240,128]{1,0:T(8,128)S(1)} collective-permute-done((f32[240,128]{1,0:T(8,128)S(1)}, f32[240,128]{1,0:T(8,128)S(1)}, u32[]{:S(2)}, u32[]{:S(2)}) %collective-permute-start.15) | collective-permute-done | bytes 122912 | tf_op jit(solution)/shard_map/ppermute | solution.py:832
  43.5 0.5 collective-permute-start.14
  44.0 0.8 collective-permute-done.16.refs_5_
  44.8 0.2 collective-permute-done.14.refs_3_
  45.0 4.5 %second.1 = (f32[2304,128]{1,0:T(8,128)S(1)}, f32[2304,128]{1,0:T(8,128)S(1)}, f32[2304,128]{1,0:T(8,128)S(1)}, f32[240,128]{1,0:T(8,128)S(1)}, f32[8,128]{1,0:T(8,128)S(1)}) custom-call(s32[2]{0:T(128)S(1)} %pad_add_fusion.ids_ref, s32[1,4]{1,0:T(1,128)S(1)} %copy-done.4, s32[1,4]{1,0:T(1,128)S(1)} %copy-done.5, ...), custom_call_target="tpu_custom_call", output_to_operand_aliasing={{0}: (13, {})} | custom-call | tf_op jit(solution)/shard_map/second/pallas_call | solution.py:799
  49.4 2.6 %collective-permute-start.24 = (f32[240,128]{1,0:T(8,128)S(1)}, f32[240,128]{1,0:T(8,128)S(1)}, u32[]{:S(2)}, u32[]{:S(2)}) collective-permute-start(f32[240,128]{1,0:T(8,128)S(1)} %get-tuple-element.63.refs_0_.refs_8_), channel_id=1, source_target_pairs={{0,24},{4,28},{8,16},{12,20},{16,8},{20,12},{24,0},{28,4},{1,25},{... | collective-permute-start | bytes 368648 | tf_op jit(solution)/shard_map/ppermute | solution.py:832
  52.1 1.8 %collective-permute-start.20 = (f32[240,128]{1,0:T(8,128)S(1)}, f32[240,128]{1,0:T(8,128)S(1)}, u32[]{:S(2)}, u32[]{:S(2)}) collective-permute-start(f32[240,128]{1,0:T(8,128)S(1)} %get-tuple-element.63.refs_0_.refs_8_), channel_id=1, source_target_pairs={{0,8},{4,12},{8,0},{12,4},{16,24},{20,28},{24,16},{28,20},{1,9},{5... | collective-permute-start | bytes 368648 | tf_op jit(solution)/shard_map/ppermute | solution.py:832
  53.9 2.0 %turn.2 = (f32[96,2304]{1,0:T(8,128)S(1)}, f32[96,2304]{1,0:T(8,128)S(1)}, bf16[192,2304]{1,0:T(8,128)(2,1)S(1)}) custom-call(f32[2304,128]{1,0:T(8,128)S(1)} %get-tuple-element.64.refs_0_, f32[2304,128]{1,0:T(8,128)S(1)} %get-tuple-element.65.refs_1_.refs_9_), custom_call_target="tpu_custom_call" | custom-call | tf_op jit(solution)/shard_map/turn/pallas_call | solution.py:799
  55.9 1.6 %collective-permute-done.24.refs_6_ = f32[240,128]{1,0:T(8,128)S(1)} collective-permute-done((f32[240,128]{1,0:T(8,128)S(1)}, f32[240,128]{1,0:T(8,128)S(1)}, u32[]{:S(2)}, u32[]{:S(2)}) %collective-permute-start.24) | collective-permute-done | bytes 122912 | tf_op jit(solution)/shard_map/ppermute | solution.py:832
  57.6 5.7 %collective-permute-done.22.refs_4_ = f32[240,128]{1,0:T(8,128)S(1)} collective-permute-done((f32[240,128]{1,0:T(8,128)S(1)}, f32[240,128]{1,0:T(8,128)S(1)}, u32[]{:S(2)}, u32[]{:S(2)}) %collective-permute-start.22) | collective-permute-done | bytes 122912 | tf_op jit(solution)/shard_map/ppermute | solution.py:832
  63.2 0.5 collective-permute-start.21
  63.8 0.0 collective-permute-start.25
  63.8 0.8 collective-permute-done.23.refs_5_
  64.6 0.2 collective-permute-done.21.refs_3_
  64.8 0.3 collective-permute-done.25.refs_7_
  65.1 3.5 %third.1 = (f32[2304,128]{1,0:T(8,128)S(1)}, f32[2304,128]{1,0:T(8,128)S(1)}, f32[2304,128]{1,0:T(8,128)S(1)}, f32[128,128]{1,0:T(8,128)S(1)}) custom-call(s32[2]{0:T(128)S(1)} %pad_add_fusion.ids_ref, s32[1,4]{1,0:T(1,128)S(1)} %copy-done.4, s32[1,4]{1,0:T(1,128)S(1)} %copy-done.5, s32[1,4]{1,0:T(1,128)S(1)} %copy-done.6, ...), custom_call_target="tpu_custom_call", output_to_operand_aliasing={{0}: (15, {})} | custom-call | tf_op jit(solution)/shard_map/third/pallas_call | solution.py:799
  68.6 1.8 %collective-permute-start.31 = (f32[128,128]{1,0:T(8,128)S(1)}, f32[128,128]{1,0:T(8,128)S(1)}, u32[]{:S(2)}, u32[]{:S(2)}) collective-permute-start(f32[128,128]{1,0:T(8,128)S(1)} %get-tuple-element.72.refs_0_), channel_id=1, source_target_pairs={{0,24},{4,28},{8,16},{12,20},{16,8},{20,12},{24,0},{28,4},{1,25},{... | collective-permute-start | bytes 196616 | tf_op jit(solution)/shard_map/ppermute | solution.py:832
  70.4 2.6 %collective-permute-start.27 = (f32[128,128]{1,0:T(8,128)S(1)}, f32[128,128]{1,0:T(8,128)S(1)}, u32[]{:S(2)}, u32[]{:S(2)}) collective-permute-start(f32[128,128]{1,0:T(8,128)S(1)} %get-tuple-element.72.refs_0_), channel_id=1, source_target_pairs={{0,8},{4,12},{8,0},{12,4},{16,24},{20,28},{24,16},{28,20},{1,9},{5... | collective-permute-start | bytes 196616 | tf_op jit(solution)/shard_map/ppermute | solution.py:832
  73.0 2.5 %turn.3 = (f32[96,2304]{1,0:T(8,128)S(1)}, f32[96,2304]{1,0:T(8,128)S(1)}, f32[96,2304]{1,0:T(8,128)S(1)}) custom-call(f32[2304,128]{1,0:T(8,128)S(1)} %get-tuple-element.73.refs_0_, f32[2304,128]{1,0:T(8,128)S(1)} %get-tuple-element.74.refs_1_, f32[2304,128]{1,0:T(8,128)S(1)} %get-tuple-element.75.refs_2_), custom_call_target="tpu_custom_call" | custom-call | tf_op jit(solution)/shard_map/turn/pallas_call | solution.py:799
  75.5 0.6 collective-permute-start.32
  76.1 1.4 %collective-permute-done.29.refs_4_ = f32[128,128]{1,0:T(8,128)S(1)} collective-permute-done((f32[128,128]{1,0:T(8,128)S(1)}, f32[128,128]{1,0:T(8,128)S(1)}, u32[]{:S(2)}, u32[]{:S(2)}) %collective-permute-start.29) | collective-permute-done | bytes 65568 | tf_op jit(solution)/shard_map/ppermute | solution.py:832
  77.5 0.0 collective-permute-start.30
  77.5 0.5 collective-permute-start.28
  78.0 0.7 collective-permute-done.30.refs_5_
  78.8 0.2 collective-permute-done.28.refs_3_
  78.9 2.8 %last.1 = (f32[3,32,2304]{2,1,0:T(8,128)}, f32[3,32,2304]{2,1,0:T(8,128)}) custom-call(s32[2]{0:T(128)S(1)} %pad_add_fusion.ids_ref, s32[1,4]{1,0:T(1,128)S(1)} %copy-done.4, s32[1,4]{1,0:T(1,128)S(1)} %copy-done.5, s32[1,4]{1,0:T(1,128)S(1)} %copy-done.6, f32[128,128]{1,0:T(8,128)S(1)} %get-tuple-element.72.refs_0_, ...), custom_call_target="tpu_custom_call" | custom-call | tf_op jit(solution)/shard_map/last/pallas_call | solution.py:799
  (27 shorter events, 0.1 us)
Async XLA Ops:
  0.6 12.9 %copy-start.2 = (bf16[256,128]{1,0:T(8,128)(2,1)S(1)}, bf16[256,128]{1,0:T(8,128)(2,1)}, u32[]{:S(2)}) copy-start(bf16[256,128]{1,0:T(8,128)(2,1)} %constant.20.clone.refs_7_) | copy-start | bytes 196612
  0.6 12.9 %copy-start.3 = (bf16[256,128]{1,0:T(8,128)(2,1)S(1)}, bf16[256,128]{1,0:T(8,128)(2,1)}, u32[]{:S(2)}) copy-start(bf16[256,128]{1,0:T(8,128)(2,1)} %constant.19.clone.refs_6_) | copy-start | bytes 196612
  0.7 12.9 %copy-start = (bf16[512,384]{1,0:T(8,128)(2,1)S(1)}, bf16[512,384]{1,0:T(8,128)(2,1)}, u32[]{:S(2)}) copy-start(bf16[512,384]{1,0:T(8,128)(2,1)} %constant.18.clone.refs_5_) | copy-start | bytes 1179652
  0.7 12.9 %copy-start.1 = (bf16[512,384]{1,0:T(8,128)(2,1)S(1)}, bf16[512,384]{1,0:T(8,128)(2,1)}, u32[]{:S(2)}) copy-start(bf16[512,384]{1,0:T(8,128)(2,1)} %constant.17.clone.refs_4_) | copy-start | bytes 1179652
  3.1 9.2 %collective-permute-start = (f32[216,128]{1,0:T(8,128)S(1)}, f32[216,128]{1,0:T(8,128)S(1)}, u32[]{:S(2)}, u32[]{:S(2)}) collective-permute-start(f32[216,128]{1,0:T(8,128)S(1)} %get-tuple-element.45), channel_id=1, source_target_pairs={{0,3},{1,2},{2,1},{3,0},{4,7},{5,6},{6,5},{7,4},{8,11},{9,10},{10,... | collective-permute-start | bytes 331784 | tf_op jit(solution)/shard_map/ppermute | solution.py:822
  7.1 6.5 %collective-permute-start.1 = (f32[216,128]{1,0:T(8,128)S(1)}, f32[216,128]{1,0:T(8,128)S(1)}, u32[]{:S(2)}, u32[]{:S(2)}) collective-permute-start(f32[216,128]{1,0:T(8,128)S(1)} %get-tuple-element.46), channel_id=1, source_target_pairs={{0,1},{1,0},{2,3},{3,2},{4,5},{5,4},{6,7},{7,6},{8,9},{9,8},{10,11... | collective-permute-start | bytes 331784 | tf_op jit(solution)/shard_map/ppermute | solution.py:822
  7.6 5.9 %collective-permute-start.2 = (f32[216,128]{1,0:T(8,128)S(1)}, f32[216,128]{1,0:T(8,128)S(1)}, u32[]{:S(2)}, u32[]{:S(2)}) collective-permute-start(f32[216,128]{1,0:T(8,128)S(1)} %get-tuple-element.47), channel_id=1, source_target_pairs={{0,2},{1,3},{2,0},{3,1},{4,6},{5,7},{6,4},{7,5},{8,10},{9,11},{10,... | collective-permute-start | bytes 331784 | tf_op jit(solution)/shard_map/ppermute | solution.py:822
  8.9 11.1 %collective-permute-start.6 = (f32[216,128]{1,0:T(8,128)S(1)}, f32[216,128]{1,0:T(8,128)S(1)}, u32[]{:S(2)}, u32[]{:S(2)}) collective-permute-start(f32[216,128]{1,0:T(8,128)S(1)} %get-tuple-element.54), channel_id=1, source_target_pairs={{0,3},{1,2},{2,1},{3,0},{4,7},{5,6},{6,5},{7,4},{8,11},{9,10},{10,... | collective-permute-start | bytes 331784 | tf_op jit(solution)/shard_map/ppermute | solution.py:822
  11.8 8.8 %collective-permute-start.7 = (f32[216,128]{1,0:T(8,128)S(1)}, f32[216,128]{1,0:T(8,128)S(1)}, u32[]{:S(2)}, u32[]{:S(2)}) collective-permute-start(f32[216,128]{1,0:T(8,128)S(1)} %get-tuple-element.55), channel_id=1, source_target_pairs={{0,1},{1,0},{2,3},{3,2},{4,5},{5,4},{6,7},{7,6},{8,9},{9,8},{10,11... | collective-permute-start | bytes 331784 | tf_op jit(solution)/shard_map/ppermute | solution.py:822
  12.3 8.3 %collective-permute-start.8 = (f32[216,128]{1,0:T(8,128)S(1)}, f32[216,128]{1,0:T(8,128)S(1)}, u32[]{:S(2)}, u32[]{:S(2)}) collective-permute-start(f32[216,128]{1,0:T(8,128)S(1)} %get-tuple-element.56), channel_id=1, source_target_pairs={{0,2},{1,3},{2,0},{3,1},{4,6},{5,7},{6,4},{7,5},{8,10},{9,11},{10,... | collective-permute-start | bytes 331784 | tf_op jit(solution)/shard_map/ppermute | solution.py:822
  13.6 17.2 %copy-start.4 = (s32[1,4]{1,0:T(1,128)S(1)}, s32[1,4]{1,0:T(1,128)}, u32[]{:S(2)}) copy-start(s32[1,4]{1,0:T(1,128)} %partner_ref.7) | copy-start | bytes 52
  16.0 29.0 %copy-start.5 = (s32[1,4]{1,0:T(1,128)S(1)}, s32[1,4]{1,0:T(1,128)}, u32[]{:S(2)}) copy-start(s32[1,4]{1,0:T(1,128)} %side_ref.5) | copy-start | bytes 52
  16.0 29.0 %copy-start.6 = (s32[1,4]{1,0:T(1,128)S(1)}, s32[1,4]{1,0:T(1,128)}, u32[]{:S(2)}) copy-start(s32[1,4]{1,0:T(1,128)} %flip_ref.5) | copy-start | bytes 52
  16.0 10.0 %collective-permute-start.3 = (f32[216,128]{1,0:T(8,128)S(1)}, f32[216,128]{1,0:T(8,128)S(1)}, u32[]{:S(2)}, u32[]{:S(2)}) collective-permute-start(f32[216,128]{1,0:T(8,128)S(1)} %get-tuple-element.49), channel_id=1, source_target_pairs={{0,3},{1,2},{2,1},{3,0},{4,7},{5,6},{6,5},{7,4},{8,11},{9,10},{10,... | collective-permute-start | bytes 331784 | tf_op jit(solution)/shard_map/ppermute | solution.py:822
  20.0 6.6 %collective-permute-start.4 = (f32[216,128]{1,0:T(8,128)S(1)}, f32[216,128]{1,0:T(8,128)S(1)}, u32[]{:S(2)}, u32[]{:S(2)}) collective-permute-start(f32[216,128]{1,0:T(8,128)S(1)} %get-tuple-element.50), channel_id=1, source_target_pairs={{0,1},{1,0},{2,3},{3,2},{4,5},{5,4},{6,7},{7,6},{8,9},{9,8},{10,11... | collective-permute-start | bytes 331784 | tf_op jit(solution)/shard_map/ppermute | solution.py:822
  20.0 6.6 %collective-permute-start.5 = (f32[216,128]{1,0:T(8,128)S(1)}, f32[216,128]{1,0:T(8,128)S(1)}, u32[]{:S(2)}, u32[]{:S(2)}) collective-permute-start(f32[216,128]{1,0:T(8,128)S(1)} %get-tuple-element.51), channel_id=1, source_target_pairs={{0,2},{1,3},{2,0},{3,1},{4,6},{5,7},{6,4},{7,5},{8,10},{9,11},{10,... | collective-permute-start | bytes 331784 | tf_op jit(solution)/shard_map/ppermute | solution.py:822
  23.1 5.7 %collective-permute-start.9 = (f32[216,128]{1,0:T(8,128)S(1)}, f32[216,128]{1,0:T(8,128)S(1)}, u32[]{:S(2)}, u32[]{:S(2)}) collective-permute-start(f32[216,128]{1,0:T(8,128)S(1)} %get-tuple-element.58), channel_id=1, source_target_pairs={{0,3},{1,2},{2,1},{3,0},{4,7},{5,6},{6,5},{7,4},{8,11},{9,10},{10,... | collective-permute-start | bytes 331784 | tf_op jit(solution)/shard_map/ppermute | solution.py:822
  26.0 4.7 %collective-permute-start.10 = (f32[216,128]{1,0:T(8,128)S(1)}, f32[216,128]{1,0:T(8,128)S(1)}, u32[]{:S(2)}, u32[]{:S(2)}) collective-permute-start(f32[216,128]{1,0:T(8,128)S(1)} %get-tuple-element.59), channel_id=1, source_target_pairs={{0,1},{1,0},{2,3},{3,2},{4,5},{5,4},{6,7},{7,6},{8,9},{9,8},{10,11... | collective-permute-start | bytes 331784 | tf_op jit(solution)/shard_map/ppermute | solution.py:822
  26.0 4.7 %collective-permute-start.11 = (f32[216,128]{1,0:T(8,128)S(1)}, f32[216,128]{1,0:T(8,128)S(1)}, u32[]{:S(2)}, u32[]{:S(2)}) collective-permute-start(f32[216,128]{1,0:T(8,128)S(1)} %get-tuple-element.60), channel_id=1, source_target_pairs={{0,2},{1,3},{2,0},{3,1},{4,6},{5,7},{6,4},{7,5},{8,10},{9,11},{10,... | collective-permute-start | bytes 331784 | tf_op jit(solution)/shard_map/ppermute | solution.py:822
  32.8 7.2 %collective-permute-start.17 = (f32[240,128]{1,0:T(8,128)S(1)}, f32[240,128]{1,0:T(8,128)S(1)}, u32[]{:S(2)}, u32[]{:S(2)}) collective-permute-start(f32[240,128]{1,0:T(8,128)S(1)} %get-tuple-element.61.refs_0_.refs_8_), channel_id=1, source_target_pairs={{0,24},{4,28},{8,16},{12,20},{16,8},{20,12},{24,0},{28,4},{1,25},{... | collective-permute-start | bytes 368648 | tf_op jit(solution)/shard_map/ppermute | solution.py:832
  37.0 6.5 %collective-permute-start.15 = (f32[240,128]{1,0:T(8,128)S(1)}, f32[240,128]{1,0:T(8,128)S(1)}, u32[]{:S(2)}, u32[]{:S(2)}) collective-permute-start(f32[240,128]{1,0:T(8,128)S(1)} %get-tuple-element.61.refs_0_.refs_8_), channel_id=1, source_target_pairs={{0,16},{4,20},{8,24},{12,28},{16,0},{20,4},{24,8},{28,12},{1,17},{... | collective-permute-start | bytes 368648 | tf_op jit(solution)/shard_map/ppermute | solution.py:832
  37.0 6.5 %collective-permute-start.13 = (f32[240,128]{1,0:T(8,128)S(1)}, f32[240,128]{1,0:T(8,128)S(1)}, u32[]{:S(2)}, u32[]{:S(2)}) collective-permute-start(f32[240,128]{1,0:T(8,128)S(1)} %get-tuple-element.61.refs_0_.refs_8_), channel_id=1, source_target_pairs={{0,8},{4,12},{8,0},{12,4},{16,24},{20,28},{24,16},{28,20},{1,9},{5... | collective-permute-start | bytes 368648 | tf_op jit(solution)/shard_map/ppermute | solution.py:832
  37.7 6.3 %collective-permute-start.12 = (f32[240,128]{1,0:T(8,128)S(1)}, f32[240,128]{1,0:T(8,128)S(1)}, u32[]{:S(2)}, u32[]{:S(2)}) collective-permute-start(f32[240,128]{1,0:T(8,128)S(1)} %get-tuple-element.61.refs_0_.refs_8_), channel_id=1, source_target_pairs={{0,4},{4,0},{8,12},{12,8},{16,20},{20,16},{24,28},{28,24},{1,5},{5... | collective-permute-start | bytes 368648 | tf_op jit(solution)/shard_map/ppermute | solution.py:836
  40.1 3.9 %collective-permute-start.18 = (f32[240,128]{1,0:T(8,128)S(1)}, f32[240,128]{1,0:T(8,128)S(1)}, u32[]{:S(2)}, u32[]{:S(2)}) collective-permute-start(f32[240,128]{1,0:T(8,128)S(1)} %collective-permute-done.17.refs_6_), channel_id=1, source_target_pairs={{0,4},{4,0},{8,12},{12,8},{16,20},{20,16},{24,28},{28,24},{1,5},{5... | collective-permute-start | bytes 368648 | tf_op jit(solution)/shard_map/ppermute | solution.py:836
  43.5 1.3 %collective-permute-start.16 = (f32[240,128]{1,0:T(8,128)S(1)}, f32[240,128]{1,0:T(8,128)S(1)}, u32[]{:S(2)}, u32[]{:S(2)}) collective-permute-start(f32[240,128]{1,0:T(8,128)S(1)} %collective-permute-done.15.refs_4_), channel_id=1, source_target_pairs={{0,4},{4,0},{8,12},{12,8},{16,20},{20,16},{24,28},{28,24},{1,5},{5... | collective-permute-start | bytes 368648 | tf_op jit(solution)/shard_map/ppermute | solution.py:836
  43.5 1.5 %collective-permute-start.14 = (f32[240,128]{1,0:T(8,128)S(1)}, f32[240,128]{1,0:T(8,128)S(1)}, u32[]{:S(2)}, u32[]{:S(2)}) collective-permute-start(f32[240,128]{1,0:T(8,128)S(1)} %collective-permute-done.13.refs_2_), channel_id=1, source_target_pairs={{0,4},{4,0},{8,12},{12,8},{16,20},{20,16},{24,28},{28,24},{1,5},{5... | collective-permute-start | bytes 368648 | tf_op jit(solution)/shard_map/ppermute | solution.py:836
  49.4 8.1 %collective-permute-start.24 = (f32[240,128]{1,0:T(8,128)S(1)}, f32[240,128]{1,0:T(8,128)S(1)}, u32[]{:S(2)}, u32[]{:S(2)}) collective-permute-start(f32[240,128]{1,0:T(8,128)S(1)} %get-tuple-element.63.refs_0_.refs_8_), channel_id=1, source_target_pairs={{0,24},{4,28},{8,16},{12,20},{16,8},{20,12},{24,0},{28,4},{1,25},{... | collective-permute-start | bytes 368648 | tf_op jit(solution)/shard_map/ppermute | solution.py:832
  52.1 11.2 %collective-permute-start.22 = (f32[240,128]{1,0:T(8,128)S(1)}, f32[240,128]{1,0:T(8,128)S(1)}, u32[]{:S(2)}, u32[]{:S(2)}) collective-permute-start(f32[240,128]{1,0:T(8,128)S(1)} %get-tuple-element.63.refs_0_.refs_8_), channel_id=1, source_target_pairs={{0,16},{4,20},{8,24},{12,28},{16,0},{20,4},{24,8},{28,12},{1,17},{... | collective-permute-start | bytes 368648 | tf_op jit(solution)/shard_map/ppermute | solution.py:832
  52.1 11.2 %collective-permute-start.20 = (f32[240,128]{1,0:T(8,128)S(1)}, f32[240,128]{1,0:T(8,128)S(1)}, u32[]{:S(2)}, u32[]{:S(2)}) collective-permute-start(f32[240,128]{1,0:T(8,128)S(1)} %get-tuple-element.63.refs_0_.refs_8_), channel_id=1, source_target_pairs={{0,8},{4,12},{8,0},{12,4},{16,24},{20,28},{24,16},{28,20},{1,9},{5... | collective-permute-start | bytes 368648 | tf_op jit(solution)/shard_map/ppermute | solution.py:832
  53.9 9.9 %collective-permute-start.19 = (f32[240,128]{1,0:T(8,128)S(1)}, f32[240,128]{1,0:T(8,128)S(1)}, u32[]{:S(2)}, u32[]{:S(2)}) collective-permute-start(f32[240,128]{1,0:T(8,128)S(1)} %get-tuple-element.63.refs_0_.refs_8_), channel_id=1, source_target_pairs={{0,4},{4,0},{8,12},{12,8},{16,20},{20,16},{24,28},{28,24},{1,5},{5... | collective-permute-start | bytes 368648 | tf_op jit(solution)/shard_map/ppermute | solution.py:836
  63.2 1.3 %collective-permute-start.23 = (f32[240,128]{1,0:T(8,128)S(1)}, f32[240,128]{1,0:T(8,128)S(1)}, u32[]{:S(2)}, u32[]{:S(2)}) collective-permute-start(f32[240,128]{1,0:T(8,128)S(1)} %collective-permute-done.22.refs_4_), channel_id=1, source_target_pairs={{0,4},{4,0},{8,12},{12,8},{16,20},{20,16},{24,28},{28,24},{1,5},{5... | collective-permute-start | bytes 368648 | tf_op jit(solution)/shard_map/ppermute | solution.py:836
  63.2 1.5 %collective-permute-start.21 = (f32[240,128]{1,0:T(8,128)S(1)}, f32[240,128]{1,0:T(8,128)S(1)}, u32[]{:S(2)}, u32[]{:S(2)}) collective-permute-start(f32[240,128]{1,0:T(8,128)S(1)} %collective-permute-done.20.refs_2_), channel_id=1, source_target_pairs={{0,4},{4,0},{8,12},{12,8},{16,20},{20,16},{24,28},{28,24},{1,5},{5... | collective-permute-start | bytes 368648 | tf_op jit(solution)/shard_map/ppermute | solution.py:836
  63.8 1.3 %collective-permute-start.25 = (f32[240,128]{1,0:T(8,128)S(1)}, f32[240,128]{1,0:T(8,128)S(1)}, u32[]{:S(2)}, u32[]{:S(2)}) collective-permute-start(f32[240,128]{1,0:T(8,128)S(1)} %collective-permute-done.24.refs_6_), channel_id=1, source_target_pairs={{0,4},{4,0},{8,12},{12,8},{16,20},{20,16},{24,28},{28,24},{1,5},{5... | collective-permute-start | bytes 368648 | tf_op jit(solution)/shard_map/ppermute | solution.py:836
  68.6 6.9 %collective-permute-start.31 = (f32[128,128]{1,0:T(8,128)S(1)}, f32[128,128]{1,0:T(8,128)S(1)}, u32[]{:S(2)}, u32[]{:S(2)}) collective-permute-start(f32[128,128]{1,0:T(8,128)S(1)} %get-tuple-element.72.refs_0_), channel_id=1, source_target_pairs={{0,24},{4,28},{8,16},{12,20},{16,8},{20,12},{24,0},{28,4},{1,25},{... | collective-permute-start | bytes 196616 | tf_op jit(solution)/shard_map/ppermute | solution.py:832
  70.4 7.1 %collective-permute-start.29 = (f32[128,128]{1,0:T(8,128)S(1)}, f32[128,128]{1,0:T(8,128)S(1)}, u32[]{:S(2)}, u32[]{:S(2)}) collective-permute-start(f32[128,128]{1,0:T(8,128)S(1)} %get-tuple-element.72.refs_0_), channel_id=1, source_target_pairs={{0,16},{4,20},{8,24},{12,28},{16,0},{20,4},{24,8},{28,12},{1,17},{... | collective-permute-start | bytes 196616 | tf_op jit(solution)/shard_map/ppermute | solution.py:832
  70.4 7.1 %collective-permute-start.27 = (f32[128,128]{1,0:T(8,128)S(1)}, f32[128,128]{1,0:T(8,128)S(1)}, u32[]{:S(2)}, u32[]{:S(2)}) collective-permute-start(f32[128,128]{1,0:T(8,128)S(1)} %get-tuple-element.72.refs_0_), channel_id=1, source_target_pairs={{0,8},{4,12},{8,0},{12,4},{16,24},{20,28},{24,16},{28,20},{1,9},{5... | collective-permute-start | bytes 196616 | tf_op jit(solution)/shard_map/ppermute | solution.py:832
  73.0 5.0 %collective-permute-start.26 = (f32[128,128]{1,0:T(8,128)S(1)}, f32[128,128]{1,0:T(8,128)S(1)}, u32[]{:S(2)}, u32[]{:S(2)}) collective-permute-start(f32[128,128]{1,0:T(8,128)S(1)} %get-tuple-element.72.refs_0_), channel_id=1, source_target_pairs={{0,4},{4,0},{8,12},{12,8},{16,20},{20,16},{24,28},{28,24},{1,5},{5... | collective-permute-start | bytes 196616 | tf_op jit(solution)/shard_map/ppermute | solution.py:836
  75.5 2.5 %collective-permute-start.32 = (f32[128,128]{1,0:T(8,128)S(1)}, f32[128,128]{1,0:T(8,128)S(1)}, u32[]{:S(2)}, u32[]{:S(2)}) collective-permute-start(f32[128,128]{1,0:T(8,128)S(1)} %collective-permute-done.31.refs_6_), channel_id=1, source_target_pairs={{0,4},{4,0},{8,12},{12,8},{16,20},{20,16},{24,28},{28,24},{1,5},{5... | collective-permute-start | bytes 196616 | tf_op jit(solution)/shard_map/ppermute | solution.py:836
  77.5 1.3 %collective-permute-start.30 = (f32[128,128]{1,0:T(8,128)S(1)}, f32[128,128]{1,0:T(8,128)S(1)}, u32[]{:S(2)}, u32[]{:S(2)}) collective-permute-start(f32[128,128]{1,0:T(8,128)S(1)} %collective-permute-done.29.refs_4_), channel_id=1, source_target_pairs={{0,4},{4,0},{8,12},{12,8},{16,20},{20,16},{24,28},{28,24},{1,5},{5... | collective-permute-start | bytes 196616 | tf_op jit(solution)/shard_map/ppermute | solution.py:836
  77.5 1.4 %collective-permute-start.28 = (f32[128,128]{1,0:T(8,128)S(1)}, f32[128,128]{1,0:T(8,128)S(1)}, u32[]{:S(2)}, u32[]{:S(2)}) collective-permute-start(f32[128,128]{1,0:T(8,128)S(1)} %collective-permute-done.27.refs_2_), channel_id=1, source_target_pairs={{0,4},{4,0},{8,12},{12,8},{16,20},{20,16},{24,28},{28,24},{1,5},{5... | collective-permute-start | bytes 196616 | tf_op jit(solution)/shard_map/ppermute | solution.py:836

commit v7 on v6

--- a/solution.py
+++ b/solution.py
@@ -171,12 +171,12 @@
     return (first + from_left) * masks[0], (last + from_right) * masks[1]
 
 
-def join_rows(ref, flags):
+def join_rows(ref, flags, pairs=range(7)):
     ex = ex_ids()
     not_first = jnp.where(ex == 0, 0.0, 1.0)
     not_last = jnp.where(ex == 7, 0.0, 1.0)
     for ix in range(6):
-        for ey in range(7):
+        for ey in pairs:
             total = get(ref, 30 + ix, ey) + get(ref, ix, ey + 1)
             put(ref, 30 + ix, ey, total)
             put(ref, ix, ey + 1, total)
@@ -250,7 +250,7 @@
         return tuple(sums)
 
     zero = jnp.zeros((8, LANES), F32)
-    sums = lax.fori_loop(0, BLOCKS, body, (zero,) * (len(products) + int(energy)))
+    sums = lax.fori_loop(0, BLOCKS, body, (zero,) * (len(products) + int(energy)), unroll=2)
     join_rows(dst, flags)
     return sums
 
@@ -336,6 +336,10 @@
         for i in range(6):
             where = side_slice(side, i)
             ref[where, :] = ref[where, :] + lines[side][i]
+
+
+def add_all(left, right):
+    return [[a + b for a, b in zip(one, two)] for one, two in zip(left, right)]
 
 
 def reverse_rows(value):
@@ -446,31 +450,28 @@
     return place if isinstance(four, int) else jnp.bitwise_xor(four, offset_of(place, size))
 
 
-def pack_kernel(step, count, dynamic, load, starts, offsets, ids_ref, velocity_ref, *refs):
+def pack_kernel(step, count, dynamic, chunk, chunks, starts, offsets, ids_ref, source_ref, *refs):
     send_refs = refs[:count]
+    load = chunk == 0
     scratch = refs[-2] if load else refs[-1]
     width = scratch.shape[1]
-    modes = velocity_ref.shape[1]
+    held_ref = refs[count] if load else source_ref
+    modes = held_ref.shape[2]
     four = ids_ref[1] if dynamic else 0
     copies = []
     if load:
-        copies = [
-            pltpu.make_async_copy(velocity_ref.at[comp], refs[count].at[comp], refs[-1].at[comp])
-            for comp in range(3)
-        ]
-        velocity_ref = refs[count]
-    for copy in copies:
-        copy.start()
+        for slot in range(chunks * count):
+            start = pick(block_of(slot % count, four, count), starts[slot // count :: chunks])
+            start = start if isinstance(start, int) else pl.multiple_of(start, LANES)
+            window = source_ref.at[:, :, pl.ds(start, width)]
+            copies.append(pltpu.make_async_copy(window, held_ref.at[slot], refs[-1].at[slot]))
+            copies[-1].start()
     for place in range(count):
         index = block_of(place, four, count)
-        table = order_table(step, pick(index, offsets), scratch)
-        if place == 0:
-            for copy in copies:
-                copy.wait()
-        start = pick(index, starts)
-        start = start if isinstance(start, int) else pl.multiple_of(start, LANES)
-        window = pl.ds(start, width)
-        rows = [velocity_ref[comp, :, window] for comp in range(3)]
+        table = order_table(step, pick(index, offsets[chunk::chunks]), scratch)
+        if load:
+            copies[place].wait()
+        rows = [held_ref[chunk * count + place, comp] for comp in range(3)]
         pad = jnp.zeros((LANES - 3 * modes, width), F32)
         high, low = halves(jnp.concatenate(rows + [pad], axis=0))
         both = jnp.concatenate([high, low], axis=0)
@@ -482,13 +483,20 @@
         values = [out[point * step : (point + 1) * step] for point in range(POINTS)]
         for at, value in enumerate(pack_lanes(values, modes)):
             send_refs[place][pl.ds(at * step, step), :] = value
-
-
-def product_kernel(modes, step, count, dynamic, ids_ref, *refs):
+    for copy in copies[count:]:
+        copy.wait()
+
+
+def product_kernel(modes, step, count, dynamic, role, ids_ref, *refs):
     recv_refs = refs[:count]
     inv_high, inv_low, back_high, back_low = refs[count : count + 4]
-    send_refs = refs[count + 4 : 2 * count + 4]
-    full, lined, phys, prod, spec = refs[2 * count + 4 :]
+    refs = refs[count + 4 :]
+    if role == 1:
+        carry_ref, refs = refs[0], refs[1:]
+    send_refs, refs = refs[:count], refs[count:]
+    if role == 0:
+        carry_ref, refs = refs[0], refs[1:]
+    full, lined, phys, prod, spec = refs
     four = ids_ref[1] if dynamic else 0
     packed = is_packed(modes)
     for place in range(count):
@@ -549,35 +557,76 @@
             mixed = jnp.where(mask[0], turned[0], jnp.where(mask[1], turned[1], turned[2]))
             nonlinear = pltpu.roll(mixed, shifts[place], 1)
             full[place, at, :] = mass * (REACTION * full[place, at, :] + nonlinear)
+    ex = None if role is None else ex_ids()
     for place in range(count):
         values = [full[place, pl.ds(point * step, step), :] for point in range(POINTS)]
+        if role is not None:
+            left = jnp.zeros((8, LANES), F32)
+            sent = []
+            for iy in range(6):
+                line = values[6 * iy : 6 * iy + 6]
+                line[5] = line[5] + jnp.where(ex < 7, pltpu.roll(line[0], 7, 0), 0.0)
+                if role == 0 and iy == 5:
+                    for ix in range(6):
+                        carry_ref[place, pl.ds(ix * 8, 8), :] = line[ix]
+                    continue
+                if role == 1 and iy == 0:
+                    line = [line[ix] + carry_ref[place, pl.ds(ix * 8, 8), :] for ix in range(6)]
+                left = jnp.where(ex == iy, pltpu.roll(line[0], iy, 0) if iy else line[0], left)
+                sent += line[1:]
+            values = sent + [left]
+            values += [left] * (-len(values) % 4)
         for at, value in enumerate(pack_lanes(values, modes)):
             send_refs[place][pl.ds(at * step, step), :] = value
 
 
-def first_kernel(modes, step, count, chunks, dynamic, ids_ref, partner_ref, *refs):
+def spread_rows(values, masks):
+    ex = ex_ids()
+    rows = (len(values) - 1) // 5
+    left = values[5 * rows]
+    points = []
+    for iy in range(rows):
+        line = values[5 * iy : 5 * iy + 5]
+        start = pltpu.roll(left, 8 - iy, 0) if iy else left
+        first = jnp.where(ex == 0, start, pltpu.roll(line[4], 1, 0))
+        points += [first * masks[0]] + line[:4] + [line[4] * masks[1]]
+    return points
+
+
+def first_kernel(modes, step, count, chunks, dynamic, lean, ids_ref, partner_ref, *refs):
     recv_refs = refs[: count * chunks]
     base_ref, lines_ref, work = refs[count * chunks :]
     four = ids_ref[1] if dynamic else 0
     rates = helmholtz_rates(ids_ref[1], modes)
     flags = glued_flags(partner_ref)
-    for chunk in range(chunks):
-        for place in range(count):
+    masks = col_masks(flags)
+    for place in range(count):
+        block = block_of(place, four, count)
+        shares = []
+        for chunk in range(chunks):
             ref = recv_refs[chunk * count + place]
             ready = ref.shape[0] // step
-            first = (block_of(place, four, count) * chunks + chunk) * step
-            values = unpack_lanes([ref[pl.ds(at * step, step), :] for at in range(ready)], modes)
+            shares.append(
+                unpack_lanes([ref[pl.ds(at * step, step), :] for at in range(ready)], modes)
+            )
+        if lean:
+            odd = spread_rows(shares[1][:31], masks)
+            shares = [spread_rows(shares[0][:26], masks) + odd[:6], odd]
+        for chunk in range(chunks):
+            first = (block * chunks + chunk) * step
             for point in range(POINTS):
                 at = point * 64 + first
                 at = at if isinstance(at, int) else pl.multiple_of(at, step)
-                base_ref[pl.ds(at, step), :] = values[point]
-    masks = col_masks(flags)
-    for ey in range(BLOCKS):
-        for iy in range(6):
-            first, last = join_cols(get(base_ref, 6 * iy, ey), get(base_ref, 6 * iy + 5, ey), masks)
-            put(base_ref, 6 * iy, ey, first)
-            put(base_ref, 6 * iy + 5, ey, last)
-    join_rows(base_ref, flags)
+                base_ref[pl.ds(at, step), :] = shares[chunk][point]
+    if not lean:
+        for ey in range(BLOCKS):
+            for iy in range(6):
+                first, last = join_cols(
+                    get(base_ref, 6 * iy, ey), get(base_ref, 6 * iy + 5, ey), masks
+                )
+                put(base_ref, 6 * iy, ey, first)
+                put(base_ref, 6 * iy + 5, ey, last)
+    join_rows(base_ref, flags, range(1, 7, 2) if lean else range(7))
     apply_local(base_ref, work, rates, flags)
     write_lines(base_ref, lines_ref, 0, modes)
     write_lines(work, lines_ref, line_rows(modes), modes)
@@ -596,8 +645,7 @@
     back = own_reaction(load_lines(lines_ref, modes), rates, flags, 1.0)
     add_lines(k0_ref, incoming_lines(sides, 0, partner_ref, flip_ref))
     apply_local(k0_ref, work, rates, flags)
-    add_lines(work, incoming_lines(sides, 1, partner_ref, flip_ref))
-    add_lines(work, back)
+    add_lines(work, add_all(incoming_lines(sides, 1, partner_ref, flip_ref), back))
     sums = apply_local(
         k1_ref, work, rates, flags,
         terms=[(1.0 / SPREAD, work), (-CENTRE / SPREAD, k0_ref)],
@@ -623,8 +671,7 @@
     incoming = incoming_lines(sides, 0, partner_ref, flip_ref)
     add_lines(k2_ref, [[value * TWICE for value in line] for line in incoming])
     apply_local(k2_ref, work, rates, flags)
-    add_lines(work, incoming_lines(sides, 1, partner_ref, flip_ref))
-    add_lines(work, back)
+    add_lines(work, add_all(incoming_lines(sides, 1, partner_ref, flip_ref), back))
     sums = apply_local(
         k3_ref, a3_ref, rates, flags,
         terms=[(TWICE, work), (-CENTRE * TWICE, k2_ref), (-1.0, k1_ref)],
@@ -852,38 +899,49 @@
     blocks = [(sent_rows, LANES)] * count
     lined = line_rows(modes)
 
+    lean = dynamic and chunks == 2 and is_packed(modes)
     spread = []
-    held_velocity = velocity
+    source = velocity
     for chunk in range(chunks):
         load = chunk == 0
         sent = call(
-            functools.partial(
-                pack_kernel, step, count, dynamic, load, starts[chunk::chunks], offsets[chunk::chunks]
-            ),
+            functools.partial(pack_kernel, step, count, dynamic, chunk, chunks, starts, offsets),
             "pack",
-            blocks + [velocity.shape] * load,
-            (ids, held_velocity),
-            [table] + [pltpu.SemaphoreType.DMA((3,))] * load,
+            blocks + [(chunks * count, 3, modes, 3 * LANES)] * load,
+            (ids, source),
+            [table] + [pltpu.SemaphoreType.DMA((chunks * count,))] * load,
             scalars=1,
             outside=load,
         )
         if load:
-            *sent, held_velocity = sent
+            *sent, source = sent
         spread.append(swap_blocks(sent, dynamic))
     local = []
+    carry = []
     for chunk in range(chunks):
+        role = chunk if lean else None
+        out = [((21, 24)[chunk] * step, LANES)] * count if lean else blocks
         sent = call(
-            functools.partial(product_kernel, modes, step, count, dynamic),
+            functools.partial(product_kernel, modes, step, count, dynamic, role),
             "products",
-            blocks,
-            (ids, *spread[chunk], inv_high, inv_low, back_high, back_low),
-            [(count, rows, LANES), (rows, count * LANES), (rows, 3 * LANES), (rows, 6 * LANES), (3, rows, LANES)],
+            out + [(count, SIDE, LANES)] * (role == 0),
+            (ids, *spread[chunk], inv_high, inv_low, back_high, back_low, *carry),
+            [
+                (count, rows, LANES),
+                (rows, count * LANES),
+                (rows, 3 * LANES),
+                (rows, 6 * LANES),
+                (3, rows, LANES),
+            ],
             scalars=1,
         )
+        if role == 0:
+            *sent, held_row = sent
+            carry = [held_row]
         local += swap_blocks(sent, dynamic)
 
     base, lines = call(
-        functools.partial(first_kernel, modes, step, count, chunks, dynamic),
+        functools.partial(first_kernel, modes, step, count, chunks, dynamic, lean),
         "first",
         [field, (2 * lined, LANES)],
         (ids, partner, *local),

time: 82.1 us -> 82.3 us (level)
  transfers between devices with their start and end apart: 33 -> 33, of which waited for: 15 -> 14; matrix products, arithmetic and copies ran while one was open for 0% -> 0% of each run, Pallas kernels for 13% -> 13%
where the time goes in v7:
time: 82.3 us; the launch traced here: 82.1 us
  starting transfers between devices  32.7 us (40%)
  Pallas kernels  26.4 us (32%)
  waiting for transfers between devices  21.9 us (27%)
  between operations  0.98 us (1%)
    pallas_call x10, Pallas kernels, call(): pl.pallas_call(kernel, name=name, out_shape=[pltpu.VMEM(one.shape, one.dt...  26.4 us
    ppermute x12, starting transfers between devices, swap_blocks(): lax.ppermute(blocks[place], 'four', [(i, i ^ offset_of(place, size)) for...  16.8 us
    ppermute x9, waiting for transfers between devices, share_lines(): lax.ppermute(lines, 'dom', [(i, i ^ slot) for i in range(parts)])  14.2 us
    ppermute x9, starting transfers between devices, share_lines(): lax.ppermute(lines, 'dom', [(i, i ^ slot) for i in range(parts)])  13.7 us
    ppermute x12, waiting for transfers between devices, swap_blocks(): lax.ppermute(blocks[place], 'four', [(i, i ^ offset_of(place, size)) for...  4.43 us
    ppermute x12, waiting for transfers between devices, share_lines(): lax.ppermute(slots[slot], 'dom', [(i, i ^ 1) for i in range(parts)])  3.23 us
    ppermute x12, starting transfers between devices, share_lines(): lax.ppermute(slots[slot], 'dom', [(i, i ^ 1) for i in range(parts)])  2.12 us
  transfers between devices with their start and end apart: 33, of which 14 were waited for; matrix products, arithmetic and copies ran while one was open for 0% of the time, Pallas kernels for 13%

profile of v7, /device:TPU:0, one launch (start us, length us, event | category | flops | bytes accessed | tf_op | source)
XLA Modules:
  0.0 82.1 jit_solution(4498437275141627526)
XLA Ops:
  0.6 0.0 copy-start.2
  0.6 0.0 copy-start.3
  0.7 0.0 copy-start
  0.7 0.0 copy-start.1
  0.7 0.1 pad_add_fusion.ids_ref
  0.8 3.2 %pack.2 = (f32[216,128]{1,0:T(8,128)S(1)}, f32[216,128]{1,0:T(8,128)S(1)}, f32[216,128]{1,0:T(8,128)S(1)}, f32[216,128]{1,0:T(8,128)S(1)}, f32[8,3,32,384]{3,2,1,0:T(8,128)S(1)}) custom-call(s32[2]{0:T(128)S(1)} %pad_add_fusion.ids_ref, f32[3,32,2304]{2,1,0:T(8,128)} %source_ref.1), custom_call_target="tpu_custom_call" | custom-call | tf_op jit(solution)/shard_map/pack/pallas_call | solution.py:846
  4.0 4.0 %collective-permute-start = (f32[216,128]{1,0:T(8,128)S(1)}, f32[216,128]{1,0:T(8,128)S(1)}, u32[]{:S(2)}, u32[]{:S(2)}) collective-permute-start(f32[216,128]{1,0:T(8,128)S(1)} %get-tuple-element.46), channel_id=1, source_target_pairs={{0,3},{1,2},{2,1},{3,0},{4,7},{5,6},{6,5},{7,4},{8,11},{9,10},{10,... | collective-permute-start | bytes 331784 | tf_op jit(solution)/shard_map/ppermute | solution.py:869
  7.9 0.5 collective-permute-start.1
  8.4 0.1 collective-permute-start.2
  8.6 1.2 %pack.3 = (f32[216,128]{1,0:T(8,128)S(1)}, f32[216,128]{1,0:T(8,128)S(1)}, f32[216,128]{1,0:T(8,128)S(1)}, f32[216,128]{1,0:T(8,128)S(1)}) custom-call(s32[2]{0:T(128)S(1)} %pad_add_fusion.ids_ref, f32[8,3,32,384]{3,2,1,0:T(8,128)S(1)} %get-tuple-element.53.source_ref), custom_call_target="tpu_custom_call" | custom-call | tf_op jit(solution)/shard_map/pack/pallas_call | solution.py:846
  9.7 2.9 %collective-permute-start.6 = (f32[216,128]{1,0:T(8,128)S(1)}, f32[216,128]{1,0:T(8,128)S(1)}, u32[]{:S(2)}, u32[]{:S(2)}) collective-permute-start(f32[216,128]{1,0:T(8,128)S(1)} %get-tuple-element.55), channel_id=1, source_target_pairs={{0,3},{1,2},{2,1},{3,0},{4,7},{5,6},{6,5},{7,4},{8,11},{9,10},{10,... | collective-permute-start | bytes 331784 | tf_op jit(solution)/shard_map/ppermute | solution.py:869
  12.6 0.5 collective-permute-start.7
  13.2 0.7 collective-permute-start.8
  13.8 0.6 collective-permute-done.1.refs_2_
  14.4 0.0 collective-permute-done.2.refs_3_
  14.4 0.0 copy-start.4
  14.4 2.4 %products.2 = (f32[168,128]{1,0:T(8,128)S(1)}, f32[168,128]{1,0:T(8,128)S(1)}, f32[168,128]{1,0:T(8,128)S(1)}, f32[168,128]{1,0:T(8,128)S(1)}, f32[4,48,128]{2,1,0:T(8,128)S(1)}) custom-call(s32[2]{0:T(128)S(1)} %pad_add_fusion.ids_ref, f32[216,128]{1,0:T(8,128)S(1)} %get-tuple-element.45.refs_0_, f32[216,128]{1,0:T(8,128)S(1)} %collective-permute-done.refs_1_, ...), custom_call_target="tpu_custom_call" | custom-call | tf_op jit(solution)/shard_map/products/pallas_call | solution.py:846
  16.8 0.0 copy-start.5
  16.8 0.0 copy-start.6
  16.8 3.9 %collective-permute-start.3 = (f32[168,128]{1,0:T(8,128)S(1)}, f32[168,128]{1,0:T(8,128)S(1)}, u32[]{:S(2)}, u32[]{:S(2)}) collective-permute-start(f32[168,128]{1,0:T(8,128)S(1)} %get-tuple-element.50), channel_id=1, source_target_pairs={{0,3},{1,2},{2,1},{3,0},{4,7},{5,6},{6,5},{7,4},{8,11},{9,10},{10,... | collective-permute-start | bytes 258056 | tf_op jit(solution)/shard_map/ppermute | solution.py:869
  20.8 0.0 collective-permute-done.6.refs_1_
  20.8 0.0 collective-permute-done.7.refs_2_
  20.8 0.0 collective-permute-done.8.refs_3_
  20.8 2.4 %products.3 = (f32[192,128]{1,0:T(8,128)S(1)}, f32[192,128]{1,0:T(8,128)S(1)}, f32[192,128]{1,0:T(8,128)S(1)}, f32[192,128]{1,0:T(8,128)S(1)}) custom-call(s32[2]{0:T(128)S(1)} %pad_add_fusion.ids_ref, f32[216,128]{1,0:T(8,128)S(1)} %get-tuple-element.54.refs_0_, f32[216,128]{1,0:T(8,128)S(1)} %collective-permute-done.6.refs_1_, ...), custom_call_target="tpu_custom_call" | custom-call | tf_op jit(solution)/shard_map/products/pallas_call | solution.py:846
  23.2 0.1 collective-permute-start.9
  23.3 1.4 %collective-permute-start.10 = (f32[192,128]{1,0:T(8,128)S(1)}, f32[192,128]{1,0:T(8,128)S(1)}, u32[]{:S(2)}, u32[]{:S(2)}) collective-permute-start(f32[192,128]{1,0:T(8,128)S(1)} %get-tuple-element.61), channel_id=1, source_target_pairs={{0,1},{1,0},{2,3},{3,2},{4,5},{5,4},{6,7},{7,6},{8,9},{9,8},{10,11... | collective-permute-start | bytes 294920 | tf_op jit(solution)/shard_map/ppermute | solution.py:869
  24.7 2.0 %collective-permute-start.11 = (f32[192,128]{1,0:T(8,128)S(1)}, f32[192,128]{1,0:T(8,128)S(1)}, u32[]{:S(2)}, u32[]{:S(2)}) collective-permute-start(f32[192,128]{1,0:T(8,128)S(1)} %get-tuple-element.62), channel_id=1, source_target_pairs={{0,2},{1,3},{2,0},{3,1},{4,6},{5,7},{6,4},{7,5},{8,10},{9,11},{10,... | collective-permute-start | bytes 294920 | tf_op jit(solution)/shard_map/ppermute | solution.py:869
  26.8 0.0 collective-permute-done.3.refs_1_
  26.8 0.6 collective-permute-start.5
  27.4 3.8 %collective-permute-done.4.refs_2_ = f32[168,128]{1,0:T(8,128)S(1)} collective-permute-done((f32[168,128]{1,0:T(8,128)S(1)}, f32[168,128]{1,0:T(8,128)S(1)}, u32[]{:S(2)}, u32[]{:S(2)}) %collective-permute-start.4) | collective-permute-done | bytes 86048 | tf_op jit(solution)/shard_map/ppermute | solution.py:869
  31.2 0.0 collective-permute-done.5.refs_3_
  31.3 0.0 collective-permute-done.9.refs_5_
  31.3 0.0 collective-permute-done.10.refs_6_
  31.3 0.0 collective-permute-done.11.refs_7_
  31.3 1.9 %first.1 = (f32[2304,128]{1,0:T(8,128)S(1)}, f32[240,128]{1,0:T(8,128)S(1)}) custom-call(s32[2]{0:T(128)S(1)} %pad_add_fusion.ids_ref, s32[1,4]{1,0:T(1,128)S(1)} %copy-done.4, f32[168,128]{1,0:T(8,128)S(1)} %get-tuple-element.49.refs_0_, f32[168,128]{1,0:T(8,128)S(1)} %collective-permute-done.3.refs_1_, f32[168,128]{1,0:T(8,128)S(1)} %collective-permute-done.4.refs_2_, ...), custom_call_target="tpu_custom_call" | custom-call | tf_op jit(solution)/shard_map/first/pallas_call | solution.py:846
  33.2 4.2 %collective-permute-start.17 = (f32[240,128]{1,0:T(8,128)S(1)}, f32[240,128]{1,0:T(8,128)S(1)}, u32[]{:S(2)}, u32[]{:S(2)}) collective-permute-start(f32[240,128]{1,0:T(8,128)S(1)} %get-tuple-element.63.refs_0_.refs_8_), channel_id=1, source_target_pairs={{0,24},{4,28},{8,16},{12,20},{16,8},{20,12},{24,0},{28,4},{1,25},{... | collective-permute-start | bytes 368648 | tf_op jit(solution)/shard_map/ppermute | solution.py:879
  37.4 0.6 collective-permute-start.13
  38.0 2.3 %collective-permute-done.17.refs_6_ = f32[240,128]{1,0:T(8,128)S(1)} collective-permute-done((f32[240,128]{1,0:T(8,128)S(1)}, f32[240,128]{1,0:T(8,128)S(1)}, u32[]{:S(2)}, u32[]{:S(2)}) %collective-permute-start.17) | collective-permute-done | bytes 122912 | tf_op jit(solution)/shard_map/ppermute | solution.py:879
  40.4 3.4 %collective-permute-done.15.refs_4_ = f32[240,128]{1,0:T(8,128)S(1)} collective-permute-done((f32[240,128]{1,0:T(8,128)S(1)}, f32[240,128]{1,0:T(8,128)S(1)}, u32[]{:S(2)}, u32[]{:S(2)}) %collective-permute-start.15) | collective-permute-done | bytes 122912 | tf_op jit(solution)/shard_map/ppermute | solution.py:879
  43.8 0.5 collective-permute-start.14
  44.3 0.8 collective-permute-done.16.refs_5_
  45.1 0.2 collective-permute-done.14.refs_3_
  45.3 4.4 %second.1 = (f32[2304,128]{1,0:T(8,128)S(1)}, f32[2304,128]{1,0:T(8,128)S(1)}, f32[2304,128]{1,0:T(8,128)S(1)}, f32[240,128]{1,0:T(8,128)S(1)}, f32[8,128]{1,0:T(8,128)S(1)}) custom-call(s32[2]{0:T(128)S(1)} %pad_add_fusion.ids_ref, s32[1,4]{1,0:T(1,128)S(1)} %copy-done.4, s32[1,4]{1,0:T(1,128)S(1)} %copy-done.5, ...), custom_call_target="tpu_custom_call", output_to_operand_aliasing={{0}: (13, {})} | custom-call | tf_op jit(solution)/shard_map/second/pallas_call | solution.py:846
  49.7 2.5 %collective-permute-start.24 = (f32[240,128]{1,0:T(8,128)S(1)}, f32[240,128]{1,0:T(8,128)S(1)}, u32[]{:S(2)}, u32[]{:S(2)}) collective-permute-start(f32[240,128]{1,0:T(8,128)S(1)} %get-tuple-element.65.refs_0_.refs_8_), channel_id=1, source_target_pairs={{0,24},{4,28},{8,16},{12,20},{16,8},{20,12},{24,0},{28,4},{1,25},{... | collective-permute-start | bytes 368648 | tf_op jit(solution)/shard_map/ppermute | solution.py:879
  52.2 1.9 %collective-permute-start.20 = (f32[240,128]{1,0:T(8,128)S(1)}, f32[240,128]{1,0:T(8,128)S(1)}, u32[]{:S(2)}, u32[]{:S(2)}) collective-permute-start(f32[240,128]{1,0:T(8,128)S(1)} %get-tuple-element.65.refs_0_.refs_8_), channel_id=1, source_target_pairs={{0,8},{4,12},{8,0},{12,4},{16,24},{20,28},{24,16},{28,20},{1,9},{5... | collective-permute-start | bytes 368648 | tf_op jit(solution)/shard_map/ppermute | solution.py:879
  54.1 2.0 %turn.2 = (f32[96,2304]{1,0:T(8,128)S(1)}, f32[96,2304]{1,0:T(8,128)S(1)}, bf16[192,2304]{1,0:T(8,128)(2,1)S(1)}) custom-call(f32[2304,128]{1,0:T(8,128)S(1)} %get-tuple-element.66.refs_0_, f32[2304,128]{1,0:T(8,128)S(1)} %get-tuple-element.67.refs_1_.refs_9_), custom_call_target="tpu_custom_call" | custom-call | tf_op jit(solution)/shard_map/turn/pallas_call | solution.py:846
  56.2 1.6 %collective-permute-done.24.refs_6_ = f32[240,128]{1,0:T(8,128)S(1)} collective-permute-done((f32[240,128]{1,0:T(8,128)S(1)}, f32[240,128]{1,0:T(8,128)S(1)}, u32[]{:S(2)}, u32[]{:S(2)}) %collective-permute-start.24) | collective-permute-done | bytes 122912 | tf_op jit(solution)/shard_map/ppermute | solution.py:879
  57.8 5.7 %collective-permute-done.22.refs_4_ = f32[240,128]{1,0:T(8,128)S(1)} collective-permute-done((f32[240,128]{1,0:T(8,128)S(1)}, f32[240,128]{1,0:T(8,128)S(1)}, u32[]{:S(2)}, u32[]{:S(2)}) %collective-permute-start.22) | collective-permute-done | bytes 122912 | tf_op jit(solution)/shard_map/ppermute | solution.py:879
  63.5 0.5 collective-permute-start.21
  64.0 0.0 collective-permute-start.25
  64.0 0.8 collective-permute-done.23.refs_5_
  64.8 0.2 collective-permute-done.21.refs_3_
  65.0 0.3 collective-permute-done.25.refs_7_
  65.4 3.5 %third.1 = (f32[2304,128]{1,0:T(8,128)S(1)}, f32[2304,128]{1,0:T(8,128)S(1)}, f32[2304,128]{1,0:T(8,128)S(1)}, f32[128,128]{1,0:T(8,128)S(1)}) custom-call(s32[2]{0:T(128)S(1)} %pad_add_fusion.ids_ref, s32[1,4]{1,0:T(1,128)S(1)} %copy-done.4, s32[1,4]{1,0:T(1,128)S(1)} %copy-done.5, s32[1,4]{1,0:T(1,128)S(1)} %copy-done.6, ...), custom_call_target="tpu_custom_call", output_to_operand_aliasing={{0}: (15, {})} | custom-call | tf_op jit(solution)/shard_map/third/pallas_call | solution.py:846
  68.8 1.9 %collective-permute-start.31 = (f32[128,128]{1,0:T(8,128)S(1)}, f32[128,128]{1,0:T(8,128)S(1)}, u32[]{:S(2)}, u32[]{:S(2)}) collective-permute-start(f32[128,128]{1,0:T(8,128)S(1)} %get-tuple-element.74.refs_0_), channel_id=1, source_target_pairs={{0,24},{4,28},{8,16},{12,20},{16,8},{20,12},{24,0},{28,4},{1,25},{... | collective-permute-start | bytes 196616 | tf_op jit(solution)/shard_map/ppermute | solution.py:879
  70.7 2.6 %collective-permute-start.27 = (f32[128,128]{1,0:T(8,128)S(1)}, f32[128,128]{1,0:T(8,128)S(1)}, u32[]{:S(2)}, u32[]{:S(2)}) collective-permute-start(f32[128,128]{1,0:T(8,128)S(1)} %get-tuple-element.74.refs_0_), channel_id=1, source_target_pairs={{0,8},{4,12},{8,0},{12,4},{16,24},{20,28},{24,16},{28,20},{1,9},{5... | collective-permute-start | bytes 196616 | tf_op jit(solution)/shard_map/ppermute | solution.py:879
  73.3 2.5 %turn.3 = (f32[96,2304]{1,0:T(8,128)S(1)}, f32[96,2304]{1,0:T(8,128)S(1)}, f32[96,2304]{1,0:T(8,128)S(1)}) custom-call(f32[2304,128]{1,0:T(8,128)S(1)} %get-tuple-element.75.refs_0_, f32[2304,128]{1,0:T(8,128)S(1)} %get-tuple-element.76.refs_1_, f32[2304,128]{1,0:T(8,128)S(1)} %get-tuple-element.77.refs_2_), custom_call_target="tpu_custom_call" | custom-call | tf_op jit(solution)/shard_map/turn/pallas_call | solution.py:846
  75.8 0.6 collective-permute-start.32
  76.4 1.2 %collective-permute-done.29.refs_4_ = f32[128,128]{1,0:T(8,128)S(1)} collective-permute-done((f32[128,128]{1,0:T(8,128)S(1)}, f32[128,128]{1,0:T(8,128)S(1)}, u32[]{:S(2)}, u32[]{:S(2)}) %collective-permute-start.29) | collective-permute-done | bytes 65568 | tf_op jit(solution)/shard_map/ppermute | solution.py:879
  77.6 0.0 collective-permute-start.30
  77.6 0.5 collective-permute-start.28
  78.1 0.7 collective-permute-done.30.refs_5_
  78.8 0.2 collective-permute-done.28.refs_3_
  79.0 2.9 %last.1 = (f32[3,32,2304]{2,1,0:T(8,128)}, f32[3,32,2304]{2,1,0:T(8,128)}) custom-call(s32[2]{0:T(128)S(1)} %pad_add_fusion.ids_ref, s32[1,4]{1,0:T(1,128)S(1)} %copy-done.4, s32[1,4]{1,0:T(1,128)S(1)} %copy-done.5, s32[1,4]{1,0:T(1,128)S(1)} %copy-done.6, f32[128,128]{1,0:T(8,128)S(1)} %get-tuple-element.74.refs_0_, ...), custom_call_target="tpu_custom_call" | custom-call | tf_op jit(solution)/shard_map/last/pallas_call | solution.py:846
  (27 shorter events, 0.1 us)
Async XLA Ops:
  0.6 13.8 %copy-start.2 = (bf16[256,128]{1,0:T(8,128)(2,1)S(1)}, bf16[256,128]{1,0:T(8,128)(2,1)}, u32[]{:S(2)}) copy-start(bf16[256,128]{1,0:T(8,128)(2,1)} %constant.20.clone.refs_7_) | copy-start | bytes 196612
  0.6 13.8 %copy-start.3 = (bf16[256,128]{1,0:T(8,128)(2,1)S(1)}, bf16[256,128]{1,0:T(8,128)(2,1)}, u32[]{:S(2)}) copy-start(bf16[256,128]{1,0:T(8,128)(2,1)} %constant.19.clone.refs_6_) | copy-start | bytes 196612
  0.7 13.7 %copy-start = (bf16[512,384]{1,0:T(8,128)(2,1)S(1)}, bf16[512,384]{1,0:T(8,128)(2,1)}, u32[]{:S(2)}) copy-start(bf16[512,384]{1,0:T(8,128)(2,1)} %constant.18.clone.refs_5_) | copy-start | bytes 1179652
  0.7 13.7 %copy-start.1 = (bf16[512,384]{1,0:T(8,128)(2,1)S(1)}, bf16[512,384]{1,0:T(8,128)(2,1)}, u32[]{:S(2)}) copy-start(bf16[512,384]{1,0:T(8,128)(2,1)} %constant.17.clone.refs_4_) | copy-start | bytes 1179652
  4.0 9.2 %collective-permute-start = (f32[216,128]{1,0:T(8,128)S(1)}, f32[216,128]{1,0:T(8,128)S(1)}, u32[]{:S(2)}, u32[]{:S(2)}) collective-permute-start(f32[216,128]{1,0:T(8,128)S(1)} %get-tuple-element.46), channel_id=1, source_target_pairs={{0,3},{1,2},{2,1},{3,0},{4,7},{5,6},{6,5},{7,4},{8,11},{9,10},{10,... | collective-permute-start | bytes 331784 | tf_op jit(solution)/shard_map/ppermute | solution.py:869
  7.9 6.5 %collective-permute-start.1 = (f32[216,128]{1,0:T(8,128)S(1)}, f32[216,128]{1,0:T(8,128)S(1)}, u32[]{:S(2)}, u32[]{:S(2)}) collective-permute-start(f32[216,128]{1,0:T(8,128)S(1)} %get-tuple-element.47), channel_id=1, source_target_pairs={{0,1},{1,0},{2,3},{3,2},{4,5},{5,4},{6,7},{7,6},{8,9},{9,8},{10,11... | collective-permute-start | bytes 331784 | tf_op jit(solution)/shard_map/ppermute | solution.py:869
  8.4 5.9 %collective-permute-start.2 = (f32[216,128]{1,0:T(8,128)S(1)}, f32[216,128]{1,0:T(8,128)S(1)}, u32[]{:S(2)}, u32[]{:S(2)}) collective-permute-start(f32[216,128]{1,0:T(8,128)S(1)} %get-tuple-element.48), channel_id=1, source_target_pairs={{0,2},{1,3},{2,0},{3,1},{4,6},{5,7},{6,4},{7,5},{8,10},{9,11},{10,... | collective-permute-start | bytes 331784 | tf_op jit(solution)/shard_map/ppermute | solution.py:869
  9.7 11.1 %collective-permute-start.6 = (f32[216,128]{1,0:T(8,128)S(1)}, f32[216,128]{1,0:T(8,128)S(1)}, u32[]{:S(2)}, u32[]{:S(2)}) collective-permute-start(f32[216,128]{1,0:T(8,128)S(1)} %get-tuple-element.55), channel_id=1, source_target_pairs={{0,3},{1,2},{2,1},{3,0},{4,7},{5,6},{6,5},{7,4},{8,11},{9,10},{10,... | collective-permute-start | bytes 331784 | tf_op jit(solution)/shard_map/ppermute | solution.py:869
  12.6 8.1 %collective-permute-start.7 = (f32[216,128]{1,0:T(8,128)S(1)}, f32[216,128]{1,0:T(8,128)S(1)}, u32[]{:S(2)}, u32[]{:S(2)}) collective-permute-start(f32[216,128]{1,0:T(8,128)S(1)} %get-tuple-element.56), channel_id=1, source_target_pairs={{0,1},{1,0},{2,3},{3,2},{4,5},{5,4},{6,7},{7,6},{8,9},{9,8},{10,11... | collective-permute-start | bytes 331784 | tf_op jit(solution)/shard_map/ppermute | solution.py:869
  13.2 7.6 %collective-permute-start.8 = (f32[216,128]{1,0:T(8,128)S(1)}, f32[216,128]{1,0:T(8,128)S(1)}, u32[]{:S(2)}, u32[]{:S(2)}) collective-permute-start(f32[216,128]{1,0:T(8,128)S(1)} %get-tuple-element.57), channel_id=1, source_target_pairs={{0,2},{1,3},{2,0},{3,1},{4,6},{5,7},{6,4},{7,5},{8,10},{9,11},{10,... | collective-permute-start | bytes 331784 | tf_op jit(solution)/shard_map/ppermute | solution.py:869
  14.4 16.9 %copy-start.4 = (s32[1,4]{1,0:T(1,128)S(1)}, s32[1,4]{1,0:T(1,128)}, u32[]{:S(2)}) copy-start(s32[1,4]{1,0:T(1,128)} %partner_ref.7) | copy-start | bytes 52
  16.8 28.5 %copy-start.5 = (s32[1,4]{1,0:T(1,128)S(1)}, s32[1,4]{1,0:T(1,128)}, u32[]{:S(2)}) copy-start(s32[1,4]{1,0:T(1,128)} %side_ref.5) | copy-start | bytes 52
  16.8 28.4 %copy-start.6 = (s32[1,4]{1,0:T(1,128)S(1)}, s32[1,4]{1,0:T(1,128)}, u32[]{:S(2)}) copy-start(s32[1,4]{1,0:T(1,128)} %flip_ref.5) | copy-start | bytes 52
  16.8 9.9 %collective-permute-start.3 = (f32[168,128]{1,0:T(8,128)S(1)}, f32[168,128]{1,0:T(8,128)S(1)}, u32[]{:S(2)}, u32[]{:S(2)}) collective-permute-start(f32[168,128]{1,0:T(8,128)S(1)} %get-tuple-element.50), channel_id=1, source_target_pairs={{0,3},{1,2},{2,1},{3,0},{4,7},{5,6},{6,5},{7,4},{8,11},{9,10},{10,... | collective-permute-start | bytes 258056 | tf_op jit(solution)/shard_map/ppermute | solution.py:869
  23.2 8.1 %collective-permute-start.9 = (f32[192,128]{1,0:T(8,128)S(1)}, f32[192,128]{1,0:T(8,128)S(1)}, u32[]{:S(2)}, u32[]{:S(2)}) collective-permute-start(f32[192,128]{1,0:T(8,128)S(1)} %get-tuple-element.60), channel_id=1, source_target_pairs={{0,3},{1,2},{2,1},{3,0},{4,7},{5,6},{6,5},{7,4},{8,11},{9,10},{10,... | collective-permute-start | bytes 294920 | tf_op jit(solution)/shard_map/ppermute | solution.py:869
  23.3 8.0 %collective-permute-start.10 = (f32[192,128]{1,0:T(8,128)S(1)}, f32[192,128]{1,0:T(8,128)S(1)}, u32[]{:S(2)}, u32[]{:S(2)}) collective-permute-start(f32[192,128]{1,0:T(8,128)S(1)} %get-tuple-element.61), channel_id=1, source_target_pairs={{0,1},{1,0},{2,3},{3,2},{4,5},{5,4},{6,7},{7,6},{8,9},{9,8},{10,11... | collective-permute-start | bytes 294920 | tf_op jit(solution)/shard_map/ppermute | solution.py:869
  24.7 6.5 %collective-permute-start.11 = (f32[192,128]{1,0:T(8,128)S(1)}, f32[192,128]{1,0:T(8,128)S(1)}, u32[]{:S(2)}, u32[]{:S(2)}) collective-permute-start(f32[192,128]{1,0:T(8,128)S(1)} %get-tuple-element.62), channel_id=1, source_target_pairs={{0,2},{1,3},{2,0},{3,1},{4,6},{5,7},{6,4},{7,5},{8,10},{9,11},{10,... | collective-permute-start | bytes 294920 | tf_op jit(solution)/shard_map/ppermute | solution.py:869
  26.8 4.5 %collective-permute-start.4 = (f32[168,128]{1,0:T(8,128)S(1)}, f32[168,128]{1,0:T(8,128)S(1)}, u32[]{:S(2)}, u32[]{:S(2)}) collective-permute-start(f32[168,128]{1,0:T(8,128)S(1)} %get-tuple-element.51), channel_id=1, source_target_pairs={{0,1},{1,0},{2,3},{3,2},{4,5},{5,4},{6,7},{7,6},{8,9},{9,8},{10,11... | collective-permute-start | bytes 258056 | tf_op jit(solution)/shard_map/ppermute | solution.py:869
  26.8 4.5 %collective-permute-start.5 = (f32[168,128]{1,0:T(8,128)S(1)}, f32[168,128]{1,0:T(8,128)S(1)}, u32[]{:S(2)}, u32[]{:S(2)}) collective-permute-start(f32[168,128]{1,0:T(8,128)S(1)} %get-tuple-element.52), channel_id=1, source_target_pairs={{0,2},{1,3},{2,0},{3,1},{4,6},{5,7},{6,4},{7,5},{8,10},{9,11},{10,... | collective-permute-start | bytes 258056 | tf_op jit(solution)/shard_map/ppermute | solution.py:869
  33.2 7.2 %collective-permute-start.17 = (f32[240,128]{1,0:T(8,128)S(1)}, f32[240,128]{1,0:T(8,128)S(1)}, u32[]{:S(2)}, u32[]{:S(2)}) collective-permute-start(f32[240,128]{1,0:T(8,128)S(1)} %get-tuple-element.63.refs_0_.refs_8_), channel_id=1, source_target_pairs={{0,24},{4,28},{8,16},{12,20},{16,8},{20,12},{24,0},{28,4},{1,25},{... | collective-permute-start | bytes 368648 | tf_op jit(solution)/shard_map/ppermute | solution.py:879
  37.4 6.3 %collective-permute-start.15 = (f32[240,128]{1,0:T(8,128)S(1)}, f32[240,128]{1,0:T(8,128)S(1)}, u32[]{:S(2)}, u32[]{:S(2)}) collective-permute-start(f32[240,128]{1,0:T(8,128)S(1)} %get-tuple-element.63.refs_0_.refs_8_), channel_id=1, source_target_pairs={{0,16},{4,20},{8,24},{12,28},{16,0},{20,4},{24,8},{28,12},{1,17},{... | collective-permute-start | bytes 368648 | tf_op jit(solution)/shard_map/ppermute | solution.py:879
  37.4 6.3 %collective-permute-start.13 = (f32[240,128]{1,0:T(8,128)S(1)}, f32[240,128]{1,0:T(8,128)S(1)}, u32[]{:S(2)}, u32[]{:S(2)}) collective-permute-start(f32[240,128]{1,0:T(8,128)S(1)} %get-tuple-element.63.refs_0_.refs_8_), channel_id=1, source_target_pairs={{0,8},{4,12},{8,0},{12,4},{16,24},{20,28},{24,16},{28,20},{1,9},{5... | collective-permute-start | bytes 368648 | tf_op jit(solution)/shard_map/ppermute | solution.py:879
  38.0 6.2 %collective-permute-start.12 = (f32[240,128]{1,0:T(8,128)S(1)}, f32[240,128]{1,0:T(8,128)S(1)}, u32[]{:S(2)}, u32[]{:S(2)}) collective-permute-start(f32[240,128]{1,0:T(8,128)S(1)} %get-tuple-element.63.refs_0_.refs_8_), channel_id=1, source_target_pairs={{0,4},{4,0},{8,12},{12,8},{16,20},{20,16},{24,28},{28,24},{1,5},{5... | collective-permute-start | bytes 368648 | tf_op jit(solution)/shard_map/ppermute | solution.py:883
  40.4 3.9 %collective-permute-start.18 = (f32[240,128]{1,0:T(8,128)S(1)}, f32[240,128]{1,0:T(8,128)S(1)}, u32[]{:S(2)}, u32[]{:S(2)}) collective-permute-start(f32[240,128]{1,0:T(8,128)S(1)} %collective-permute-done.17.refs_6_), channel_id=1, source_target_pairs={{0,4},{4,0},{8,12},{12,8},{16,20},{20,16},{24,28},{28,24},{1,5},{5... | collective-permute-start | bytes 368648 | tf_op jit(solution)/shard_map/ppermute | solution.py:883
  43.7 1.3 %collective-permute-start.16 = (f32[240,128]{1,0:T(8,128)S(1)}, f32[240,128]{1,0:T(8,128)S(1)}, u32[]{:S(2)}, u32[]{:S(2)}) collective-permute-start(f32[240,128]{1,0:T(8,128)S(1)} %collective-permute-done.15.refs_4_), channel_id=1, source_target_pairs={{0,4},{4,0},{8,12},{12,8},{16,20},{20,16},{24,28},{28,24},{1,5},{5... | collective-permute-start | bytes 368648 | tf_op jit(solution)/shard_map/ppermute | solution.py:883
  43.8 1.5 %collective-permute-start.14 = (f32[240,128]{1,0:T(8,128)S(1)}, f32[240,128]{1,0:T(8,128)S(1)}, u32[]{:S(2)}, u32[]{:S(2)}) collective-permute-start(f32[240,128]{1,0:T(8,128)S(1)} %collective-permute-done.13.refs_2_), channel_id=1, source_target_pairs={{0,4},{4,0},{8,12},{12,8},{16,20},{20,16},{24,28},{28,24},{1,5},{5... | collective-permute-start | bytes 368648 | tf_op jit(solution)/shard_map/ppermute | solution.py:883
  49.7 8.1 %collective-permute-start.24 = (f32[240,128]{1,0:T(8,128)S(1)}, f32[240,128]{1,0:T(8,128)S(1)}, u32[]{:S(2)}, u32[]{:S(2)}) collective-permute-start(f32[240,128]{1,0:T(8,128)S(1)} %get-tuple-element.65.refs_0_.refs_8_), channel_id=1, source_target_pairs={{0,24},{4,28},{8,16},{12,20},{16,8},{20,12},{24,0},{28,4},{1,25},{... | collective-permute-start | bytes 368648 | tf_op jit(solution)/shard_map/ppermute | solution.py:879
  52.2 11.3 %collective-permute-start.22 = (f32[240,128]{1,0:T(8,128)S(1)}, f32[240,128]{1,0:T(8,128)S(1)}, u32[]{:S(2)}, u32[]{:S(2)}) collective-permute-start(f32[240,128]{1,0:T(8,128)S(1)} %get-tuple-element.65.refs_0_.refs_8_), channel_id=1, source_target_pairs={{0,16},{4,20},{8,24},{12,28},{16,0},{20,4},{24,8},{28,12},{1,17},{... | collective-permute-start | bytes 368648 | tf_op jit(solution)/shard_map/ppermute | solution.py:879
  52.2 11.3 %collective-permute-start.20 = (f32[240,128]{1,0:T(8,128)S(1)}, f32[240,128]{1,0:T(8,128)S(1)}, u32[]{:S(2)}, u32[]{:S(2)}) collective-permute-start(f32[240,128]{1,0:T(8,128)S(1)} %get-tuple-element.65.refs_0_.refs_8_), channel_id=1, source_target_pairs={{0,8},{4,12},{8,0},{12,4},{16,24},{20,28},{24,16},{28,20},{1,9},{5... | collective-permute-start | bytes 368648 | tf_op jit(solution)/shard_map/ppermute | solution.py:879
  54.1 9.9 %collective-permute-start.19 = (f32[240,128]{1,0:T(8,128)S(1)}, f32[240,128]{1,0:T(8,128)S(1)}, u32[]{:S(2)}, u32[]{:S(2)}) collective-permute-start(f32[240,128]{1,0:T(8,128)S(1)} %get-tuple-element.65.refs_0_.refs_8_), channel_id=1, source_target_pairs={{0,4},{4,0},{8,12},{12,8},{16,20},{20,16},{24,28},{28,24},{1,5},{5... | collective-permute-start | bytes 368648 | tf_op jit(solution)/shard_map/ppermute | solution.py:883
  63.5 1.3 %collective-permute-start.23 = (f32[240,128]{1,0:T(8,128)S(1)}, f32[240,128]{1,0:T(8,128)S(1)}, u32[]{:S(2)}, u32[]{:S(2)}) collective-permute-start(f32[240,128]{1,0:T(8,128)S(1)} %collective-permute-done.22.refs_4_), channel_id=1, source_target_pairs={{0,4},{4,0},{8,12},{12,8},{16,20},{20,16},{24,28},{28,24},{1,5},{5... | collective-permute-start | bytes 368648 | tf_op jit(solution)/shard_map/ppermute | solution.py:883
  63.5 1.5 %collective-permute-start.21 = (f32[240,128]{1,0:T(8,128)S(1)}, f32[240,128]{1,0:T(8,128)S(1)}, u32[]{:S(2)}, u32[]{:S(2)}) collective-permute-start(f32[240,128]{1,0:T(8,128)S(1)} %collective-permute-done.20.refs_2_), channel_id=1, source_target_pairs={{0,4},{4,0},{8,12},{12,8},{16,20},{20,16},{24,28},{28,24},{1,5},{5... | collective-permute-start | bytes 368648 | tf_op jit(solution)/shard_map/ppermute | solution.py:883
  64.0 1.3 %collective-permute-start.25 = (f32[240,128]{1,0:T(8,128)S(1)}, f32[240,128]{1,0:T(8,128)S(1)}, u32[]{:S(2)}, u32[]{:S(2)}) collective-permute-start(f32[240,128]{1,0:T(8,128)S(1)} %collective-permute-done.24.refs_6_), channel_id=1, source_target_pairs={{0,4},{4,0},{8,12},{12,8},{16,20},{20,16},{24,28},{28,24},{1,5},{5... | collective-permute-start | bytes 368648 | tf_op jit(solution)/shard_map/ppermute | solution.py:883
  68.8 7.0 %collective-permute-start.31 = (f32[128,128]{1,0:T(8,128)S(1)}, f32[128,128]{1,0:T(8,128)S(1)}, u32[]{:S(2)}, u32[]{:S(2)}) collective-permute-start(f32[128,128]{1,0:T(8,128)S(1)} %get-tuple-element.74.refs_0_), channel_id=1, source_target_pairs={{0,24},{4,28},{8,16},{12,20},{16,8},{20,12},{24,0},{28,4},{1,25},{... | collective-permute-start | bytes 196616 | tf_op jit(solution)/shard_map/ppermute | solution.py:879
  70.7 6.9 %collective-permute-start.29 = (f32[128,128]{1,0:T(8,128)S(1)}, f32[128,128]{1,0:T(8,128)S(1)}, u32[]{:S(2)}, u32[]{:S(2)}) collective-permute-start(f32[128,128]{1,0:T(8,128)S(1)} %get-tuple-element.74.refs_0_), channel_id=1, source_target_pairs={{0,16},{4,20},{8,24},{12,28},{16,0},{20,4},{24,8},{28,12},{1,17},{... | collective-permute-start | bytes 196616 | tf_op jit(solution)/shard_map/ppermute | solution.py:879
  70.7 6.9 %collective-permute-start.27 = (f32[128,128]{1,0:T(8,128)S(1)}, f32[128,128]{1,0:T(8,128)S(1)}, u32[]{:S(2)}, u32[]{:S(2)}) collective-permute-start(f32[128,128]{1,0:T(8,128)S(1)} %get-tuple-element.74.refs_0_), channel_id=1, source_target_pairs={{0,8},{4,12},{8,0},{12,4},{16,24},{20,28},{24,16},{28,20},{1,9},{5... | collective-permute-start | bytes 196616 | tf_op jit(solution)/shard_map/ppermute | solution.py:879
  73.3 4.8 %collective-permute-start.26 = (f32[128,128]{1,0:T(8,128)S(1)}, f32[128,128]{1,0:T(8,128)S(1)}, u32[]{:S(2)}, u32[]{:S(2)}) collective-permute-start(f32[128,128]{1,0:T(8,128)S(1)} %get-tuple-element.74.refs_0_), channel_id=1, source_target_pairs={{0,4},{4,0},{8,12},{12,8},{16,20},{20,16},{24,28},{28,24},{1,5},{5... | collective-permute-start | bytes 196616 | tf_op jit(solution)/shard_map/ppermute | solution.py:883
  75.8 2.3 %collective-permute-start.32 = (f32[128,128]{1,0:T(8,128)S(1)}, f32[128,128]{1,0:T(8,128)S(1)}, u32[]{:S(2)}, u32[]{:S(2)}) collective-permute-start(f32[128,128]{1,0:T(8,128)S(1)} %collective-permute-done.31.refs_6_), channel_id=1, source_target_pairs={{0,4},{4,0},{8,12},{12,8},{16,20},{20,16},{24,28},{28,24},{1,5},{5... | collective-permute-start | bytes 196616 | tf_op jit(solution)/shard_map/ppermute | solution.py:883
  77.6 1.3 %collective-permute-start.30 = (f32[128,128]{1,0:T(8,128)S(1)}, f32[128,128]{1,0:T(8,128)S(1)}, u32[]{:S(2)}, u32[]{:S(2)}) collective-permute-start(f32[128,128]{1,0:T(8,128)S(1)} %collective-permute-done.29.refs_4_), channel_id=1, source_target_pairs={{0,4},{4,0},{8,12},{12,8},{16,20},{20,16},{24,28},{28,24},{1,5},{5... | collective-permute-start | bytes 196616 | tf_op jit(solution)/shard_map/ppermute | solution.py:883
  77.6 1.4 %collective-permute-start.28 = (f32[128,128]{1,0:T(8,128)S(1)}, f32[128,128]{1,0:T(8,128)S(1)}, u32[]{:S(2)}, u32[]{:S(2)}) collective-permute-start(f32[128,128]{1,0:T(8,128)S(1)} %collective-permute-done.27.refs_2_), channel_id=1, source_target_pairs={{0,4},{4,0},{8,12},{12,8},{16,20},{20,16},{24,28},{28,24},{1,5},{5... | collective-permute-start | bytes 196616 | tf_op jit(solution)/shard_map/ppermute | solution.py:883

commit v8 on v7

--- a/solution.py
+++ b/solution.py
@@ -456,22 +456,25 @@
     scratch = refs[-2] if load else refs[-1]
     width = scratch.shape[1]
     held_ref = refs[count] if load else source_ref
-    modes = held_ref.shape[2]
+    modes = held_ref.shape[1]
     four = ids_ref[1] if dynamic else 0
     copies = []
     if load:
-        for slot in range(chunks * count):
-            start = pick(block_of(slot % count, four, count), starts[slot // count :: chunks])
-            start = start if isinstance(start, int) else pl.multiple_of(start, LANES)
-            window = source_ref.at[:, :, pl.ds(start, width)]
-            copies.append(pltpu.make_async_copy(window, held_ref.at[slot], refs[-1].at[slot]))
+        for slot in range(3 * modes // 8):
+            at = slot // (modes // 8), pl.ds(slot % (modes // 8) * 8, 8)
+            copies.append(
+                pltpu.make_async_copy(source_ref.at[at], held_ref.at[at], refs[-1].at[slot])
+            )
             copies[-1].start()
     for place in range(count):
         index = block_of(place, four, count)
         table = order_table(step, pick(index, offsets[chunk::chunks]), scratch)
-        if load:
-            copies[place].wait()
-        rows = [held_ref[chunk * count + place, comp] for comp in range(3)]
+        if place == 0:
+            for copy in copies:
+                copy.wait()
+        start = pick(index, starts[chunk::chunks])
+        start = start if isinstance(start, int) else pl.multiple_of(start, LANES)
+        rows = [held_ref[comp, :, pl.ds(start, width)] for comp in range(3)]
         pad = jnp.zeros((LANES - 3 * modes, width), F32)
         high, low = halves(jnp.concatenate(rows + [pad], axis=0))
         both = jnp.concatenate([high, low], axis=0)
@@ -483,8 +486,6 @@
         values = [out[point * step : (point + 1) * step] for point in range(POINTS)]
         for at, value in enumerate(pack_lanes(values, modes)):
             send_refs[place][pl.ds(at * step, step), :] = value
-    for copy in copies[count:]:
-        copy.wait()
 
 
 def product_kernel(modes, step, count, dynamic, role, ids_ref, *refs):
@@ -907,9 +908,9 @@
         sent = call(
             functools.partial(pack_kernel, step, count, dynamic, chunk, chunks, starts, offsets),
             "pack",
-            blocks + [(chunks * count, 3, modes, 3 * LANES)] * load,
+            blocks + [velocity.shape] * load,
             (ids, source),
-            [table] + [pltpu.SemaphoreType.DMA((chunks * count,))] * load,
+            [table] + [pltpu.SemaphoreType.DMA((3 * modes // 8,))] * load,
             scalars=1,
             outside=load,
         )
@@ -938,6 +939,8 @@
         if role == 0:
             *sent, held_row = sent
             carry = [held_row]
+        if role == 1:
+            sent, local = lax.optimization_barrier((sent, local))
         local += swap_blocks(sent, dynamic)
 
     base, lines = call(

time: 82.3 us -> 83.9 us (1.019)
  starting transfers between devices: 32.7 us -> 34 us
  waiting for transfers between devices: 21.9 us -> 22.8 us
    ppermute x12, starting transfers between devices: 16.8 us -> 18.2 us  [swap_blocks(): lax.ppermute(blocks[place], 'four', [(i, i ^ offset_of(place, size)) for...]
    ppermute x12, waiting for transfers between devices: 4.43 us -> 5.34 us  [swap_blocks(): lax.ppermute(blocks[place], 'four', [(i, i ^ offset_of(place, size)) for...]
  transfers between devices with their start and end apart: 33 -> 33, of which waited for: 14 -> 17; matrix products, arithmetic and copies ran while one was open for 0% -> 0% of each run, Pallas kernels for 13% -> 12%
where the time goes in v8:
time: 83.9 us; the launch traced here: 83.8 us
  starting transfers between devices  34 us (41%)
  Pallas kernels  25.9 us (31%)
  waiting for transfers between devices  22.8 us (27%)
  between operations  0.97 us (1%)
    pallas_call x10, Pallas kernels, call(): pl.pallas_call(kernel, name=name, out_shape=[pltpu.VMEM(one.shape, one.dt...  25.9 us
    ppermute x12, starting transfers between devices, swap_blocks(): lax.ppermute(blocks[place], 'four', [(i, i ^ offset_of(place, size)) for...  18.2 us
    ppermute x9, waiting for transfers between devices, share_lines(): lax.ppermute(lines, 'dom', [(i, i ^ slot) for i in range(parts)])  14.2 us
    ppermute x9, starting transfers between devices, share_lines(): lax.ppermute(lines, 'dom', [(i, i ^ slot) for i in range(parts)])  13.7 us
    ppermute x12, waiting for transfers between devices, swap_blocks(): lax.ppermute(blocks[place], 'four', [(i, i ^ offset_of(place, size)) for...  5.34 us
    ppermute x12, waiting for transfers between devices, share_lines(): lax.ppermute(slots[slot], 'dom', [(i, i ^ 1) for i in range(parts)])  3.23 us
    ppermute x12, starting transfers between devices, share_lines(): lax.ppermute(slots[slot], 'dom', [(i, i ^ 1) for i in range(parts)])  2.12 us
  transfers between devices with their start and end apart: 33, of which 17 were waited for; matrix products, arithmetic and copies ran while one was open for 0% of the time, Pallas kernels for 12%

profile of v8, /device:TPU:0, one launch (start us, length us, event | category | flops | bytes accessed | tf_op | source)
XLA Modules:
  0.0 83.8 jit_solution(6351033054180818996)
XLA Ops:
  0.6 0.0 copy-start.2
  0.6 0.0 copy-start.3
  0.7 0.0 copy-start
  0.7 0.0 copy-start.1
  0.7 0.1 pad_add_fusion.ids_ref
  0.8 2.5 %pack.2 = (f32[216,128]{1,0:T(8,128)S(1)}, f32[216,128]{1,0:T(8,128)S(1)}, f32[216,128]{1,0:T(8,128)S(1)}, f32[216,128]{1,0:T(8,128)S(1)}, f32[3,32,2304]{2,1,0:T(8,128)S(1)}) custom-call(s32[2]{0:T(128)S(1)} %pad_add_fusion.ids_ref, f32[3,32,2304]{2,1,0:T(8,128)} %source_ref.1), custom_call_target="tpu_custom_call" | custom-call | tf_op jit(solution)/shard_map/pack/pallas_call | solution.py:847
  3.3 4.0 %collective-permute-start.3 = (f32[216,128]{1,0:T(8,128)S(1)}, f32[216,128]{1,0:T(8,128)S(1)}, u32[]{:S(2)}, u32[]{:S(2)}) collective-permute-start(f32[216,128]{1,0:T(8,128)S(1)} %get-tuple-element.59), channel_id=1, source_target_pairs={{0,3},{1,2},{2,1},{3,0},{4,7},{5,6},{6,5},{7,4},{8,11},{9,10},{10,... | collective-permute-start | bytes 331784 | tf_op jit(solution)/shard_map/ppermute | solution.py:870
  7.2 0.5 collective-permute-start.4
  7.8 0.1 collective-permute-start.5
  7.9 1.2 %pack.3 = (f32[216,128]{1,0:T(8,128)S(1)}, f32[216,128]{1,0:T(8,128)S(1)}, f32[216,128]{1,0:T(8,128)S(1)}, f32[216,128]{1,0:T(8,128)S(1)}) custom-call(s32[2]{0:T(128)S(1)} %pad_add_fusion.ids_ref, f32[3,32,2304]{2,1,0:T(8,128)S(1)} %get-tuple-element.53.source_ref), custom_call_target="tpu_custom_call" | custom-call | tf_op jit(solution)/shard_map/pack/pallas_call | solution.py:847
  9.0 2.9 %collective-permute-start = (f32[216,128]{1,0:T(8,128)S(1)}, f32[216,128]{1,0:T(8,128)S(1)}, u32[]{:S(2)}, u32[]{:S(2)}) collective-permute-start(f32[216,128]{1,0:T(8,128)S(1)} %get-tuple-element.55), channel_id=1, source_target_pairs={{0,3},{1,2},{2,1},{3,0},{4,7},{5,6},{6,5},{7,4},{8,11},{9,10},{10,... | collective-permute-start | bytes 331784 | tf_op jit(solution)/shard_map/ppermute | solution.py:870
  12.0 0.5 collective-permute-start.1
  12.5 0.0 collective-permute-done.3.refs_1_
  12.5 0.7 collective-permute-start.2
  13.2 0.6 collective-permute-done.4.refs_2_
  13.7 0.0 collective-permute-done.5.refs_3_
  13.7 0.0 copy-start.4
  13.8 2.4 %products.2 = (f32[168,128]{1,0:T(8,128)S(1)}, f32[168,128]{1,0:T(8,128)S(1)}, f32[168,128]{1,0:T(8,128)S(1)}, f32[168,128]{1,0:T(8,128)S(1)}, f32[4,48,128]{2,1,0:T(8,128)S(1)}) custom-call(s32[2]{0:T(128)S(1)} %pad_add_fusion.ids_ref, f32[216,128]{1,0:T(8,128)S(1)} %get-tuple-element.58.refs_0_, f32[216,128]{1,0:T(8,128)S(1)} %collective-permute-done.3.refs_1_, ...), custom_call_target="tpu_custom_call" | custom-call | tf_op jit(solution)/shard_map/products/pallas_call | solution.py:847
  16.1 0.0 copy-start.5
  16.1 0.0 copy-start.6
  16.1 3.9 %collective-permute-start.6 = (f32[168,128]{1,0:T(8,128)S(1)}, f32[168,128]{1,0:T(8,128)S(1)}, u32[]{:S(2)}, u32[]{:S(2)}) collective-permute-start(f32[168,128]{1,0:T(8,128)S(1)} %get-tuple-element.68), channel_id=1, source_target_pairs={{0,3},{1,2},{2,1},{3,0},{4,7},{5,6},{6,5},{7,4},{8,11},{9,10},{10,... | collective-permute-start | bytes 258056 | tf_op jit(solution)/shard_map/ppermute | solution.py:870
  20.1 0.0 collective-permute-start.7
  20.1 0.0 collective-permute-done.refs_1_
  20.1 0.6 collective-permute-start.8
  20.7 2.4 %products.3 = (f32[192,128]{1,0:T(8,128)S(1)}, f32[192,128]{1,0:T(8,128)S(1)}, f32[192,128]{1,0:T(8,128)S(1)}, f32[192,128]{1,0:T(8,128)S(1)}) custom-call(s32[2]{0:T(128)S(1)} %pad_add_fusion.ids_ref, f32[216,128]{1,0:T(8,128)S(1)} %get-tuple-element.54.refs_0_, f32[216,128]{1,0:T(8,128)S(1)} %collective-permute-done.refs_1_, ...), custom_call_target="tpu_custom_call" | custom-call | tf_op jit(solution)/shard_map/products/pallas_call | solution.py:847
  23.2 0.0 collective-permute-done.6.refs_1_
  23.2 1.6 %collective-permute-done.7.refs_2_ = f32[168,128]{1,0:T(8,128)S(1)} collective-permute-done((f32[168,128]{1,0:T(8,128)S(1)}, f32[168,128]{1,0:T(8,128)S(1)}, u32[]{:S(2)}, u32[]{:S(2)}) %collective-permute-start.7) | collective-permute-done | bytes 86048 | tf_op jit(solution)/shard_map/ppermute | solution.py:870
  24.8 2.5 %collective-permute-start.9 = (f32[192,128]{1,0:T(8,128)S(1)}, f32[192,128]{1,0:T(8,128)S(1)}, u32[]{:S(2)}, u32[]{:S(2)}) collective-permute-start(f32[192,128]{1,0:T(8,128)S(1)} %get-tuple-element.76), channel_id=1, source_target_pairs={{0,3},{1,2},{2,1},{3,0},{4,7},{5,6},{6,5},{7,4},{8,11},{9,10},{10,... | collective-permute-start | bytes 294920 | tf_op jit(solution)/shard_map/ppermute | solution.py:870
  27.3 1.0 %collective-permute-start.10 = (f32[192,128]{1,0:T(8,128)S(1)}, f32[192,128]{1,0:T(8,128)S(1)}, u32[]{:S(2)}, u32[]{:S(2)}) collective-permute-start(f32[192,128]{1,0:T(8,128)S(1)} %get-tuple-element.77), channel_id=1, source_target_pairs={{0,1},{1,0},{2,3},{3,2},{4,5},{5,4},{6,7},{7,6},{8,9},{9,8},{10,11... | collective-permute-start | bytes 294920 | tf_op jit(solution)/shard_map/ppermute | solution.py:870
  28.3 1.5 %collective-permute-start.11 = (f32[192,128]{1,0:T(8,128)S(1)}, f32[192,128]{1,0:T(8,128)S(1)}, u32[]{:S(2)}, u32[]{:S(2)}) collective-permute-start(f32[192,128]{1,0:T(8,128)S(1)} %get-tuple-element.78), channel_id=1, source_target_pairs={{0,2},{1,3},{2,0},{3,1},{4,6},{5,7},{6,4},{7,5},{8,10},{9,11},{10,... | collective-permute-start | bytes 294920 | tf_op jit(solution)/shard_map/ppermute | solution.py:870
  29.7 0.6 collective-permute-done.9.refs_5_
  30.3 1.6 %collective-permute-done.10.refs_6_ = f32[192,128]{1,0:T(8,128)S(1)} collective-permute-done((f32[192,128]{1,0:T(8,128)S(1)}, f32[192,128]{1,0:T(8,128)S(1)}, u32[]{:S(2)}, u32[]{:S(2)}) %collective-permute-start.10) | collective-permute-done | bytes 98336 | tf_op jit(solution)/shard_map/ppermute | solution.py:870
  31.9 1.0 %collective-permute-done.11.refs_7_ = f32[192,128]{1,0:T(8,128)S(1)} collective-permute-done((f32[192,128]{1,0:T(8,128)S(1)}, f32[192,128]{1,0:T(8,128)S(1)}, u32[]{:S(2)}, u32[]{:S(2)}) %collective-permute-start.11) | collective-permute-done | bytes 98336 | tf_op jit(solution)/shard_map/ppermute | solution.py:870
  32.9 1.9 %first.1 = (f32[2304,128]{1,0:T(8,128)S(1)}, f32[240,128]{1,0:T(8,128)S(1)}) custom-call(s32[2]{0:T(128)S(1)} %pad_add_fusion.ids_ref, s32[1,4]{1,0:T(1,128)S(1)} %copy-done.4, f32[168,128]{1,0:T(8,128)S(1)} %get-tuple-element.71.refs_0_, f32[168,128]{1,0:T(8,128)S(1)} %collective-permute-done.6.refs_1_, f32[168,128]{1,0:T(8,128)S(1)} %collective-permute-done.7.refs_2_, ...), custom_call_target="tpu_custom_call" | custom-call | tf_op jit(solution)/shard_map/first/pallas_call | solution.py:847
  34.8 4.1 %collective-permute-start.17 = (f32[240,128]{1,0:T(8,128)S(1)}, f32[240,128]{1,0:T(8,128)S(1)}, u32[]{:S(2)}, u32[]{:S(2)}) collective-permute-start(f32[240,128]{1,0:T(8,128)S(1)} %get-tuple-element.79.refs_0_.refs_8_), channel_id=1, source_target_pairs={{0,24},{4,28},{8,16},{12,20},{16,8},{20,12},{24,0},{28,4},{1,25},{... | collective-permute-start | bytes 368648 | tf_op jit(solution)/shard_map/ppermute | solution.py:880
  39.0 0.6 collective-permute-start.13
  39.6 2.3 %collective-permute-done.17.refs_6_ = f32[240,128]{1,0:T(8,128)S(1)} collective-permute-done((f32[240,128]{1,0:T(8,128)S(1)}, f32[240,128]{1,0:T(8,128)S(1)}, u32[]{:S(2)}, u32[]{:S(2)}) %collective-permute-start.17) | collective-permute-done | bytes 122912 | tf_op jit(solution)/shard_map/ppermute | solution.py:880
  41.9 3.3 %collective-permute-done.15.refs_4_ = f32[240,128]{1,0:T(8,128)S(1)} collective-permute-done((f32[240,128]{1,0:T(8,128)S(1)}, f32[240,128]{1,0:T(8,128)S(1)}, u32[]{:S(2)}, u32[]{:S(2)}) %collective-permute-start.15) | collective-permute-done | bytes 122912 | tf_op jit(solution)/shard_map/ppermute | solution.py:880
  45.2 0.5 collective-permute-start.14
  45.7 0.8 collective-permute-done.16.refs_5_
  46.5 0.2 collective-permute-done.14.refs_3_
  46.7 4.5 %second.1 = (f32[2304,128]{1,0:T(8,128)S(1)}, f32[2304,128]{1,0:T(8,128)S(1)}, f32[2304,128]{1,0:T(8,128)S(1)}, f32[240,128]{1,0:T(8,128)S(1)}, f32[8,128]{1,0:T(8,128)S(1)}) custom-call(s32[2]{0:T(128)S(1)} %pad_add_fusion.ids_ref, s32[1,4]{1,0:T(1,128)S(1)} %copy-done.4, s32[1,4]{1,0:T(1,128)S(1)} %copy-done.5, ...), custom_call_target="tpu_custom_call", output_to_operand_aliasing={{0}: (13, {})} | custom-call | tf_op jit(solution)/shard_map/second/pallas_call | solution.py:847
  51.2 2.4 %collective-permute-start.24 = (f32[240,128]{1,0:T(8,128)S(1)}, f32[240,128]{1,0:T(8,128)S(1)}, u32[]{:S(2)}, u32[]{:S(2)}) collective-permute-start(f32[240,128]{1,0:T(8,128)S(1)} %get-tuple-element.81.refs_0_.refs_8_), channel_id=1, source_target_pairs={{0,24},{4,28},{8,16},{12,20},{16,8},{20,12},{24,0},{28,4},{1,25},{... | collective-permute-start | bytes 368648 | tf_op jit(solution)/shard_map/ppermute | solution.py:880
  53.6 0.3 collective-permute-start.22
  53.9 1.8 %collective-permute-start.20 = (f32[240,128]{1,0:T(8,128)S(1)}, f32[240,128]{1,0:T(8,128)S(1)}, u32[]{:S(2)}, u32[]{:S(2)}) collective-permute-start(f32[240,128]{1,0:T(8,128)S(1)} %get-tuple-element.81.refs_0_.refs_8_), channel_id=1, source_target_pairs={{0,8},{4,12},{8,0},{12,4},{16,24},{20,28},{24,16},{28,20},{1,9},{5... | collective-permute-start | bytes 368648 | tf_op jit(solution)/shard_map/ppermute | solution.py:880
  55.6 2.0 %turn.2 = (f32[96,2304]{1,0:T(8,128)S(1)}, f32[96,2304]{1,0:T(8,128)S(1)}, bf16[192,2304]{1,0:T(8,128)(2,1)S(1)}) custom-call(f32[2304,128]{1,0:T(8,128)S(1)} %get-tuple-element.82.refs_0_, f32[2304,128]{1,0:T(8,128)S(1)} %get-tuple-element.83.refs_1_.refs_9_), custom_call_target="tpu_custom_call" | custom-call | tf_op jit(solution)/shard_map/turn/pallas_call | solution.py:847
  57.7 1.6 %collective-permute-done.24.refs_6_ = f32[240,128]{1,0:T(8,128)S(1)} collective-permute-done((f32[240,128]{1,0:T(8,128)S(1)}, f32[240,128]{1,0:T(8,128)S(1)}, u32[]{:S(2)}, u32[]{:S(2)}) %collective-permute-start.24) | collective-permute-done | bytes 122912 | tf_op jit(solution)/shard_map/ppermute | solution.py:880
  59.3 5.7 %collective-permute-done.22.refs_4_ = f32[240,128]{1,0:T(8,128)S(1)} collective-permute-done((f32[240,128]{1,0:T(8,128)S(1)}, f32[240,128]{1,0:T(8,128)S(1)}, u32[]{:S(2)}, u32[]{:S(2)}) %collective-permute-start.22) | collective-permute-done | bytes 122912 | tf_op jit(solution)/shard_map/ppermute | solution.py:880
  65.1 0.5 collective-permute-start.21
  65.6 0.0 collective-permute-start.25
  65.6 0.8 collective-permute-done.23.refs_5_
  66.4 0.2 collective-permute-done.21.refs_3_
  66.6 0.3 collective-permute-done.25.refs_7_
  66.9 3.5 %third.1 = (f32[2304,128]{1,0:T(8,128)S(1)}, f32[2304,128]{1,0:T(8,128)S(1)}, f32[2304,128]{1,0:T(8,128)S(1)}, f32[128,128]{1,0:T(8,128)S(1)}) custom-call(s32[2]{0:T(128)S(1)} %pad_add_fusion.ids_ref, s32[1,4]{1,0:T(1,128)S(1)} %copy-done.4, s32[1,4]{1,0:T(1,128)S(1)} %copy-done.5, s32[1,4]{1,0:T(1,128)S(1)} %copy-done.6, ...), custom_call_target="tpu_custom_call", output_to_operand_aliasing={{0}: (15, {})} | custom-call | tf_op jit(solution)/shard_map/third/pallas_call | solution.py:847
  70.5 1.5 %collective-permute-start.31 = (f32[128,128]{1,0:T(8,128)S(1)}, f32[128,128]{1,0:T(8,128)S(1)}, u32[]{:S(2)}, u32[]{:S(2)}) collective-permute-start(f32[128,128]{1,0:T(8,128)S(1)} %get-tuple-element.90.refs_0_), channel_id=1, source_target_pairs={{0,24},{4,28},{8,16},{12,20},{16,8},{20,12},{24,0},{28,4},{1,25},{... | collective-permute-start | bytes 196616 | tf_op jit(solution)/shard_map/ppermute | solution.py:880
  72.0 2.9 %collective-permute-start.27 = (f32[128,128]{1,0:T(8,128)S(1)}, f32[128,128]{1,0:T(8,128)S(1)}, u32[]{:S(2)}, u32[]{:S(2)}) collective-permute-start(f32[128,128]{1,0:T(8,128)S(1)} %get-tuple-element.90.refs_0_), channel_id=1, source_target_pairs={{0,8},{4,12},{8,0},{12,4},{16,24},{20,28},{24,16},{28,20},{1,9},{5... | collective-permute-start | bytes 196616 | tf_op jit(solution)/shard_map/ppermute | solution.py:880
  74.9 2.5 %turn.3 = (f32[96,2304]{1,0:T(8,128)S(1)}, f32[96,2304]{1,0:T(8,128)S(1)}, f32[96,2304]{1,0:T(8,128)S(1)}) custom-call(f32[2304,128]{1,0:T(8,128)S(1)} %get-tuple-element.91.refs_0_, f32[2304,128]{1,0:T(8,128)S(1)} %get-tuple-element.92.refs_1_, f32[2304,128]{1,0:T(8,128)S(1)} %get-tuple-element.93.refs_2_), custom_call_target="tpu_custom_call" | custom-call | tf_op jit(solution)/shard_map/turn/pallas_call | solution.py:847
  77.4 0.6 collective-permute-start.32
  78.0 1.2 %collective-permute-done.29.refs_4_ = f32[128,128]{1,0:T(8,128)S(1)} collective-permute-done((f32[128,128]{1,0:T(8,128)S(1)}, f32[128,128]{1,0:T(8,128)S(1)}, u32[]{:S(2)}, u32[]{:S(2)}) %collective-permute-start.29) | collective-permute-done | bytes 65568 | tf_op jit(solution)/shard_map/ppermute | solution.py:880
  79.2 0.0 collective-permute-start.30
  79.2 0.5 collective-permute-start.28
  79.7 0.7 collective-permute-done.30.refs_5_
  80.5 0.2 collective-permute-done.28.refs_3_
  80.6 3.0 %last.1 = (f32[3,32,2304]{2,1,0:T(8,128)}, f32[3,32,2304]{2,1,0:T(8,128)}) custom-call(s32[2]{0:T(128)S(1)} %pad_add_fusion.ids_ref, s32[1,4]{1,0:T(1,128)S(1)} %copy-done.4, s32[1,4]{1,0:T(1,128)S(1)} %copy-done.5, s32[1,4]{1,0:T(1,128)S(1)} %copy-done.6, f32[128,128]{1,0:T(8,128)S(1)} %get-tuple-element.90.refs_0_, ...), custom_call_target="tpu_custom_call" | custom-call | tf_op jit(solution)/shard_map/last/pallas_call | solution.py:847
  (27 shorter events, 0.1 us)
Async XLA Ops:
  0.6 13.1 %copy-start.2 = (bf16[256,128]{1,0:T(8,128)(2,1)S(1)}, bf16[256,128]{1,0:T(8,128)(2,1)}, u32[]{:S(2)}) copy-start(bf16[256,128]{1,0:T(8,128)(2,1)} %constant.20.clone.refs_7_) | copy-start | bytes 196612
  0.6 13.1 %copy-start.3 = (bf16[256,128]{1,0:T(8,128)(2,1)S(1)}, bf16[256,128]{1,0:T(8,128)(2,1)}, u32[]{:S(2)}) copy-start(bf16[256,128]{1,0:T(8,128)(2,1)} %constant.19.clone.refs_6_) | copy-start | bytes 196612
  0.7 13.1 %copy-start = (bf16[512,384]{1,0:T(8,128)(2,1)S(1)}, bf16[512,384]{1,0:T(8,128)(2,1)}, u32[]{:S(2)}) copy-start(bf16[512,384]{1,0:T(8,128)(2,1)} %constant.18.clone.refs_5_) | copy-start | bytes 1179652
  0.7 13.1 %copy-start.1 = (bf16[512,384]{1,0:T(8,128)(2,1)S(1)}, bf16[512,384]{1,0:T(8,128)(2,1)}, u32[]{:S(2)}) copy-start(bf16[512,384]{1,0:T(8,128)(2,1)} %constant.17.clone.refs_4_) | copy-start | bytes 1179652
  3.3 9.2 %collective-permute-start.3 = (f32[216,128]{1,0:T(8,128)S(1)}, f32[216,128]{1,0:T(8,128)S(1)}, u32[]{:S(2)}, u32[]{:S(2)}) collective-permute-start(f32[216,128]{1,0:T(8,128)S(1)} %get-tuple-element.59), channel_id=1, source_target_pairs={{0,3},{1,2},{2,1},{3,0},{4,7},{5,6},{6,5},{7,4},{8,11},{9,10},{10,... | collective-permute-start | bytes 331784 | tf_op jit(solution)/shard_map/ppermute | solution.py:870
  7.2 6.5 %collective-permute-start.4 = (f32[216,128]{1,0:T(8,128)S(1)}, f32[216,128]{1,0:T(8,128)S(1)}, u32[]{:S(2)}, u32[]{:S(2)}) collective-permute-start(f32[216,128]{1,0:T(8,128)S(1)} %get-tuple-element.60), channel_id=1, source_target_pairs={{0,1},{1,0},{2,3},{3,2},{4,5},{5,4},{6,7},{7,6},{8,9},{9,8},{10,11... | collective-permute-start | bytes 331784 | tf_op jit(solution)/shard_map/ppermute | solution.py:870
  7.8 5.9 %collective-permute-start.5 = (f32[216,128]{1,0:T(8,128)S(1)}, f32[216,128]{1,0:T(8,128)S(1)}, u32[]{:S(2)}, u32[]{:S(2)}) collective-permute-start(f32[216,128]{1,0:T(8,128)S(1)} %get-tuple-element.61), channel_id=1, source_target_pairs={{0,2},{1,3},{2,0},{3,1},{4,6},{5,7},{6,4},{7,5},{8,10},{9,11},{10,... | collective-permute-start | bytes 331784 | tf_op jit(solution)/shard_map/ppermute | solution.py:870
  9.0 11.0 %collective-permute-start = (f32[216,128]{1,0:T(8,128)S(1)}, f32[216,128]{1,0:T(8,128)S(1)}, u32[]{:S(2)}, u32[]{:S(2)}) collective-permute-start(f32[216,128]{1,0:T(8,128)S(1)} %get-tuple-element.55), channel_id=1, source_target_pairs={{0,3},{1,2},{2,1},{3,0},{4,7},{5,6},{6,5},{7,4},{8,11},{9,10},{10,... | collective-permute-start | bytes 331784 | tf_op jit(solution)/shard_map/ppermute | solution.py:870
  12.0 8.8 %collective-permute-start.1 = (f32[216,128]{1,0:T(8,128)S(1)}, f32[216,128]{1,0:T(8,128)S(1)}, u32[]{:S(2)}, u32[]{:S(2)}) collective-permute-start(f32[216,128]{1,0:T(8,128)S(1)} %get-tuple-element.56), channel_id=1, source_target_pairs={{0,1},{1,0},{2,3},{3,2},{4,5},{5,4},{6,7},{7,6},{8,9},{9,8},{10,11... | collective-permute-start | bytes 331784 | tf_op jit(solution)/shard_map/ppermute | solution.py:870
  12.5 8.2 %collective-permute-start.2 = (f32[216,128]{1,0:T(8,128)S(1)}, f32[216,128]{1,0:T(8,128)S(1)}, u32[]{:S(2)}, u32[]{:S(2)}) collective-permute-start(f32[216,128]{1,0:T(8,128)S(1)} %get-tuple-element.57), channel_id=1, source_target_pairs={{0,2},{1,3},{2,0},{3,1},{4,6},{5,7},{6,4},{7,5},{8,10},{9,11},{10,... | collective-permute-start | bytes 331784 | tf_op jit(solution)/shard_map/ppermute | solution.py:870
  13.7 19.2 %copy-start.4 = (s32[1,4]{1,0:T(1,128)S(1)}, s32[1,4]{1,0:T(1,128)}, u32[]{:S(2)}) copy-start(s32[1,4]{1,0:T(1,128)} %partner_ref.7) | copy-start | bytes 52
  16.1 30.6 %copy-start.5 = (s32[1,4]{1,0:T(1,128)S(1)}, s32[1,4]{1,0:T(1,128)}, u32[]{:S(2)}) copy-start(s32[1,4]{1,0:T(1,128)} %side_ref.5) | copy-start | bytes 52
  16.1 30.6 %copy-start.6 = (s32[1,4]{1,0:T(1,128)S(1)}, s32[1,4]{1,0:T(1,128)}, u32[]{:S(2)}) copy-start(s32[1,4]{1,0:T(1,128)} %flip_ref.5) | copy-start | bytes 52
  16.1 7.0 %collective-permute-start.6 = (f32[168,128]{1,0:T(8,128)S(1)}, f32[168,128]{1,0:T(8,128)S(1)}, u32[]{:S(2)}, u32[]{:S(2)}) collective-permute-start(f32[168,128]{1,0:T(8,128)S(1)} %get-tuple-element.68), channel_id=1, source_target_pairs={{0,3},{1,2},{2,1},{3,0},{4,7},{5,6},{6,5},{7,4},{8,11},{9,10},{10,... | collective-permute-start | bytes 258056 | tf_op jit(solution)/shard_map/ppermute | solution.py:870
  20.1 4.7 %collective-permute-start.7 = (f32[168,128]{1,0:T(8,128)S(1)}, f32[168,128]{1,0:T(8,128)S(1)}, u32[]{:S(2)}, u32[]{:S(2)}) collective-permute-start(f32[168,128]{1,0:T(8,128)S(1)} %get-tuple-element.69), channel_id=1, source_target_pairs={{0,1},{1,0},{2,3},{3,2},{4,5},{5,4},{6,7},{7,6},{8,9},{9,8},{10,11... | collective-permute-start | bytes 258056 | tf_op jit(solution)/shard_map/ppermute | solution.py:870
  20.1 4.7 %collective-permute-start.8 = (f32[168,128]{1,0:T(8,128)S(1)}, f32[168,128]{1,0:T(8,128)S(1)}, u32[]{:S(2)}, u32[]{:S(2)}) collective-permute-start(f32[168,128]{1,0:T(8,128)S(1)} %get-tuple-element.70), channel_id=1, source_target_pairs={{0,2},{1,3},{2,0},{3,1},{4,6},{5,7},{6,4},{7,5},{8,10},{9,11},{10,... | collective-permute-start | bytes 258056 | tf_op jit(solution)/shard_map/ppermute | solution.py:870
  24.8 5.5 %collective-permute-start.9 = (f32[192,128]{1,0:T(8,128)S(1)}, f32[192,128]{1,0:T(8,128)S(1)}, u32[]{:S(2)}, u32[]{:S(2)}) collective-permute-start(f32[192,128]{1,0:T(8,128)S(1)} %get-tuple-element.76), channel_id=1, source_target_pairs={{0,3},{1,2},{2,1},{3,0},{4,7},{5,6},{6,5},{7,4},{8,11},{9,10},{10,... | collective-permute-start | bytes 294920 | tf_op jit(solution)/shard_map/ppermute | solution.py:870
  27.3 4.7 %collective-permute-start.10 = (f32[192,128]{1,0:T(8,128)S(1)}, f32[192,128]{1,0:T(8,128)S(1)}, u32[]{:S(2)}, u32[]{:S(2)}) collective-permute-start(f32[192,128]{1,0:T(8,128)S(1)} %get-tuple-element.77), channel_id=1, source_target_pairs={{0,1},{1,0},{2,3},{3,2},{4,5},{5,4},{6,7},{7,6},{8,9},{9,8},{10,11... | collective-permute-start | bytes 294920 | tf_op jit(solution)/shard_map/ppermute | solution.py:870
  28.3 4.6 %collective-permute-start.11 = (f32[192,128]{1,0:T(8,128)S(1)}, f32[192,128]{1,0:T(8,128)S(1)}, u32[]{:S(2)}, u32[]{:S(2)}) collective-permute-start(f32[192,128]{1,0:T(8,128)S(1)} %get-tuple-element.78), channel_id=1, source_target_pairs={{0,2},{1,3},{2,0},{3,1},{4,6},{5,7},{6,4},{7,5},{8,10},{9,11},{10,... | collective-permute-start | bytes 294920 | tf_op jit(solution)/shard_map/ppermute | solution.py:870
  34.8 7.1 %collective-permute-start.17 = (f32[240,128]{1,0:T(8,128)S(1)}, f32[240,128]{1,0:T(8,128)S(1)}, u32[]{:S(2)}, u32[]{:S(2)}) collective-permute-start(f32[240,128]{1,0:T(8,128)S(1)} %get-tuple-element.79.refs_0_.refs_8_), channel_id=1, source_target_pairs={{0,24},{4,28},{8,16},{12,20},{16,8},{20,12},{24,0},{28,4},{1,25},{... | collective-permute-start | bytes 368648 | tf_op jit(solution)/shard_map/ppermute | solution.py:880
  39.0 6.2 %collective-permute-start.15 = (f32[240,128]{1,0:T(8,128)S(1)}, f32[240,128]{1,0:T(8,128)S(1)}, u32[]{:S(2)}, u32[]{:S(2)}) collective-permute-start(f32[240,128]{1,0:T(8,128)S(1)} %get-tuple-element.79.refs_0_.refs_8_), channel_id=1, source_target_pairs={{0,16},{4,20},{8,24},{12,28},{16,0},{20,4},{24,8},{28,12},{1,17},{... | collective-permute-start | bytes 368648 | tf_op jit(solution)/shard_map/ppermute | solution.py:880
  39.0 6.2 %collective-permute-start.13 = (f32[240,128]{1,0:T(8,128)S(1)}, f32[240,128]{1,0:T(8,128)S(1)}, u32[]{:S(2)}, u32[]{:S(2)}) collective-permute-start(f32[240,128]{1,0:T(8,128)S(1)} %get-tuple-element.79.refs_0_.refs_8_), channel_id=1, source_target_pairs={{0,8},{4,12},{8,0},{12,4},{16,24},{20,28},{24,16},{28,20},{1,9},{5... | collective-permute-start | bytes 368648 | tf_op jit(solution)/shard_map/ppermute | solution.py:880
  39.6 6.1 %collective-permute-start.12 = (f32[240,128]{1,0:T(8,128)S(1)}, f32[240,128]{1,0:T(8,128)S(1)}, u32[]{:S(2)}, u32[]{:S(2)}) collective-permute-start(f32[240,128]{1,0:T(8,128)S(1)} %get-tuple-element.79.refs_0_.refs_8_), channel_id=1, source_target_pairs={{0,4},{4,0},{8,12},{12,8},{16,20},{20,16},{24,28},{28,24},{1,5},{5... | collective-permute-start | bytes 368648 | tf_op jit(solution)/shard_map/ppermute | solution.py:884
  41.9 3.8 %collective-permute-start.18 = (f32[240,128]{1,0:T(8,128)S(1)}, f32[240,128]{1,0:T(8,128)S(1)}, u32[]{:S(2)}, u32[]{:S(2)}) collective-permute-start(f32[240,128]{1,0:T(8,128)S(1)} %collective-permute-done.17.refs_6_), channel_id=1, source_target_pairs={{0,4},{4,0},{8,12},{12,8},{16,20},{20,16},{24,28},{28,24},{1,5},{5... | collective-permute-start | bytes 368648 | tf_op jit(solution)/shard_map/ppermute | solution.py:884
  45.2 1.3 %collective-permute-start.16 = (f32[240,128]{1,0:T(8,128)S(1)}, f32[240,128]{1,0:T(8,128)S(1)}, u32[]{:S(2)}, u32[]{:S(2)}) collective-permute-start(f32[240,128]{1,0:T(8,128)S(1)} %collective-permute-done.15.refs_4_), channel_id=1, source_target_pairs={{0,4},{4,0},{8,12},{12,8},{16,20},{20,16},{24,28},{28,24},{1,5},{5... | collective-permute-start | bytes 368648 | tf_op jit(solution)/shard_map/ppermute | solution.py:884
  45.2 1.5 %collective-permute-start.14 = (f32[240,128]{1,0:T(8,128)S(1)}, f32[240,128]{1,0:T(8,128)S(1)}, u32[]{:S(2)}, u32[]{:S(2)}) collective-permute-start(f32[240,128]{1,0:T(8,128)S(1)} %collective-permute-done.13.refs_2_), channel_id=1, source_target_pairs={{0,4},{4,0},{8,12},{12,8},{16,20},{20,16},{24,28},{28,24},{1,5},{5... | collective-permute-start | bytes 368648 | tf_op jit(solution)/shard_map/ppermute | solution.py:884
  51.2 8.1 %collective-permute-start.24 = (f32[240,128]{1,0:T(8,128)S(1)}, f32[240,128]{1,0:T(8,128)S(1)}, u32[]{:S(2)}, u32[]{:S(2)}) collective-permute-start(f32[240,128]{1,0:T(8,128)S(1)} %get-tuple-element.81.refs_0_.refs_8_), channel_id=1, source_target_pairs={{0,24},{4,28},{8,16},{12,20},{16,8},{20,12},{24,0},{28,4},{1,25},{... | collective-permute-start | bytes 368648 | tf_op jit(solution)/shard_map/ppermute | solution.py:880
  53.6 11.5 %collective-permute-start.22 = (f32[240,128]{1,0:T(8,128)S(1)}, f32[240,128]{1,0:T(8,128)S(1)}, u32[]{:S(2)}, u32[]{:S(2)}) collective-permute-start(f32[240,128]{1,0:T(8,128)S(1)} %get-tuple-element.81.refs_0_.refs_8_), channel_id=1, source_target_pairs={{0,16},{4,20},{8,24},{12,28},{16,0},{20,4},{24,8},{28,12},{1,17},{... | collective-permute-start | bytes 368648 | tf_op jit(solution)/shard_map/ppermute | solution.py:880
  53.9 11.2 %collective-permute-start.20 = (f32[240,128]{1,0:T(8,128)S(1)}, f32[240,128]{1,0:T(8,128)S(1)}, u32[]{:S(2)}, u32[]{:S(2)}) collective-permute-start(f32[240,128]{1,0:T(8,128)S(1)} %get-tuple-element.81.refs_0_.refs_8_), channel_id=1, source_target_pairs={{0,8},{4,12},{8,0},{12,4},{16,24},{20,28},{24,16},{28,20},{1,9},{5... | collective-permute-start | bytes 368648 | tf_op jit(solution)/shard_map/ppermute | solution.py:880
  55.6 9.9 %collective-permute-start.19 = (f32[240,128]{1,0:T(8,128)S(1)}, f32[240,128]{1,0:T(8,128)S(1)}, u32[]{:S(2)}, u32[]{:S(2)}) collective-permute-start(f32[240,128]{1,0:T(8,128)S(1)} %get-tuple-element.81.refs_0_.refs_8_), channel_id=1, source_target_pairs={{0,4},{4,0},{8,12},{12,8},{16,20},{20,16},{24,28},{28,24},{1,5},{5... | collective-permute-start | bytes 368648 | tf_op jit(solution)/shard_map/ppermute | solution.py:884
  65.1 1.3 %collective-permute-start.23 = (f32[240,128]{1,0:T(8,128)S(1)}, f32[240,128]{1,0:T(8,128)S(1)}, u32[]{:S(2)}, u32[]{:S(2)}) collective-permute-start(f32[240,128]{1,0:T(8,128)S(1)} %collective-permute-done.22.refs_4_), channel_id=1, source_target_pairs={{0,4},{4,0},{8,12},{12,8},{16,20},{20,16},{24,28},{28,24},{1,5},{5... | collective-permute-start | bytes 368648 | tf_op jit(solution)/shard_map/ppermute | solution.py:884
  65.1 1.5 %collective-permute-start.21 = (f32[240,128]{1,0:T(8,128)S(1)}, f32[240,128]{1,0:T(8,128)S(1)}, u32[]{:S(2)}, u32[]{:S(2)}) collective-permute-start(f32[240,128]{1,0:T(8,128)S(1)} %collective-permute-done.20.refs_2_), channel_id=1, source_target_pairs={{0,4},{4,0},{8,12},{12,8},{16,20},{20,16},{24,28},{28,24},{1,5},{5... | collective-permute-start | bytes 368648 | tf_op jit(solution)/shard_map/ppermute | solution.py:884
  65.6 1.3 %collective-permute-start.25 = (f32[240,128]{1,0:T(8,128)S(1)}, f32[240,128]{1,0:T(8,128)S(1)}, u32[]{:S(2)}, u32[]{:S(2)}) collective-permute-start(f32[240,128]{1,0:T(8,128)S(1)} %collective-permute-done.24.refs_6_), channel_id=1, source_target_pairs={{0,4},{4,0},{8,12},{12,8},{16,20},{20,16},{24,28},{28,24},{1,5},{5... | collective-permute-start | bytes 368648 | tf_op jit(solution)/shard_map/ppermute | solution.py:884
  70.5 7.0 %collective-permute-start.31 = (f32[128,128]{1,0:T(8,128)S(1)}, f32[128,128]{1,0:T(8,128)S(1)}, u32[]{:S(2)}, u32[]{:S(2)}) collective-permute-start(f32[128,128]{1,0:T(8,128)S(1)} %get-tuple-element.90.refs_0_), channel_id=1, source_target_pairs={{0,24},{4,28},{8,16},{12,20},{16,8},{20,12},{24,0},{28,4},{1,25},{... | collective-permute-start | bytes 196616 | tf_op jit(solution)/shard_map/ppermute | solution.py:880
  72.0 7.2 %collective-permute-start.29 = (f32[128,128]{1,0:T(8,128)S(1)}, f32[128,128]{1,0:T(8,128)S(1)}, u32[]{:S(2)}, u32[]{:S(2)}) collective-permute-start(f32[128,128]{1,0:T(8,128)S(1)} %get-tuple-element.90.refs_0_), channel_id=1, source_target_pairs={{0,16},{4,20},{8,24},{12,28},{16,0},{20,4},{24,8},{28,12},{1,17},{... | collective-permute-start | bytes 196616 | tf_op jit(solution)/shard_map/ppermute | solution.py:880
  72.0 7.3 %collective-permute-start.27 = (f32[128,128]{1,0:T(8,128)S(1)}, f32[128,128]{1,0:T(8,128)S(1)}, u32[]{:S(2)}, u32[]{:S(2)}) collective-permute-start(f32[128,128]{1,0:T(8,128)S(1)} %get-tuple-element.90.refs_0_), channel_id=1, source_target_pairs={{0,8},{4,12},{8,0},{12,4},{16,24},{20,28},{24,16},{28,20},{1,9},{5... | collective-permute-start | bytes 196616 | tf_op jit(solution)/shard_map/ppermute | solution.py:880
  74.9 4.8 %collective-permute-start.26 = (f32[128,128]{1,0:T(8,128)S(1)}, f32[128,128]{1,0:T(8,128)S(1)}, u32[]{:S(2)}, u32[]{:S(2)}) collective-permute-start(f32[128,128]{1,0:T(8,128)S(1)} %get-tuple-element.90.refs_0_), channel_id=1, source_target_pairs={{0,4},{4,0},{8,12},{12,8},{16,20},{20,16},{24,28},{28,24},{1,5},{5... | collective-permute-start | bytes 196616 | tf_op jit(solution)/shard_map/ppermute | solution.py:884
  77.4 2.3 %collective-permute-start.32 = (f32[128,128]{1,0:T(8,128)S(1)}, f32[128,128]{1,0:T(8,128)S(1)}, u32[]{:S(2)}, u32[]{:S(2)}) collective-permute-start(f32[128,128]{1,0:T(8,128)S(1)} %collective-permute-done.31.refs_6_), channel_id=1, source_target_pairs={{0,4},{4,0},{8,12},{12,8},{16,20},{20,16},{24,28},{28,24},{1,5},{5... | collective-permute-start | bytes 196616 | tf_op jit(solution)/shard_map/ppermute | solution.py:884
  79.2 1.3 %collective-permute-start.30 = (f32[128,128]{1,0:T(8,128)S(1)}, f32[128,128]{1,0:T(8,128)S(1)}, u32[]{:S(2)}, u32[]{:S(2)}) collective-permute-start(f32[128,128]{1,0:T(8,128)S(1)} %collective-permute-done.29.refs_4_), channel_id=1, source_target_pairs={{0,4},{4,0},{8,12},{12,8},{16,20},{20,16},{24,28},{28,24},{1,5},{5... | collective-permute-start | bytes 196616 | tf_op jit(solution)/shard_map/ppermute | solution.py:884
  79.2 1.4 %collective-permute-start.28 = (f32[128,128]{1,0:T(8,128)S(1)}, f32[128,128]{1,0:T(8,128)S(1)}, u32[]{:S(2)}, u32[]{:S(2)}) collective-permute-start(f32[128,128]{1,0:T(8,128)S(1)} %collective-permute-done.27.refs_2_), channel_id=1, source_target_pairs={{0,4},{4,0},{8,12},{12,8},{16,20},{20,16},{24,28},{28,24},{1,5},{5... | collective-permute-start | bytes 196616 | tf_op jit(solution)/shard_map/ppermute | solution.py:884

commit v9 on v8

--- a/solution.py
+++ b/solution.py
@@ -460,10 +460,9 @@
     four = ids_ref[1] if dynamic else 0
     copies = []
     if load:
-        for slot in range(3 * modes // 8):
-            at = slot // (modes // 8), pl.ds(slot % (modes // 8) * 8, 8)
+        for comp in range(3):
             copies.append(
-                pltpu.make_async_copy(source_ref.at[at], held_ref.at[at], refs[-1].at[slot])
+                pltpu.make_async_copy(source_ref.at[comp], held_ref.at[comp], refs[-1].at[comp])
             )
             copies[-1].start()
     for place in range(count):
@@ -576,7 +575,7 @@
                 left = jnp.where(ex == iy, pltpu.roll(line[0], iy, 0) if iy else line[0], left)
                 sent += line[1:]
             values = sent + [left]
-            values += [left] * (-len(values) % 4)
+            values += [left] * (32 - len(values))
         for at, value in enumerate(pack_lanes(values, modes)):
             send_refs[place][pl.ds(at * step, step), :] = value
 
@@ -910,7 +909,7 @@
             "pack",
             blocks + [velocity.shape] * load,
             (ids, source),
-            [table] + [pltpu.SemaphoreType.DMA((3 * modes // 8,))] * load,
+            [table] + [pltpu.SemaphoreType.DMA((3,))] * load,
             scalars=1,
             outside=load,
         )
@@ -921,7 +920,7 @@
     carry = []
     for chunk in range(chunks):
         role = chunk if lean else None
-        out = [((21, 24)[chunk] * step, LANES)] * count if lean else blocks
+        out = [(24 * step, LANES)] * count if lean else blocks
         sent = call(
             functools.partial(product_kernel, modes, step, count, dynamic, role),
             "products",
@@ -939,8 +938,6 @@
         if role == 0:
             *sent, held_row = sent
             carry = [held_row]
-        if role == 1:
-            sent, local = lax.optimization_barrier((sent, local))
         local += swap_blocks(sent, dynamic)
 
     base, lines = call(

time: 83.9 us -> 81.4 us (0.970)
  starting transfers between devices: 34 us -> 32.7 us
    ppermute x12, starting transfers between devices: 18.2 us -> 16.9 us  [swap_blocks(): lax.ppermute(blocks[place], 'four', [(i, i ^ offset_of(place, size)) for...]
  transfers between devices with their start and end apart: 33 -> 33, of which waited for: 17 -> 15; matrix products, arithmetic and copies ran while one was open for 0% -> 0% of each run, Pallas kernels for 12% -> 13%
where the time goes in v9:
time: 81.4 us; the launch traced here: 81.2 us
  starting transfers between devices  32.7 us (40%)
  Pallas kernels  25.2 us (31%)
  waiting for transfers between devices  22.2 us (27%)
  between operations  0.96 us (1%)
    pallas_call x10, Pallas kernels, call(): pl.pallas_call(kernel, name=name, out_shape=[pltpu.VMEM(one.shape, one.dt...  25.2 us
    ppermute x12, starting transfers between devices, swap_blocks(): lax.ppermute(blocks[place], 'four', [(i, i ^ offset_of(place, size)) for...  16.9 us
    ppermute x9, waiting for transfers between devices, share_lines(): lax.ppermute(lines, 'dom', [(i, i ^ slot) for i in range(parts)])  14.4 us
    ppermute x9, starting transfers between devices, share_lines(): lax.ppermute(lines, 'dom', [(i, i ^ slot) for i in range(parts)])  13.7 us
    ppermute x12, waiting for transfers between devices, swap_blocks(): lax.ppermute(blocks[place], 'four', [(i, i ^ offset_of(place, size)) for...  4.54 us
    ppermute x12, waiting for transfers between devices, share_lines(): lax.ppermute(slots[slot], 'dom', [(i, i ^ 1) for i in range(parts)])  3.23 us
    ppermute x12, starting transfers between devices, share_lines(): lax.ppermute(slots[slot], 'dom', [(i, i ^ 1) for i in range(parts)])  2.12 us
  transfers between devices with their start and end apart: 33, of which 15 were waited for; matrix products, arithmetic and copies ran while one was open for 0% of the time, Pallas kernels for 13%

profile of v9, /device:TPU:0, one launch (start us, length us, event | category | flops | bytes accessed | tf_op | source)
XLA Modules:
  0.0 81.2 jit_solution(17379334910049558167)
XLA Ops:
  0.6 0.0 copy-start.2
  0.6 0.0 copy-start.3
  0.7 0.0 copy-start
  0.7 0.0 copy-start.1
  0.7 0.1 pad_add_fusion.ids_ref
  0.8 2.3 %pack.2 = (f32[216,128]{1,0:T(8,128)S(1)}, f32[216,128]{1,0:T(8,128)S(1)}, f32[216,128]{1,0:T(8,128)S(1)}, f32[216,128]{1,0:T(8,128)S(1)}, f32[3,32,2304]{2,1,0:T(8,128)S(1)}) custom-call(s32[2]{0:T(128)S(1)} %pad_add_fusion.ids_ref, f32[3,32,2304]{2,1,0:T(8,128)} %source_ref.1), custom_call_target="tpu_custom_call" | custom-call | tf_op jit(solution)/shard_map/pack/pallas_call | solution.py:846
  3.1 4.0 %collective-permute-start = (f32[216,128]{1,0:T(8,128)S(1)}, f32[216,128]{1,0:T(8,128)S(1)}, u32[]{:S(2)}, u32[]{:S(2)}) collective-permute-start(f32[216,128]{1,0:T(8,128)S(1)} %get-tuple-element.46), channel_id=1, source_target_pairs={{0,3},{1,2},{2,1},{3,0},{4,7},{5,6},{6,5},{7,4},{8,11},{9,10},{10,... | collective-permute-start | bytes 331784 | tf_op jit(solution)/shard_map/ppermute | solution.py:869
  7.1 0.5 collective-permute-start.1
  7.6 0.1 collective-permute-start.2
  7.7 1.2 %pack.3 = (f32[216,128]{1,0:T(8,128)S(1)}, f32[216,128]{1,0:T(8,128)S(1)}, f32[216,128]{1,0:T(8,128)S(1)}, f32[216,128]{1,0:T(8,128)S(1)}) custom-call(s32[2]{0:T(128)S(1)} %pad_add_fusion.ids_ref, f32[3,32,2304]{2,1,0:T(8,128)S(1)} %get-tuple-element.53.source_ref), custom_call_target="tpu_custom_call" | custom-call | tf_op jit(solution)/shard_map/pack/pallas_call | solution.py:846
  8.9 2.9 %collective-permute-start.6 = (f32[216,128]{1,0:T(8,128)S(1)}, f32[216,128]{1,0:T(8,128)S(1)}, u32[]{:S(2)}, u32[]{:S(2)}) collective-permute-start(f32[216,128]{1,0:T(8,128)S(1)} %get-tuple-element.55), channel_id=1, source_target_pairs={{0,3},{1,2},{2,1},{3,0},{4,7},{5,6},{6,5},{7,4},{8,11},{9,10},{10,... | collective-permute-start | bytes 331784 | tf_op jit(solution)/shard_map/ppermute | solution.py:869
  11.8 0.5 collective-permute-start.7
  12.3 0.7 collective-permute-start.8
  13.0 0.6 collective-permute-done.1.refs_2_
  13.5 0.0 collective-permute-done.2.refs_3_
  13.6 0.0 copy-start.4
  13.6 2.3 %products.2 = (f32[192,128]{1,0:T(8,128)S(1)}, f32[192,128]{1,0:T(8,128)S(1)}, f32[192,128]{1,0:T(8,128)S(1)}, f32[192,128]{1,0:T(8,128)S(1)}, f32[4,48,128]{2,1,0:T(8,128)S(1)}) custom-call(s32[2]{0:T(128)S(1)} %pad_add_fusion.ids_ref, f32[216,128]{1,0:T(8,128)S(1)} %get-tuple-element.45.refs_0_, f32[216,128]{1,0:T(8,128)S(1)} %collective-permute-done.refs_1_, ...), custom_call_target="tpu_custom_call" | custom-call | tf_op jit(solution)/shard_map/products/pallas_call | solution.py:846
  15.9 0.0 copy-start.5
  15.9 0.0 copy-start.6
  15.9 4.0 %collective-permute-start.3 = (f32[192,128]{1,0:T(8,128)S(1)}, f32[192,128]{1,0:T(8,128)S(1)}, u32[]{:S(2)}, u32[]{:S(2)}) collective-permute-start(f32[192,128]{1,0:T(8,128)S(1)} %get-tuple-element.50), channel_id=1, source_target_pairs={{0,3},{1,2},{2,1},{3,0},{4,7},{5,6},{6,5},{7,4},{8,11},{9,10},{10,... | collective-permute-start | bytes 294920 | tf_op jit(solution)/shard_map/ppermute | solution.py:869
  19.9 0.6 collective-permute-start.5
  20.5 2.4 %products.3 = (f32[192,128]{1,0:T(8,128)S(1)}, f32[192,128]{1,0:T(8,128)S(1)}, f32[192,128]{1,0:T(8,128)S(1)}, f32[192,128]{1,0:T(8,128)S(1)}) custom-call(s32[2]{0:T(128)S(1)} %pad_add_fusion.ids_ref, f32[216,128]{1,0:T(8,128)S(1)} %get-tuple-element.54.refs_0_, f32[216,128]{1,0:T(8,128)S(1)} %collective-permute-done.6.refs_1_, ...), custom_call_target="tpu_custom_call" | custom-call | tf_op jit(solution)/shard_map/products/pallas_call | solution.py:846
  23.0 2.9 %collective-permute-start.9 = (f32[192,128]{1,0:T(8,128)S(1)}, f32[192,128]{1,0:T(8,128)S(1)}, u32[]{:S(2)}, u32[]{:S(2)}) collective-permute-start(f32[192,128]{1,0:T(8,128)S(1)} %get-tuple-element.60), channel_id=1, source_target_pairs={{0,3},{1,2},{2,1},{3,0},{4,7},{5,6},{6,5},{7,4},{8,11},{9,10},{10,... | collective-permute-start | bytes 294920 | tf_op jit(solution)/shard_map/ppermute | solution.py:869
  25.9 0.0 collective-permute-start.10
  25.9 0.0 collective-permute-done.3.refs_1_
  25.9 0.6 collective-permute-start.11
  26.5 0.0 collective-permute-done.5.refs_3_
  26.5 2.0 %collective-permute-done.9.refs_5_ = f32[192,128]{1,0:T(8,128)S(1)} collective-permute-done((f32[192,128]{1,0:T(8,128)S(1)}, f32[192,128]{1,0:T(8,128)S(1)}, u32[]{:S(2)}, u32[]{:S(2)}) %collective-permute-start.9) | collective-permute-done | bytes 98336 | tf_op jit(solution)/shard_map/ppermute | solution.py:869
  28.5 2.0 %collective-permute-done.10.refs_6_ = f32[192,128]{1,0:T(8,128)S(1)} collective-permute-done((f32[192,128]{1,0:T(8,128)S(1)}, f32[192,128]{1,0:T(8,128)S(1)}, u32[]{:S(2)}, u32[]{:S(2)}) %collective-permute-start.10) | collective-permute-done | bytes 98336 | tf_op jit(solution)/shard_map/ppermute | solution.py:869
  30.5 0.0 collective-permute-done.11.refs_7_
  30.5 1.9 %first.1 = (f32[2304,128]{1,0:T(8,128)S(1)}, f32[240,128]{1,0:T(8,128)S(1)}) custom-call(s32[2]{0:T(128)S(1)} %pad_add_fusion.ids_ref, s32[1,4]{1,0:T(1,128)S(1)} %copy-done.4, f32[192,128]{1,0:T(8,128)S(1)} %get-tuple-element.49.refs_0_, f32[192,128]{1,0:T(8,128)S(1)} %collective-permute-done.3.refs_1_, f32[192,128]{1,0:T(8,128)S(1)} %collective-permute-done.4.refs_2_, ...), custom_call_target="tpu_custom_call" | custom-call | tf_op jit(solution)/shard_map/first/pallas_call | solution.py:846
  32.4 4.2 %collective-permute-start.17 = (f32[240,128]{1,0:T(8,128)S(1)}, f32[240,128]{1,0:T(8,128)S(1)}, u32[]{:S(2)}, u32[]{:S(2)}) collective-permute-start(f32[240,128]{1,0:T(8,128)S(1)} %get-tuple-element.63.refs_0_.refs_8_), channel_id=1, source_target_pairs={{0,24},{4,28},{8,16},{12,20},{16,8},{20,12},{24,0},{28,4},{1,25},{... | collective-permute-start | bytes 368648 | tf_op jit(solution)/shard_map/ppermute | solution.py:879
  36.6 0.6 collective-permute-start.13
  37.2 2.3 %collective-permute-done.17.refs_6_ = f32[240,128]{1,0:T(8,128)S(1)} collective-permute-done((f32[240,128]{1,0:T(8,128)S(1)}, f32[240,128]{1,0:T(8,128)S(1)}, u32[]{:S(2)}, u32[]{:S(2)}) %collective-permute-start.17) | collective-permute-done | bytes 122912 | tf_op jit(solution)/shard_map/ppermute | solution.py:879
  39.6 3.3 %collective-permute-done.15.refs_4_ = f32[240,128]{1,0:T(8,128)S(1)} collective-permute-done((f32[240,128]{1,0:T(8,128)S(1)}, f32[240,128]{1,0:T(8,128)S(1)}, u32[]{:S(2)}, u32[]{:S(2)}) %collective-permute-start.15) | collective-permute-done | bytes 122912 | tf_op jit(solution)/shard_map/ppermute | solution.py:879
  42.8 0.0 collective-permute-start.16
  42.8 0.0 collective-permute-done.13.refs_2_
  42.9 0.5 collective-permute-start.14
  43.4 0.0 collective-permute-done.12.refs_1_
  43.4 0.8 %collective-permute-done.16.refs_5_ = f32[240,128]{1,0:T(8,128)S(1)} collective-permute-done((f32[240,128]{1,0:T(8,128)S(1)}, f32[240,128]{1,0:T(8,128)S(1)}, u32[]{:S(2)}, u32[]{:S(2)}) %collective-permute-start.16) | collective-permute-done | bytes 122912 | tf_op jit(solution)/shard_map/ppermute | solution.py:883
  44.2 0.2 collective-permute-done.14.refs_3_
  44.4 4.3 %second.1 = (f32[2304,128]{1,0:T(8,128)S(1)}, f32[2304,128]{1,0:T(8,128)S(1)}, f32[2304,128]{1,0:T(8,128)S(1)}, f32[240,128]{1,0:T(8,128)S(1)}, f32[8,128]{1,0:T(8,128)S(1)}) custom-call(s32[2]{0:T(128)S(1)} %pad_add_fusion.ids_ref, s32[1,4]{1,0:T(1,128)S(1)} %copy-done.4, s32[1,4]{1,0:T(1,128)S(1)} %copy-done.5, ...), custom_call_target="tpu_custom_call", output_to_operand_aliasing={{0}: (13, {})} | custom-call | tf_op jit(solution)/shard_map/second/pallas_call | solution.py:846
  48.7 2.5 %collective-permute-start.24 = (f32[240,128]{1,0:T(8,128)S(1)}, f32[240,128]{1,0:T(8,128)S(1)}, u32[]{:S(2)}, u32[]{:S(2)}) collective-permute-start(f32[240,128]{1,0:T(8,128)S(1)} %get-tuple-element.65.refs_0_.refs_8_), channel_id=1, source_target_pairs={{0,24},{4,28},{8,16},{12,20},{16,8},{20,12},{24,0},{28,4},{1,25},{... | collective-permute-start | bytes 368648 | tf_op jit(solution)/shard_map/ppermute | solution.py:879
  51.2 0.3 collective-permute-start.22
  51.5 1.6 %collective-permute-start.20 = (f32[240,128]{1,0:T(8,128)S(1)}, f32[240,128]{1,0:T(8,128)S(1)}, u32[]{:S(2)}, u32[]{:S(2)}) collective-permute-start(f32[240,128]{1,0:T(8,128)S(1)} %get-tuple-element.65.refs_0_.refs_8_), channel_id=1, source_target_pairs={{0,8},{4,12},{8,0},{12,4},{16,24},{20,28},{24,16},{28,20},{1,9},{5... | collective-permute-start | bytes 368648 | tf_op jit(solution)/shard_map/ppermute | solution.py:879
  53.2 2.0 %turn.2 = (f32[96,2304]{1,0:T(8,128)S(1)}, f32[96,2304]{1,0:T(8,128)S(1)}, bf16[192,2304]{1,0:T(8,128)(2,1)S(1)}) custom-call(f32[2304,128]{1,0:T(8,128)S(1)} %get-tuple-element.66.refs_0_, f32[2304,128]{1,0:T(8,128)S(1)} %get-tuple-element.67.refs_1_.refs_9_), custom_call_target="tpu_custom_call" | custom-call | tf_op jit(solution)/shard_map/turn/pallas_call | solution.py:846
  55.2 1.6 %collective-permute-done.24.refs_6_ = f32[240,128]{1,0:T(8,128)S(1)} collective-permute-done((f32[240,128]{1,0:T(8,128)S(1)}, f32[240,128]{1,0:T(8,128)S(1)}, u32[]{:S(2)}, u32[]{:S(2)}) %collective-permute-start.24) | collective-permute-done | bytes 122912 | tf_op jit(solution)/shard_map/ppermute | solution.py:879
  56.8 5.8 %collective-permute-done.22.refs_4_ = f32[240,128]{1,0:T(8,128)S(1)} collective-permute-done((f32[240,128]{1,0:T(8,128)S(1)}, f32[240,128]{1,0:T(8,128)S(1)}, u32[]{:S(2)}, u32[]{:S(2)}) %collective-permute-start.22) | collective-permute-done | bytes 122912 | tf_op jit(solution)/shard_map/ppermute | solution.py:879
  62.6 0.5 collective-permute-start.21
  63.1 0.0 collective-permute-start.25
  63.2 0.8 %collective-permute-done.23.refs_5_ = f32[240,128]{1,0:T(8,128)S(1)} collective-permute-done((f32[240,128]{1,0:T(8,128)S(1)}, f32[240,128]{1,0:T(8,128)S(1)}, u32[]{:S(2)}, u32[]{:S(2)}) %collective-permute-start.23) | collective-permute-done | bytes 122912 | tf_op jit(solution)/shard_map/ppermute | solution.py:883
  64.0 0.2 collective-permute-done.21.refs_3_
  64.1 0.3 collective-permute-done.25.refs_7_
  64.5 3.4 %third.1 = (f32[2304,128]{1,0:T(8,128)S(1)}, f32[2304,128]{1,0:T(8,128)S(1)}, f32[2304,128]{1,0:T(8,128)S(1)}, f32[128,128]{1,0:T(8,128)S(1)}) custom-call(s32[2]{0:T(128)S(1)} %pad_add_fusion.ids_ref, s32[1,4]{1,0:T(1,128)S(1)} %copy-done.4, s32[1,4]{1,0:T(1,128)S(1)} %copy-done.5, s32[1,4]{1,0:T(1,128)S(1)} %copy-done.6, ...), custom_call_target="tpu_custom_call", output_to_operand_aliasing={{0}: (15, {})} | custom-call | tf_op jit(solution)/shard_map/third/pallas_call | solution.py:846
  67.9 1.8 %collective-permute-start.31 = (f32[128,128]{1,0:T(8,128)S(1)}, f32[128,128]{1,0:T(8,128)S(1)}, u32[]{:S(2)}, u32[]{:S(2)}) collective-permute-start(f32[128,128]{1,0:T(8,128)S(1)} %get-tuple-element.74.refs_0_), channel_id=1, source_target_pairs={{0,24},{4,28},{8,16},{12,20},{16,8},{20,12},{24,0},{28,4},{1,25},{... | collective-permute-start | bytes 196616 | tf_op jit(solution)/shard_map/ppermute | solution.py:879
  69.7 2.6 %collective-permute-start.27 = (f32[128,128]{1,0:T(8,128)S(1)}, f32[128,128]{1,0:T(8,128)S(1)}, u32[]{:S(2)}, u32[]{:S(2)}) collective-permute-start(f32[128,128]{1,0:T(8,128)S(1)} %get-tuple-element.74.refs_0_), channel_id=1, source_target_pairs={{0,8},{4,12},{8,0},{12,4},{16,24},{20,28},{24,16},{28,20},{1,9},{5... | collective-permute-start | bytes 196616 | tf_op jit(solution)/shard_map/ppermute | solution.py:879
  72.3 2.5 %turn.3 = (f32[96,2304]{1,0:T(8,128)S(1)}, f32[96,2304]{1,0:T(8,128)S(1)}, f32[96,2304]{1,0:T(8,128)S(1)}) custom-call(f32[2304,128]{1,0:T(8,128)S(1)} %get-tuple-element.75.refs_0_, f32[2304,128]{1,0:T(8,128)S(1)} %get-tuple-element.76.refs_1_, f32[2304,128]{1,0:T(8,128)S(1)} %get-tuple-element.77.refs_2_), custom_call_target="tpu_custom_call" | custom-call | tf_op jit(solution)/shard_map/turn/pallas_call | solution.py:846
  74.8 0.6 collective-permute-start.32
  75.4 1.4 %collective-permute-done.29.refs_4_ = f32[128,128]{1,0:T(8,128)S(1)} collective-permute-done((f32[128,128]{1,0:T(8,128)S(1)}, f32[128,128]{1,0:T(8,128)S(1)}, u32[]{:S(2)}, u32[]{:S(2)}) %collective-permute-start.29) | collective-permute-done | bytes 65568 | tf_op jit(solution)/shard_map/ppermute | solution.py:879
  76.8 0.0 collective-permute-start.30
  76.8 0.5 collective-permute-start.28
  77.3 0.7 collective-permute-done.30.refs_5_
  78.1 0.2 collective-permute-done.28.refs_3_
  78.2 2.8 %last.1 = (f32[3,32,2304]{2,1,0:T(8,128)}, f32[3,32,2304]{2,1,0:T(8,128)}) custom-call(s32[2]{0:T(128)S(1)} %pad_add_fusion.ids_ref, s32[1,4]{1,0:T(1,128)S(1)} %copy-done.4, s32[1,4]{1,0:T(1,128)S(1)} %copy-done.5, s32[1,4]{1,0:T(1,128)S(1)} %copy-done.6, f32[128,128]{1,0:T(8,128)S(1)} %get-tuple-element.74.refs_0_, ...), custom_call_target="tpu_custom_call" | custom-call | tf_op jit(solution)/shard_map/last/pallas_call | solution.py:846
  (27 shorter events, 0.1 us)
Async XLA Ops:
  0.6 12.9 %copy-start.2 = (bf16[256,128]{1,0:T(8,128)(2,1)S(1)}, bf16[256,128]{1,0:T(8,128)(2,1)}, u32[]{:S(2)}) copy-start(bf16[256,128]{1,0:T(8,128)(2,1)} %constant.20.clone.refs_7_) | copy-start | bytes 196612
  0.6 12.9 %copy-start.3 = (bf16[256,128]{1,0:T(8,128)(2,1)S(1)}, bf16[256,128]{1,0:T(8,128)(2,1)}, u32[]{:S(2)}) copy-start(bf16[256,128]{1,0:T(8,128)(2,1)} %constant.19.clone.refs_6_) | copy-start | bytes 196612
  0.7 12.9 %copy-start = (bf16[512,384]{1,0:T(8,128)(2,1)S(1)}, bf16[512,384]{1,0:T(8,128)(2,1)}, u32[]{:S(2)}) copy-start(bf16[512,384]{1,0:T(8,128)(2,1)} %constant.18.clone.refs_5_) | copy-start | bytes 1179652
  0.7 12.9 %copy-start.1 = (bf16[512,384]{1,0:T(8,128)(2,1)S(1)}, bf16[512,384]{1,0:T(8,128)(2,1)}, u32[]{:S(2)}) copy-start(bf16[512,384]{1,0:T(8,128)(2,1)} %constant.17.clone.refs_4_) | copy-start | bytes 1179652
  3.1 9.2 %collective-permute-start = (f32[216,128]{1,0:T(8,128)S(1)}, f32[216,128]{1,0:T(8,128)S(1)}, u32[]{:S(2)}, u32[]{:S(2)}) collective-permute-start(f32[216,128]{1,0:T(8,128)S(1)} %get-tuple-element.46), channel_id=1, source_target_pairs={{0,3},{1,2},{2,1},{3,0},{4,7},{5,6},{6,5},{7,4},{8,11},{9,10},{10,... | collective-permute-start | bytes 331784 | tf_op jit(solution)/shard_map/ppermute | solution.py:869
  7.1 6.5 %collective-permute-start.1 = (f32[216,128]{1,0:T(8,128)S(1)}, f32[216,128]{1,0:T(8,128)S(1)}, u32[]{:S(2)}, u32[]{:S(2)}) collective-permute-start(f32[216,128]{1,0:T(8,128)S(1)} %get-tuple-element.47), channel_id=1, source_target_pairs={{0,1},{1,0},{2,3},{3,2},{4,5},{5,4},{6,7},{7,6},{8,9},{9,8},{10,11... | collective-permute-start | bytes 331784 | tf_op jit(solution)/shard_map/ppermute | solution.py:869
  7.6 5.9 %collective-permute-start.2 = (f32[216,128]{1,0:T(8,128)S(1)}, f32[216,128]{1,0:T(8,128)S(1)}, u32[]{:S(2)}, u32[]{:S(2)}) collective-permute-start(f32[216,128]{1,0:T(8,128)S(1)} %get-tuple-element.48), channel_id=1, source_target_pairs={{0,2},{1,3},{2,0},{3,1},{4,6},{5,7},{6,4},{7,5},{8,10},{9,11},{10,... | collective-permute-start | bytes 331784 | tf_op jit(solution)/shard_map/ppermute | solution.py:869
  8.9 11.0 %collective-permute-start.6 = (f32[216,128]{1,0:T(8,128)S(1)}, f32[216,128]{1,0:T(8,128)S(1)}, u32[]{:S(2)}, u32[]{:S(2)}) collective-permute-start(f32[216,128]{1,0:T(8,128)S(1)} %get-tuple-element.55), channel_id=1, source_target_pairs={{0,3},{1,2},{2,1},{3,0},{4,7},{5,6},{6,5},{7,4},{8,11},{9,10},{10,... | collective-permute-start | bytes 331784 | tf_op jit(solution)/shard_map/ppermute | solution.py:869
  11.8 8.8 %collective-permute-start.7 = (f32[216,128]{1,0:T(8,128)S(1)}, f32[216,128]{1,0:T(8,128)S(1)}, u32[]{:S(2)}, u32[]{:S(2)}) collective-permute-start(f32[216,128]{1,0:T(8,128)S(1)} %get-tuple-element.56), channel_id=1, source_target_pairs={{0,1},{1,0},{2,3},{3,2},{4,5},{5,4},{6,7},{7,6},{8,9},{9,8},{10,11... | collective-permute-start | bytes 331784 | tf_op jit(solution)/shard_map/ppermute | solution.py:869
  12.3 8.2 %collective-permute-start.8 = (f32[216,128]{1,0:T(8,128)S(1)}, f32[216,128]{1,0:T(8,128)S(1)}, u32[]{:S(2)}, u32[]{:S(2)}) collective-permute-start(f32[216,128]{1,0:T(8,128)S(1)} %get-tuple-element.57), channel_id=1, source_target_pairs={{0,2},{1,3},{2,0},{3,1},{4,6},{5,7},{6,4},{7,5},{8,10},{9,11},{10,... | collective-permute-start | bytes 331784 | tf_op jit(solution)/shard_map/ppermute | solution.py:869
  13.6 17.0 %copy-start.4 = (s32[1,4]{1,0:T(1,128)S(1)}, s32[1,4]{1,0:T(1,128)}, u32[]{:S(2)}) copy-start(s32[1,4]{1,0:T(1,128)} %partner_ref.7) | copy-start | bytes 52
  15.9 28.4 %copy-start.5 = (s32[1,4]{1,0:T(1,128)S(1)}, s32[1,4]{1,0:T(1,128)}, u32[]{:S(2)}) copy-start(s32[1,4]{1,0:T(1,128)} %side_ref.5) | copy-start | bytes 52
  15.9 28.4 %copy-start.6 = (s32[1,4]{1,0:T(1,128)S(1)}, s32[1,4]{1,0:T(1,128)}, u32[]{:S(2)}) copy-start(s32[1,4]{1,0:T(1,128)} %flip_ref.5) | copy-start | bytes 52
  15.9 9.9 %collective-permute-start.3 = (f32[192,128]{1,0:T(8,128)S(1)}, f32[192,128]{1,0:T(8,128)S(1)}, u32[]{:S(2)}, u32[]{:S(2)}) collective-permute-start(f32[192,128]{1,0:T(8,128)S(1)} %get-tuple-element.50), channel_id=1, source_target_pairs={{0,3},{1,2},{2,1},{3,0},{4,7},{5,6},{6,5},{7,4},{8,11},{9,10},{10,... | collective-permute-start | bytes 294920 | tf_op jit(solution)/shard_map/ppermute | solution.py:869
  19.9 6.6 %collective-permute-start.4 = (f32[192,128]{1,0:T(8,128)S(1)}, f32[192,128]{1,0:T(8,128)S(1)}, u32[]{:S(2)}, u32[]{:S(2)}) collective-permute-start(f32[192,128]{1,0:T(8,128)S(1)} %get-tuple-element.51), channel_id=1, source_target_pairs={{0,1},{1,0},{2,3},{3,2},{4,5},{5,4},{6,7},{7,6},{8,9},{9,8},{10,11... | collective-permute-start | bytes 294920 | tf_op jit(solution)/shard_map/ppermute | solution.py:869
  19.9 6.6 %collective-permute-start.5 = (f32[192,128]{1,0:T(8,128)S(1)}, f32[192,128]{1,0:T(8,128)S(1)}, u32[]{:S(2)}, u32[]{:S(2)}) collective-permute-start(f32[192,128]{1,0:T(8,128)S(1)} %get-tuple-element.52), channel_id=1, source_target_pairs={{0,2},{1,3},{2,0},{3,1},{4,6},{5,7},{6,4},{7,5},{8,10},{9,11},{10,... | collective-permute-start | bytes 294920 | tf_op jit(solution)/shard_map/ppermute | solution.py:869
  23.0 5.6 %collective-permute-start.9 = (f32[192,128]{1,0:T(8,128)S(1)}, f32[192,128]{1,0:T(8,128)S(1)}, u32[]{:S(2)}, u32[]{:S(2)}) collective-permute-start(f32[192,128]{1,0:T(8,128)S(1)} %get-tuple-element.60), channel_id=1, source_target_pairs={{0,3},{1,2},{2,1},{3,0},{4,7},{5,6},{6,5},{7,4},{8,11},{9,10},{10,... | collective-permute-start | bytes 294920 | tf_op jit(solution)/shard_map/ppermute | solution.py:869
  25.9 4.6 %collective-permute-start.10 = (f32[192,128]{1,0:T(8,128)S(1)}, f32[192,128]{1,0:T(8,128)S(1)}, u32[]{:S(2)}, u32[]{:S(2)}) collective-permute-start(f32[192,128]{1,0:T(8,128)S(1)} %get-tuple-element.61), channel_id=1, source_target_pairs={{0,1},{1,0},{2,3},{3,2},{4,5},{5,4},{6,7},{7,6},{8,9},{9,8},{10,11... | collective-permute-start | bytes 294920 | tf_op jit(solution)/shard_map/ppermute | solution.py:869
  25.9 4.6 %collective-permute-start.11 = (f32[192,128]{1,0:T(8,128)S(1)}, f32[192,128]{1,0:T(8,128)S(1)}, u32[]{:S(2)}, u32[]{:S(2)}) collective-permute-start(f32[192,128]{1,0:T(8,128)S(1)} %get-tuple-element.62), channel_id=1, source_target_pairs={{0,2},{1,3},{2,0},{3,1},{4,6},{5,7},{6,4},{7,5},{8,10},{9,11},{10,... | collective-permute-start | bytes 294920 | tf_op jit(solution)/shard_map/ppermute | solution.py:869
  32.4 7.1 %collective-permute-start.17 = (f32[240,128]{1,0:T(8,128)S(1)}, f32[240,128]{1,0:T(8,128)S(1)}, u32[]{:S(2)}, u32[]{:S(2)}) collective-permute-start(f32[240,128]{1,0:T(8,128)S(1)} %get-tuple-element.63.refs_0_.refs_8_), channel_id=1, source_target_pairs={{0,24},{4,28},{8,16},{12,20},{16,8},{20,12},{24,0},{28,4},{1,25},{... | collective-permute-start | bytes 368648 | tf_op jit(solution)/shard_map/ppermute | solution.py:879
  36.6 6.2 %collective-permute-start.15 = (f32[240,128]{1,0:T(8,128)S(1)}, f32[240,128]{1,0:T(8,128)S(1)}, u32[]{:S(2)}, u32[]{:S(2)}) collective-permute-start(f32[240,128]{1,0:T(8,128)S(1)} %get-tuple-element.63.refs_0_.refs_8_), channel_id=1, source_target_pairs={{0,16},{4,20},{8,24},{12,28},{16,0},{20,4},{24,8},{28,12},{1,17},{... | collective-permute-start | bytes 368648 | tf_op jit(solution)/shard_map/ppermute | solution.py:879
  36.6 6.2 %collective-permute-start.13 = (f32[240,128]{1,0:T(8,128)S(1)}, f32[240,128]{1,0:T(8,128)S(1)}, u32[]{:S(2)}, u32[]{:S(2)}) collective-permute-start(f32[240,128]{1,0:T(8,128)S(1)} %get-tuple-element.63.refs_0_.refs_8_), channel_id=1, source_target_pairs={{0,8},{4,12},{8,0},{12,4},{16,24},{20,28},{24,16},{28,20},{1,9},{5... | collective-permute-start | bytes 368648 | tf_op jit(solution)/shard_map/ppermute | solution.py:879
  37.2 6.1 %collective-permute-start.12 = (f32[240,128]{1,0:T(8,128)S(1)}, f32[240,128]{1,0:T(8,128)S(1)}, u32[]{:S(2)}, u32[]{:S(2)}) collective-permute-start(f32[240,128]{1,0:T(8,128)S(1)} %get-tuple-element.63.refs_0_.refs_8_), channel_id=1, source_target_pairs={{0,4},{4,0},{8,12},{12,8},{16,20},{20,16},{24,28},{28,24},{1,5},{5... | collective-permute-start | bytes 368648 | tf_op jit(solution)/shard_map/ppermute | solution.py:883
  39.6 3.8 %collective-permute-start.18 = (f32[240,128]{1,0:T(8,128)S(1)}, f32[240,128]{1,0:T(8,128)S(1)}, u32[]{:S(2)}, u32[]{:S(2)}) collective-permute-start(f32[240,128]{1,0:T(8,128)S(1)} %collective-permute-done.17.refs_6_), channel_id=1, source_target_pairs={{0,4},{4,0},{8,12},{12,8},{16,20},{20,16},{24,28},{28,24},{1,5},{5... | collective-permute-start | bytes 368648 | tf_op jit(solution)/shard_map/ppermute | solution.py:883
  42.8 1.3 %collective-permute-start.16 = (f32[240,128]{1,0:T(8,128)S(1)}, f32[240,128]{1,0:T(8,128)S(1)}, u32[]{:S(2)}, u32[]{:S(2)}) collective-permute-start(f32[240,128]{1,0:T(8,128)S(1)} %collective-permute-done.15.refs_4_), channel_id=1, source_target_pairs={{0,4},{4,0},{8,12},{12,8},{16,20},{20,16},{24,28},{28,24},{1,5},{5... | collective-permute-start | bytes 368648 | tf_op jit(solution)/shard_map/ppermute | solution.py:883
  42.9 1.5 %collective-permute-start.14 = (f32[240,128]{1,0:T(8,128)S(1)}, f32[240,128]{1,0:T(8,128)S(1)}, u32[]{:S(2)}, u32[]{:S(2)}) collective-permute-start(f32[240,128]{1,0:T(8,128)S(1)} %collective-permute-done.13.refs_2_), channel_id=1, source_target_pairs={{0,4},{4,0},{8,12},{12,8},{16,20},{20,16},{24,28},{28,24},{1,5},{5... | collective-permute-start | bytes 368648 | tf_op jit(solution)/shard_map/ppermute | solution.py:883
  48.7 8.1 %collective-permute-start.24 = (f32[240,128]{1,0:T(8,128)S(1)}, f32[240,128]{1,0:T(8,128)S(1)}, u32[]{:S(2)}, u32[]{:S(2)}) collective-permute-start(f32[240,128]{1,0:T(8,128)S(1)} %get-tuple-element.65.refs_0_.refs_8_), channel_id=1, source_target_pairs={{0,24},{4,28},{8,16},{12,20},{16,8},{20,12},{24,0},{28,4},{1,25},{... | collective-permute-start | bytes 368648 | tf_op jit(solution)/shard_map/ppermute | solution.py:879
  51.2 11.4 %collective-permute-start.22 = (f32[240,128]{1,0:T(8,128)S(1)}, f32[240,128]{1,0:T(8,128)S(1)}, u32[]{:S(2)}, u32[]{:S(2)}) collective-permute-start(f32[240,128]{1,0:T(8,128)S(1)} %get-tuple-element.65.refs_0_.refs_8_), channel_id=1, source_target_pairs={{0,16},{4,20},{8,24},{12,28},{16,0},{20,4},{24,8},{28,12},{1,17},{... | collective-permute-start | bytes 368648 | tf_op jit(solution)/shard_map/ppermute | solution.py:879
  51.5 11.1 %collective-permute-start.20 = (f32[240,128]{1,0:T(8,128)S(1)}, f32[240,128]{1,0:T(8,128)S(1)}, u32[]{:S(2)}, u32[]{:S(2)}) collective-permute-start(f32[240,128]{1,0:T(8,128)S(1)} %get-tuple-element.65.refs_0_.refs_8_), channel_id=1, source_target_pairs={{0,8},{4,12},{8,0},{12,4},{16,24},{20,28},{24,16},{28,20},{1,9},{5... | collective-permute-start | bytes 368648 | tf_op jit(solution)/shard_map/ppermute | solution.py:879
  53.2 10.0 %collective-permute-start.19 = (f32[240,128]{1,0:T(8,128)S(1)}, f32[240,128]{1,0:T(8,128)S(1)}, u32[]{:S(2)}, u32[]{:S(2)}) collective-permute-start(f32[240,128]{1,0:T(8,128)S(1)} %get-tuple-element.65.refs_0_.refs_8_), channel_id=1, source_target_pairs={{0,4},{4,0},{8,12},{12,8},{16,20},{20,16},{24,28},{28,24},{1,5},{5... | collective-permute-start | bytes 368648 | tf_op jit(solution)/shard_map/ppermute | solution.py:883
  62.6 1.3 %collective-permute-start.23 = (f32[240,128]{1,0:T(8,128)S(1)}, f32[240,128]{1,0:T(8,128)S(1)}, u32[]{:S(2)}, u32[]{:S(2)}) collective-permute-start(f32[240,128]{1,0:T(8,128)S(1)} %collective-permute-done.22.refs_4_), channel_id=1, source_target_pairs={{0,4},{4,0},{8,12},{12,8},{16,20},{20,16},{24,28},{28,24},{1,5},{5... | collective-permute-start | bytes 368648 | tf_op jit(solution)/shard_map/ppermute | solution.py:883
  62.6 1.5 %collective-permute-start.21 = (f32[240,128]{1,0:T(8,128)S(1)}, f32[240,128]{1,0:T(8,128)S(1)}, u32[]{:S(2)}, u32[]{:S(2)}) collective-permute-start(f32[240,128]{1,0:T(8,128)S(1)} %collective-permute-done.20.refs_2_), channel_id=1, source_target_pairs={{0,4},{4,0},{8,12},{12,8},{16,20},{20,16},{24,28},{28,24},{1,5},{5... | collective-permute-start | bytes 368648 | tf_op jit(solution)/shard_map/ppermute | solution.py:883
  63.1 1.3 %collective-permute-start.25 = (f32[240,128]{1,0:T(8,128)S(1)}, f32[240,128]{1,0:T(8,128)S(1)}, u32[]{:S(2)}, u32[]{:S(2)}) collective-permute-start(f32[240,128]{1,0:T(8,128)S(1)} %collective-permute-done.24.refs_6_), channel_id=1, source_target_pairs={{0,4},{4,0},{8,12},{12,8},{16,20},{20,16},{24,28},{28,24},{1,5},{5... | collective-permute-start | bytes 368648 | tf_op jit(solution)/shard_map/ppermute | solution.py:883
  67.9 7.0 %collective-permute-start.31 = (f32[128,128]{1,0:T(8,128)S(1)}, f32[128,128]{1,0:T(8,128)S(1)}, u32[]{:S(2)}, u32[]{:S(2)}) collective-permute-start(f32[128,128]{1,0:T(8,128)S(1)} %get-tuple-element.74.refs_0_), channel_id=1, source_target_pairs={{0,24},{4,28},{8,16},{12,20},{16,8},{20,12},{24,0},{28,4},{1,25},{... | collective-permute-start | bytes 196616 | tf_op jit(solution)/shard_map/ppermute | solution.py:879
  69.7 7.1 %collective-permute-start.29 = (f32[128,128]{1,0:T(8,128)S(1)}, f32[128,128]{1,0:T(8,128)S(1)}, u32[]{:S(2)}, u32[]{:S(2)}) collective-permute-start(f32[128,128]{1,0:T(8,128)S(1)} %get-tuple-element.74.refs_0_), channel_id=1, source_target_pairs={{0,16},{4,20},{8,24},{12,28},{16,0},{20,4},{24,8},{28,12},{1,17},{... | collective-permute-start | bytes 196616 | tf_op jit(solution)/shard_map/ppermute | solution.py:879
  69.7 7.1 %collective-permute-start.27 = (f32[128,128]{1,0:T(8,128)S(1)}, f32[128,128]{1,0:T(8,128)S(1)}, u32[]{:S(2)}, u32[]{:S(2)}) collective-permute-start(f32[128,128]{1,0:T(8,128)S(1)} %get-tuple-element.74.refs_0_), channel_id=1, source_target_pairs={{0,8},{4,12},{8,0},{12,4},{16,24},{20,28},{24,16},{28,20},{1,9},{5... | collective-permute-start | bytes 196616 | tf_op jit(solution)/shard_map/ppermute | solution.py:879
  72.3 5.0 %collective-permute-start.26 = (f32[128,128]{1,0:T(8,128)S(1)}, f32[128,128]{1,0:T(8,128)S(1)}, u32[]{:S(2)}, u32[]{:S(2)}) collective-permute-start(f32[128,128]{1,0:T(8,128)S(1)} %get-tuple-element.74.refs_0_), channel_id=1, source_target_pairs={{0,4},{4,0},{8,12},{12,8},{16,20},{20,16},{24,28},{28,24},{1,5},{5... | collective-permute-start | bytes 196616 | tf_op jit(solution)/shard_map/ppermute | solution.py:883
  74.8 2.5 %collective-permute-start.32 = (f32[128,128]{1,0:T(8,128)S(1)}, f32[128,128]{1,0:T(8,128)S(1)}, u32[]{:S(2)}, u32[]{:S(2)}) collective-permute-start(f32[128,128]{1,0:T(8,128)S(1)} %collective-permute-done.31.refs_6_), channel_id=1, source_target_pairs={{0,4},{4,0},{8,12},{12,8},{16,20},{20,16},{24,28},{28,24},{1,5},{5... | collective-permute-start | bytes 196616 | tf_op jit(solution)/shard_map/ppermute | solution.py:883
  76.8 1.3 %collective-permute-start.30 = (f32[128,128]{1,0:T(8,128)S(1)}, f32[128,128]{1,0:T(8,128)S(1)}, u32[]{:S(2)}, u32[]{:S(2)}) collective-permute-start(f32[128,128]{1,0:T(8,128)S(1)} %collective-permute-done.29.refs_4_), channel_id=1, source_target_pairs={{0,4},{4,0},{8,12},{12,8},{16,20},{20,16},{24,28},{28,24},{1,5},{5... | collective-permute-start | bytes 196616 | tf_op jit(solution)/shard_map/ppermute | solution.py:883
  76.8 1.4 %collective-permute-start.28 = (f32[128,128]{1,0:T(8,128)S(1)}, f32[128,128]{1,0:T(8,128)S(1)}, u32[]{:S(2)}, u32[]{:S(2)}) collective-permute-start(f32[128,128]{1,0:T(8,128)S(1)} %collective-permute-done.27.refs_2_), channel_id=1, source_target_pairs={{0,4},{4,0},{8,12},{12,8},{16,20},{20,16},{24,28},{28,24},{1,5},{5... | collective-permute-start | bytes 196616 | tf_op jit(solution)/shard_map/ppermute | solution.py:883

commit v10 on v9

--- a/solution.py
+++ b/solution.py
@@ -70,7 +70,7 @@
 def split_table(table):
     high = np.asarray(table, np.float32).astype(jnp.bfloat16)
     low = (np.asarray(table, np.float64) - high.astype(np.float64)).astype(np.float32)
-    return high, low.astype(jnp.bfloat16)
+    return np.concatenate([high, low.astype(jnp.bfloat16)], axis=1)
 
 
 def transform_tables(count):
@@ -125,10 +125,12 @@
     return lax.dot_general(left, right, (dims, ((), ())), preferred_element_type=F32)
 
 
-def dot3(left, right_high, right_low):
+def dot3(left, right):
     high, low = halves(left)
     dims = ((1,), (0,))
-    return dot(high, right_high, dims) + (dot(low, right_high, dims) + dot(high, right_low, dims))
+    width = right.shape[1] // 2
+    both = dot(high, right, dims)
+    return both[:, :width] + (both[:, width:] + dot(low, right[:, :width], dims))
 
 
 def start_of(point, ey):
@@ -489,8 +491,8 @@
 
 def product_kernel(modes, step, count, dynamic, role, ids_ref, *refs):
     recv_refs = refs[:count]
-    inv_high, inv_low, back_high, back_low = refs[count : count + 4]
-    refs = refs[count + 4 :]
+    inverse_ref, back_ref = refs[count : count + 2]
+    refs = refs[count + 2 :]
     if role == 1:
         carry_ref, refs = refs[0], refs[1:]
     send_refs, refs = refs[:count], refs[count:]
@@ -511,7 +513,7 @@
         first = index * LANES
         first = first if isinstance(first, int) else pl.multiple_of(first, LANES)
         lined[:, pl.ds(first, LANES)] = full[place]
-    phys[...] = dot3(lined[...], inv_high[...], inv_low[...])
+    phys[...] = dot3(lined[...], inverse_ref[...])
     width = 2 * LANES
 
     def field(point, comp):
@@ -537,7 +539,7 @@
             for iy in range(6):
                 at = pl.ds((6 * iy + ix) * step, step)
                 prod[at, wide] = prod[at, wide] + out[iy]
-        spec[comp] = dot3(prod[:, comp * width : (comp + 1) * width], back_high[...], back_low[...])
+        spec[comp] = dot3(prod[:, comp * width : (comp + 1) * width], back_ref[...])
 
     lane_block = lax.div(lax.broadcasted_iota(jnp.int32, (step, LANES), 1), jnp.int32(modes))
     masks = []
@@ -789,7 +791,6 @@
     else:
         parts = [ref[where, :] for ref in gath_refs]
     sums = functools.reduce(lambda left, right: left + right, parts)
-    collect_sides(gath_refs, ids_ref[0], partner_ref, side_ref, sides, modes)
     g00, g01, g11, g12, g22, g23, g33, energy = [
         jnp.broadcast_to(sums[place : place + 1, :], (8, LANES)) for place in range(8)
     ]
@@ -810,31 +811,35 @@
     columns = jnp.transpose(
         jnp.concatenate([value[:1] for value in factors] + [jnp.zeros((LANES - 9, LANES), F32)], axis=0)
     )
+    copies = []
+
+    def send(comp, place, buffer, out):
+        copies.append(pltpu.make_async_copy(buffer.at[comp], out.at[comp], sems.at[2 * comp + place]))
+        copies[-1].start()
+
+    def scaled(at, first):
+        rows = [ref[at : at + 8, :] for ref in turned[: 5 if first else 4]]
+        terms = [columns[at : at + 8, first + k : first + k + 1] * row for k, row in enumerate(rows)]
+        return functools.reduce(lambda left, right: left + right, terms)
+
+    for comp in range(3):
+        for first in range(0, modes, 8):
+            sol_ref[comp, first : first + 8, :] = scaled(comp * modes + first, 0)
+        send(comp, 0, sol_ref, sol_out)
+    collect_sides(gath_refs, ids_ref[0], partner_ref, side_ref, sides, modes)
     incoming = incoming_lines(sides, 0, partner_ref, flip_ref)
     for side in range(4):
         for i in range(6):
             lines[pl.ds(side * SIDE + i * 8, 8), :] = incoming[side][i] * on_a3
     high, low = halves(jnp.transpose(lines[...])[:used])
     added = dot(jnp.concatenate([high, low], axis=0), scatter_ref[...], ((1,), (0,)))
-    copies = []
     for comp in range(3):
         for first in range(0, modes, 8):
             at = comp * modes + first
-            rows = [ref[at : at + 8, :] for ref in turned]
-            scale = [columns[at : at + 8, place : place + 1] for place in range(9)]
-            sol_ref[comp, first : first + 8, :] = (scale[0] * rows[0] + scale[1] * rows[1]) + (
-                scale[2] * rows[2] + scale[3] * rows[3]
+            res_ref[comp, first : first + 8, :] = scaled(at, 4) + (
+                added[at : at + 8] + added[used + at : used + at + 8]
             )
-            res_ref[comp, first : first + 8, :] = (
-                (scale[4] * rows[0] + scale[5] * rows[1])
-                + (scale[6] * rows[2] + scale[7] * rows[3])
-                + (scale[8] * rows[4] + (added[at : at + 8] + added[used + at : used + at + 8]))
-            )
-        for place, (buffer, out) in enumerate(((sol_ref, sol_out), (res_ref, res_out))):
-            copies.append(
-                pltpu.make_async_copy(buffer.at[comp], out.at[comp], sems.at[2 * comp + place])
-            )
-            copies[-1].start()
+        send(comp, 1, res_ref, res_out)
     for copy in copies:
         copy.wait()
 
@@ -891,7 +896,7 @@
     rows = POINTS * step
     sent_rows = 3 * rows // 4 if is_packed(modes) else rows
     dynamic = step == BLOCKS
-    (inv_high, inv_low), (back_high, back_low) = transform_tables(count)
+    inverse, back = transform_tables(count)
     starts, offsets = unit_windows(count)
     table = (rows, 3 * LANES)
     ids = jnp.stack([lax.axis_index("dom"), lax.axis_index("four")]).astype(jnp.int32)
@@ -925,7 +930,7 @@
             functools.partial(product_kernel, modes, step, count, dynamic, role),
             "products",
             out + [(count, SIDE, LANES)] * (role == 0),
-            (ids, *spread[chunk], inv_high, inv_low, back_high, back_low, *carry),
+            (ids, *spread[chunk], inverse, back, *carry),
             [
                 (count, rows, LANES),
                 (rows, count * LANES),

time: 81.4 us -> 80.8 us (level)
  transfers between devices with their start and end apart: 33 -> 33, of which waited for: 15 -> 15; matrix products, arithmetic and copies ran while one was open for 0% -> 0% of each run, Pallas kernels for 13% -> 12%
where the time goes in v10:
time: 80.8 us; the launch traced here: 80.6 us
  starting transfers between devices  32.7 us (40%)
  Pallas kernels  25 us (31%)
  waiting for transfers between devices  21.9 us (27%)
  between operations  0.93 us (1%)
    pallas_call x10, Pallas kernels, call(): pl.pallas_call(kernel, name=name, out_shape=[pltpu.VMEM(one.shape, one.dt...  25 us
    ppermute x12, starting transfers between devices, swap_blocks(): lax.ppermute(blocks[place], 'four', [(i, i ^ offset_of(place, size)) for...  16.8 us
    ppermute x9, waiting for transfers between devices, share_lines(): lax.ppermute(lines, 'dom', [(i, i ^ slot) for i in range(parts)])  14.2 us
    ppermute x9, starting transfers between devices, share_lines(): lax.ppermute(lines, 'dom', [(i, i ^ slot) for i in range(parts)])  13.7 us
    ppermute x12, waiting for transfers between devices, swap_blocks(): lax.ppermute(blocks[place], 'four', [(i, i ^ offset_of(place, size)) for...  4.54 us
    ppermute x12, waiting for transfers between devices, share_lines(): lax.ppermute(slots[slot], 'dom', [(i, i ^ 1) for i in range(parts)])  3.23 us
    ppermute x12, starting transfers between devices, share_lines(): lax.ppermute(slots[slot], 'dom', [(i, i ^ 1) for i in range(parts)])  2.12 us
  transfers between devices with their start and end apart: 33, of which 15 were waited for; matrix products, arithmetic and copies ran while one was open for 0% of the time, Pallas kernels for 12%

profile of v10, /device:TPU:0, one launch (start us, length us, event | category | flops | bytes accessed | tf_op | source)
XLA Modules:
  0.0 80.6 jit_solution(3106311323484968164)
XLA Ops:
  0.6 0.0 copy-start.1
  0.6 0.0 copy-start
  0.7 0.1 pad_add_fusion.ids_ref
  0.7 2.3 %pack.2 = (f32[216,128]{1,0:T(8,128)S(1)}, f32[216,128]{1,0:T(8,128)S(1)}, f32[216,128]{1,0:T(8,128)S(1)}, f32[216,128]{1,0:T(8,128)S(1)}, f32[3,32,2304]{2,1,0:T(8,128)S(1)}) custom-call(s32[2]{0:T(128)S(1)} %pad_add_fusion.ids_ref, f32[3,32,2304]{2,1,0:T(8,128)} %source_ref.1), custom_call_target="tpu_custom_call" | custom-call | tf_op jit(solution)/shard_map/pack/pallas_call | solution.py:851
  3.1 4.0 %collective-permute-start = (f32[216,128]{1,0:T(8,128)S(1)}, f32[216,128]{1,0:T(8,128)S(1)}, u32[]{:S(2)}, u32[]{:S(2)}) collective-permute-start(f32[216,128]{1,0:T(8,128)S(1)} %get-tuple-element.46), channel_id=1, source_target_pairs={{0,3},{1,2},{2,1},{3,0},{4,7},{5,6},{6,5},{7,4},{8,11},{9,10},{10,... | collective-permute-start | bytes 331784 | tf_op jit(solution)/shard_map/ppermute | solution.py:874
  7.0 0.5 collective-permute-start.1
  7.6 0.1 collective-permute-start.2
  7.7 1.2 %pack.3 = (f32[216,128]{1,0:T(8,128)S(1)}, f32[216,128]{1,0:T(8,128)S(1)}, f32[216,128]{1,0:T(8,128)S(1)}, f32[216,128]{1,0:T(8,128)S(1)}) custom-call(s32[2]{0:T(128)S(1)} %pad_add_fusion.ids_ref, f32[3,32,2304]{2,1,0:T(8,128)S(1)} %get-tuple-element.53.source_ref), custom_call_target="tpu_custom_call" | custom-call | tf_op jit(solution)/shard_map/pack/pallas_call | solution.py:851
  8.8 2.9 %collective-permute-start.6 = (f32[216,128]{1,0:T(8,128)S(1)}, f32[216,128]{1,0:T(8,128)S(1)}, u32[]{:S(2)}, u32[]{:S(2)}) collective-permute-start(f32[216,128]{1,0:T(8,128)S(1)} %get-tuple-element.55), channel_id=1, source_target_pairs={{0,3},{1,2},{2,1},{3,0},{4,7},{5,6},{6,5},{7,4},{8,11},{9,10},{10,... | collective-permute-start | bytes 331784 | tf_op jit(solution)/shard_map/ppermute | solution.py:874
  11.8 0.5 collective-permute-start.7
  12.3 0.0 collective-permute-done.refs_1_
  12.3 0.7 collective-permute-start.8
  12.9 0.6 collective-permute-done.1.refs_2_
  13.5 0.0 copy-start.2
  13.5 2.1 %products.2 = (f32[192,128]{1,0:T(8,128)S(1)}, f32[192,128]{1,0:T(8,128)S(1)}, f32[192,128]{1,0:T(8,128)S(1)}, f32[192,128]{1,0:T(8,128)S(1)}, f32[4,48,128]{2,1,0:T(8,128)S(1)}) custom-call(s32[2]{0:T(128)S(1)} %pad_add_fusion.ids_ref, f32[216,128]{1,0:T(8,128)S(1)} %get-tuple-element.45.refs_0_, f32[216,128]{1,0:T(8,128)S(1)} %collective-permute-done.refs_1_, ...), custom_call_target="tpu_custom_call" | custom-call | tf_op jit(solution)/shard_map/products/pallas_call | solution.py:851
  15.7 0.0 copy-start.3
  15.7 0.0 copy-start.4
  15.7 3.9 %collective-permute-start.3 = (f32[192,128]{1,0:T(8,128)S(1)}, f32[192,128]{1,0:T(8,128)S(1)}, u32[]{:S(2)}, u32[]{:S(2)}) collective-permute-start(f32[192,128]{1,0:T(8,128)S(1)} %get-tuple-element.50), channel_id=1, source_target_pairs={{0,3},{1,2},{2,1},{3,0},{4,7},{5,6},{6,5},{7,4},{8,11},{9,10},{10,... | collective-permute-start | bytes 294920 | tf_op jit(solution)/shard_map/ppermute | solution.py:874
  19.6 0.0 collective-permute-start.4
  19.6 0.0 collective-permute-done.6.refs_1_
  19.6 0.6 collective-permute-start.5
  20.3 0.0 collective-permute-done.8.refs_3_
  20.3 2.2 %products.3 = (f32[192,128]{1,0:T(8,128)S(1)}, f32[192,128]{1,0:T(8,128)S(1)}, f32[192,128]{1,0:T(8,128)S(1)}, f32[192,128]{1,0:T(8,128)S(1)}) custom-call(s32[2]{0:T(128)S(1)} %pad_add_fusion.ids_ref, f32[216,128]{1,0:T(8,128)S(1)} %get-tuple-element.54.refs_0_, f32[216,128]{1,0:T(8,128)S(1)} %collective-permute-done.6.refs_1_, ...), custom_call_target="tpu_custom_call" | custom-call | tf_op jit(solution)/shard_map/products/pallas_call | solution.py:851
  22.5 2.9 %collective-permute-start.9 = (f32[192,128]{1,0:T(8,128)S(1)}, f32[192,128]{1,0:T(8,128)S(1)}, u32[]{:S(2)}, u32[]{:S(2)}) collective-permute-start(f32[192,128]{1,0:T(8,128)S(1)} %get-tuple-element.60), channel_id=1, source_target_pairs={{0,3},{1,2},{2,1},{3,0},{4,7},{5,6},{6,5},{7,4},{8,11},{9,10},{10,... | collective-permute-start | bytes 294920 | tf_op jit(solution)/shard_map/ppermute | solution.py:874
  25.4 0.0 collective-permute-done.3.refs_1_
  25.4 0.6 collective-permute-start.11
  26.1 0.0 collective-permute-done.4.refs_2_
  26.1 0.0 collective-permute-done.5.refs_3_
  26.1 2.0 %collective-permute-done.9.refs_5_ = f32[192,128]{1,0:T(8,128)S(1)} collective-permute-done((f32[192,128]{1,0:T(8,128)S(1)}, f32[192,128]{1,0:T(8,128)S(1)}, u32[]{:S(2)}, u32[]{:S(2)}) %collective-permute-start.9) | collective-permute-done | bytes 98336 | tf_op jit(solution)/shard_map/ppermute | solution.py:874
  28.1 1.9 %collective-permute-done.10.refs_6_ = f32[192,128]{1,0:T(8,128)S(1)} collective-permute-done((f32[192,128]{1,0:T(8,128)S(1)}, f32[192,128]{1,0:T(8,128)S(1)}, u32[]{:S(2)}, u32[]{:S(2)}) %collective-permute-start.10) | collective-permute-done | bytes 98336 | tf_op jit(solution)/shard_map/ppermute | solution.py:874
  30.0 0.0 collective-permute-done.11.refs_7_
  30.0 1.9 %first.1 = (f32[2304,128]{1,0:T(8,128)S(1)}, f32[240,128]{1,0:T(8,128)S(1)}) custom-call(s32[2]{0:T(128)S(1)} %pad_add_fusion.ids_ref, s32[1,4]{1,0:T(1,128)S(1)} %copy-done.2, f32[192,128]{1,0:T(8,128)S(1)} %get-tuple-element.49.refs_0_, f32[192,128]{1,0:T(8,128)S(1)} %collective-permute-done.3.refs_1_, f32[192,128]{1,0:T(8,128)S(1)} %collective-permute-done.4.refs_2_, ...), custom_call_target="tpu_custom_call" | custom-call | tf_op jit(solution)/shard_map/first/pallas_call | solution.py:851
  31.9 4.2 %collective-permute-start.17 = (f32[240,128]{1,0:T(8,128)S(1)}, f32[240,128]{1,0:T(8,128)S(1)}, u32[]{:S(2)}, u32[]{:S(2)}) collective-permute-start(f32[240,128]{1,0:T(8,128)S(1)} %get-tuple-element.63.refs_0_.refs_8_), channel_id=1, source_target_pairs={{0,24},{4,28},{8,16},{12,20},{16,8},{20,12},{24,0},{28,4},{1,25},{... | collective-permute-start | bytes 368648 | tf_op jit(solution)/shard_map/ppermute | solution.py:884
  36.1 0.6 collective-permute-start.13
  36.8 2.3 %collective-permute-done.17.refs_6_ = f32[240,128]{1,0:T(8,128)S(1)} collective-permute-done((f32[240,128]{1,0:T(8,128)S(1)}, f32[240,128]{1,0:T(8,128)S(1)}, u32[]{:S(2)}, u32[]{:S(2)}) %collective-permute-start.17) | collective-permute-done | bytes 122912 | tf_op jit(solution)/shard_map/ppermute | solution.py:884
  39.1 0.0 collective-permute-start.18
  39.1 3.3 %collective-permute-done.15.refs_4_ = f32[240,128]{1,0:T(8,128)S(1)} collective-permute-done((f32[240,128]{1,0:T(8,128)S(1)}, f32[240,128]{1,0:T(8,128)S(1)}, u32[]{:S(2)}, u32[]{:S(2)}) %collective-permute-start.15) | collective-permute-done | bytes 122912 | tf_op jit(solution)/shard_map/ppermute | solution.py:884
  42.4 0.0 collective-permute-start.16
  42.4 0.5 collective-permute-start.14
  42.9 0.8 %collective-permute-done.16.refs_5_ = f32[240,128]{1,0:T(8,128)S(1)} collective-permute-done((f32[240,128]{1,0:T(8,128)S(1)}, f32[240,128]{1,0:T(8,128)S(1)}, u32[]{:S(2)}, u32[]{:S(2)}) %collective-permute-start.16) | collective-permute-done | bytes 122912 | tf_op jit(solution)/shard_map/ppermute | solution.py:888
  43.8 0.2 collective-permute-done.14.refs_3_
  43.9 4.4 %second.1 = (f32[2304,128]{1,0:T(8,128)S(1)}, f32[2304,128]{1,0:T(8,128)S(1)}, f32[2304,128]{1,0:T(8,128)S(1)}, f32[240,128]{1,0:T(8,128)S(1)}, f32[8,128]{1,0:T(8,128)S(1)}) custom-call(s32[2]{0:T(128)S(1)} %pad_add_fusion.ids_ref, s32[1,4]{1,0:T(1,128)S(1)} %copy-done.2, s32[1,4]{1,0:T(1,128)S(1)} %copy-done.3, ...), custom_call_target="tpu_custom_call", output_to_operand_aliasing={{0}: (13, {})} | custom-call | tf_op jit(solution)/shard_map/second/pallas_call | solution.py:851
  48.4 2.5 %collective-permute-start.24 = (f32[240,128]{1,0:T(8,128)S(1)}, f32[240,128]{1,0:T(8,128)S(1)}, u32[]{:S(2)}, u32[]{:S(2)}) collective-permute-start(f32[240,128]{1,0:T(8,128)S(1)} %get-tuple-element.65.refs_0_.refs_8_), channel_id=1, source_target_pairs={{0,24},{4,28},{8,16},{12,20},{16,8},{20,12},{24,0},{28,4},{1,25},{... | collective-permute-start | bytes 368648 | tf_op jit(solution)/shard_map/ppermute | solution.py:884
  50.9 0.1 collective-permute-start.22
  51.0 1.8 %collective-permute-start.20 = (f32[240,128]{1,0:T(8,128)S(1)}, f32[240,128]{1,0:T(8,128)S(1)}, u32[]{:S(2)}, u32[]{:S(2)}) collective-permute-start(f32[240,128]{1,0:T(8,128)S(1)} %get-tuple-element.65.refs_0_.refs_8_), channel_id=1, source_target_pairs={{0,8},{4,12},{8,0},{12,4},{16,24},{20,28},{24,16},{28,20},{1,9},{5... | collective-permute-start | bytes 368648 | tf_op jit(solution)/shard_map/ppermute | solution.py:884
  52.8 2.0 %turn.2 = (f32[96,2304]{1,0:T(8,128)S(1)}, f32[96,2304]{1,0:T(8,128)S(1)}, bf16[192,2304]{1,0:T(8,128)(2,1)S(1)}) custom-call(f32[2304,128]{1,0:T(8,128)S(1)} %get-tuple-element.66.refs_0_, f32[2304,128]{1,0:T(8,128)S(1)} %get-tuple-element.67.refs_1_.refs_9_), custom_call_target="tpu_custom_call" | custom-call | tf_op jit(solution)/shard_map/turn/pallas_call | solution.py:851
  54.9 1.6 %collective-permute-done.24.refs_6_ = f32[240,128]{1,0:T(8,128)S(1)} collective-permute-done((f32[240,128]{1,0:T(8,128)S(1)}, f32[240,128]{1,0:T(8,128)S(1)}, u32[]{:S(2)}, u32[]{:S(2)}) %collective-permute-start.24) | collective-permute-done | bytes 122912 | tf_op jit(solution)/shard_map/ppermute | solution.py:884
  56.5 5.7 %collective-permute-done.22.refs_4_ = f32[240,128]{1,0:T(8,128)S(1)} collective-permute-done((f32[240,128]{1,0:T(8,128)S(1)}, f32[240,128]{1,0:T(8,128)S(1)}, u32[]{:S(2)}, u32[]{:S(2)}) %collective-permute-start.22) | collective-permute-done | bytes 122912 | tf_op jit(solution)/shard_map/ppermute | solution.py:884
  62.2 0.5 collective-permute-start.21
  62.7 0.0 collective-permute-start.25
  62.7 0.8 %collective-permute-done.23.refs_5_ = f32[240,128]{1,0:T(8,128)S(1)} collective-permute-done((f32[240,128]{1,0:T(8,128)S(1)}, f32[240,128]{1,0:T(8,128)S(1)}, u32[]{:S(2)}, u32[]{:S(2)}) %collective-permute-start.23) | collective-permute-done | bytes 122912 | tf_op jit(solution)/shard_map/ppermute | solution.py:888
  63.5 0.2 collective-permute-done.21.refs_3_
  63.7 0.3 collective-permute-done.25.refs_7_
  64.0 3.5 %third.1 = (f32[2304,128]{1,0:T(8,128)S(1)}, f32[2304,128]{1,0:T(8,128)S(1)}, f32[2304,128]{1,0:T(8,128)S(1)}, f32[128,128]{1,0:T(8,128)S(1)}) custom-call(s32[2]{0:T(128)S(1)} %pad_add_fusion.ids_ref, s32[1,4]{1,0:T(1,128)S(1)} %copy-done.2, s32[1,4]{1,0:T(1,128)S(1)} %copy-done.3, s32[1,4]{1,0:T(1,128)S(1)} %copy-done.4, ...), custom_call_target="tpu_custom_call", output_to_operand_aliasing={{0}: (15, {})} | custom-call | tf_op jit(solution)/shard_map/third/pallas_call | solution.py:851
  67.5 1.8 %collective-permute-start.31 = (f32[128,128]{1,0:T(8,128)S(1)}, f32[128,128]{1,0:T(8,128)S(1)}, u32[]{:S(2)}, u32[]{:S(2)}) collective-permute-start(f32[128,128]{1,0:T(8,128)S(1)} %get-tuple-element.74.refs_0_), channel_id=1, source_target_pairs={{0,24},{4,28},{8,16},{12,20},{16,8},{20,12},{24,0},{28,4},{1,25},{... | collective-permute-start | bytes 196616 | tf_op jit(solution)/shard_map/ppermute | solution.py:884
  69.3 2.6 %collective-permute-start.27 = (f32[128,128]{1,0:T(8,128)S(1)}, f32[128,128]{1,0:T(8,128)S(1)}, u32[]{:S(2)}, u32[]{:S(2)}) collective-permute-start(f32[128,128]{1,0:T(8,128)S(1)} %get-tuple-element.74.refs_0_), channel_id=1, source_target_pairs={{0,8},{4,12},{8,0},{12,4},{16,24},{20,28},{24,16},{28,20},{1,9},{5... | collective-permute-start | bytes 196616 | tf_op jit(solution)/shard_map/ppermute | solution.py:884
  71.9 2.5 %turn.3 = (f32[96,2304]{1,0:T(8,128)S(1)}, f32[96,2304]{1,0:T(8,128)S(1)}, f32[96,2304]{1,0:T(8,128)S(1)}) custom-call(f32[2304,128]{1,0:T(8,128)S(1)} %get-tuple-element.75.refs_0_, f32[2304,128]{1,0:T(8,128)S(1)} %get-tuple-element.76.refs_1_, f32[2304,128]{1,0:T(8,128)S(1)} %get-tuple-element.77.refs_2_), custom_call_target="tpu_custom_call" | custom-call | tf_op jit(solution)/shard_map/turn/pallas_call | solution.py:851
  74.4 0.6 collective-permute-start.32
  75.0 1.2 %collective-permute-done.29.refs_4_ = f32[128,128]{1,0:T(8,128)S(1)} collective-permute-done((f32[128,128]{1,0:T(8,128)S(1)}, f32[128,128]{1,0:T(8,128)S(1)}, u32[]{:S(2)}, u32[]{:S(2)}) %collective-permute-start.29) | collective-permute-done | bytes 65568 | tf_op jit(solution)/shard_map/ppermute | solution.py:884
  76.2 0.0 collective-permute-start.30
  76.3 0.5 collective-permute-start.28
  76.8 0.7 collective-permute-done.30.refs_5_
  77.5 0.2 collective-permute-done.28.refs_3_
  77.7 2.8 %last.1 = (f32[3,32,2304]{2,1,0:T(8,128)}, f32[3,32,2304]{2,1,0:T(8,128)}) custom-call(s32[2]{0:T(128)S(1)} %pad_add_fusion.ids_ref, s32[1,4]{1,0:T(1,128)S(1)} %copy-done.2, s32[1,4]{1,0:T(1,128)S(1)} %copy-done.3, s32[1,4]{1,0:T(1,128)S(1)} %copy-done.4, f32[128,128]{1,0:T(8,128)S(1)} %get-tuple-element.74.refs_0_, ...), custom_call_target="tpu_custom_call" | custom-call | tf_op jit(solution)/shard_map/last/pallas_call | solution.py:851
  (23 shorter events, 0.1 us)
Async XLA Ops:
  0.6 12.9 %copy-start.1 = (bf16[256,256]{1,0:T(8,128)(2,1)S(1)}, bf16[256,256]{1,0:T(8,128)(2,1)}, u32[]{:S(2)}) copy-start(bf16[256,256]{1,0:T(8,128)(2,1)} %constant.14.clone.refs_5_) | copy-start | bytes 393220
  0.6 12.9 %copy-start = (bf16[512,768]{1,0:T(8,128)(2,1)S(1)}, bf16[512,768]{1,0:T(8,128)(2,1)}, u32[]{:S(2)}) copy-start(bf16[512,768]{1,0:T(8,128)(2,1)} %constant.13.clone.refs_4_) | copy-start | bytes 2359300
  3.1 9.2 %collective-permute-start = (f32[216,128]{1,0:T(8,128)S(1)}, f32[216,128]{1,0:T(8,128)S(1)}, u32[]{:S(2)}, u32[]{:S(2)}) collective-permute-start(f32[216,128]{1,0:T(8,128)S(1)} %get-tuple-element.46), channel_id=1, source_target_pairs={{0,3},{1,2},{2,1},{3,0},{4,7},{5,6},{6,5},{7,4},{8,11},{9,10},{10,... | collective-permute-start | bytes 331784 | tf_op jit(solution)/shard_map/ppermute | solution.py:874
  7.0 6.5 %collective-permute-start.1 = (f32[216,128]{1,0:T(8,128)S(1)}, f32[216,128]{1,0:T(8,128)S(1)}, u32[]{:S(2)}, u32[]{:S(2)}) collective-permute-start(f32[216,128]{1,0:T(8,128)S(1)} %get-tuple-element.47), channel_id=1, source_target_pairs={{0,1},{1,0},{2,3},{3,2},{4,5},{5,4},{6,7},{7,6},{8,9},{9,8},{10,11... | collective-permute-start | bytes 331784 | tf_op jit(solution)/shard_map/ppermute | solution.py:874
  7.6 5.9 %collective-permute-start.2 = (f32[216,128]{1,0:T(8,128)S(1)}, f32[216,128]{1,0:T(8,128)S(1)}, u32[]{:S(2)}, u32[]{:S(2)}) collective-permute-start(f32[216,128]{1,0:T(8,128)S(1)} %get-tuple-element.48), channel_id=1, source_target_pairs={{0,2},{1,3},{2,0},{3,1},{4,6},{5,7},{6,4},{7,5},{8,10},{9,11},{10,... | collective-permute-start | bytes 331784 | tf_op jit(solution)/shard_map/ppermute | solution.py:874
  8.8 10.8 %collective-permute-start.6 = (f32[216,128]{1,0:T(8,128)S(1)}, f32[216,128]{1,0:T(8,128)S(1)}, u32[]{:S(2)}, u32[]{:S(2)}) collective-permute-start(f32[216,128]{1,0:T(8,128)S(1)} %get-tuple-element.55), channel_id=1, source_target_pairs={{0,3},{1,2},{2,1},{3,0},{4,7},{5,6},{6,5},{7,4},{8,11},{9,10},{10,... | collective-permute-start | bytes 331784 | tf_op jit(solution)/shard_map/ppermute | solution.py:874
  11.8 8.5 %collective-permute-start.7 = (f32[216,128]{1,0:T(8,128)S(1)}, f32[216,128]{1,0:T(8,128)S(1)}, u32[]{:S(2)}, u32[]{:S(2)}) collective-permute-start(f32[216,128]{1,0:T(8,128)S(1)} %get-tuple-element.56), channel_id=1, source_target_pairs={{0,1},{1,0},{2,3},{3,2},{4,5},{5,4},{6,7},{7,6},{8,9},{9,8},{10,11... | collective-permute-start | bytes 331784 | tf_op jit(solution)/shard_map/ppermute | solution.py:874
  12.3 8.0 %collective-permute-start.8 = (f32[216,128]{1,0:T(8,128)S(1)}, f32[216,128]{1,0:T(8,128)S(1)}, u32[]{:S(2)}, u32[]{:S(2)}) collective-permute-start(f32[216,128]{1,0:T(8,128)S(1)} %get-tuple-element.57), channel_id=1, source_target_pairs={{0,2},{1,3},{2,0},{3,1},{4,6},{5,7},{6,4},{7,5},{8,10},{9,11},{10,... | collective-permute-start | bytes 331784 | tf_op jit(solution)/shard_map/ppermute | solution.py:874
  13.5 16.5 %copy-start.2 = (s32[1,4]{1,0:T(1,128)S(1)}, s32[1,4]{1,0:T(1,128)}, u32[]{:S(2)}) copy-start(s32[1,4]{1,0:T(1,128)} %partner_ref.7) | copy-start | bytes 52
  15.7 28.3 %copy-start.3 = (s32[1,4]{1,0:T(1,128)S(1)}, s32[1,4]{1,0:T(1,128)}, u32[]{:S(2)}) copy-start(s32[1,4]{1,0:T(1,128)} %side_ref.5) | copy-start | bytes 52
  15.7 28.3 %copy-start.4 = (s32[1,4]{1,0:T(1,128)S(1)}, s32[1,4]{1,0:T(1,128)}, u32[]{:S(2)}) copy-start(s32[1,4]{1,0:T(1,128)} %flip_ref.5) | copy-start | bytes 52
  15.7 9.7 %collective-permute-start.3 = (f32[192,128]{1,0:T(8,128)S(1)}, f32[192,128]{1,0:T(8,128)S(1)}, u32[]{:S(2)}, u32[]{:S(2)}) collective-permute-start(f32[192,128]{1,0:T(8,128)S(1)} %get-tuple-element.50), channel_id=1, source_target_pairs={{0,3},{1,2},{2,1},{3,0},{4,7},{5,6},{6,5},{7,4},{8,11},{9,10},{10,... | collective-permute-start | bytes 294920 | tf_op jit(solution)/shard_map/ppermute | solution.py:874
  19.6 6.4 %collective-permute-start.4 = (f32[192,128]{1,0:T(8,128)S(1)}, f32[192,128]{1,0:T(8,128)S(1)}, u32[]{:S(2)}, u32[]{:S(2)}) collective-permute-start(f32[192,128]{1,0:T(8,128)S(1)} %get-tuple-element.51), channel_id=1, source_target_pairs={{0,1},{1,0},{2,3},{3,2},{4,5},{5,4},{6,7},{7,6},{8,9},{9,8},{10,11... | collective-permute-start | bytes 294920 | tf_op jit(solution)/shard_map/ppermute | solution.py:874
  19.6 6.4 %collective-permute-start.5 = (f32[192,128]{1,0:T(8,128)S(1)}, f32[192,128]{1,0:T(8,128)S(1)}, u32[]{:S(2)}, u32[]{:S(2)}) collective-permute-start(f32[192,128]{1,0:T(8,128)S(1)} %get-tuple-element.52), channel_id=1, source_target_pairs={{0,2},{1,3},{2,0},{3,1},{4,6},{5,7},{6,4},{7,5},{8,10},{9,11},{10,... | collective-permute-start | bytes 294920 | tf_op jit(solution)/shard_map/ppermute | solution.py:874
  22.5 5.6 %collective-permute-start.9 = (f32[192,128]{1,0:T(8,128)S(1)}, f32[192,128]{1,0:T(8,128)S(1)}, u32[]{:S(2)}, u32[]{:S(2)}) collective-permute-start(f32[192,128]{1,0:T(8,128)S(1)} %get-tuple-element.60), channel_id=1, source_target_pairs={{0,3},{1,2},{2,1},{3,0},{4,7},{5,6},{6,5},{7,4},{8,11},{9,10},{10,... | collective-permute-start | bytes 294920 | tf_op jit(solution)/shard_map/ppermute | solution.py:874
  25.4 4.6 %collective-permute-start.10 = (f32[192,128]{1,0:T(8,128)S(1)}, f32[192,128]{1,0:T(8,128)S(1)}, u32[]{:S(2)}, u32[]{:S(2)}) collective-permute-start(f32[192,128]{1,0:T(8,128)S(1)} %get-tuple-element.61), channel_id=1, source_target_pairs={{0,1},{1,0},{2,3},{3,2},{4,5},{5,4},{6,7},{7,6},{8,9},{9,8},{10,11... | collective-permute-start | bytes 294920 | tf_op jit(solution)/shard_map/ppermute | solution.py:874
  25.4 4.6 %collective-permute-start.11 = (f32[192,128]{1,0:T(8,128)S(1)}, f32[192,128]{1,0:T(8,128)S(1)}, u32[]{:S(2)}, u32[]{:S(2)}) collective-permute-start(f32[192,128]{1,0:T(8,128)S(1)} %get-tuple-element.62), channel_id=1, source_target_pairs={{0,2},{1,3},{2,0},{3,1},{4,6},{5,7},{6,4},{7,5},{8,10},{9,11},{10,... | collective-permute-start | bytes 294920 | tf_op jit(solution)/shard_map/ppermute | solution.py:874
  31.9 7.2 %collective-permute-start.17 = (f32[240,128]{1,0:T(8,128)S(1)}, f32[240,128]{1,0:T(8,128)S(1)}, u32[]{:S(2)}, u32[]{:S(2)}) collective-permute-start(f32[240,128]{1,0:T(8,128)S(1)} %get-tuple-element.63.refs_0_.refs_8_), channel_id=1, source_target_pairs={{0,24},{4,28},{8,16},{12,20},{16,8},{20,12},{24,0},{28,4},{1,25},{... | collective-permute-start | bytes 368648 | tf_op jit(solution)/shard_map/ppermute | solution.py:884
  36.1 6.3 %collective-permute-start.15 = (f32[240,128]{1,0:T(8,128)S(1)}, f32[240,128]{1,0:T(8,128)S(1)}, u32[]{:S(2)}, u32[]{:S(2)}) collective-permute-start(f32[240,128]{1,0:T(8,128)S(1)} %get-tuple-element.63.refs_0_.refs_8_), channel_id=1, source_target_pairs={{0,16},{4,20},{8,24},{12,28},{16,0},{20,4},{24,8},{28,12},{1,17},{... | collective-permute-start | bytes 368648 | tf_op jit(solution)/shard_map/ppermute | solution.py:884
  36.1 6.3 %collective-permute-start.13 = (f32[240,128]{1,0:T(8,128)S(1)}, f32[240,128]{1,0:T(8,128)S(1)}, u32[]{:S(2)}, u32[]{:S(2)}) collective-permute-start(f32[240,128]{1,0:T(8,128)S(1)} %get-tuple-element.63.refs_0_.refs_8_), channel_id=1, source_target_pairs={{0,8},{4,12},{8,0},{12,4},{16,24},{20,28},{24,16},{28,20},{1,9},{5... | collective-permute-start | bytes 368648 | tf_op jit(solution)/shard_map/ppermute | solution.py:884
  36.8 6.2 %collective-permute-start.12 = (f32[240,128]{1,0:T(8,128)S(1)}, f32[240,128]{1,0:T(8,128)S(1)}, u32[]{:S(2)}, u32[]{:S(2)}) collective-permute-start(f32[240,128]{1,0:T(8,128)S(1)} %get-tuple-element.63.refs_0_.refs_8_), channel_id=1, source_target_pairs={{0,4},{4,0},{8,12},{12,8},{16,20},{20,16},{24,28},{28,24},{1,5},{5... | collective-permute-start | bytes 368648 | tf_op jit(solution)/shard_map/ppermute | solution.py:888
  39.1 3.8 %collective-permute-start.18 = (f32[240,128]{1,0:T(8,128)S(1)}, f32[240,128]{1,0:T(8,128)S(1)}, u32[]{:S(2)}, u32[]{:S(2)}) collective-permute-start(f32[240,128]{1,0:T(8,128)S(1)} %collective-permute-done.17.refs_6_), channel_id=1, source_target_pairs={{0,4},{4,0},{8,12},{12,8},{16,20},{20,16},{24,28},{28,24},{1,5},{5... | collective-permute-start | bytes 368648 | tf_op jit(solution)/shard_map/ppermute | solution.py:888
  42.4 1.3 %collective-permute-start.16 = (f32[240,128]{1,0:T(8,128)S(1)}, f32[240,128]{1,0:T(8,128)S(1)}, u32[]{:S(2)}, u32[]{:S(2)}) collective-permute-start(f32[240,128]{1,0:T(8,128)S(1)} %collective-permute-done.15.refs_4_), channel_id=1, source_target_pairs={{0,4},{4,0},{8,12},{12,8},{16,20},{20,16},{24,28},{28,24},{1,5},{5... | collective-permute-start | bytes 368648 | tf_op jit(solution)/shard_map/ppermute | solution.py:888
  42.4 1.5 %collective-permute-start.14 = (f32[240,128]{1,0:T(8,128)S(1)}, f32[240,128]{1,0:T(8,128)S(1)}, u32[]{:S(2)}, u32[]{:S(2)}) collective-permute-start(f32[240,128]{1,0:T(8,128)S(1)} %collective-permute-done.13.refs_2_), channel_id=1, source_target_pairs={{0,4},{4,0},{8,12},{12,8},{16,20},{20,16},{24,28},{28,24},{1,5},{5... | collective-permute-start | bytes 368648 | tf_op jit(solution)/shard_map/ppermute | solution.py:888
  48.4 8.1 %collective-permute-start.24 = (f32[240,128]{1,0:T(8,128)S(1)}, f32[240,128]{1,0:T(8,128)S(1)}, u32[]{:S(2)}, u32[]{:S(2)}) collective-permute-start(f32[240,128]{1,0:T(8,128)S(1)} %get-tuple-element.65.refs_0_.refs_8_), channel_id=1, source_target_pairs={{0,24},{4,28},{8,16},{12,20},{16,8},{20,12},{24,0},{28,4},{1,25},{... | collective-permute-start | bytes 368648 | tf_op jit(solution)/shard_map/ppermute | solution.py:884
  50.9 11.3 %collective-permute-start.22 = (f32[240,128]{1,0:T(8,128)S(1)}, f32[240,128]{1,0:T(8,128)S(1)}, u32[]{:S(2)}, u32[]{:S(2)}) collective-permute-start(f32[240,128]{1,0:T(8,128)S(1)} %get-tuple-element.65.refs_0_.refs_8_), channel_id=1, source_target_pairs={{0,16},{4,20},{8,24},{12,28},{16,0},{20,4},{24,8},{28,12},{1,17},{... | collective-permute-start | bytes 368648 | tf_op jit(solution)/shard_map/ppermute | solution.py:884
  51.0 11.2 %collective-permute-start.20 = (f32[240,128]{1,0:T(8,128)S(1)}, f32[240,128]{1,0:T(8,128)S(1)}, u32[]{:S(2)}, u32[]{:S(2)}) collective-permute-start(f32[240,128]{1,0:T(8,128)S(1)} %get-tuple-element.65.refs_0_.refs_8_), channel_id=1, source_target_pairs={{0,8},{4,12},{8,0},{12,4},{16,24},{20,28},{24,16},{28,20},{1,9},{5... | collective-permute-start | bytes 368648 | tf_op jit(solution)/shard_map/ppermute | solution.py:884
  52.8 9.9 %collective-permute-start.19 = (f32[240,128]{1,0:T(8,128)S(1)}, f32[240,128]{1,0:T(8,128)S(1)}, u32[]{:S(2)}, u32[]{:S(2)}) collective-permute-start(f32[240,128]{1,0:T(8,128)S(1)} %get-tuple-element.65.refs_0_.refs_8_), channel_id=1, source_target_pairs={{0,4},{4,0},{8,12},{12,8},{16,20},{20,16},{24,28},{28,24},{1,5},{5... | collective-permute-start | bytes 368648 | tf_op jit(solution)/shard_map/ppermute | solution.py:888
  62.2 1.3 %collective-permute-start.23 = (f32[240,128]{1,0:T(8,128)S(1)}, f32[240,128]{1,0:T(8,128)S(1)}, u32[]{:S(2)}, u32[]{:S(2)}) collective-permute-start(f32[240,128]{1,0:T(8,128)S(1)} %collective-permute-done.22.refs_4_), channel_id=1, source_target_pairs={{0,4},{4,0},{8,12},{12,8},{16,20},{20,16},{24,28},{28,24},{1,5},{5... | collective-permute-start | bytes 368648 | tf_op jit(solution)/shard_map/ppermute | solution.py:888
  62.2 1.5 %collective-permute-start.21 = (f32[240,128]{1,0:T(8,128)S(1)}, f32[240,128]{1,0:T(8,128)S(1)}, u32[]{:S(2)}, u32[]{:S(2)}) collective-permute-start(f32[240,128]{1,0:T(8,128)S(1)} %collective-permute-done.20.refs_2_), channel_id=1, source_target_pairs={{0,4},{4,0},{8,12},{12,8},{16,20},{20,16},{24,28},{28,24},{1,5},{5... | collective-permute-start | bytes 368648 | tf_op jit(solution)/shard_map/ppermute | solution.py:888
  62.7 1.3 %collective-permute-start.25 = (f32[240,128]{1,0:T(8,128)S(1)}, f32[240,128]{1,0:T(8,128)S(1)}, u32[]{:S(2)}, u32[]{:S(2)}) collective-permute-start(f32[240,128]{1,0:T(8,128)S(1)} %collective-permute-done.24.refs_6_), channel_id=1, source_target_pairs={{0,4},{4,0},{8,12},{12,8},{16,20},{20,16},{24,28},{28,24},{1,5},{5... | collective-permute-start | bytes 368648 | tf_op jit(solution)/shard_map/ppermute | solution.py:888
  67.5 7.0 %collective-permute-start.31 = (f32[128,128]{1,0:T(8,128)S(1)}, f32[128,128]{1,0:T(8,128)S(1)}, u32[]{:S(2)}, u32[]{:S(2)}) collective-permute-start(f32[128,128]{1,0:T(8,128)S(1)} %get-tuple-element.74.refs_0_), channel_id=1, source_target_pairs={{0,24},{4,28},{8,16},{12,20},{16,8},{20,12},{24,0},{28,4},{1,25},{... | collective-permute-start | bytes 196616 | tf_op jit(solution)/shard_map/ppermute | solution.py:884
  69.3 6.9 %collective-permute-start.29 = (f32[128,128]{1,0:T(8,128)S(1)}, f32[128,128]{1,0:T(8,128)S(1)}, u32[]{:S(2)}, u32[]{:S(2)}) collective-permute-start(f32[128,128]{1,0:T(8,128)S(1)} %get-tuple-element.74.refs_0_), channel_id=1, source_target_pairs={{0,16},{4,20},{8,24},{12,28},{16,0},{20,4},{24,8},{28,12},{1,17},{... | collective-permute-start | bytes 196616 | tf_op jit(solution)/shard_map/ppermute | solution.py:884
  69.3 6.9 %collective-permute-start.27 = (f32[128,128]{1,0:T(8,128)S(1)}, f32[128,128]{1,0:T(8,128)S(1)}, u32[]{:S(2)}, u32[]{:S(2)}) collective-permute-start(f32[128,128]{1,0:T(8,128)S(1)} %get-tuple-element.74.refs_0_), channel_id=1, source_target_pairs={{0,8},{4,12},{8,0},{12,4},{16,24},{20,28},{24,16},{28,20},{1,9},{5... | collective-permute-start | bytes 196616 | tf_op jit(solution)/shard_map/ppermute | solution.py:884
  71.9 4.8 %collective-permute-start.26 = (f32[128,128]{1,0:T(8,128)S(1)}, f32[128,128]{1,0:T(8,128)S(1)}, u32[]{:S(2)}, u32[]{:S(2)}) collective-permute-start(f32[128,128]{1,0:T(8,128)S(1)} %get-tuple-element.74.refs_0_), channel_id=1, source_target_pairs={{0,4},{4,0},{8,12},{12,8},{16,20},{20,16},{24,28},{28,24},{1,5},{5... | collective-permute-start | bytes 196616 | tf_op jit(solution)/shard_map/ppermute | solution.py:888
  74.4 2.3 %collective-permute-start.32 = (f32[128,128]{1,0:T(8,128)S(1)}, f32[128,128]{1,0:T(8,128)S(1)}, u32[]{:S(2)}, u32[]{:S(2)}) collective-permute-start(f32[128,128]{1,0:T(8,128)S(1)} %collective-permute-done.31.refs_6_), channel_id=1, source_target_pairs={{0,4},{4,0},{8,12},{12,8},{16,20},{20,16},{24,28},{28,24},{1,5},{5... | collective-permute-start | bytes 196616 | tf_op jit(solution)/shard_map/ppermute | solution.py:888
  76.2 1.3 %collective-permute-start.30 = (f32[128,128]{1,0:T(8,128)S(1)}, f32[128,128]{1,0:T(8,128)S(1)}, u32[]{:S(2)}, u32[]{:S(2)}) collective-permute-start(f32[128,128]{1,0:T(8,128)S(1)} %collective-permute-done.29.refs_4_), channel_id=1, source_target_pairs={{0,4},{4,0},{8,12},{12,8},{16,20},{20,16},{24,28},{28,24},{1,5},{5... | collective-permute-start | bytes 196616 | tf_op jit(solution)/shard_map/ppermute | solution.py:888
  76.3 1.4 %collective-permute-start.28 = (f32[128,128]{1,0:T(8,128)S(1)}, f32[128,128]{1,0:T(8,128)S(1)}, u32[]{:S(2)}, u32[]{:S(2)}) collective-permute-start(f32[128,128]{1,0:T(8,128)S(1)} %collective-permute-done.27.refs_2_), channel_id=1, source_target_pairs={{0,4},{4,0},{8,12},{12,8},{16,20},{20,16},{24,28},{28,24},{1,5},{5... | collective-permute-start | bytes 196616 | tf_op jit(solution)/shard_map/ppermute | solution.py:888

commit v11 on v10

--- a/solution.py
+++ b/solution.py
@@ -882,7 +882,7 @@
     slots = [lines] + [None] * (parts - 1)
     for slot in range(2, parts, 2):
         slots[slot] = lax.ppermute(lines, "dom", [(i, i ^ slot) for i in range(parts)])
-        if beside and slot == parts - 2:
+        if beside and slot == parts // 2:
             slots[slot], *beside = lax.optimization_barrier((slots[slot], *beside))
     for slot in range(0, parts, 2):
         slots[slot + 1] = lax.ppermute(slots[slot], "dom", [(i, i ^ 1) for i in range(parts)])

time: 80.8 us -> 80.7 us (level)
  waiting for transfers between devices: 21.9 us -> 23.7 us
  starting transfers between devices: 32.7 us -> 31.1 us
    ppermute x9, waiting for transfers between devices: 14.2 us -> 15.9 us  [share_lines(): lax.ppermute(lines, 'dom', [(i, i ^ slot) for i in range(parts)])]
    ppermute x12, starting transfers between devices: 2.12 us -> 1.04 us  [share_lines(): lax.ppermute(slots[slot], 'dom', [(i, i ^ 1) for i in range(parts)])]
  transfers between devices with their start and end apart: 33 -> 33, of which waited for: 15 -> 16; matrix products, arithmetic and copies ran while one was open for 0% -> 0% of each run, Pallas kernels for 12% -> 12%
where the time goes in v11:
time: 80.7 us; the launch traced here: 80.5 us
  starting transfers between devices  31.1 us (39%)
  Pallas kernels  24.7 us (31%)
  waiting for transfers between devices  23.7 us (29%)
  between operations  0.92 us (1%)
    pallas_call x10, Pallas kernels, call(): pl.pallas_call(kernel, name=name, out_shape=[pltpu.VMEM(one.shape, one.dt...  24.7 us
    ppermute x12, starting transfers between devices, swap_blocks(): lax.ppermute(blocks[place], 'four', [(i, i ^ offset_of(place, size)) for...  16.8 us
    ppermute x9, waiting for transfers between devices, share_lines(): lax.ppermute(lines, 'dom', [(i, i ^ slot) for i in range(parts)])  15.9 us
    ppermute x9, starting transfers between devices, share_lines(): lax.ppermute(lines, 'dom', [(i, i ^ slot) for i in range(parts)])  13.2 us
    ppermute x12, waiting for transfers between devices, swap_blocks(): lax.ppermute(blocks[place], 'four', [(i, i ^ offset_of(place, size)) for...  4.54 us
    ppermute x12, waiting for transfers between devices, share_lines(): lax.ppermute(slots[slot], 'dom', [(i, i ^ 1) for i in range(parts)])  3.25 us
  transfers between devices with their start and end apart: 33, of which 16 were waited for; matrix products, arithmetic and copies ran while one was open for 0% of the time, Pallas kernels for 12%

profile of v11, /device:TPU:0, one launch (start us, length us, event | category | flops | bytes accessed | tf_op | source)
XLA Modules:
  0.0 80.5 jit_solution(9960634590846075079)
XLA Ops:
  0.6 0.0 copy-start.1
  0.6 0.0 copy-start
  0.7 0.1 pad_add_fusion.ids_ref
  0.7 2.3 %pack.2 = (f32[216,128]{1,0:T(8,128)S(1)}, f32[216,128]{1,0:T(8,128)S(1)}, f32[216,128]{1,0:T(8,128)S(1)}, f32[216,128]{1,0:T(8,128)S(1)}, f32[3,32,2304]{2,1,0:T(8,128)S(1)}) custom-call(s32[2]{0:T(128)S(1)} %pad_add_fusion.ids_ref, f32[3,32,2304]{2,1,0:T(8,128)} %source_ref.1), custom_call_target="tpu_custom_call" | custom-call | tf_op jit(solution)/shard_map/pack/pallas_call | solution.py:851
  3.1 4.0 %collective-permute-start = (f32[216,128]{1,0:T(8,128)S(1)}, f32[216,128]{1,0:T(8,128)S(1)}, u32[]{:S(2)}, u32[]{:S(2)}) collective-permute-start(f32[216,128]{1,0:T(8,128)S(1)} %get-tuple-element.46), channel_id=1, source_target_pairs={{0,3},{1,2},{2,1},{3,0},{4,7},{5,6},{6,5},{7,4},{8,11},{9,10},{10,... | collective-permute-start | bytes 331784 | tf_op jit(solution)/shard_map/ppermute | solution.py:874
  7.0 0.5 collective-permute-start.1
  7.6 0.1 collective-permute-start.2
  7.7 1.2 %pack.3 = (f32[216,128]{1,0:T(8,128)S(1)}, f32[216,128]{1,0:T(8,128)S(1)}, f32[216,128]{1,0:T(8,128)S(1)}, f32[216,128]{1,0:T(8,128)S(1)}) custom-call(s32[2]{0:T(128)S(1)} %pad_add_fusion.ids_ref, f32[3,32,2304]{2,1,0:T(8,128)S(1)} %get-tuple-element.53.source_ref), custom_call_target="tpu_custom_call" | custom-call | tf_op jit(solution)/shard_map/pack/pallas_call | solution.py:851
  8.8 2.9 %collective-permute-start.6 = (f32[216,128]{1,0:T(8,128)S(1)}, f32[216,128]{1,0:T(8,128)S(1)}, u32[]{:S(2)}, u32[]{:S(2)}) collective-permute-start(f32[216,128]{1,0:T(8,128)S(1)} %get-tuple-element.55), channel_id=1, source_target_pairs={{0,3},{1,2},{2,1},{3,0},{4,7},{5,6},{6,5},{7,4},{8,11},{9,10},{10,... | collective-permute-start | bytes 331784 | tf_op jit(solution)/shard_map/ppermute | solution.py:874
  11.8 0.5 collective-permute-start.7
  12.3 0.0 collective-permute-done.refs_1_
  12.3 0.7 collective-permute-start.8
  12.9 0.6 collective-permute-done.1.refs_2_
  13.5 0.0 copy-start.2
  13.5 2.1 %products.2 = (f32[192,128]{1,0:T(8,128)S(1)}, f32[192,128]{1,0:T(8,128)S(1)}, f32[192,128]{1,0:T(8,128)S(1)}, f32[192,128]{1,0:T(8,128)S(1)}, f32[4,48,128]{2,1,0:T(8,128)S(1)}) custom-call(s32[2]{0:T(128)S(1)} %pad_add_fusion.ids_ref, f32[216,128]{1,0:T(8,128)S(1)} %get-tuple-element.45.refs_0_, f32[216,128]{1,0:T(8,128)S(1)} %collective-permute-done.refs_1_, ...), custom_call_target="tpu_custom_call" | custom-call | tf_op jit(solution)/shard_map/products/pallas_call | solution.py:851
  15.7 0.0 copy-start.3
  15.7 0.0 copy-start.4
  15.7 3.9 %collective-permute-start.3 = (f32[192,128]{1,0:T(8,128)S(1)}, f32[192,128]{1,0:T(8,128)S(1)}, u32[]{:S(2)}, u32[]{:S(2)}) collective-permute-start(f32[192,128]{1,0:T(8,128)S(1)} %get-tuple-element.50), channel_id=1, source_target_pairs={{0,3},{1,2},{2,1},{3,0},{4,7},{5,6},{6,5},{7,4},{8,11},{9,10},{10,... | collective-permute-start | bytes 294920 | tf_op jit(solution)/shard_map/ppermute | solution.py:874
  19.6 0.0 collective-permute-start.4
  19.6 0.0 collective-permute-done.6.refs_1_
  19.6 0.6 collective-permute-start.5
  20.3 0.0 collective-permute-done.7.refs_2_
  20.3 0.0 collective-permute-done.8.refs_3_
  20.3 2.2 %products.3 = (f32[192,128]{1,0:T(8,128)S(1)}, f32[192,128]{1,0:T(8,128)S(1)}, f32[192,128]{1,0:T(8,128)S(1)}, f32[192,128]{1,0:T(8,128)S(1)}) custom-call(s32[2]{0:T(128)S(1)} %pad_add_fusion.ids_ref, f32[216,128]{1,0:T(8,128)S(1)} %get-tuple-element.54.refs_0_, f32[216,128]{1,0:T(8,128)S(1)} %collective-permute-done.6.refs_1_, ...), custom_call_target="tpu_custom_call" | custom-call | tf_op jit(solution)/shard_map/products/pallas_call | solution.py:851
  22.5 2.9 %collective-permute-start.9 = (f32[192,128]{1,0:T(8,128)S(1)}, f32[192,128]{1,0:T(8,128)S(1)}, u32[]{:S(2)}, u32[]{:S(2)}) collective-permute-start(f32[192,128]{1,0:T(8,128)S(1)} %get-tuple-element.60), channel_id=1, source_target_pairs={{0,3},{1,2},{2,1},{3,0},{4,7},{5,6},{6,5},{7,4},{8,11},{9,10},{10,... | collective-permute-start | bytes 294920 | tf_op jit(solution)/shard_map/ppermute | solution.py:874
  25.4 0.0 collective-permute-start.10
  25.4 0.0 collective-permute-done.3.refs_1_
  25.4 0.6 collective-permute-start.11
  26.1 0.0 collective-permute-done.4.refs_2_
  26.1 0.0 collective-permute-done.5.refs_3_
  26.1 2.0 %collective-permute-done.9.refs_5_ = f32[192,128]{1,0:T(8,128)S(1)} collective-permute-done((f32[192,128]{1,0:T(8,128)S(1)}, f32[192,128]{1,0:T(8,128)S(1)}, u32[]{:S(2)}, u32[]{:S(2)}) %collective-permute-start.9) | collective-permute-done | bytes 98336 | tf_op jit(solution)/shard_map/ppermute | solution.py:874
  28.1 1.9 %collective-permute-done.10.refs_6_ = f32[192,128]{1,0:T(8,128)S(1)} collective-permute-done((f32[192,128]{1,0:T(8,128)S(1)}, f32[192,128]{1,0:T(8,128)S(1)}, u32[]{:S(2)}, u32[]{:S(2)}) %collective-permute-start.10) | collective-permute-done | bytes 98336 | tf_op jit(solution)/shard_map/ppermute | solution.py:874
  30.0 0.0 collective-permute-done.11.refs_7_
  30.0 1.9 %first.1 = (f32[2304,128]{1,0:T(8,128)S(1)}, f32[240,128]{1,0:T(8,128)S(1)}) custom-call(s32[2]{0:T(128)S(1)} %pad_add_fusion.ids_ref, s32[1,4]{1,0:T(1,128)S(1)} %copy-done.2, f32[192,128]{1,0:T(8,128)S(1)} %get-tuple-element.49.refs_0_, f32[192,128]{1,0:T(8,128)S(1)} %collective-permute-done.3.refs_1_, f32[192,128]{1,0:T(8,128)S(1)} %collective-permute-done.4.refs_2_, ...), custom_call_target="tpu_custom_call" | custom-call | tf_op jit(solution)/shard_map/first/pallas_call | solution.py:851
  31.9 4.2 %collective-permute-start.17 = (f32[240,128]{1,0:T(8,128)S(1)}, f32[240,128]{1,0:T(8,128)S(1)}, u32[]{:S(2)}, u32[]{:S(2)}) collective-permute-start(f32[240,128]{1,0:T(8,128)S(1)} %get-tuple-element.63.refs_0_.refs_8_), channel_id=1, source_target_pairs={{0,24},{4,28},{8,16},{12,20},{16,8},{20,12},{24,0},{28,4},{1,25},{... | collective-permute-start | bytes 368648 | tf_op jit(solution)/shard_map/ppermute | solution.py:884
  36.1 0.0 collective-permute-start.15
  36.1 0.6 collective-permute-start.13
  36.8 0.0 collective-permute-start.12
  36.8 2.3 %collective-permute-done.17.refs_6_ = f32[240,128]{1,0:T(8,128)S(1)} collective-permute-done((f32[240,128]{1,0:T(8,128)S(1)}, f32[240,128]{1,0:T(8,128)S(1)}, u32[]{:S(2)}, u32[]{:S(2)}) %collective-permute-start.17) | collective-permute-done | bytes 122912 | tf_op jit(solution)/shard_map/ppermute | solution.py:884
  39.1 0.0 collective-permute-start.18
  39.1 3.3 %collective-permute-done.15.refs_4_ = f32[240,128]{1,0:T(8,128)S(1)} collective-permute-done((f32[240,128]{1,0:T(8,128)S(1)}, f32[240,128]{1,0:T(8,128)S(1)}, u32[]{:S(2)}, u32[]{:S(2)}) %collective-permute-start.15) | collective-permute-done | bytes 122912 | tf_op jit(solution)/shard_map/ppermute | solution.py:884
  42.4 0.0 collective-permute-start.16
  42.4 0.5 collective-permute-start.14
  42.9 0.8 %collective-permute-done.16.refs_5_ = f32[240,128]{1,0:T(8,128)S(1)} collective-permute-done((f32[240,128]{1,0:T(8,128)S(1)}, f32[240,128]{1,0:T(8,128)S(1)}, u32[]{:S(2)}, u32[]{:S(2)}) %collective-permute-start.16) | collective-permute-done | bytes 122912 | tf_op jit(solution)/shard_map/ppermute | solution.py:888
  43.8 0.2 collective-permute-done.14.refs_3_
  43.9 4.3 %second.1 = (f32[2304,128]{1,0:T(8,128)S(1)}, f32[2304,128]{1,0:T(8,128)S(1)}, f32[2304,128]{1,0:T(8,128)S(1)}, f32[240,128]{1,0:T(8,128)S(1)}, f32[8,128]{1,0:T(8,128)S(1)}) custom-call(s32[2]{0:T(128)S(1)} %pad_add_fusion.ids_ref, s32[1,4]{1,0:T(1,128)S(1)} %copy-done.2, s32[1,4]{1,0:T(1,128)S(1)} %copy-done.3, ...), custom_call_target="tpu_custom_call", output_to_operand_aliasing={{0}: (13, {})} | custom-call | tf_op jit(solution)/shard_map/second/pallas_call | solution.py:851
  48.3 1.5 %collective-permute-start.22 = (f32[240,128]{1,0:T(8,128)S(1)}, f32[240,128]{1,0:T(8,128)S(1)}, u32[]{:S(2)}, u32[]{:S(2)}) collective-permute-start(f32[240,128]{1,0:T(8,128)S(1)} %get-tuple-element.65.refs_0_.refs_8_), channel_id=1, source_target_pairs={{0,16},{4,20},{8,24},{12,28},{16,0},{20,4},{24,8},{28,12},{1,17},{... | collective-permute-start | bytes 368648 | tf_op jit(solution)/shard_map/ppermute | solution.py:884
  49.8 2.1 %collective-permute-start.24 = (f32[240,128]{1,0:T(8,128)S(1)}, f32[240,128]{1,0:T(8,128)S(1)}, u32[]{:S(2)}, u32[]{:S(2)}) collective-permute-start(f32[240,128]{1,0:T(8,128)S(1)} %get-tuple-element.65.refs_0_.refs_8_), channel_id=1, source_target_pairs={{0,24},{4,28},{8,16},{12,20},{16,8},{20,12},{24,0},{28,4},{1,25},{... | collective-permute-start | bytes 368648 | tf_op jit(solution)/shard_map/ppermute | solution.py:884
  51.9 2.0 %turn.2 = (f32[96,2304]{1,0:T(8,128)S(1)}, f32[96,2304]{1,0:T(8,128)S(1)}, bf16[192,2304]{1,0:T(8,128)(2,1)S(1)}) custom-call(f32[2304,128]{1,0:T(8,128)S(1)} %get-tuple-element.66.refs_0_, f32[2304,128]{1,0:T(8,128)S(1)} %get-tuple-element.67.refs_1_.refs_9_), custom_call_target="tpu_custom_call" | custom-call | tf_op jit(solution)/shard_map/turn/pallas_call | solution.py:851
  53.9 6.6 %collective-permute-done.22.refs_4_ = f32[240,128]{1,0:T(8,128)S(1)} collective-permute-done((f32[240,128]{1,0:T(8,128)S(1)}, f32[240,128]{1,0:T(8,128)S(1)}, u32[]{:S(2)}, u32[]{:S(2)}) %collective-permute-start.22) | collective-permute-done | bytes 122912 | tf_op jit(solution)/shard_map/ppermute | solution.py:884
  60.6 1.0 %collective-permute-done.20.refs_2_ = f32[240,128]{1,0:T(8,128)S(1)} collective-permute-done((f32[240,128]{1,0:T(8,128)S(1)}, f32[240,128]{1,0:T(8,128)S(1)}, u32[]{:S(2)}, u32[]{:S(2)}) %collective-permute-start.20) | collective-permute-done | bytes 122912 | tf_op jit(solution)/shard_map/ppermute | solution.py:884
  61.5 0.5 collective-permute-start.23
  62.0 0.8 %collective-permute-done.21.refs_3_ = f32[240,128]{1,0:T(8,128)S(1)} collective-permute-done((f32[240,128]{1,0:T(8,128)S(1)}, f32[240,128]{1,0:T(8,128)S(1)}, u32[]{:S(2)}, u32[]{:S(2)}) %collective-permute-start.21) | collective-permute-done | bytes 122912 | tf_op jit(solution)/shard_map/ppermute | solution.py:888
  62.9 0.2 collective-permute-done.23.refs_5_
  63.0 3.4 %third.1 = (f32[2304,128]{1,0:T(8,128)S(1)}, f32[2304,128]{1,0:T(8,128)S(1)}, f32[2304,128]{1,0:T(8,128)S(1)}, f32[128,128]{1,0:T(8,128)S(1)}) custom-call(s32[2]{0:T(128)S(1)} %pad_add_fusion.ids_ref, s32[1,4]{1,0:T(1,128)S(1)} %copy-done.2, s32[1,4]{1,0:T(1,128)S(1)} %copy-done.3, s32[1,4]{1,0:T(1,128)S(1)} %copy-done.4, ...), custom_call_target="tpu_custom_call", output_to_operand_aliasing={{0}: (15, {})} | custom-call | tf_op jit(solution)/shard_map/third/pallas_call | solution.py:851
  66.4 2.8 %collective-permute-start.29 = (f32[128,128]{1,0:T(8,128)S(1)}, f32[128,128]{1,0:T(8,128)S(1)}, u32[]{:S(2)}, u32[]{:S(2)}) collective-permute-start(f32[128,128]{1,0:T(8,128)S(1)} %get-tuple-element.74.refs_0_), channel_id=1, source_target_pairs={{0,16},{4,20},{8,24},{12,28},{16,0},{20,4},{24,8},{28,12},{1,17},{... | collective-permute-start | bytes 196616 | tf_op jit(solution)/shard_map/ppermute | solution.py:884
  69.3 1.9 %collective-permute-start.31 = (f32[128,128]{1,0:T(8,128)S(1)}, f32[128,128]{1,0:T(8,128)S(1)}, u32[]{:S(2)}, u32[]{:S(2)}) collective-permute-start(f32[128,128]{1,0:T(8,128)S(1)} %get-tuple-element.74.refs_0_), channel_id=1, source_target_pairs={{0,24},{4,28},{8,16},{12,20},{16,8},{20,12},{24,0},{28,4},{1,25},{... | collective-permute-start | bytes 196616 | tf_op jit(solution)/shard_map/ppermute | solution.py:884
  71.2 2.5 %turn.3 = (f32[96,2304]{1,0:T(8,128)S(1)}, f32[96,2304]{1,0:T(8,128)S(1)}, f32[96,2304]{1,0:T(8,128)S(1)}) custom-call(f32[2304,128]{1,0:T(8,128)S(1)} %get-tuple-element.75.refs_0_, f32[2304,128]{1,0:T(8,128)S(1)} %get-tuple-element.76.refs_1_, f32[2304,128]{1,0:T(8,128)S(1)} %get-tuple-element.77.refs_2_), custom_call_target="tpu_custom_call" | custom-call | tf_op jit(solution)/shard_map/turn/pallas_call | solution.py:851
  73.7 0.7 collective-permute-done.29.refs_4_
  74.4 1.3 %collective-permute-done.31.refs_6_ = f32[128,128]{1,0:T(8,128)S(1)} collective-permute-done((f32[128,128]{1,0:T(8,128)S(1)}, f32[128,128]{1,0:T(8,128)S(1)}, u32[]{:S(2)}, u32[]{:S(2)}) %collective-permute-start.31) | collective-permute-done | bytes 65568 | tf_op jit(solution)/shard_map/ppermute | solution.py:884
  75.7 0.6 collective-permute-done.27.refs_2_
  76.3 0.7 collective-permute-done.32.refs_7_
  77.0 0.6 collective-permute-done.28.refs_3_
  77.6 2.7 %last.1 = (f32[3,32,2304]{2,1,0:T(8,128)}, f32[3,32,2304]{2,1,0:T(8,128)}) custom-call(s32[2]{0:T(128)S(1)} %pad_add_fusion.ids_ref, s32[1,4]{1,0:T(1,128)S(1)} %copy-done.2, s32[1,4]{1,0:T(1,128)S(1)} %copy-done.3, s32[1,4]{1,0:T(1,128)S(1)} %copy-done.4, f32[128,128]{1,0:T(8,128)S(1)} %get-tuple-element.74.refs_0_, ...), custom_call_target="tpu_custom_call" | custom-call | tf_op jit(solution)/shard_map/last/pallas_call | solution.py:851
  (23 shorter events, 0.1 us)
Async XLA Ops:
  0.6 12.9 %copy-start.1 = (bf16[256,256]{1,0:T(8,128)(2,1)S(1)}, bf16[256,256]{1,0:T(8,128)(2,1)}, u32[]{:S(2)}) copy-start(bf16[256,256]{1,0:T(8,128)(2,1)} %constant.14.clone.refs_5_) | copy-start | bytes 393220
  0.6 12.9 %copy-start = (bf16[512,768]{1,0:T(8,128)(2,1)S(1)}, bf16[512,768]{1,0:T(8,128)(2,1)}, u32[]{:S(2)}) copy-start(bf16[512,768]{1,0:T(8,128)(2,1)} %constant.13.clone.refs_4_) | copy-start | bytes 2359300
  3.1 9.2 %collective-permute-start = (f32[216,128]{1,0:T(8,128)S(1)}, f32[216,128]{1,0:T(8,128)S(1)}, u32[]{:S(2)}, u32[]{:S(2)}) collective-permute-start(f32[216,128]{1,0:T(8,128)S(1)} %get-tuple-element.46), channel_id=1, source_target_pairs={{0,3},{1,2},{2,1},{3,0},{4,7},{5,6},{6,5},{7,4},{8,11},{9,10},{10,... | collective-permute-start | bytes 331784 | tf_op jit(solution)/shard_map/ppermute | solution.py:874
  7.0 6.5 %collective-permute-start.1 = (f32[216,128]{1,0:T(8,128)S(1)}, f32[216,128]{1,0:T(8,128)S(1)}, u32[]{:S(2)}, u32[]{:S(2)}) collective-permute-start(f32[216,128]{1,0:T(8,128)S(1)} %get-tuple-element.47), channel_id=1, source_target_pairs={{0,1},{1,0},{2,3},{3,2},{4,5},{5,4},{6,7},{7,6},{8,9},{9,8},{10,11... | collective-permute-start | bytes 331784 | tf_op jit(solution)/shard_map/ppermute | solution.py:874
  7.6 5.9 %collective-permute-start.2 = (f32[216,128]{1,0:T(8,128)S(1)}, f32[216,128]{1,0:T(8,128)S(1)}, u32[]{:S(2)}, u32[]{:S(2)}) collective-permute-start(f32[216,128]{1,0:T(8,128)S(1)} %get-tuple-element.48), channel_id=1, source_target_pairs={{0,2},{1,3},{2,0},{3,1},{4,6},{5,7},{6,4},{7,5},{8,10},{9,11},{10,... | collective-permute-start | bytes 331784 | tf_op jit(solution)/shard_map/ppermute | solution.py:874
  8.8 10.8 %collective-permute-start.6 = (f32[216,128]{1,0:T(8,128)S(1)}, f32[216,128]{1,0:T(8,128)S(1)}, u32[]{:S(2)}, u32[]{:S(2)}) collective-permute-start(f32[216,128]{1,0:T(8,128)S(1)} %get-tuple-element.55), channel_id=1, source_target_pairs={{0,3},{1,2},{2,1},{3,0},{4,7},{5,6},{6,5},{7,4},{8,11},{9,10},{10,... | collective-permute-start | bytes 331784 | tf_op jit(solution)/shard_map/ppermute | solution.py:874
  11.8 8.5 %collective-permute-start.7 = (f32[216,128]{1,0:T(8,128)S(1)}, f32[216,128]{1,0:T(8,128)S(1)}, u32[]{:S(2)}, u32[]{:S(2)}) collective-permute-start(f32[216,128]{1,0:T(8,128)S(1)} %get-tuple-element.56), channel_id=1, source_target_pairs={{0,1},{1,0},{2,3},{3,2},{4,5},{5,4},{6,7},{7,6},{8,9},{9,8},{10,11... | collective-permute-start | bytes 331784 | tf_op jit(solution)/shard_map/ppermute | solution.py:874
  12.3 8.0 %collective-permute-start.8 = (f32[216,128]{1,0:T(8,128)S(1)}, f32[216,128]{1,0:T(8,128)S(1)}, u32[]{:S(2)}, u32[]{:S(2)}) collective-permute-start(f32[216,128]{1,0:T(8,128)S(1)} %get-tuple-element.57), channel_id=1, source_target_pairs={{0,2},{1,3},{2,0},{3,1},{4,6},{5,7},{6,4},{7,5},{8,10},{9,11},{10,... | collective-permute-start | bytes 331784 | tf_op jit(solution)/shard_map/ppermute | solution.py:874
  13.5 16.5 %copy-start.2 = (s32[1,4]{1,0:T(1,128)S(1)}, s32[1,4]{1,0:T(1,128)}, u32[]{:S(2)}) copy-start(s32[1,4]{1,0:T(1,128)} %partner_ref.7) | copy-start | bytes 52
  15.7 28.3 %copy-start.3 = (s32[1,4]{1,0:T(1,128)S(1)}, s32[1,4]{1,0:T(1,128)}, u32[]{:S(2)}) copy-start(s32[1,4]{1,0:T(1,128)} %side_ref.5) | copy-start | bytes 52
  15.7 28.3 %copy-start.4 = (s32[1,4]{1,0:T(1,128)S(1)}, s32[1,4]{1,0:T(1,128)}, u32[]{:S(2)}) copy-start(s32[1,4]{1,0:T(1,128)} %flip_ref.5) | copy-start | bytes 52
  15.7 9.7 %collective-permute-start.3 = (f32[192,128]{1,0:T(8,128)S(1)}, f32[192,128]{1,0:T(8,128)S(1)}, u32[]{:S(2)}, u32[]{:S(2)}) collective-permute-start(f32[192,128]{1,0:T(8,128)S(1)} %get-tuple-element.50), channel_id=1, source_target_pairs={{0,3},{1,2},{2,1},{3,0},{4,7},{5,6},{6,5},{7,4},{8,11},{9,10},{10,... | collective-permute-start | bytes 294920 | tf_op jit(solution)/shard_map/ppermute | solution.py:874
  19.6 6.4 %collective-permute-start.4 = (f32[192,128]{1,0:T(8,128)S(1)}, f32[192,128]{1,0:T(8,128)S(1)}, u32[]{:S(2)}, u32[]{:S(2)}) collective-permute-start(f32[192,128]{1,0:T(8,128)S(1)} %get-tuple-element.51), channel_id=1, source_target_pairs={{0,1},{1,0},{2,3},{3,2},{4,5},{5,4},{6,7},{7,6},{8,9},{9,8},{10,11... | collective-permute-start | bytes 294920 | tf_op jit(solution)/shard_map/ppermute | solution.py:874
  19.6 6.4 %collective-permute-start.5 = (f32[192,128]{1,0:T(8,128)S(1)}, f32[192,128]{1,0:T(8,128)S(1)}, u32[]{:S(2)}, u32[]{:S(2)}) collective-permute-start(f32[192,128]{1,0:T(8,128)S(1)} %get-tuple-element.52), channel_id=1, source_target_pairs={{0,2},{1,3},{2,0},{3,1},{4,6},{5,7},{6,4},{7,5},{8,10},{9,11},{10,... | collective-permute-start | bytes 294920 | tf_op jit(solution)/shard_map/ppermute | solution.py:874
  22.5 5.6 %collective-permute-start.9 = (f32[192,128]{1,0:T(8,128)S(1)}, f32[192,128]{1,0:T(8,128)S(1)}, u32[]{:S(2)}, u32[]{:S(2)}) collective-permute-start(f32[192,128]{1,0:T(8,128)S(1)} %get-tuple-element.60), channel_id=1, source_target_pairs={{0,3},{1,2},{2,1},{3,0},{4,7},{5,6},{6,5},{7,4},{8,11},{9,10},{10,... | collective-permute-start | bytes 294920 | tf_op jit(solution)/shard_map/ppermute | solution.py:874
  25.4 4.6 %collective-permute-start.10 = (f32[192,128]{1,0:T(8,128)S(1)}, f32[192,128]{1,0:T(8,128)S(1)}, u32[]{:S(2)}, u32[]{:S(2)}) collective-permute-start(f32[192,128]{1,0:T(8,128)S(1)} %get-tuple-element.61), channel_id=1, source_target_pairs={{0,1},{1,0},{2,3},{3,2},{4,5},{5,4},{6,7},{7,6},{8,9},{9,8},{10,11... | collective-permute-start | bytes 294920 | tf_op jit(solution)/shard_map/ppermute | solution.py:874
  25.4 4.6 %collective-permute-start.11 = (f32[192,128]{1,0:T(8,128)S(1)}, f32[192,128]{1,0:T(8,128)S(1)}, u32[]{:S(2)}, u32[]{:S(2)}) collective-permute-start(f32[192,128]{1,0:T(8,128)S(1)} %get-tuple-element.62), channel_id=1, source_target_pairs={{0,2},{1,3},{2,0},{3,1},{4,6},{5,7},{6,4},{7,5},{8,10},{9,11},{10,... | collective-permute-start | bytes 294920 | tf_op jit(solution)/shard_map/ppermute | solution.py:874
  31.9 7.2 %collective-permute-start.17 = (f32[240,128]{1,0:T(8,128)S(1)}, f32[240,128]{1,0:T(8,128)S(1)}, u32[]{:S(2)}, u32[]{:S(2)}) collective-permute-start(f32[240,128]{1,0:T(8,128)S(1)} %get-tuple-element.63.refs_0_.refs_8_), channel_id=1, source_target_pairs={{0,24},{4,28},{8,16},{12,20},{16,8},{20,12},{24,0},{28,4},{1,25},{... | collective-permute-start | bytes 368648 | tf_op jit(solution)/shard_map/ppermute | solution.py:884
  36.1 6.3 %collective-permute-start.15 = (f32[240,128]{1,0:T(8,128)S(1)}, f32[240,128]{1,0:T(8,128)S(1)}, u32[]{:S(2)}, u32[]{:S(2)}) collective-permute-start(f32[240,128]{1,0:T(8,128)S(1)} %get-tuple-element.63.refs_0_.refs_8_), channel_id=1, source_target_pairs={{0,16},{4,20},{8,24},{12,28},{16,0},{20,4},{24,8},{28,12},{1,17},{... | collective-permute-start | bytes 368648 | tf_op jit(solution)/shard_map/ppermute | solution.py:884
  36.1 6.3 %collective-permute-start.13 = (f32[240,128]{1,0:T(8,128)S(1)}, f32[240,128]{1,0:T(8,128)S(1)}, u32[]{:S(2)}, u32[]{:S(2)}) collective-permute-start(f32[240,128]{1,0:T(8,128)S(1)} %get-tuple-element.63.refs_0_.refs_8_), channel_id=1, source_target_pairs={{0,8},{4,12},{8,0},{12,4},{16,24},{20,28},{24,16},{28,20},{1,9},{5... | collective-permute-start | bytes 368648 | tf_op jit(solution)/shard_map/ppermute | solution.py:884
  36.8 6.2 %collective-permute-start.12 = (f32[240,128]{1,0:T(8,128)S(1)}, f32[240,128]{1,0:T(8,128)S(1)}, u32[]{:S(2)}, u32[]{:S(2)}) collective-permute-start(f32[240,128]{1,0:T(8,128)S(1)} %get-tuple-element.63.refs_0_.refs_8_), channel_id=1, source_target_pairs={{0,4},{4,0},{8,12},{12,8},{16,20},{20,16},{24,28},{28,24},{1,5},{5... | collective-permute-start | bytes 368648 | tf_op jit(solution)/shard_map/ppermute | solution.py:888
  39.1 3.8 %collective-permute-start.18 = (f32[240,128]{1,0:T(8,128)S(1)}, f32[240,128]{1,0:T(8,128)S(1)}, u32[]{:S(2)}, u32[]{:S(2)}) collective-permute-start(f32[240,128]{1,0:T(8,128)S(1)} %collective-permute-done.17.refs_6_), channel_id=1, source_target_pairs={{0,4},{4,0},{8,12},{12,8},{16,20},{20,16},{24,28},{28,24},{1,5},{5... | collective-permute-start | bytes 368648 | tf_op jit(solution)/shard_map/ppermute | solution.py:888
  42.4 1.3 %collective-permute-start.16 = (f32[240,128]{1,0:T(8,128)S(1)}, f32[240,128]{1,0:T(8,128)S(1)}, u32[]{:S(2)}, u32[]{:S(2)}) collective-permute-start(f32[240,128]{1,0:T(8,128)S(1)} %collective-permute-done.15.refs_4_), channel_id=1, source_target_pairs={{0,4},{4,0},{8,12},{12,8},{16,20},{20,16},{24,28},{28,24},{1,5},{5... | collective-permute-start | bytes 368648 | tf_op jit(solution)/shard_map/ppermute | solution.py:888
  42.4 1.5 %collective-permute-start.14 = (f32[240,128]{1,0:T(8,128)S(1)}, f32[240,128]{1,0:T(8,128)S(1)}, u32[]{:S(2)}, u32[]{:S(2)}) collective-permute-start(f32[240,128]{1,0:T(8,128)S(1)} %collective-permute-done.13.refs_2_), channel_id=1, source_target_pairs={{0,4},{4,0},{8,12},{12,8},{16,20},{20,16},{24,28},{28,24},{1,5},{5... | collective-permute-start | bytes 368648 | tf_op jit(solution)/shard_map/ppermute | solution.py:888
  48.3 12.3 %collective-permute-start.22 = (f32[240,128]{1,0:T(8,128)S(1)}, f32[240,128]{1,0:T(8,128)S(1)}, u32[]{:S(2)}, u32[]{:S(2)}) collective-permute-start(f32[240,128]{1,0:T(8,128)S(1)} %get-tuple-element.65.refs_0_.refs_8_), channel_id=1, source_target_pairs={{0,16},{4,20},{8,24},{12,28},{16,0},{20,4},{24,8},{28,12},{1,17},{... | collective-permute-start | bytes 368648 | tf_op jit(solution)/shard_map/ppermute | solution.py:884
  49.8 10.8 %collective-permute-start.24 = (f32[240,128]{1,0:T(8,128)S(1)}, f32[240,128]{1,0:T(8,128)S(1)}, u32[]{:S(2)}, u32[]{:S(2)}) collective-permute-start(f32[240,128]{1,0:T(8,128)S(1)} %get-tuple-element.65.refs_0_.refs_8_), channel_id=1, source_target_pairs={{0,24},{4,28},{8,16},{12,20},{16,8},{20,12},{24,0},{28,4},{1,25},{... | collective-permute-start | bytes 368648 | tf_op jit(solution)/shard_map/ppermute | solution.py:884
  51.9 9.6 %collective-permute-start.20 = (f32[240,128]{1,0:T(8,128)S(1)}, f32[240,128]{1,0:T(8,128)S(1)}, u32[]{:S(2)}, u32[]{:S(2)}) collective-permute-start(f32[240,128]{1,0:T(8,128)S(1)} %get-tuple-element.65.refs_0_.refs_8_), channel_id=1, source_target_pairs={{0,8},{4,12},{8,0},{12,4},{16,24},{20,28},{24,16},{28,20},{1,9},{5... | collective-permute-start | bytes 368648 | tf_op jit(solution)/shard_map/ppermute | solution.py:884
  51.9 10.2 %collective-permute-start.19 = (f32[240,128]{1,0:T(8,128)S(1)}, f32[240,128]{1,0:T(8,128)S(1)}, u32[]{:S(2)}, u32[]{:S(2)}) collective-permute-start(f32[240,128]{1,0:T(8,128)S(1)} %get-tuple-element.65.refs_0_.refs_8_), channel_id=1, source_target_pairs={{0,4},{4,0},{8,12},{12,8},{16,20},{20,16},{24,28},{28,24},{1,5},{5... | collective-permute-start | bytes 368648 | tf_op jit(solution)/shard_map/ppermute | solution.py:888
  60.6 1.5 %collective-permute-start.25 = (f32[240,128]{1,0:T(8,128)S(1)}, f32[240,128]{1,0:T(8,128)S(1)}, u32[]{:S(2)}, u32[]{:S(2)}) collective-permute-start(f32[240,128]{1,0:T(8,128)S(1)} %collective-permute-done.24.refs_6_), channel_id=1, source_target_pairs={{0,4},{4,0},{8,12},{12,8},{16,20},{20,16},{24,28},{28,24},{1,5},{5... | collective-permute-start | bytes 368648 | tf_op jit(solution)/shard_map/ppermute | solution.py:888
  61.5 1.3 %collective-permute-start.21 = (f32[240,128]{1,0:T(8,128)S(1)}, f32[240,128]{1,0:T(8,128)S(1)}, u32[]{:S(2)}, u32[]{:S(2)}) collective-permute-start(f32[240,128]{1,0:T(8,128)S(1)} %collective-permute-done.20.refs_2_), channel_id=1, source_target_pairs={{0,4},{4,0},{8,12},{12,8},{16,20},{20,16},{24,28},{28,24},{1,5},{5... | collective-permute-start | bytes 368648 | tf_op jit(solution)/shard_map/ppermute | solution.py:888
  61.5 1.5 %collective-permute-start.23 = (f32[240,128]{1,0:T(8,128)S(1)}, f32[240,128]{1,0:T(8,128)S(1)}, u32[]{:S(2)}, u32[]{:S(2)}) collective-permute-start(f32[240,128]{1,0:T(8,128)S(1)} %collective-permute-done.22.refs_4_), channel_id=1, source_target_pairs={{0,4},{4,0},{8,12},{12,8},{16,20},{20,16},{24,28},{28,24},{1,5},{5... | collective-permute-start | bytes 368648 | tf_op jit(solution)/shard_map/ppermute | solution.py:888
  66.4 8.0 %collective-permute-start.29 = (f32[128,128]{1,0:T(8,128)S(1)}, f32[128,128]{1,0:T(8,128)S(1)}, u32[]{:S(2)}, u32[]{:S(2)}) collective-permute-start(f32[128,128]{1,0:T(8,128)S(1)} %get-tuple-element.74.refs_0_), channel_id=1, source_target_pairs={{0,16},{4,20},{8,24},{12,28},{16,0},{20,4},{24,8},{28,12},{1,17},{... | collective-permute-start | bytes 196616 | tf_op jit(solution)/shard_map/ppermute | solution.py:884
  69.3 6.5 %collective-permute-start.31 = (f32[128,128]{1,0:T(8,128)S(1)}, f32[128,128]{1,0:T(8,128)S(1)}, u32[]{:S(2)}, u32[]{:S(2)}) collective-permute-start(f32[128,128]{1,0:T(8,128)S(1)} %get-tuple-element.74.refs_0_), channel_id=1, source_target_pairs={{0,24},{4,28},{8,16},{12,20},{16,8},{20,12},{24,0},{28,4},{1,25},{... | collective-permute-start | bytes 196616 | tf_op jit(solution)/shard_map/ppermute | solution.py:884
  71.2 5.2 %collective-permute-start.27 = (f32[128,128]{1,0:T(8,128)S(1)}, f32[128,128]{1,0:T(8,128)S(1)}, u32[]{:S(2)}, u32[]{:S(2)}) collective-permute-start(f32[128,128]{1,0:T(8,128)S(1)} %get-tuple-element.74.refs_0_), channel_id=1, source_target_pairs={{0,8},{4,12},{8,0},{12,4},{16,24},{20,28},{24,16},{28,20},{1,9},{5... | collective-permute-start | bytes 196616 | tf_op jit(solution)/shard_map/ppermute | solution.py:884
  71.2 5.2 %collective-permute-start.26 = (f32[128,128]{1,0:T(8,128)S(1)}, f32[128,128]{1,0:T(8,128)S(1)}, u32[]{:S(2)}, u32[]{:S(2)}) collective-permute-start(f32[128,128]{1,0:T(8,128)S(1)} %get-tuple-element.74.refs_0_), channel_id=1, source_target_pairs={{0,4},{4,0},{8,12},{12,8},{16,20},{20,16},{24,28},{28,24},{1,5},{5... | collective-permute-start | bytes 196616 | tf_op jit(solution)/shard_map/ppermute | solution.py:888
  74.4 2.6 %collective-permute-start.30 = (f32[128,128]{1,0:T(8,128)S(1)}, f32[128,128]{1,0:T(8,128)S(1)}, u32[]{:S(2)}, u32[]{:S(2)}) collective-permute-start(f32[128,128]{1,0:T(8,128)S(1)} %collective-permute-done.29.refs_4_), channel_id=1, source_target_pairs={{0,4},{4,0},{8,12},{12,8},{16,20},{20,16},{24,28},{28,24},{1,5},{5... | collective-permute-start | bytes 196616 | tf_op jit(solution)/shard_map/ppermute | solution.py:888
  75.7 1.3 %collective-permute-start.32 = (f32[128,128]{1,0:T(8,128)S(1)}, f32[128,128]{1,0:T(8,128)S(1)}, u32[]{:S(2)}, u32[]{:S(2)}) collective-permute-start(f32[128,128]{1,0:T(8,128)S(1)} %collective-permute-done.31.refs_6_), channel_id=1, source_target_pairs={{0,4},{4,0},{8,12},{12,8},{16,20},{20,16},{24,28},{28,24},{1,5},{5... | collective-permute-start | bytes 196616 | tf_op jit(solution)/shard_map/ppermute | solution.py:888
  76.3 1.3 %collective-permute-start.28 = (f32[128,128]{1,0:T(8,128)S(1)}, f32[128,128]{1,0:T(8,128)S(1)}, u32[]{:S(2)}, u32[]{:S(2)}) collective-permute-start(f32[128,128]{1,0:T(8,128)S(1)} %collective-permute-done.27.refs_2_), channel_id=1, source_target_pairs={{0,4},{4,0},{8,12},{12,8},{16,20},{20,16},{24,28},{28,24},{1,5},{5... | collective-permute-start | bytes 196616 | tf_op jit(solution)/shard_map/ppermute | solution.py:888

commit v12 on v11

--- a/solution.py
+++ b/solution.py
@@ -954,7 +954,7 @@
         scalars=2,
     )
     tables = (ids, partner, partner_side, flipped)
-    gathered, _ = share_lines(lines)
+    gathered, (base,) = share_lines(lines, (base,))
     slots = len(gathered)
     k0, k1, base, lines, sums = call(
         functools.partial(second_kernel, modes, slots),

time: 80.7 us -> 81.3 us (level)
  waiting for transfers between devices: 23.7 us -> 24.6 us
    ppermute x9, waiting for transfers between devices: 15.9 us -> 16.8 us  [share_lines(): lax.ppermute(lines, 'dom', [(i, i ^ slot) for i in range(parts)])]
  transfers between devices with their start and end apart: 33 -> 33, of which waited for: 16 -> 17; matrix products, arithmetic and copies ran while one was open for 0% -> 0% of each run, Pallas kernels for 12% -> 12%
where the time goes in v12:
time: 81.3 us
  starting transfers between devices  30.9 us (38%)
  Pallas kernels  24.7 us (30%)
  waiting for transfers between devices  24.6 us (30%)
  between operations  0.92 us (1%)
    pallas_call x10, Pallas kernels, call(): pl.pallas_call(kernel, name=name, out_shape=[pltpu.VMEM(one.shape, one.dt...  24.7 us
    ppermute x12, starting transfers between devices, swap_blocks(): lax.ppermute(blocks[place], 'four', [(i, i ^ offset_of(place, size)) for...  16.8 us
    ppermute x9, waiting for transfers between devices, share_lines(): lax.ppermute(lines, 'dom', [(i, i ^ slot) for i in range(parts)])  16.8 us
    ppermute x9, starting transfers between devices, share_lines(): lax.ppermute(lines, 'dom', [(i, i ^ slot) for i in range(parts)])  13.2 us
    ppermute x12, waiting for transfers between devices, swap_blocks(): lax.ppermute(blocks[place], 'four', [(i, i ^ offset_of(place, size)) for...  4.54 us
    ppermute x12, waiting for transfers between devices, share_lines(): lax.ppermute(slots[slot], 'dom', [(i, i ^ 1) for i in range(parts)])  3.26 us
  transfers between devices with their start and end apart: 33, of which 17 were waited for; matrix products, arithmetic and copies ran while one was open for 0% of the time, Pallas kernels for 12%

profile of v12, /device:TPU:0, one launch (start us, length us, event | category | flops | bytes accessed | tf_op | source)
XLA Modules:
  0.0 81.3 jit_solution(1396082890260479150)
XLA Ops:
  0.6 0.0 copy-start.1
  0.6 0.0 copy-start
  0.7 0.1 pad_add_fusion.ids_ref
  0.7 2.3 %pack.2 = (f32[216,128]{1,0:T(8,128)S(1)}, f32[216,128]{1,0:T(8,128)S(1)}, f32[216,128]{1,0:T(8,128)S(1)}, f32[216,128]{1,0:T(8,128)S(1)}, f32[3,32,2304]{2,1,0:T(8,128)S(1)}) custom-call(s32[2]{0:T(128)S(1)} %pad_add_fusion.ids_ref, f32[3,32,2304]{2,1,0:T(8,128)} %source_ref.1), custom_call_target="tpu_custom_call" | custom-call | tf_op jit(solution)/shard_map/pack/pallas_call | solution.py:851
  3.1 4.0 %collective-permute-start = (f32[216,128]{1,0:T(8,128)S(1)}, f32[216,128]{1,0:T(8,128)S(1)}, u32[]{:S(2)}, u32[]{:S(2)}) collective-permute-start(f32[216,128]{1,0:T(8,128)S(1)} %get-tuple-element.48), channel_id=1, source_target_pairs={{0,3},{1,2},{2,1},{3,0},{4,7},{5,6},{6,5},{7,4},{8,11},{9,10},{10,... | collective-permute-start | bytes 331784 | tf_op jit(solution)/shard_map/ppermute | solution.py:874
  7.0 0.5 collective-permute-start.1
  7.6 0.1 collective-permute-start.2
  7.7 1.2 %pack.3 = (f32[216,128]{1,0:T(8,128)S(1)}, f32[216,128]{1,0:T(8,128)S(1)}, f32[216,128]{1,0:T(8,128)S(1)}, f32[216,128]{1,0:T(8,128)S(1)}) custom-call(s32[2]{0:T(128)S(1)} %pad_add_fusion.ids_ref, f32[3,32,2304]{2,1,0:T(8,128)S(1)} %get-tuple-element.55.source_ref), custom_call_target="tpu_custom_call" | custom-call | tf_op jit(solution)/shard_map/pack/pallas_call | solution.py:851
  8.8 2.9 %collective-permute-start.6 = (f32[216,128]{1,0:T(8,128)S(1)}, f32[216,128]{1,0:T(8,128)S(1)}, u32[]{:S(2)}, u32[]{:S(2)}) collective-permute-start(f32[216,128]{1,0:T(8,128)S(1)} %get-tuple-element.57), channel_id=1, source_target_pairs={{0,3},{1,2},{2,1},{3,0},{4,7},{5,6},{6,5},{7,4},{8,11},{9,10},{10,... | collective-permute-start | bytes 331784 | tf_op jit(solution)/shard_map/ppermute | solution.py:874
  11.8 0.5 collective-permute-start.7
  12.3 0.0 collective-permute-done.refs_1_
  12.3 0.7 collective-permute-start.8
  12.9 0.6 collective-permute-done.1.refs_2_
  13.5 0.0 collective-permute-done.2.refs_3_
  13.5 0.0 copy-start.2
  13.5 2.1 %products.2 = (f32[192,128]{1,0:T(8,128)S(1)}, f32[192,128]{1,0:T(8,128)S(1)}, f32[192,128]{1,0:T(8,128)S(1)}, f32[192,128]{1,0:T(8,128)S(1)}, f32[4,48,128]{2,1,0:T(8,128)S(1)}) custom-call(s32[2]{0:T(128)S(1)} %pad_add_fusion.ids_ref, f32[216,128]{1,0:T(8,128)S(1)} %get-tuple-element.47.refs_0_, f32[216,128]{1,0:T(8,128)S(1)} %collective-permute-done.refs_1_, ...), custom_call_target="tpu_custom_call" | custom-call | tf_op jit(solution)/shard_map/products/pallas_call | solution.py:851
  15.7 0.0 copy-start.3
  15.7 0.0 copy-start.4
  15.7 3.9 %collective-permute-start.3 = (f32[192,128]{1,0:T(8,128)S(1)}, f32[192,128]{1,0:T(8,128)S(1)}, u32[]{:S(2)}, u32[]{:S(2)}) collective-permute-start(f32[192,128]{1,0:T(8,128)S(1)} %get-tuple-element.52), channel_id=1, source_target_pairs={{0,3},{1,2},{2,1},{3,0},{4,7},{5,6},{6,5},{7,4},{8,11},{9,10},{10,... | collective-permute-start | bytes 294920 | tf_op jit(solution)/shard_map/ppermute | solution.py:874
  19.6 0.0 collective-permute-start.4
  19.6 0.0 collective-permute-done.6.refs_1_
  19.6 0.6 collective-permute-start.5
  20.3 2.2 %products.3 = (f32[192,128]{1,0:T(8,128)S(1)}, f32[192,128]{1,0:T(8,128)S(1)}, f32[192,128]{1,0:T(8,128)S(1)}, f32[192,128]{1,0:T(8,128)S(1)}) custom-call(s32[2]{0:T(128)S(1)} %pad_add_fusion.ids_ref, f32[216,128]{1,0:T(8,128)S(1)} %get-tuple-element.56.refs_0_, f32[216,128]{1,0:T(8,128)S(1)} %collective-permute-done.6.refs_1_, ...), custom_call_target="tpu_custom_call" | custom-call | tf_op jit(solution)/shard_map/products/pallas_call | solution.py:851
  22.5 2.9 %collective-permute-start.9 = (f32[192,128]{1,0:T(8,128)S(1)}, f32[192,128]{1,0:T(8,128)S(1)}, u32[]{:S(2)}, u32[]{:S(2)}) collective-permute-start(f32[192,128]{1,0:T(8,128)S(1)} %get-tuple-element.62), channel_id=1, source_target_pairs={{0,3},{1,2},{2,1},{3,0},{4,7},{5,6},{6,5},{7,4},{8,11},{9,10},{10,... | collective-permute-start | bytes 294920 | tf_op jit(solution)/shard_map/ppermute | solution.py:874
  25.4 0.6 collective-permute-start.11
  26.1 0.0 collective-permute-done.4.refs_2_
  26.1 0.0 collective-permute-done.5.refs_3_
  26.1 2.0 %collective-permute-done.9.refs_5_ = f32[192,128]{1,0:T(8,128)S(1)} collective-permute-done((f32[192,128]{1,0:T(8,128)S(1)}, f32[192,128]{1,0:T(8,128)S(1)}, u32[]{:S(2)}, u32[]{:S(2)}) %collective-permute-start.9) | collective-permute-done | bytes 98336 | tf_op jit(solution)/shard_map/ppermute | solution.py:874
  28.1 1.9 %collective-permute-done.10.refs_6_ = f32[192,128]{1,0:T(8,128)S(1)} collective-permute-done((f32[192,128]{1,0:T(8,128)S(1)}, f32[192,128]{1,0:T(8,128)S(1)}, u32[]{:S(2)}, u32[]{:S(2)}) %collective-permute-start.10) | collective-permute-done | bytes 98336 | tf_op jit(solution)/shard_map/ppermute | solution.py:874
  30.0 0.0 collective-permute-done.11.refs_7_
  30.0 1.9 %first.1 = (f32[2304,128]{1,0:T(8,128)S(1)}, f32[240,128]{1,0:T(8,128)S(1)}) custom-call(s32[2]{0:T(128)S(1)} %pad_add_fusion.ids_ref, s32[1,4]{1,0:T(1,128)S(1)} %copy-done.2, f32[192,128]{1,0:T(8,128)S(1)} %get-tuple-element.51.refs_0_, f32[192,128]{1,0:T(8,128)S(1)} %collective-permute-done.3.refs_1_, f32[192,128]{1,0:T(8,128)S(1)} %collective-permute-done.4.refs_2_, ...), custom_call_target="tpu_custom_call" | custom-call | tf_op jit(solution)/shard_map/first/pallas_call | solution.py:851
  31.9 3.2 %collective-permute-start.15 = (f32[240,128]{1,0:T(8,128)S(1)}, f32[240,128]{1,0:T(8,128)S(1)}, u32[]{:S(2)}, u32[]{:S(2)}) collective-permute-start(f32[240,128]{1,0:T(8,128)S(1)} %get-tuple-element.65.refs_0_.refs_8_), channel_id=1, source_target_pairs={{0,16},{4,20},{8,24},{12,28},{16,0},{20,4},{24,8},{28,12},{1,17},{... | collective-permute-start | bytes 368648 | tf_op jit(solution)/shard_map/ppermute | solution.py:884
  35.1 1.3 %collective-permute-start.17 = (f32[240,128]{1,0:T(8,128)S(1)}, f32[240,128]{1,0:T(8,128)S(1)}, u32[]{:S(2)}, u32[]{:S(2)}) collective-permute-start(f32[240,128]{1,0:T(8,128)S(1)} %get-tuple-element.65.refs_0_.refs_8_), channel_id=1, source_target_pairs={{0,24},{4,28},{8,16},{12,20},{16,8},{20,12},{24,0},{28,4},{1,25},{... | collective-permute-start | bytes 368648 | tf_op jit(solution)/shard_map/ppermute | solution.py:884
  36.5 0.2 collective-permute-start.13
  36.7 0.0 collective-permute-start.12
  36.7 2.9 %collective-permute-done.15.refs_4_ = f32[240,128]{1,0:T(8,128)S(1)} collective-permute-done((f32[240,128]{1,0:T(8,128)S(1)}, f32[240,128]{1,0:T(8,128)S(1)}, u32[]{:S(2)}, u32[]{:S(2)}) %collective-permute-start.15) | collective-permute-done | bytes 122912 | tf_op jit(solution)/shard_map/ppermute | solution.py:884
  39.6 2.3 %collective-permute-done.17.refs_6_ = f32[240,128]{1,0:T(8,128)S(1)} collective-permute-done((f32[240,128]{1,0:T(8,128)S(1)}, f32[240,128]{1,0:T(8,128)S(1)}, u32[]{:S(2)}, u32[]{:S(2)}) %collective-permute-start.17) | collective-permute-done | bytes 122912 | tf_op jit(solution)/shard_map/ppermute | solution.py:884
  42.0 0.0 collective-permute-start.18
  42.0 0.7 collective-permute-done.13.refs_2_
  42.7 0.6 collective-permute-done.18.refs_7_
  43.3 0.0 collective-permute-done.16.refs_5_
  43.3 0.7 collective-permute-done.14.refs_3_
  44.0 4.3 %second.1 = (f32[2304,128]{1,0:T(8,128)S(1)}, f32[2304,128]{1,0:T(8,128)S(1)}, f32[2304,128]{1,0:T(8,128)S(1)}, f32[240,128]{1,0:T(8,128)S(1)}, f32[8,128]{1,0:T(8,128)S(1)}) custom-call(s32[2]{0:T(128)S(1)} %pad_add_fusion.ids_ref, s32[1,4]{1,0:T(1,128)S(1)} %copy-done.2, s32[1,4]{1,0:T(1,128)S(1)} %copy-done.3, ...), custom_call_target="tpu_custom_call", output_to_operand_aliasing={{0}: (13, {})} | custom-call | tf_op jit(solution)/shard_map/second/pallas_call | solution.py:851
  48.3 2.5 %collective-permute-start.22 = (f32[240,128]{1,0:T(8,128)S(1)}, f32[240,128]{1,0:T(8,128)S(1)}, u32[]{:S(2)}, u32[]{:S(2)}) collective-permute-start(f32[240,128]{1,0:T(8,128)S(1)} %get-tuple-element.69.refs_0_.refs_8_), channel_id=1, source_target_pairs={{0,16},{4,20},{8,24},{12,28},{16,0},{20,4},{24,8},{28,12},{1,17},{... | collective-permute-start | bytes 368648 | tf_op jit(solution)/shard_map/ppermute | solution.py:884
  50.9 0.8 collective-permute-start.24
  51.6 0.5 collective-permute-start.20
  52.1 2.0 %turn.2 = (f32[96,2304]{1,0:T(8,128)S(1)}, f32[96,2304]{1,0:T(8,128)S(1)}, bf16[192,2304]{1,0:T(8,128)(2,1)S(1)}) custom-call(f32[2304,128]{1,0:T(8,128)S(1)} %get-tuple-element.70.refs_0_, f32[2304,128]{1,0:T(8,128)S(1)} %get-tuple-element.71.refs_1_.refs_9_), custom_call_target="tpu_custom_call" | custom-call | tf_op jit(solution)/shard_map/turn/pallas_call | solution.py:851
  54.2 6.5 %collective-permute-done.22.refs_4_ = f32[240,128]{1,0:T(8,128)S(1)} collective-permute-done((f32[240,128]{1,0:T(8,128)S(1)}, f32[240,128]{1,0:T(8,128)S(1)}, u32[]{:S(2)}, u32[]{:S(2)}) %collective-permute-start.22) | collective-permute-done | bytes 122912 | tf_op jit(solution)/shard_map/ppermute | solution.py:884
  60.6 0.0 collective-permute-done.24.refs_6_
  60.6 1.0 %collective-permute-done.20.refs_2_ = f32[240,128]{1,0:T(8,128)S(1)} collective-permute-done((f32[240,128]{1,0:T(8,128)S(1)}, f32[240,128]{1,0:T(8,128)S(1)}, u32[]{:S(2)}, u32[]{:S(2)}) %collective-permute-start.20) | collective-permute-done | bytes 122912 | tf_op jit(solution)/shard_map/ppermute | solution.py:884
  61.7 0.5 collective-permute-start.23
  62.2 0.8 %collective-permute-done.21.refs_3_ = f32[240,128]{1,0:T(8,128)S(1)} collective-permute-done((f32[240,128]{1,0:T(8,128)S(1)}, f32[240,128]{1,0:T(8,128)S(1)}, u32[]{:S(2)}, u32[]{:S(2)}) %collective-permute-start.21) | collective-permute-done | bytes 122912 | tf_op jit(solution)/shard_map/ppermute | solution.py:888
  63.0 0.2 collective-permute-done.23.refs_5_
  63.2 3.4 %third.1 = (f32[2304,128]{1,0:T(8,128)S(1)}, f32[2304,128]{1,0:T(8,128)S(1)}, f32[2304,128]{1,0:T(8,128)S(1)}, f32[128,128]{1,0:T(8,128)S(1)}) custom-call(s32[2]{0:T(128)S(1)} %pad_add_fusion.ids_ref, s32[1,4]{1,0:T(1,128)S(1)} %copy-done.2, s32[1,4]{1,0:T(1,128)S(1)} %copy-done.3, s32[1,4]{1,0:T(1,128)S(1)} %copy-done.4, ...), custom_call_target="tpu_custom_call", output_to_operand_aliasing={{0}: (15, {})} | custom-call | tf_op jit(solution)/shard_map/third/pallas_call | solution.py:851
  66.6 3.7 %collective-permute-start.29 = (f32[128,128]{1,0:T(8,128)S(1)}, f32[128,128]{1,0:T(8,128)S(1)}, u32[]{:S(2)}, u32[]{:S(2)}) collective-permute-start(f32[128,128]{1,0:T(8,128)S(1)} %get-tuple-element.78.refs_0_), channel_id=1, source_target_pairs={{0,16},{4,20},{8,24},{12,28},{16,0},{20,4},{24,8},{28,12},{1,17},{... | collective-permute-start | bytes 196616 | tf_op jit(solution)/shard_map/ppermute | solution.py:884
  70.3 1.0 %collective-permute-start.31 = (f32[128,128]{1,0:T(8,128)S(1)}, f32[128,128]{1,0:T(8,128)S(1)}, u32[]{:S(2)}, u32[]{:S(2)}) collective-permute-start(f32[128,128]{1,0:T(8,128)S(1)} %get-tuple-element.78.refs_0_), channel_id=1, source_target_pairs={{0,24},{4,28},{8,16},{12,20},{16,8},{20,12},{24,0},{28,4},{1,25},{... | collective-permute-start | bytes 196616 | tf_op jit(solution)/shard_map/ppermute | solution.py:884
  71.3 2.5 %turn.3 = (f32[96,2304]{1,0:T(8,128)S(1)}, f32[96,2304]{1,0:T(8,128)S(1)}, f32[96,2304]{1,0:T(8,128)S(1)}) custom-call(f32[2304,128]{1,0:T(8,128)S(1)} %get-tuple-element.79.refs_0_, f32[2304,128]{1,0:T(8,128)S(1)} %get-tuple-element.80.refs_1_, f32[2304,128]{1,0:T(8,128)S(1)} %get-tuple-element.81.refs_2_), custom_call_target="tpu_custom_call" | custom-call | tf_op jit(solution)/shard_map/turn/pallas_call | solution.py:851
  73.8 0.9 %collective-permute-done.29.refs_4_ = f32[128,128]{1,0:T(8,128)S(1)} collective-permute-done((f32[128,128]{1,0:T(8,128)S(1)}, f32[128,128]{1,0:T(8,128)S(1)}, u32[]{:S(2)}, u32[]{:S(2)}) %collective-permute-start.29) | collective-permute-done | bytes 65568 | tf_op jit(solution)/shard_map/ppermute | solution.py:884
  74.6 2.3 %collective-permute-done.31.refs_6_ = f32[128,128]{1,0:T(8,128)S(1)} collective-permute-done((f32[128,128]{1,0:T(8,128)S(1)}, f32[128,128]{1,0:T(8,128)S(1)}, u32[]{:S(2)}, u32[]{:S(2)}) %collective-permute-start.31) | collective-permute-done | bytes 65568 | tf_op jit(solution)/shard_map/ppermute | solution.py:884
  76.9 0.2 collective-permute-done.27.refs_2_
  77.1 0.3 collective-permute-start.28
  77.5 0.7 collective-permute-done.32.refs_7_
  78.2 0.2 collective-permute-done.28.refs_3_
  78.4 2.7 %last.1 = (f32[3,32,2304]{2,1,0:T(8,128)}, f32[3,32,2304]{2,1,0:T(8,128)}) custom-call(s32[2]{0:T(128)S(1)} %pad_add_fusion.ids_ref, s32[1,4]{1,0:T(1,128)S(1)} %copy-done.2, s32[1,4]{1,0:T(1,128)S(1)} %copy-done.3, s32[1,4]{1,0:T(1,128)S(1)} %copy-done.4, f32[128,128]{1,0:T(8,128)S(1)} %get-tuple-element.78.refs_0_, ...), custom_call_target="tpu_custom_call" | custom-call | tf_op jit(solution)/shard_map/last/pallas_call | solution.py:851
  (23 shorter events, 0.1 us)
Async XLA Ops:
  0.6 12.9 %copy-start.1 = (bf16[256,256]{1,0:T(8,128)(2,1)S(1)}, bf16[256,256]{1,0:T(8,128)(2,1)}, u32[]{:S(2)}) copy-start(bf16[256,256]{1,0:T(8,128)(2,1)} %constant.14.clone.refs_5_) | copy-start | bytes 393220
  0.6 12.9 %copy-start = (bf16[512,768]{1,0:T(8,128)(2,1)S(1)}, bf16[512,768]{1,0:T(8,128)(2,1)}, u32[]{:S(2)}) copy-start(bf16[512,768]{1,0:T(8,128)(2,1)} %constant.13.clone.refs_4_) | copy-start | bytes 2359300
  3.1 9.2 %collective-permute-start = (f32[216,128]{1,0:T(8,128)S(1)}, f32[216,128]{1,0:T(8,128)S(1)}, u32[]{:S(2)}, u32[]{:S(2)}) collective-permute-start(f32[216,128]{1,0:T(8,128)S(1)} %get-tuple-element.48), channel_id=1, source_target_pairs={{0,3},{1,2},{2,1},{3,0},{4,7},{5,6},{6,5},{7,4},{8,11},{9,10},{10,... | collective-permute-start | bytes 331784 | tf_op jit(solution)/shard_map/ppermute | solution.py:874
  7.0 6.5 %collective-permute-start.1 = (f32[216,128]{1,0:T(8,128)S(1)}, f32[216,128]{1,0:T(8,128)S(1)}, u32[]{:S(2)}, u32[]{:S(2)}) collective-permute-start(f32[216,128]{1,0:T(8,128)S(1)} %get-tuple-element.49), channel_id=1, source_target_pairs={{0,1},{1,0},{2,3},{3,2},{4,5},{5,4},{6,7},{7,6},{8,9},{9,8},{10,11... | collective-permute-start | bytes 331784 | tf_op jit(solution)/shard_map/ppermute | solution.py:874
  7.6 5.9 %collective-permute-start.2 = (f32[216,128]{1,0:T(8,128)S(1)}, f32[216,128]{1,0:T(8,128)S(1)}, u32[]{:S(2)}, u32[]{:S(2)}) collective-permute-start(f32[216,128]{1,0:T(8,128)S(1)} %get-tuple-element.50), channel_id=1, source_target_pairs={{0,2},{1,3},{2,0},{3,1},{4,6},{5,7},{6,4},{7,5},{8,10},{9,11},{10,... | collective-permute-start | bytes 331784 | tf_op jit(solution)/shard_map/ppermute | solution.py:874
  8.8 10.8 %collective-permute-start.6 = (f32[216,128]{1,0:T(8,128)S(1)}, f32[216,128]{1,0:T(8,128)S(1)}, u32[]{:S(2)}, u32[]{:S(2)}) collective-permute-start(f32[216,128]{1,0:T(8,128)S(1)} %get-tuple-element.57), channel_id=1, source_target_pairs={{0,3},{1,2},{2,1},{3,0},{4,7},{5,6},{6,5},{7,4},{8,11},{9,10},{10,... | collective-permute-start | bytes 331784 | tf_op jit(solution)/shard_map/ppermute | solution.py:874
  11.8 8.5 %collective-permute-start.7 = (f32[216,128]{1,0:T(8,128)S(1)}, f32[216,128]{1,0:T(8,128)S(1)}, u32[]{:S(2)}, u32[]{:S(2)}) collective-permute-start(f32[216,128]{1,0:T(8,128)S(1)} %get-tuple-element.58), channel_id=1, source_target_pairs={{0,1},{1,0},{2,3},{3,2},{4,5},{5,4},{6,7},{7,6},{8,9},{9,8},{10,11... | collective-permute-start | bytes 331784 | tf_op jit(solution)/shard_map/ppermute | solution.py:874
  12.3 8.0 %collective-permute-start.8 = (f32[216,128]{1,0:T(8,128)S(1)}, f32[216,128]{1,0:T(8,128)S(1)}, u32[]{:S(2)}, u32[]{:S(2)}) collective-permute-start(f32[216,128]{1,0:T(8,128)S(1)} %get-tuple-element.59), channel_id=1, source_target_pairs={{0,2},{1,3},{2,0},{3,1},{4,6},{5,7},{6,4},{7,5},{8,10},{9,11},{10,... | collective-permute-start | bytes 331784 | tf_op jit(solution)/shard_map/ppermute | solution.py:874
  13.5 16.5 %copy-start.2 = (s32[1,4]{1,0:T(1,128)S(1)}, s32[1,4]{1,0:T(1,128)}, u32[]{:S(2)}) copy-start(s32[1,4]{1,0:T(1,128)} %partner_ref.7) | copy-start | bytes 52
  15.7 28.3 %copy-start.3 = (s32[1,4]{1,0:T(1,128)S(1)}, s32[1,4]{1,0:T(1,128)}, u32[]{:S(2)}) copy-start(s32[1,4]{1,0:T(1,128)} %side_ref.5) | copy-start | bytes 52
  15.7 28.3 %copy-start.4 = (s32[1,4]{1,0:T(1,128)S(1)}, s32[1,4]{1,0:T(1,128)}, u32[]{:S(2)}) copy-start(s32[1,4]{1,0:T(1,128)} %flip_ref.5) | copy-start | bytes 52
  15.7 9.7 %collective-permute-start.3 = (f32[192,128]{1,0:T(8,128)S(1)}, f32[192,128]{1,0:T(8,128)S(1)}, u32[]{:S(2)}, u32[]{:S(2)}) collective-permute-start(f32[192,128]{1,0:T(8,128)S(1)} %get-tuple-element.52), channel_id=1, source_target_pairs={{0,3},{1,2},{2,1},{3,0},{4,7},{5,6},{6,5},{7,4},{8,11},{9,10},{10,... | collective-permute-start | bytes 294920 | tf_op jit(solution)/shard_map/ppermute | solution.py:874
  19.6 6.4 %collective-permute-start.4 = (f32[192,128]{1,0:T(8,128)S(1)}, f32[192,128]{1,0:T(8,128)S(1)}, u32[]{:S(2)}, u32[]{:S(2)}) collective-permute-start(f32[192,128]{1,0:T(8,128)S(1)} %get-tuple-element.53), channel_id=1, source_target_pairs={{0,1},{1,0},{2,3},{3,2},{4,5},{5,4},{6,7},{7,6},{8,9},{9,8},{10,11... | collective-permute-start | bytes 294920 | tf_op jit(solution)/shard_map/ppermute | solution.py:874
  19.6 6.4 %collective-permute-start.5 = (f32[192,128]{1,0:T(8,128)S(1)}, f32[192,128]{1,0:T(8,128)S(1)}, u32[]{:S(2)}, u32[]{:S(2)}) collective-permute-start(f32[192,128]{1,0:T(8,128)S(1)} %get-tuple-element.54), channel_id=1, source_target_pairs={{0,2},{1,3},{2,0},{3,1},{4,6},{5,7},{6,4},{7,5},{8,10},{9,11},{10,... | collective-permute-start | bytes 294920 | tf_op jit(solution)/shard_map/ppermute | solution.py:874
  22.5 5.6 %collective-permute-start.9 = (f32[192,128]{1,0:T(8,128)S(1)}, f32[192,128]{1,0:T(8,128)S(1)}, u32[]{:S(2)}, u32[]{:S(2)}) collective-permute-start(f32[192,128]{1,0:T(8,128)S(1)} %get-tuple-element.62), channel_id=1, source_target_pairs={{0,3},{1,2},{2,1},{3,0},{4,7},{5,6},{6,5},{7,4},{8,11},{9,10},{10,... | collective-permute-start | bytes 294920 | tf_op jit(solution)/shard_map/ppermute | solution.py:874
  25.4 4.6 %collective-permute-start.10 = (f32[192,128]{1,0:T(8,128)S(1)}, f32[192,128]{1,0:T(8,128)S(1)}, u32[]{:S(2)}, u32[]{:S(2)}) collective-permute-start(f32[192,128]{1,0:T(8,128)S(1)} %get-tuple-element.63), channel_id=1, source_target_pairs={{0,1},{1,0},{2,3},{3,2},{4,5},{5,4},{6,7},{7,6},{8,9},{9,8},{10,11... | collective-permute-start | bytes 294920 | tf_op jit(solution)/shard_map/ppermute | solution.py:874
  25.4 4.6 %collective-permute-start.11 = (f32[192,128]{1,0:T(8,128)S(1)}, f32[192,128]{1,0:T(8,128)S(1)}, u32[]{:S(2)}, u32[]{:S(2)}) collective-permute-start(f32[192,128]{1,0:T(8,128)S(1)} %get-tuple-element.64), channel_id=1, source_target_pairs={{0,2},{1,3},{2,0},{3,1},{4,6},{5,7},{6,4},{7,5},{8,10},{9,11},{10,... | collective-permute-start | bytes 294920 | tf_op jit(solution)/shard_map/ppermute | solution.py:874
  31.9 7.7 %collective-permute-start.15 = (f32[240,128]{1,0:T(8,128)S(1)}, f32[240,128]{1,0:T(8,128)S(1)}, u32[]{:S(2)}, u32[]{:S(2)}) collective-permute-start(f32[240,128]{1,0:T(8,128)S(1)} %get-tuple-element.65.refs_0_.refs_8_), channel_id=1, source_target_pairs={{0,16},{4,20},{8,24},{12,28},{16,0},{20,4},{24,8},{28,12},{1,17},{... | collective-permute-start | bytes 368648 | tf_op jit(solution)/shard_map/ppermute | solution.py:884
  35.1 6.8 %collective-permute-start.17 = (f32[240,128]{1,0:T(8,128)S(1)}, f32[240,128]{1,0:T(8,128)S(1)}, u32[]{:S(2)}, u32[]{:S(2)}) collective-permute-start(f32[240,128]{1,0:T(8,128)S(1)} %get-tuple-element.65.refs_0_.refs_8_), channel_id=1, source_target_pairs={{0,24},{4,28},{8,16},{12,20},{16,8},{20,12},{24,0},{28,4},{1,25},{... | collective-permute-start | bytes 368648 | tf_op jit(solution)/shard_map/ppermute | solution.py:884
  36.5 6.2 %collective-permute-start.13 = (f32[240,128]{1,0:T(8,128)S(1)}, f32[240,128]{1,0:T(8,128)S(1)}, u32[]{:S(2)}, u32[]{:S(2)}) collective-permute-start(f32[240,128]{1,0:T(8,128)S(1)} %get-tuple-element.65.refs_0_.refs_8_), channel_id=1, source_target_pairs={{0,8},{4,12},{8,0},{12,4},{16,24},{20,28},{24,16},{28,20},{1,9},{5... | collective-permute-start | bytes 368648 | tf_op jit(solution)/shard_map/ppermute | solution.py:884
  36.7 6.0 %collective-permute-start.12 = (f32[240,128]{1,0:T(8,128)S(1)}, f32[240,128]{1,0:T(8,128)S(1)}, u32[]{:S(2)}, u32[]{:S(2)}) collective-permute-start(f32[240,128]{1,0:T(8,128)S(1)} %get-tuple-element.65.refs_0_.refs_8_), channel_id=1, source_target_pairs={{0,4},{4,0},{8,12},{12,8},{16,20},{20,16},{24,28},{28,24},{1,5},{5... | collective-permute-start | bytes 368648 | tf_op jit(solution)/shard_map/ppermute | solution.py:888
  39.6 3.7 %collective-permute-start.16 = (f32[240,128]{1,0:T(8,128)S(1)}, f32[240,128]{1,0:T(8,128)S(1)}, u32[]{:S(2)}, u32[]{:S(2)}) collective-permute-start(f32[240,128]{1,0:T(8,128)S(1)} %collective-permute-done.15.refs_4_), channel_id=1, source_target_pairs={{0,4},{4,0},{8,12},{12,8},{16,20},{20,16},{24,28},{28,24},{1,5},{5... | collective-permute-start | bytes 368648 | tf_op jit(solution)/shard_map/ppermute | solution.py:888
  42.0 1.3 %collective-permute-start.18 = (f32[240,128]{1,0:T(8,128)S(1)}, f32[240,128]{1,0:T(8,128)S(1)}, u32[]{:S(2)}, u32[]{:S(2)}) collective-permute-start(f32[240,128]{1,0:T(8,128)S(1)} %collective-permute-done.17.refs_6_), channel_id=1, source_target_pairs={{0,4},{4,0},{8,12},{12,8},{16,20},{20,16},{24,28},{28,24},{1,5},{5... | collective-permute-start | bytes 368648 | tf_op jit(solution)/shard_map/ppermute | solution.py:888
  42.7 1.3 %collective-permute-start.14 = (f32[240,128]{1,0:T(8,128)S(1)}, f32[240,128]{1,0:T(8,128)S(1)}, u32[]{:S(2)}, u32[]{:S(2)}) collective-permute-start(f32[240,128]{1,0:T(8,128)S(1)} %collective-permute-done.13.refs_2_), channel_id=1, source_target_pairs={{0,4},{4,0},{8,12},{12,8},{16,20},{20,16},{24,28},{28,24},{1,5},{5... | collective-permute-start | bytes 368648 | tf_op jit(solution)/shard_map/ppermute | solution.py:888
  48.3 12.3 %collective-permute-start.22 = (f32[240,128]{1,0:T(8,128)S(1)}, f32[240,128]{1,0:T(8,128)S(1)}, u32[]{:S(2)}, u32[]{:S(2)}) collective-permute-start(f32[240,128]{1,0:T(8,128)S(1)} %get-tuple-element.69.refs_0_.refs_8_), channel_id=1, source_target_pairs={{0,16},{4,20},{8,24},{12,28},{16,0},{20,4},{24,8},{28,12},{1,17},{... | collective-permute-start | bytes 368648 | tf_op jit(solution)/shard_map/ppermute | solution.py:884
  50.9 9.8 %collective-permute-start.24 = (f32[240,128]{1,0:T(8,128)S(1)}, f32[240,128]{1,0:T(8,128)S(1)}, u32[]{:S(2)}, u32[]{:S(2)}) collective-permute-start(f32[240,128]{1,0:T(8,128)S(1)} %get-tuple-element.69.refs_0_.refs_8_), channel_id=1, source_target_pairs={{0,24},{4,28},{8,16},{12,20},{16,8},{20,12},{24,0},{28,4},{1,25},{... | collective-permute-start | bytes 368648 | tf_op jit(solution)/shard_map/ppermute | solution.py:884
  51.6 10.0 %collective-permute-start.20 = (f32[240,128]{1,0:T(8,128)S(1)}, f32[240,128]{1,0:T(8,128)S(1)}, u32[]{:S(2)}, u32[]{:S(2)}) collective-permute-start(f32[240,128]{1,0:T(8,128)S(1)} %get-tuple-element.69.refs_0_.refs_8_), channel_id=1, source_target_pairs={{0,8},{4,12},{8,0},{12,4},{16,24},{20,28},{24,16},{28,20},{1,9},{5... | collective-permute-start | bytes 368648 | tf_op jit(solution)/shard_map/ppermute | solution.py:884
  52.1 10.1 %collective-permute-start.19 = (f32[240,128]{1,0:T(8,128)S(1)}, f32[240,128]{1,0:T(8,128)S(1)}, u32[]{:S(2)}, u32[]{:S(2)}) collective-permute-start(f32[240,128]{1,0:T(8,128)S(1)} %get-tuple-element.69.refs_0_.refs_8_), channel_id=1, source_target_pairs={{0,4},{4,0},{8,12},{12,8},{16,20},{20,16},{24,28},{28,24},{1,5},{5... | collective-permute-start | bytes 368648 | tf_op jit(solution)/shard_map/ppermute | solution.py:888
  60.6 1.6 %collective-permute-start.25 = (f32[240,128]{1,0:T(8,128)S(1)}, f32[240,128]{1,0:T(8,128)S(1)}, u32[]{:S(2)}, u32[]{:S(2)}) collective-permute-start(f32[240,128]{1,0:T(8,128)S(1)} %collective-permute-done.24.refs_6_), channel_id=1, source_target_pairs={{0,4},{4,0},{8,12},{12,8},{16,20},{20,16},{24,28},{28,24},{1,5},{5... | collective-permute-start | bytes 368648 | tf_op jit(solution)/shard_map/ppermute | solution.py:888
  61.7 1.3 %collective-permute-start.21 = (f32[240,128]{1,0:T(8,128)S(1)}, f32[240,128]{1,0:T(8,128)S(1)}, u32[]{:S(2)}, u32[]{:S(2)}) collective-permute-start(f32[240,128]{1,0:T(8,128)S(1)} %collective-permute-done.20.refs_2_), channel_id=1, source_target_pairs={{0,4},{4,0},{8,12},{12,8},{16,20},{20,16},{24,28},{28,24},{1,5},{5... | collective-permute-start | bytes 368648 | tf_op jit(solution)/shard_map/ppermute | solution.py:888
  61.7 1.5 %collective-permute-start.23 = (f32[240,128]{1,0:T(8,128)S(1)}, f32[240,128]{1,0:T(8,128)S(1)}, u32[]{:S(2)}, u32[]{:S(2)}) collective-permute-start(f32[240,128]{1,0:T(8,128)S(1)} %collective-permute-done.22.refs_4_), channel_id=1, source_target_pairs={{0,4},{4,0},{8,12},{12,8},{16,20},{20,16},{24,28},{28,24},{1,5},{5... | collective-permute-start | bytes 368648 | tf_op jit(solution)/shard_map/ppermute | solution.py:888
  66.6 8.1 %collective-permute-start.29 = (f32[128,128]{1,0:T(8,128)S(1)}, f32[128,128]{1,0:T(8,128)S(1)}, u32[]{:S(2)}, u32[]{:S(2)}) collective-permute-start(f32[128,128]{1,0:T(8,128)S(1)} %get-tuple-element.78.refs_0_), channel_id=1, source_target_pairs={{0,16},{4,20},{8,24},{12,28},{16,0},{20,4},{24,8},{28,12},{1,17},{... | collective-permute-start | bytes 196616 | tf_op jit(solution)/shard_map/ppermute | solution.py:884
  70.3 6.7 %collective-permute-start.31 = (f32[128,128]{1,0:T(8,128)S(1)}, f32[128,128]{1,0:T(8,128)S(1)}, u32[]{:S(2)}, u32[]{:S(2)}) collective-permute-start(f32[128,128]{1,0:T(8,128)S(1)} %get-tuple-element.78.refs_0_), channel_id=1, source_target_pairs={{0,24},{4,28},{8,16},{12,20},{16,8},{20,12},{24,0},{28,4},{1,25},{... | collective-permute-start | bytes 196616 | tf_op jit(solution)/shard_map/ppermute | solution.py:884
  71.3 5.9 %collective-permute-start.27 = (f32[128,128]{1,0:T(8,128)S(1)}, f32[128,128]{1,0:T(8,128)S(1)}, u32[]{:S(2)}, u32[]{:S(2)}) collective-permute-start(f32[128,128]{1,0:T(8,128)S(1)} %get-tuple-element.78.refs_0_), channel_id=1, source_target_pairs={{0,8},{4,12},{8,0},{12,4},{16,24},{20,28},{24,16},{28,20},{1,9},{5... | collective-permute-start | bytes 196616 | tf_op jit(solution)/shard_map/ppermute | solution.py:884
  71.3 6.2 %collective-permute-start.26 = (f32[128,128]{1,0:T(8,128)S(1)}, f32[128,128]{1,0:T(8,128)S(1)}, u32[]{:S(2)}, u32[]{:S(2)}) collective-permute-start(f32[128,128]{1,0:T(8,128)S(1)} %get-tuple-element.78.refs_0_), channel_id=1, source_target_pairs={{0,4},{4,0},{8,12},{12,8},{16,20},{20,16},{24,28},{28,24},{1,5},{5... | collective-permute-start | bytes 196616 | tf_op jit(solution)/shard_map/ppermute | solution.py:888
  74.6 3.6 %collective-permute-start.30 = (f32[128,128]{1,0:T(8,128)S(1)}, f32[128,128]{1,0:T(8,128)S(1)}, u32[]{:S(2)}, u32[]{:S(2)}) collective-permute-start(f32[128,128]{1,0:T(8,128)S(1)} %collective-permute-done.29.refs_4_), channel_id=1, source_target_pairs={{0,4},{4,0},{8,12},{12,8},{16,20},{20,16},{24,28},{28,24},{1,5},{5... | collective-permute-start | bytes 196616 | tf_op jit(solution)/shard_map/ppermute | solution.py:888
  76.9 1.3 %collective-permute-start.32 = (f32[128,128]{1,0:T(8,128)S(1)}, f32[128,128]{1,0:T(8,128)S(1)}, u32[]{:S(2)}, u32[]{:S(2)}) collective-permute-start(f32[128,128]{1,0:T(8,128)S(1)} %collective-permute-done.31.refs_6_), channel_id=1, source_target_pairs={{0,4},{4,0},{8,12},{12,8},{16,20},{20,16},{24,28},{28,24},{1,5},{5... | collective-permute-start | bytes 196616 | tf_op jit(solution)/shard_map/ppermute | solution.py:888
  77.1 1.3 %collective-permute-start.28 = (f32[128,128]{1,0:T(8,128)S(1)}, f32[128,128]{1,0:T(8,128)S(1)}, u32[]{:S(2)}, u32[]{:S(2)}) collective-permute-start(f32[128,128]{1,0:T(8,128)S(1)} %collective-permute-done.27.refs_2_), channel_id=1, source_target_pairs={{0,4},{4,0},{8,12},{12,8},{16,20},{20,16},{24,28},{28,24},{1,5},{5... | collective-permute-start | bytes 196616 | tf_op jit(solution)/shard_map/ppermute | solution.py:888
